TPU v7x, 32 devices: a whole 2x2x4 slice. The times are simulated.
32 devices in a mesh: groups: 2 (over y), expert: 8 (over z, x), tensor: 2 (over core).
Axes of the slice: x: 2, y: 2, z: 4, core: 2. Of those that a mesh axis runs over, the one named last changes fastest.
Arguments:
- tokens: bfloat16 [2, 1024, 2048], P(None, ('groups', 'expert')), parts along dimension 1, may hold values from -6 to 6
- routes: int32 [2, 1024, 8], P(None, ('groups', 'expert')), parts along dimension 1, may hold values from 0 to 7, as said below
- probs: float32 [2, 1024, 8], P(None, ('groups', 'expert')), parts along dimension 1, may hold values from 0.02 to 0.3
- up_weight: bfloat16 [8, 2048, 768], P('expert', None, 'tensor'), may hold values from -0.125 to 0.125
- down_weight: bfloat16 [8, 768, 2048], P('expert', None, 'tensor'), may hold values from -0.21875 to 0.21875
- old_place: int32 [16], P('groups'), parts along dimension 0, may hold values from 0 to 7, as said below
- new_place: int32 [32], P('groups'), parts along dimension 0, may hold values from 0 to 7, as said below
Outputs:
- mixed: bfloat16 [2, 1024, 2048], P(None, ('groups', 'expert'), 'tensor'), parts along dimension 1
- slot_rows: int32 [32], P(('groups', 'expert')), parts along dimension 0
There are 2 independent parts, one for each index of `groups`. A program takes and returns all parts, laid end to end along the dimension named above; an argument that names none is the same for every part. Nothing has to cross between parts.
Inputs may be any that keep to these rules, and one draw needn't show every extreme that they name: `routes`: each token names 8 different experts. `old_place`: each expert is held by exactly one old slot. `new_place`: new slot 2 * s holds the expert of old slot s; no expert is held by more than 4 new slots, and some expert by exactly 4.
All inputs are finite; a program needn't handle non-finite values.
Results may differ from a plain program's by a relative error of at most 0.0058.
Values may be sent and summed in bfloat16 or wider, within the bound.
No kernel may reach another device: no remote copies, remote signals or barrier semaphores. Data moves between devices by JAX's collectives and lax.ppermute only.
A program may use at most 128 MiB of HBM per device.

v0:
```python
import functools

import jax
import jax.numpy as jnp
from jax import lax
from jax.experimental import pallas as pl
from jax.experimental.pallas import tpu as pltpu
from jax.sharding import PartitionSpec as P

REPLICAS = 4
LANES = 128
VMEM_BYTES = 67043328


def earlier_same(labels):
    positions = jnp.arange(labels.shape[0], dtype=jnp.int32)
    earlier = positions[None, :] < positions[:, None]
    same_label = labels[:, None] == labels[None, :]
    return jnp.sum((earlier & same_label).astype(jnp.int32), axis=1)


def holder_index(labels, holders):
    matches = labels[:, None] == holders[None, :]
    positions = jnp.arange(holders.shape[0], dtype=jnp.int32)
    return jnp.sum(matches.astype(jnp.int32) * positions[None, :], axis=1)


def replica_slots(flat_routes, new_place, source_index):
    positions = jnp.arange(new_place.shape[0], dtype=jnp.int32)
    same_slot = new_place[:, None] == new_place[None, :]
    occurrence = jnp.sum(
        (same_slot & (positions[None, :] < positions[:, None])).astype(jnp.int32), axis=1
    )
    matches = flat_routes[:, None] == new_place[None, :]
    replicas = jnp.sum(matches.astype(jnp.int32), axis=1)
    wanted = (earlier_same(flat_routes) + source_index) % replicas
    chosen = matches & (occurrence[None, :] == wanted[:, None])
    slot_ids = jnp.sum(chosen.astype(jnp.int32) * positions[None, :], axis=1)
    return (slot_ids, chosen)


def capacity_for(block_rows, targets, token_count):
    return min(token_count, max(2, (5 * block_rows + 4 * targets - 1) // (4 * targets)))


def serve_cells(tokens_mb, probs_mb, cell_ids, target_count, block, up_local, down_local):
    token_count = tokens_mb.shape[0]
    topk_count = cell_ids.shape[0] // token_count
    slots_here = up_local.shape[0]
    cells = jnp.arange(target_count * block, dtype=jnp.int32)
    placed = (cells[:, None] == cell_ids[None, :]).astype(jnp.bfloat16)
    by_token = jnp.sum(placed.reshape(target_count * block, token_count, topk_count), axis=2)
    send_rows = jnp.dot(by_token, tokens_mb, preferred_element_type=jnp.float32).astype(
        jnp.bfloat16
    )
    send_rows = send_rows.reshape(target_count, block, -1)
    received = lax.all_to_all(send_rows, "expert", split_axis=0, concat_axis=0, tiled=True)
    sources = received.shape[0] // slots_here
    grid = received.reshape(sources, slots_here, received.shape[1], received.shape[2])
    hidden = jax.nn.silu(
        jnp.einsum("nscd,sdf->nscf", grid, up_local, preferred_element_type=jnp.float32)
    ).astype(jnp.bfloat16)
    hidden = lax.all_gather(hidden, "tensor", axis=3, tiled=True)
    outputs = jnp.einsum(
        "nscf,sfd->nscd", hidden, down_local, preferred_element_type=jnp.float32
    ).astype(jnp.bfloat16)
    outputs = outputs.reshape(received.shape[0], received.shape[1], -1)
    returned = lax.all_to_all(outputs, "expert", split_axis=0, concat_axis=0, tiled=True)
    flat_back = returned.reshape(target_count * block, -1)
    picked = lax.dot_general(
        placed, flat_back, (((0,), (0,)), ((), ())), preferred_element_type=jnp.float32
    )
    weighted = picked.reshape(token_count, topk_count, -1) * probs_mb[:, :, None]
    return jnp.sum(weighted, axis=1).astype(jnp.bfloat16)


def by_capacity(tokens, routes, probs, up_weight, down_weight, old_place, new_place):
    source_index = lax.axis_index("expert")
    devices = lax.axis_size("expert")
    token_count = tokens.shape[1]
    topk_count = routes.shape[2]
    block_rows = token_count * topk_count
    expert_count = old_place.shape[0]
    slot_count = new_place.shape[0]
    early_cap = capacity_for(block_rows, expert_count, token_count)
    later_cap = capacity_for(block_rows, slot_count, token_count)
    early_routes = routes[0].reshape(-1)
    later_routes = routes[1].reshape(-1)
    early_slots = holder_index(early_routes, old_place)
    early_rank = earlier_same(early_slots)
    early_cells = jnp.where(early_rank < early_cap, early_slots * early_cap + early_rank, -1)
    later_slots, chosen = replica_slots(later_routes, new_place, source_index)
    slot_counts = lax.psum(jnp.sum(chosen.astype(jnp.int32), axis=0), "expert")
    slot_dev = slot_count // devices
    slot_rows = lax.dynamic_slice_in_dim(slot_counts, source_index * slot_dev, slot_dev, 0)
    later_rank = earlier_same(later_slots)
    later_kept = later_rank < later_cap
    early_out = serve_cells(
        tokens[0], probs[0], early_cells, expert_count, early_cap, up_weight, down_weight
    )
    homes = holder_index(later_routes, old_place)
    home_block = min(token_count, REPLICAS * later_cap)
    home_labels = jnp.where(later_kept, homes, -1)
    home_rank = earlier_same(home_labels)
    later_cells = jnp.where(later_kept, homes * home_block + home_rank, -1)
    later_out = serve_cells(
        tokens[1], probs[1], later_cells, expert_count, home_block, up_weight, down_weight
    )
    return (jnp.stack([early_out, later_out]), slot_rows)


def ring_order(mesh):
    line = mesh.devices[0, :, 0]
    count = len(line)
    if count > 16 or not all(hasattr(d, "coords") for d in line):
        return tuple(range(count))
    spots = [tuple(d.coords) for d in line]

    def near(a, b):
        return sum(abs(i - j) for i, j in zip(spots[a], spots[b])) == 1

    def extend(path):
        if len(path) == count:
            return path if near(path[-1], path[0]) else None
        for spot in range(count):
            if spot not in path and near(path[-1], spot):
                if found := extend(path + [spot]):
                    return found
        return None

    return tuple(extend([0]) or range(count))


def pack_kernel(caps, routes_in, probs_in, old_in, new_in, tokens, first, second, slot_rows, *scratch):
    routes, probs, old_place, new_place, sems = scratch
    core = lax.axis_index("tensor")
    width = tokens.shape[2]
    token_count = routes.shape[2]
    experts, slots = old_place.shape[0], new_place.shape[0]
    lanes = first.shape[1] - width
    pairs = (
        (old_in, old_place),
        (new_in, new_place),
        (routes_in, routes),
        (probs_in, probs),
        (tokens.at[core], first.at[:, :width]),
        (tokens.at[1 - core], second.at[:, :width]),
    )
    copies = [pltpu.make_async_copy(src, dst, sems.at[i]) for i, (src, dst) in enumerate(pairs)]
    for copy in copies:
        copy.start()
    for copy in copies[:4]:
        copy.wait()
    token = lax.broadcasted_iota(jnp.int32, (1, token_count), 1)

    def holders_of(expert):
        return sum((new_place[s] == expert).astype(jnp.int32) for s in range(slots))

    limits = [[caps[0]] * experts, [caps[1] * holders_of(old_place[e]) for e in range(experts)]]
    for out, batch in ((first, core), (second, 1 - core)):
        highs, lows = [], []
        for e in range(experts):
            named = routes[batch] == old_place[e]
            weight = jnp.sum(jnp.where(named, probs[batch], 0.0), axis=0, keepdims=True)
            served = jnp.where(batch == 0, limits[0][e], limits[1][e])
            weight = jnp.where(token < served, weight, 0.0)
            high = weight.astype(jnp.bfloat16).astype(jnp.float32)
            highs.append(high)
            lows.append(weight - high)
        pad = jnp.zeros((lanes - 2 * experts, token_count), jnp.float32)
        out[:, width:] = jnp.concatenate(highs + lows + [pad], axis=0).T.astype(jnp.bfloat16)

    devices = lax.axis_size("expert")
    mine = slots // devices
    for j in range(mine):
        slot = lax.axis_index("expert") * mine + j
        expert = new_place[slot]
        holders = holders_of(expert)
        place = sum(
            ((new_place[s] == expert) & (s < slot)).astype(jnp.int32) for s in range(slots)
        )
        count = jnp.int32(0)
        for source in range(devices):
            start = lax.rem(place - source + devices * holders, holders)
            count += lax.div(token_count - 1 - start + holders, holders)
        slot_rows[j] = count
    for copy in copies[4:]:
        copy.wait()


def pack(caps, tokens, routes, probs, old_place, new_place):
    token_count, width = tokens.shape[1:]
    experts = old_place.shape[0]
    lanes = -(-2 * experts // LANES) * LANES
    chunk = jax.ShapeDtypeStruct((token_count, width + lanes), tokens.dtype)
    vmem, smem = pl.BlockSpec(memory_space=pltpu.VMEM), pl.BlockSpec(memory_space=pltpu.SMEM)
    mine = new_place.shape[0] // lax.axis_size("expert")
    routes, probs = routes.transpose(0, 2, 1), probs.transpose(0, 2, 1)
    return pl.pallas_call(
        functools.partial(pack_kernel, caps),
        out_shape=(chunk, chunk, jax.ShapeDtypeStruct((mine,), jnp.int32)),
        in_specs=[pl.BlockSpec(memory_space=pltpu.HBM)] * 5,
        out_specs=(vmem, vmem, smem),
        scratch_shapes=[
            pltpu.VMEM(routes.shape, routes.dtype),
            pltpu.VMEM(probs.shape, probs.dtype),
            pltpu.SMEM(old_place.shape, jnp.int32),
            pltpu.SMEM(new_place.shape, jnp.int32),
            pltpu.SemaphoreType.DMA((6,)),
        ],
        compiler_params=pltpu.CompilerParams(
            vmem_limit_bytes=VMEM_BYTES - (4 << 20)
        ),
    )(routes, probs, old_place, new_place, tokens)


def load_kernel(up, down, up_here, down_here, sems):
    copies = [
        pltpu.make_async_copy(up, up_here, sems.at[0]),
        pltpu.make_async_copy(down, down_here, sems.at[1]),
    ]
    for copy in copies:
        copy.start()
    for copy in copies:
        copy.wait()


def load(up, down):
    vmem = pl.BlockSpec(memory_space=pltpu.VMEM)
    return pl.pallas_call(
        load_kernel,
        out_shape=(
            jax.ShapeDtypeStruct(up.shape, up.dtype),
            jax.ShapeDtypeStruct(down.shape, down.dtype),
        ),
        in_specs=[pl.BlockSpec(memory_space=pltpu.HBM)] * 2,
        out_specs=(vmem, vmem),
        scratch_shapes=[pltpu.SemaphoreType.DMA((2,))],
        compiler_params=pltpu.CompilerParams(vmem_limit_bytes=VMEM_BYTES - (14 << 20)),
        cost_estimate=pl.CostEstimate(
            flops=0, bytes_accessed=4 * (up.size + down.size), transcendentals=0
        ),
    )(up, down)


def expert_kernel(chunks, width, experts, *refs):
    rows, refs = refs[:chunks], refs[chunks:]
    (up_own, up_pair, down_own, down_pair), refs = refs[:4], refs[4:]
    outs, x_buf = refs[:chunks], refs[chunks]
    slot, core = lax.axis_index("expert"), lax.axis_index("tensor")
    size = rows[0].shape[0]
    lane = lax.broadcasted_iota(jnp.int32, (size, rows[0].shape[1] - width), 1)
    mine = (lane == slot) | (lane == experts + slot)
    scales = []
    for i, row in enumerate(rows):
        x_buf[i * size : (i + 1) * size, :] = row[:, :width]
        side = row[:, width:].astype(jnp.float32)
        scales.append(jnp.sum(jnp.where(mine, side, 0.0), axis=1, keepdims=True))
    scale = jnp.concatenate(scales, axis=0)
    x = x_buf[...]
    parts = []
    for up in (up_own, up_pair):
        v = jnp.dot(x, up[...], preferred_element_type=jnp.float32)
        parts.append((v / (1.0 + jnp.exp(-v))).astype(jnp.bfloat16))
    low = jnp.where(core == 0, parts[0], parts[1])
    high = jnp.where(core == 0, parts[1], parts[0])
    hidden = jnp.concatenate([low, high], axis=1)
    half = down_own.shape[1]
    for j, down in enumerate((down_own, down_pair)):
        y = jnp.dot(hidden, down[...], preferred_element_type=jnp.float32)
        y = y.astype(jnp.bfloat16).astype(jnp.float32) * scale
        for i, out in enumerate(outs):
            out[:, j * half : (j + 1) * half] = y[i * size : (i + 1) * size].astype(out.dtype)


def expert_rows(rows, weights, width, experts, out_types):
    chunks, size = len(rows), rows[0].shape[0]
    up = weights[0]
    total = chunks * size
    vmem = pl.BlockSpec(memory_space=pltpu.VMEM)
    return pl.pallas_call(
        functools.partial(expert_kernel, chunks, width, experts),
        out_shape=[jax.ShapeDtypeStruct((size, width), t) for t in out_types],
        in_specs=[vmem] * (chunks + 4),
        out_specs=[vmem] * chunks,
        scratch_shapes=[pltpu.VMEM((total, width), jnp.bfloat16)],
        compiler_params=pltpu.CompilerParams(vmem_limit_bytes=20 << 20),
        cost_estimate=pl.CostEstimate(
            flops=2 * total * width * 4 * up.shape[1],
            bytes_accessed=8 * total * width,
            transcendentals=2 * total * up.shape[1],
        ),
    )(*rows, *weights)


def last_add_kernel(part, arrived, kept, leaving):
    half = kept.shape[1]
    kept[...] = part[:, :half] + arrived[:, :half].astype(jnp.float32)
    leaving[...] = (part[:, half:] + arrived[:, half:].astype(jnp.float32)).astype(leaving.dtype)


def last_add(part, arrived):
    size, half = part.shape[0], part.shape[1] // 2
    vmem = pl.BlockSpec(memory_space=pltpu.VMEM)
    return pl.pallas_call(
        last_add_kernel,
        out_shape=(
            jax.ShapeDtypeStruct((size, half), jnp.float32),
            jax.ShapeDtypeStruct((size, half), jnp.bfloat16),
        ),
        in_specs=[vmem, vmem],
        out_specs=(vmem, vmem),
        compiler_params=pltpu.CompilerParams(vmem_limit_bytes=4 << 20),
    )(part, arrived)


def finish_kernel(kept, from_second, second, from_first, mixed):
    core = lax.axis_index("tensor")
    half = mixed.shape[2]
    mixed[core] = (kept[...] + from_second[...].astype(jnp.float32)).astype(mixed.dtype)
    other = second[:, :half].astype(jnp.float32) + from_first[...].astype(jnp.float32)
    mixed[1 - core] = other.astype(mixed.dtype)


def finish(kept, from_second, second, from_first):
    vmem = pl.BlockSpec(memory_space=pltpu.VMEM)
    return pl.pallas_call(
        finish_kernel,
        out_shape=jax.ShapeDtypeStruct((2, *kept.shape), jnp.bfloat16),
        in_specs=[vmem] * 4,
        out_specs=vmem,
        compiler_params=pltpu.CompilerParams(vmem_limit_bytes=4 << 20),
    )(kept, from_second, second, from_first)


def by_ring(ring, tokens, routes, probs, up_weight, down_weight, old_place, new_place):
    devices = lax.axis_size("expert")
    token_count, width = tokens.shape[1], tokens.shape[2]
    experts = old_place.shape[0]
    block_rows = token_count * routes.shape[2]
    both = ("expert", "tensor")
    steps = devices // 2
    ahead = []
    for spot, here in enumerate(ring):
        there = ring[(spot + 1) % devices]
        ahead += [(2 * here, 2 * there), (2 * there + 1, 2 * here + 1)]
    back = [(b, a) for a, b in ahead]
    swap = [(0, 1), (1, 0)]
    f32, bf16 = jnp.float32, jnp.bfloat16

    caps = (
        capacity_for(block_rows, experts, token_count),
        capacity_for(block_rows, new_place.shape[0], token_count),
    )
    own_first, own_second, slot_rows = pack(caps, tokens, routes, probs, old_place, new_place)

    first, second = [own_first], [own_second]
    for step in range(1, steps + 1):
        first.append(lax.ppermute(first[-1], both, ahead))
        if step < steps:
            second.append(lax.ppermute(second[-1], both, ahead))
    up_own, down_own = up_weight[0], down_weight[0]
    up_pair = lax.ppermute(up_own, "tensor", swap)
    down_pair = lax.ppermute(down_own, "tensor", swap)
    up_here, down_here = load(up_own, down_own)
    weights = (up_here, up_pair, down_here, down_pair)

    def run(rows, out_types):
        return expert_rows(rows, weights, width, experts, out_types)

    part_first, part_second = [None] * (steps + 1), [None] * steps
    part_first[0], part_first[1], part_second[1] = run([first[0], first[1], second[1]], [f32] * 3)
    for step in range(2, steps):
        part_first[step], part_second[step] = run(
            [first[step], second[step]], [f32, bf16 if step == steps - 1 else f32]
        )
    (part_first[steps],) = run([first[steps]], [bf16])

    sum_first, sum_second = part_first[steps], part_second[steps - 1]
    for step in range(steps - 1, -1, -1):
        sum_first = lax.ppermute(sum_first, both, back)
        if step > 0:
            sum_first = (part_first[step] + sum_first.astype(f32)).astype(bf16)
        if step < steps - 1:
            sum_second = lax.ppermute(sum_second, both, back)
            if step > 0:
                sum_second = (part_second[step] + sum_second.astype(f32)).astype(bf16)
    kept, leaving = last_add(part_first[0], sum_first)
    from_second = lax.ppermute(sum_second[:, width // 2 :], "tensor", swap)
    from_first = lax.ppermute(leaving, "tensor", swap)
    return (finish(kept, from_second, sum_second, from_first), slot_rows)


def on_device(ring, tokens, routes, probs, up_weight, down_weight, old_place, new_place):
    devices = lax.axis_size("expert")
    experts = old_place.shape[0]
    arrays = (tokens, routes, probs, up_weight, down_weight, old_place, new_place)
    if (
        experts == routes.shape[2]
        and experts == devices
        and devices >= 6
        and devices % 2 == 0
        and lax.axis_size("tensor") == 2
        and tokens.shape[0] == 2
    ):
        return by_ring(ring, *arrays)
    return by_capacity(*arrays)


def solution(mesh):
    placed = (
        P(None, ("groups", "expert"), None),
        P(None, ("groups", "expert"), None),
        P(None, ("groups", "expert"), None),
        P("expert", None, "tensor"),
        P("expert", None, "tensor"),
        P("groups"),
        P("groups"),
    )
    return jax.shard_map(
        functools.partial(on_device, ring_order(mesh)),
        mesh=mesh,
        in_specs=placed,
        out_specs=(P(None, ("groups", "expert"), "tensor"), P(("groups", "expert"))),
        check_vma=False,
    )
```

profile of v0, /device:TPU:0, one launch (start us, length us, event | category | flops | bytes accessed | tf_op | source)
XLA Modules:
  0.0 63.4 jit_solution(17168922391227759739)
XLA Ops:
  0.6 0.6 collective-permute-start.2
  1.2 0.1 collective-permute-start.3
  1.3 2.0 %shard_map.86 = (bf16[64,2176]{1,0:T(8,128)(2,1)}, bf16[64,2176]{1,0:T(8,128)(2,1)}, s32[2]{0:T(128)}) custom-call(s32[2,8,64]{2,1,0:T(8,128)} %bitcast.8, f32[2,8,64]{2,1,0:T(8,128)} %bitcast.9, s32[8]{0:T(128)} %old_in.1, s32[16]{0:T(128)} %new_in.1, bf16[2,64,2048]{2,1,0:T(8,128)(2,1)} %tokens.1), custom_call_target="tpu_custom_call" | custom-call | tf_op jit(solution)/shard_map/pallas_call | solution.py:199
  3.2 3.0 %collective-permute-start = (bf16[64,2176]{1,0:T(8,128)(2,1)}, bf16[64,2176]{1,0:T(8,128)(2,1)S(1)}, u32[]{:S(2)}, u32[]{:S(2)}) collective-permute-start(bf16[64,2176]{1,0:T(8,128)(2,1)} %get-tuple-element.16.refs_0_), channel_id=1, source_target_pairs={{0,2},{3,1},{2,6},{7,3},{6,10},{11,7},{10,14},{15,11},{14,12},{13,... | collective-permute-start | bytes 835592 | tf_op jit(solution)/shard_map/ppermute | solution.py:359
  6.2 4.8 %collective-permute-done.refs_1_ = bf16[64,2176]{1,0:T(8,128)(2,1)S(1)} collective-permute-done((bf16[64,2176]{1,0:T(8,128)(2,1)}, bf16[64,2176]{1,0:T(8,128)(2,1)S(1)}, u32[]{:S(2)}, u32[]{:S(2)}) %collective-permute-start) | collective-permute-done | bytes 278560 | tf_op jit(solution)/shard_map/ppermute | solution.py:359
  11.0 1.9 %collective-permute-start.4 = (bf16[64,2176]{1,0:T(8,128)(2,1)S(1)}, bf16[64,2176]{1,0:T(8,128)(2,1)S(1)}, u32[]{:S(2)}, u32[]{:S(2)}) collective-permute-start(bf16[64,2176]{1,0:T(8,128)(2,1)S(1)} %collective-permute-done.refs_1_), channel_id=1, source_target_pairs={{0,2},{3,1},{2,6},{7,3},{6,10},{11,7},{10,14},{15,11},{14,12},{13,... | collective-permute-start | bytes 835592 | tf_op jit(solution)/shard_map/ppermute | solution.py:359
  13.0 1.6 %collective-permute-start.1 = (bf16[64,2176]{1,0:T(8,128)(2,1)}, bf16[64,2176]{1,0:T(8,128)(2,1)S(1)}, u32[]{:S(2)}, u32[]{:S(2)}) collective-permute-start(bf16[64,2176]{1,0:T(8,128)(2,1)} %get-tuple-element.17), channel_id=1, source_target_pairs={{0,2},{3,1},{2,6},{7,3},{6,10},{11,7},{10,14},{15,11},{14,12},{13,... | collective-permute-start | bytes 835592 | tf_op jit(solution)/shard_map/ppermute | solution.py:361
  14.5 3.0 %collective-permute-done.4.refs_0_ = bf16[64,2176]{1,0:T(8,128)(2,1)S(1)} collective-permute-done((bf16[64,2176]{1,0:T(8,128)(2,1)S(1)}, bf16[64,2176]{1,0:T(8,128)(2,1)S(1)}, u32[]{:S(2)}, u32[]{:S(2)}) %collective-permute-start.4) | collective-permute-done | bytes 278560 | tf_op jit(solution)/shard_map/ppermute | solution.py:359
  17.6 1.9 %collective-permute-start.6 = (bf16[64,2176]{1,0:T(8,128)(2,1)S(1)}, bf16[64,2176]{1,0:T(8,128)(2,1)S(1)}, u32[]{:S(2)}, u32[]{:S(2)}) collective-permute-start(bf16[64,2176]{1,0:T(8,128)(2,1)S(1)} %collective-permute-done.4.refs_0_), channel_id=1, source_target_pairs={{0,2},{3,1},{2,6},{7,3},{6,10},{11,7},{10,14},{15,11},{14,12},{13,... | collective-permute-start | bytes 835592 | tf_op jit(solution)/shard_map/ppermute | solution.py:359
  19.5 1.0 %collective-permute-done.1.refs_2_ = bf16[64,2176]{1,0:T(8,128)(2,1)S(1)} collective-permute-done((bf16[64,2176]{1,0:T(8,128)(2,1)}, bf16[64,2176]{1,0:T(8,128)(2,1)S(1)}, u32[]{:S(2)}, u32[]{:S(2)}) %collective-permute-start.1) | collective-permute-done | bytes 278560 | tf_op jit(solution)/shard_map/ppermute | solution.py:361
  20.6 1.9 %collective-permute-start.5 = (bf16[64,2176]{1,0:T(8,128)(2,1)S(1)}, bf16[64,2176]{1,0:T(8,128)(2,1)S(1)}, u32[]{:S(2)}, u32[]{:S(2)}) collective-permute-start(bf16[64,2176]{1,0:T(8,128)(2,1)S(1)} %collective-permute-done.1.refs_2_), channel_id=1, source_target_pairs={{0,2},{3,1},{2,6},{7,3},{6,10},{11,7},{10,14},{15,11},{14,12},{13,... | collective-permute-start | bytes 835592 | tf_op jit(solution)/shard_map/ppermute | solution.py:361
  22.5 1.6 %collective-permute-done.6.refs_0_ = bf16[64,2176]{1,0:T(8,128)(2,1)S(1)} collective-permute-done((bf16[64,2176]{1,0:T(8,128)(2,1)S(1)}, bf16[64,2176]{1,0:T(8,128)(2,1)S(1)}, u32[]{:S(2)}, u32[]{:S(2)}) %collective-permute-start.6) | collective-permute-done | bytes 278560 | tf_op jit(solution)/shard_map/ppermute | solution.py:359
  24.1 1.9 %collective-permute-start.8 = (bf16[64,2176]{1,0:T(8,128)(2,1)S(1)}, bf16[64,2176]{1,0:T(8,128)(2,1)S(1)}, u32[]{:S(2)}, u32[]{:S(2)}) collective-permute-start(bf16[64,2176]{1,0:T(8,128)(2,1)S(1)} %collective-permute-done.6.refs_0_), channel_id=1, source_target_pairs={{0,2},{3,1},{2,6},{7,3},{6,10},{11,7},{10,14},{15,11},{14,12},{13,... | collective-permute-start | bytes 835592 | tf_op jit(solution)/shard_map/ppermute | solution.py:359
  26.1 1.0 %collective-permute-done.5.refs_1_ = bf16[64,2176]{1,0:T(8,128)(2,1)S(1)} collective-permute-done((bf16[64,2176]{1,0:T(8,128)(2,1)S(1)}, bf16[64,2176]{1,0:T(8,128)(2,1)S(1)}, u32[]{:S(2)}, u32[]{:S(2)}) %collective-permute-start.5) | collective-permute-done | bytes 278560 | tf_op jit(solution)/shard_map/ppermute | solution.py:361
  27.1 1.9 %collective-permute-start.7 = (bf16[64,2176]{1,0:T(8,128)(2,1)S(1)}, bf16[64,2176]{1,0:T(8,128)(2,1)S(1)}, u32[]{:S(2)}, u32[]{:S(2)}) collective-permute-start(bf16[64,2176]{1,0:T(8,128)(2,1)S(1)} %collective-permute-done.5.refs_1_), channel_id=1, source_target_pairs={{0,2},{3,1},{2,6},{7,3},{6,10},{11,7},{10,14},{15,11},{14,12},{13,... | collective-permute-start | bytes 835592 | tf_op jit(solution)/shard_map/ppermute | solution.py:361
  29.0 1.9 %shard_map.87 = (bf16[2048,384]{1,0:T(8,128)(2,1)S(1)}, bf16[768,1024]{1,0:T(8,128)(2,1)S(1)}) custom-call(bf16[2048,384]{1,0:T(8,128)(2,1)} %bitcast.5, bf16[768,1024]{1,0:T(8,128)(2,1)} %bitcast.7), custom_call_target="tpu_custom_call" | custom-call | bytes 6291456 | tf_op jit(solution)/shard_map/pallas_call | solution.py:230
  30.9 0.0 collective-permute-done.8.refs_0_
  31.0 0.0 collective-permute-done.2.refs_4_.refs_3_.refs_2_
  31.0 0.0 collective-permute-done.3.refs_6_.refs_5_.refs_4_
  31.0 1.3 %shard_map.91 = bf16[64,2048]{1,0:T(8,128)(2,1)S(1)} custom-call(bf16[64,2176]{1,0:T(8,128)(2,1)S(1)} %collective-permute-done.8.refs_0_, bf16[2048,384]{1,0:T(8,128)(2,1)S(1)} %get-tuple-element.18.refs_3_.refs_2_.refs_1_, bf16[2048,384]{1,0:T(8,128)(2,1)S(1)} %collective-permute-done.2.refs_4_.refs_3_.refs_2_, ...), custom_call_target="tpu_custom_call" | custom-call | flops 402653184 | bytes 1048576 | tf_op jit(solution)/shard_map/pallas_call | solution.py:281
  32.3 1.8 %collective-permute-start.9 = (bf16[64,2048]{1,0:T(8,128)(2,1)S(1)}, bf16[64,2048]{1,0:T(8,128)(2,1)S(1)}, u32[]{:S(2)}, u32[]{:S(2)}) collective-permute-start(bf16[64,2048]{1,0:T(8,128)(2,1)S(1)} %shard_map.91), channel_id=1, source_target_pairs={{2,0},{1,3},{6,2},{3,7},{10,6},{7,11},{14,10},{11,15},{12,14},{15,... | collective-permute-start | bytes 786440 | tf_op jit(solution)/shard_map/ppermute | solution.py:381
  34.0 0.9 %collective-permute-done.7.refs_1_ = bf16[64,2176]{1,0:T(8,128)(2,1)S(1)} collective-permute-done((bf16[64,2176]{1,0:T(8,128)(2,1)S(1)}, bf16[64,2176]{1,0:T(8,128)(2,1)S(1)}, u32[]{:S(2)}, u32[]{:S(2)}) %collective-permute-start.7) | collective-permute-done | bytes 278560 | tf_op jit(solution)/shard_map/ppermute | solution.py:361
  34.9 1.3 %shard_map.90 = (f32[64,2048]{1,0:T(8,128)S(1)}, bf16[64,2048]{1,0:T(8,128)(2,1)S(1)}) custom-call(bf16[64,2176]{1,0:T(8,128)(2,1)S(1)} %collective-permute-done.6.refs_0_, bf16[64,2176]{1,0:T(8,128)(2,1)S(1)} %collective-permute-done.7.refs_1_, bf16[2048,384]{1,0:T(8,128)(2,1)S(1)} %get-tuple-element.18.refs_3_.refs_2_.refs_1_, ...), custom_call_target="tpu_custom_call" | custom-call | flops 805306368 | bytes 2097152 | tf_op jit(solution)/shard_map/pallas_call | solution.py:281
  36.2 0.0 copy-start
  36.2 2.4 %collective-permute-start.13 = (bf16[64,2048]{1,0:T(8,128)(2,1)S(1)}, bf16[64,2048]{1,0:T(8,128)(2,1)S(1)}, u32[]{:S(2)}, u32[]{:S(2)}) collective-permute-start(bf16[64,2048]{1,0:T(8,128)(2,1)S(1)} %get-tuple-element.27), channel_id=1, source_target_pairs={{2,0},{1,3},{6,2},{3,7},{10,6},{7,11},{14,10},{11,15},{12,14},{15,... | collective-permute-start | bytes 786440 | tf_op jit(solution)/shard_map/ppermute | solution.py:385
  38.6 1.3 %shard_map.89 = (f32[64,2048]{1,0:T(8,128)S(1)}, f32[64,2048]{1,0:T(8,128)S(1)}) custom-call(bf16[64,2176]{1,0:T(8,128)(2,1)S(1)} %collective-permute-done.4.refs_0_, bf16[64,2176]{1,0:T(8,128)(2,1)S(1)} %collective-permute-done.5.refs_1_, bf16[2048,384]{1,0:T(8,128)(2,1)S(1)} %get-tuple-element.18.refs_3_.refs_2_.refs_1_, ...), custom_call_target="tpu_custom_call" | custom-call | flops 805306368 | bytes 2097152 | tf_op jit(solution)/shard_map/pallas_call | solution.py:281
  39.9 0.0 copy-done
  39.9 1.8 %shard_map.88 = (f32[64,2048]{1,0:T(8,128)S(1)}, f32[64,2048]{1,0:T(8,128)S(1)}, f32[64,2048]{1,0:T(8,128)S(1)}) custom-call(bf16[64,2176]{1,0:T(8,128)(2,1)S(1)} %copy-done, bf16[64,2176]{1,0:T(8,128)(2,1)S(1)} %collective-permute-done.refs_1_, bf16[64,2176]{1,0:T(8,128)(2,1)S(1)} %collective-permute-done.1.refs_2_, ...), custom_call_target="tpu_custom_call" | custom-call | flops 1207959552 | bytes 3145728 | tf_op jit(solution)/shard_map/pallas_call | solution.py:281
  41.7 0.0 collective-permute-done.9
  41.7 1.6 %collective-permute-start.10 = (bf16[64,2048]{1,0:T(8,128)(2,1)S(1)}, bf16[64,2048]{1,0:T(8,128)(2,1)S(1)}, u32[]{:S(2)}, u32[]{:S(2)}) collective-permute-start(bf16[64,2048]{1,0:T(8,128)(2,1)S(1)} %add_convert_fusion.4), channel_id=1, source_target_pairs={{2,0},{1,3},{6,2},{3,7},{10,6},{7,11},{14,10},{11,15},{12,14},{15,... | collective-permute-start | bytes 786440 | tf_op jit(solution)/shard_map/ppermute | solution.py:381
  43.4 0.0 collective-permute-done.13
  43.4 1.7 %collective-permute-start.14 = (bf16[64,2048]{1,0:T(8,128)(2,1)S(1)}, bf16[64,2048]{1,0:T(8,128)(2,1)S(1)}, u32[]{:S(2)}, u32[]{:S(2)}) collective-permute-start(bf16[64,2048]{1,0:T(8,128)(2,1)S(1)} %add_convert_fusion.1), channel_id=1, source_target_pairs={{2,0},{1,3},{6,2},{3,7},{10,6},{7,11},{14,10},{11,15},{12,14},{15,... | collective-permute-start | bytes 786440 | tf_op jit(solution)/shard_map/ppermute | solution.py:385
  45.1 3.0 %collective-permute-done.10 = bf16[64,2048]{1,0:T(8,128)(2,1)S(1)} collective-permute-done((bf16[64,2048]{1,0:T(8,128)(2,1)S(1)}, bf16[64,2048]{1,0:T(8,128)(2,1)S(1)}, u32[]{:S(2)}, u32[]{:S(2)}) %collective-permute-start.10) | collective-permute-done | bytes 262176 | tf_op jit(solution)/shard_map/ppermute | solution.py:381
  48.2 1.6 %collective-permute-start.11 = (bf16[64,2048]{1,0:T(8,128)(2,1)S(1)}, bf16[64,2048]{1,0:T(8,128)(2,1)S(1)}, u32[]{:S(2)}, u32[]{:S(2)}) collective-permute-start(bf16[64,2048]{1,0:T(8,128)(2,1)S(1)} %add_convert_fusion.3), channel_id=1, source_target_pairs={{2,0},{1,3},{6,2},{3,7},{10,6},{7,11},{14,10},{11,15},{12,14},{15,... | collective-permute-start | bytes 786440 | tf_op jit(solution)/shard_map/ppermute | solution.py:381
  49.8 1.1 %collective-permute-done.14 = bf16[64,2048]{1,0:T(8,128)(2,1)S(1)} collective-permute-done((bf16[64,2048]{1,0:T(8,128)(2,1)S(1)}, bf16[64,2048]{1,0:T(8,128)(2,1)S(1)}, u32[]{:S(2)}, u32[]{:S(2)}) %collective-permute-start.14) | collective-permute-done | bytes 262176 | tf_op jit(solution)/shard_map/ppermute | solution.py:385
  51.0 1.6 %collective-permute-start.15 = (bf16[64,2048]{1,0:T(8,128)(2,1)S(1)}, bf16[64,2048]{1,0:T(8,128)(2,1)S(1)}, u32[]{:S(2)}, u32[]{:S(2)}) collective-permute-start(bf16[64,2048]{1,0:T(8,128)(2,1)S(1)} %add_convert_fusion), channel_id=1, source_target_pairs={{2,0},{1,3},{6,2},{3,7},{10,6},{7,11},{14,10},{11,15},{12,14},{15,... | collective-permute-start | bytes 786440 | tf_op jit(solution)/shard_map/ppermute | solution.py:385
  52.7 2.0 %collective-permute-done.11 = bf16[64,2048]{1,0:T(8,128)(2,1)S(1)} collective-permute-done((bf16[64,2048]{1,0:T(8,128)(2,1)S(1)}, bf16[64,2048]{1,0:T(8,128)(2,1)S(1)}, u32[]{:S(2)}, u32[]{:S(2)}) %collective-permute-start.11) | collective-permute-done | bytes 262176 | tf_op jit(solution)/shard_map/ppermute | solution.py:381
  54.6 0.1 add_convert_fusion.2
  54.7 1.6 %collective-permute-start.12 = (bf16[64,2048]{1,0:T(8,128)(2,1)S(1)}, bf16[64,2048]{1,0:T(8,128)(2,1)S(1)}, u32[]{:S(2)}, u32[]{:S(2)}) collective-permute-start(bf16[64,2048]{1,0:T(8,128)(2,1)S(1)} %add_convert_fusion.2), channel_id=1, source_target_pairs={{2,0},{1,3},{6,2},{3,7},{10,6},{7,11},{14,10},{11,15},{12,14},{15,... | collective-permute-start | bytes 786440 | tf_op jit(solution)/shard_map/ppermute | solution.py:381
  56.3 1.1 %collective-permute-done.15.second = bf16[64,2048]{1,0:T(8,128)(2,1)S(1)} collective-permute-done((bf16[64,2048]{1,0:T(8,128)(2,1)S(1)}, bf16[64,2048]{1,0:T(8,128)(2,1)S(1)}, u32[]{:S(2)}, u32[]{:S(2)}) %collective-permute-start.15) | collective-permute-done | bytes 262176 | tf_op jit(solution)/shard_map/ppermute | solution.py:385
  57.5 0.1 collective-permute-start.16
  57.5 3.6 %collective-permute-done.12.arrived = bf16[64,2048]{1,0:T(8,128)(2,1)S(1)} collective-permute-done((bf16[64,2048]{1,0:T(8,128)(2,1)S(1)}, bf16[64,2048]{1,0:T(8,128)(2,1)S(1)}, u32[]{:S(2)}, u32[]{:S(2)}) %collective-permute-start.12) | collective-permute-done | bytes 262176 | tf_op jit(solution)/shard_map/ppermute | solution.py:381
  61.1 0.1 shard_map.92
  61.2 0.1 collective-permute-start.17
  61.3 0.0 collective-permute-done.16.from_second
  61.3 1.3 %collective-permute-done.17.from_first = bf16[64,1024]{1,0:T(8,128)(2,1)S(1)} collective-permute-done((bf16[64,1024]{1,0:T(8,128)(2,1)S(1)}, bf16[64,1024]{1,0:T(8,128)(2,1)S(1)}, u32[]{:S(2)}, u32[]{:S(2)}) %collective-permute-start.17) | collective-permute-done | bytes 131104 | tf_op jit(solution)/shard_map/ppermute | solution.py:390
  62.6 0.8 %shard_map.93 = bf16[2,64,1024]{2,1,0:T(8,128)(2,1)} custom-call(f32[64,1024]{1,0:T(8,128)S(1)} %get-tuple-element.24.kept, bf16[64,1024]{1,0:T(8,128)(2,1)S(1)} %collective-permute-done.16.from_second, bf16[64,2048]{1,0:T(8,128)(2,1)S(1)} %collective-permute-done.15.second, bf16[64,1024]{1,0:T(8,128)(2,1)S(1)} %collective-permute-done.17.from_first), custom_call_target="tpu_custom_call" | custom-call | tf_op jit(solution)/shard_map/pallas_call | solution.py:327
  (5 shorter events, 0.2 us)
Async XLA Ops:
  0.6 30.3 %collective-permute-start.2 = (bf16[2048,384]{1,0:T(8,128)(2,1)}, bf16[2048,384]{1,0:T(8,128)(2,1)S(1)}, u32[]{:S(2)}, u32[]{:S(2)}) collective-permute-start(bf16[2048,384]{1,0:T(8,128)(2,1)} %bitcast.4), channel_id=1, source_target_pairs={{0,1},{1,0},{2,3},{3,2},{4,5},{5,4},{6,7},{7,6},{8,9},{9,8},{10,11... | collective-permute-start | bytes 4718600 | tf_op jit(solution)/shard_map/ppermute | solution.py:363
  1.2 29.8 %collective-permute-start.3 = (bf16[768,1024]{1,0:T(8,128)(2,1)}, bf16[768,1024]{1,0:T(8,128)(2,1)S(1)}, u32[]{:S(2)}, u32[]{:S(2)}) collective-permute-start(bf16[768,1024]{1,0:T(8,128)(2,1)} %bitcast.6), channel_id=1, source_target_pairs={{0,1},{1,0},{2,3},{3,2},{4,5},{5,4},{6,7},{7,6},{8,9},{9,8},{10,11... | collective-permute-start | bytes 4718600 | tf_op jit(solution)/shard_map/ppermute | solution.py:364
  3.2 7.8 %collective-permute-start = (bf16[64,2176]{1,0:T(8,128)(2,1)}, bf16[64,2176]{1,0:T(8,128)(2,1)S(1)}, u32[]{:S(2)}, u32[]{:S(2)}) collective-permute-start(bf16[64,2176]{1,0:T(8,128)(2,1)} %get-tuple-element.16.refs_0_), channel_id=1, source_target_pairs={{0,2},{3,1},{2,6},{7,3},{6,10},{11,7},{10,14},{15,11},{14,12},{13,... | collective-permute-start | bytes 835592 | tf_op jit(solution)/shard_map/ppermute | solution.py:359
  11.0 6.5 %collective-permute-start.4 = (bf16[64,2176]{1,0:T(8,128)(2,1)S(1)}, bf16[64,2176]{1,0:T(8,128)(2,1)S(1)}, u32[]{:S(2)}, u32[]{:S(2)}) collective-permute-start(bf16[64,2176]{1,0:T(8,128)(2,1)S(1)} %collective-permute-done.refs_1_), channel_id=1, source_target_pairs={{0,2},{3,1},{2,6},{7,3},{6,10},{11,7},{10,14},{15,11},{14,12},{13,... | collective-permute-start | bytes 835592 | tf_op jit(solution)/shard_map/ppermute | solution.py:359
  13.0 7.6 %collective-permute-start.1 = (bf16[64,2176]{1,0:T(8,128)(2,1)}, bf16[64,2176]{1,0:T(8,128)(2,1)S(1)}, u32[]{:S(2)}, u32[]{:S(2)}) collective-permute-start(bf16[64,2176]{1,0:T(8,128)(2,1)} %get-tuple-element.17), channel_id=1, source_target_pairs={{0,2},{3,1},{2,6},{7,3},{6,10},{11,7},{10,14},{15,11},{14,12},{13,... | collective-permute-start | bytes 835592 | tf_op jit(solution)/shard_map/ppermute | solution.py:361
  17.6 6.5 %collective-permute-start.6 = (bf16[64,2176]{1,0:T(8,128)(2,1)S(1)}, bf16[64,2176]{1,0:T(8,128)(2,1)S(1)}, u32[]{:S(2)}, u32[]{:S(2)}) collective-permute-start(bf16[64,2176]{1,0:T(8,128)(2,1)S(1)} %collective-permute-done.4.refs_0_), channel_id=1, source_target_pairs={{0,2},{3,1},{2,6},{7,3},{6,10},{11,7},{10,14},{15,11},{14,12},{13,... | collective-permute-start | bytes 835592 | tf_op jit(solution)/shard_map/ppermute | solution.py:359
  20.6 6.5 %collective-permute-start.5 = (bf16[64,2176]{1,0:T(8,128)(2,1)S(1)}, bf16[64,2176]{1,0:T(8,128)(2,1)S(1)}, u32[]{:S(2)}, u32[]{:S(2)}) collective-permute-start(bf16[64,2176]{1,0:T(8,128)(2,1)S(1)} %collective-permute-done.1.refs_2_), channel_id=1, source_target_pairs={{0,2},{3,1},{2,6},{7,3},{6,10},{11,7},{10,14},{15,11},{14,12},{13,... | collective-permute-start | bytes 835592 | tf_op jit(solution)/shard_map/ppermute | solution.py:361
  24.1 6.8 %collective-permute-start.8 = (bf16[64,2176]{1,0:T(8,128)(2,1)S(1)}, bf16[64,2176]{1,0:T(8,128)(2,1)S(1)}, u32[]{:S(2)}, u32[]{:S(2)}) collective-permute-start(bf16[64,2176]{1,0:T(8,128)(2,1)S(1)} %collective-permute-done.6.refs_0_), channel_id=1, source_target_pairs={{0,2},{3,1},{2,6},{7,3},{6,10},{11,7},{10,14},{15,11},{14,12},{13,... | collective-permute-start | bytes 835592 | tf_op jit(solution)/shard_map/ppermute | solution.py:359
  27.1 7.8 %collective-permute-start.7 = (bf16[64,2176]{1,0:T(8,128)(2,1)S(1)}, bf16[64,2176]{1,0:T(8,128)(2,1)S(1)}, u32[]{:S(2)}, u32[]{:S(2)}) collective-permute-start(bf16[64,2176]{1,0:T(8,128)(2,1)S(1)} %collective-permute-done.5.refs_1_), channel_id=1, source_target_pairs={{0,2},{3,1},{2,6},{7,3},{6,10},{11,7},{10,14},{15,11},{14,12},{13,... | collective-permute-start | bytes 835592 | tf_op jit(solution)/shard_map/ppermute | solution.py:361
  32.3 9.4 %collective-permute-start.9 = (bf16[64,2048]{1,0:T(8,128)(2,1)S(1)}, bf16[64,2048]{1,0:T(8,128)(2,1)S(1)}, u32[]{:S(2)}, u32[]{:S(2)}) collective-permute-start(bf16[64,2048]{1,0:T(8,128)(2,1)S(1)} %shard_map.91), channel_id=1, source_target_pairs={{2,0},{1,3},{6,2},{3,7},{10,6},{7,11},{14,10},{11,15},{12,14},{15,... | collective-permute-start | bytes 786440 | tf_op jit(solution)/shard_map/ppermute | solution.py:381
  36.2 3.7 %copy-start = (bf16[64,2176]{1,0:T(8,128)(2,1)S(1)}, bf16[64,2176]{1,0:T(8,128)(2,1)}, u32[]{:S(2)}) copy-start(bf16[64,2176]{1,0:T(8,128)(2,1)} %get-tuple-element.16.refs_0_) | copy-start | bytes 835588
  36.2 7.2 %collective-permute-start.13 = (bf16[64,2048]{1,0:T(8,128)(2,1)S(1)}, bf16[64,2048]{1,0:T(8,128)(2,1)S(1)}, u32[]{:S(2)}, u32[]{:S(2)}) collective-permute-start(bf16[64,2048]{1,0:T(8,128)(2,1)S(1)} %get-tuple-element.27), channel_id=1, source_target_pairs={{2,0},{1,3},{6,2},{3,7},{10,6},{7,11},{14,10},{11,15},{12,14},{15,... | collective-permute-start | bytes 786440 | tf_op jit(solution)/shard_map/ppermute | solution.py:385
  41.7 6.4 %collective-permute-start.10 = (bf16[64,2048]{1,0:T(8,128)(2,1)S(1)}, bf16[64,2048]{1,0:T(8,128)(2,1)S(1)}, u32[]{:S(2)}, u32[]{:S(2)}) collective-permute-start(bf16[64,2048]{1,0:T(8,128)(2,1)S(1)} %add_convert_fusion.4), channel_id=1, source_target_pairs={{2,0},{1,3},{6,2},{3,7},{10,6},{7,11},{14,10},{11,15},{12,14},{15,... | collective-permute-start | bytes 786440 | tf_op jit(solution)/shard_map/ppermute | solution.py:381
  43.4 7.5 %collective-permute-start.14 = (bf16[64,2048]{1,0:T(8,128)(2,1)S(1)}, bf16[64,2048]{1,0:T(8,128)(2,1)S(1)}, u32[]{:S(2)}, u32[]{:S(2)}) collective-permute-start(bf16[64,2048]{1,0:T(8,128)(2,1)S(1)} %add_convert_fusion.1), channel_id=1, source_target_pairs={{2,0},{1,3},{6,2},{3,7},{10,6},{7,11},{14,10},{11,15},{12,14},{15,... | collective-permute-start | bytes 786440 | tf_op jit(solution)/shard_map/ppermute | solution.py:385
  48.2 6.4 %collective-permute-start.11 = (bf16[64,2048]{1,0:T(8,128)(2,1)S(1)}, bf16[64,2048]{1,0:T(8,128)(2,1)S(1)}, u32[]{:S(2)}, u32[]{:S(2)}) collective-permute-start(bf16[64,2048]{1,0:T(8,128)(2,1)S(1)} %add_convert_fusion.3), channel_id=1, source_target_pairs={{2,0},{1,3},{6,2},{3,7},{10,6},{7,11},{14,10},{11,15},{12,14},{15,... | collective-permute-start | bytes 786440 | tf_op jit(solution)/shard_map/ppermute | solution.py:381
  51.0 6.4 %collective-permute-start.15 = (bf16[64,2048]{1,0:T(8,128)(2,1)S(1)}, bf16[64,2048]{1,0:T(8,128)(2,1)S(1)}, u32[]{:S(2)}, u32[]{:S(2)}) collective-permute-start(bf16[64,2048]{1,0:T(8,128)(2,1)S(1)} %add_convert_fusion), channel_id=1, source_target_pairs={{2,0},{1,3},{6,2},{3,7},{10,6},{7,11},{14,10},{11,15},{12,14},{15,... | collective-permute-start | bytes 786440 | tf_op jit(solution)/shard_map/ppermute | solution.py:385
  54.7 6.4 %collective-permute-start.12 = (bf16[64,2048]{1,0:T(8,128)(2,1)S(1)}, bf16[64,2048]{1,0:T(8,128)(2,1)S(1)}, u32[]{:S(2)}, u32[]{:S(2)}) collective-permute-start(bf16[64,2048]{1,0:T(8,128)(2,1)S(1)} %add_convert_fusion.2), channel_id=1, source_target_pairs={{2,0},{1,3},{6,2},{3,7},{10,6},{7,11},{14,10},{11,15},{12,14},{15,... | collective-permute-start | bytes 786440 | tf_op jit(solution)/shard_map/ppermute | solution.py:381
  57.5 3.8 %collective-permute-start.16 = (bf16[64,1024]{1,0:T(8,128)(2,1)S(1)}, bf16[64,1024]{1,0:T(8,128)(2,1)S(1)}, u32[]{:S(2)}, u32[]{:S(2)}) collective-permute-start(bf16[64,1024]{1,0:T(8,128)(2,1)S(1)} %slice.4), channel_id=1, source_target_pairs={{0,1},{1,0},{2,3},{3,2},{4,5},{5,4},{6,7},{7,6},{8,9},{9,8},{10,11... | collective-permute-start | bytes 393224 | tf_op jit(solution)/shard_map/ppermute | solution.py:389
  61.2 1.4 %collective-permute-start.17 = (bf16[64,1024]{1,0:T(8,128)(2,1)S(1)}, bf16[64,1024]{1,0:T(8,128)(2,1)S(1)}, u32[]{:S(2)}, u32[]{:S(2)}) collective-permute-start(bf16[64,1024]{1,0:T(8,128)(2,1)S(1)} %get-tuple-element.28), channel_id=1, source_target_pairs={{0,1},{1,0},{2,3},{3,2},{4,5},{5,4},{6,7},{7,6},{8,9},{9,8},{10,11... | collective-permute-start | bytes 393224 | tf_op jit(solution)/shard_map/ppermute | solution.py:390
where the time goes:
time: 63.5 us; the launch traced here: 63.4 us
  starting transfers between devices  27.4 us (43%)
  waiting for transfers between devices  24.7 us (39%)
  Pallas kernels  10.2 us (16%)
  between operations  0.79 us (1%)
    ppermute x4, waiting for transfers between devices, by_ring(): first.append(lax.ppermute(first[-1], both, ahead))  9.49 us
    ppermute x4, starting transfers between devices, by_ring(): first.append(lax.ppermute(first[-1], both, ahead))  8.76 us
    ppermute x4, waiting for transfers between devices, by_ring(): sum_first = lax.ppermute(sum_first, both, back)  8.6 us
    ppermute x4, starting transfers between devices, by_ring(): sum_first = lax.ppermute(sum_first, both, back)  6.66 us
    ppermute x3, starting transfers between devices, by_ring(): sum_second = lax.ppermute(sum_second, both, back)  5.73 us
    pallas_call x4, Pallas kernels, expert_rows(): pl.pallas_call(functools.partial(expert_kernel, chunks, width, experts),...  5.57 us
    ppermute x3, starting transfers between devices, by_ring(): second.append(lax.ppermute(second[-1], both, ahead))  5.45 us
    ppermute x3, waiting for transfers between devices, by_ring(): second.append(lax.ppermute(second[-1], both, ahead))  3.01 us
  transfers between devices with their start and end apart: 18, of which 12 were waited for; matrix products, arithmetic and copies ran while one was open for 0% of the time, Pallas kernels for 15%

commit v1 on v0

--- a/solution.py
+++ b/solution.py
@@ -10,6 +10,8 @@
 REPLICAS = 4
 LANES = 128
 VMEM_BYTES = 67043328
+PIECES = 2
+SUBLANES = 16
 
 
 def earlier_same(labels):
@@ -131,122 +133,119 @@
     return tuple(extend([0]) or range(count))
 
 
-def pack_kernel(caps, routes_in, probs_in, old_in, new_in, tokens, first, second, slot_rows, *scratch):
-    routes, probs, old_place, new_place, sems = scratch
+def count_of(new_place, expert, stop):
+    return sum(
+        ((new_place[s] == expert) & (s < stop)).astype(jnp.int32)
+        for s in range(new_place.shape[0])
+    )
+
+
+def pack_kernel(caps, pieces, routes_in, probs_in, old_in, new_in, tokens, *refs):
+    outs, (routes, probs, old_place, new_place, sems) = refs[: 2 * pieces], refs[2 * pieces :]
     core = lax.axis_index("tensor")
     width = tokens.shape[2]
     token_count = routes.shape[2]
     experts, slots = old_place.shape[0], new_place.shape[0]
-    lanes = first.shape[1] - width
-    pairs = (
-        (old_in, old_place),
-        (new_in, new_place),
-        (routes_in, routes),
-        (probs_in, probs),
-        (tokens.at[core], first.at[:, :width]),
-        (tokens.at[1 - core], second.at[:, :width]),
-    )
+    size = token_count // pieces
+    lanes = outs[0].shape[1] - width
+    pairs = [(old_in, old_place), (new_in, new_place), (routes_in, routes), (probs_in, probs)]
+    for i, out in enumerate(outs):
+        batch = core if i < pieces else 1 - core
+        rows = pl.ds(i % pieces * size, size)
+        pairs.append((tokens.at[batch, rows], out.at[:, :width]))
     copies = [pltpu.make_async_copy(src, dst, sems.at[i]) for i, (src, dst) in enumerate(pairs)]
     for copy in copies:
         copy.start()
     for copy in copies[:4]:
         copy.wait()
     token = lax.broadcasted_iota(jnp.int32, (1, token_count), 1)
-
-    def holders_of(expert):
-        return sum((new_place[s] == expert).astype(jnp.int32) for s in range(slots))
-
-    limits = [[caps[0]] * experts, [caps[1] * holders_of(old_place[e]) for e in range(experts)]]
-    for out, batch in ((first, core), (second, 1 - core)):
+    limits = [caps[1] * count_of(new_place, old_place[e], slots) for e in range(experts)]
+    for i, batch in enumerate((core, 1 - core)):
         highs, lows = [], []
         for e in range(experts):
             named = routes[batch] == old_place[e]
             weight = jnp.sum(jnp.where(named, probs[batch], 0.0), axis=0, keepdims=True)
-            served = jnp.where(batch == 0, limits[0][e], limits[1][e])
+            served = jnp.where(batch == 0, caps[0], limits[e])
             weight = jnp.where(token < served, weight, 0.0)
             high = weight.astype(jnp.bfloat16).astype(jnp.float32)
             highs.append(high)
             lows.append(weight - high)
         pad = jnp.zeros((lanes - 2 * experts, token_count), jnp.float32)
-        out[:, width:] = jnp.concatenate(highs + lows + [pad], axis=0).T.astype(jnp.bfloat16)
-
-    devices = lax.axis_size("expert")
-    mine = slots // devices
-    for j in range(mine):
-        slot = lax.axis_index("expert") * mine + j
-        expert = new_place[slot]
-        holders = holders_of(expert)
-        place = sum(
-            ((new_place[s] == expert) & (s < slot)).astype(jnp.int32) for s in range(slots)
-        )
-        count = jnp.int32(0)
-        for source in range(devices):
-            start = lax.rem(place - source + devices * holders, holders)
-            count += lax.div(token_count - 1 - start + holders, holders)
-        slot_rows[j] = count
+        side = jnp.concatenate(highs + lows + [pad], axis=0).T.astype(jnp.bfloat16)
+        for j in range(pieces):
+            outs[i * pieces + j][:, width:] = side[j * size : (j + 1) * size]
     for copy in copies[4:]:
         copy.wait()
 
 
-def pack(caps, tokens, routes, probs, old_place, new_place):
+def pack(caps, pieces, tokens, routes, probs, old_place, new_place):
     token_count, width = tokens.shape[1:]
     experts = old_place.shape[0]
     lanes = -(-2 * experts // LANES) * LANES
-    chunk = jax.ShapeDtypeStruct((token_count, width + lanes), tokens.dtype)
-    vmem, smem = pl.BlockSpec(memory_space=pltpu.VMEM), pl.BlockSpec(memory_space=pltpu.SMEM)
-    mine = new_place.shape[0] // lax.axis_size("expert")
+    chunk = jax.ShapeDtypeStruct((token_count // pieces, width + lanes), tokens.dtype)
     routes, probs = routes.transpose(0, 2, 1), probs.transpose(0, 2, 1)
     return pl.pallas_call(
-        functools.partial(pack_kernel, caps),
-        out_shape=(chunk, chunk, jax.ShapeDtypeStruct((mine,), jnp.int32)),
+        functools.partial(pack_kernel, caps, pieces),
+        out_shape=[chunk] * (2 * pieces),
         in_specs=[pl.BlockSpec(memory_space=pltpu.HBM)] * 5,
-        out_specs=(vmem, vmem, smem),
+        out_specs=[pl.BlockSpec(memory_space=pltpu.VMEM)] * (2 * pieces),
         scratch_shapes=[
             pltpu.VMEM(routes.shape, routes.dtype),
             pltpu.VMEM(probs.shape, probs.dtype),
             pltpu.SMEM(old_place.shape, jnp.int32),
             pltpu.SMEM(new_place.shape, jnp.int32),
-            pltpu.SemaphoreType.DMA((6,)),
+            pltpu.SemaphoreType.DMA((4 + 2 * pieces,)),
         ],
-        compiler_params=pltpu.CompilerParams(
-            vmem_limit_bytes=VMEM_BYTES - (4 << 20)
-        ),
+        compiler_params=pltpu.CompilerParams(vmem_limit_bytes=VMEM_BYTES - (4 << 20)),
     )(routes, probs, old_place, new_place, tokens)
 
 
-def load_kernel(up, down, up_here, down_here, sems):
+def load_kernel(devices, token_count, new_place, up, down, up_here, down_here, slot_rows, sems):
     copies = [
         pltpu.make_async_copy(up, up_here, sems.at[0]),
         pltpu.make_async_copy(down, down_here, sems.at[1]),
     ]
     for copy in copies:
         copy.start()
+    mine = slot_rows.shape[0]
+    for j in range(mine):
+        slot = lax.axis_index("expert") * mine + j
+        expert = new_place[slot]
+        holders = count_of(new_place, expert, new_place.shape[0])
+        place = count_of(new_place, expert, slot)
+        count = jnp.int32(0)
+        for source in range(devices):
+            start = lax.rem(place - source + devices * holders, holders)
+            count += lax.div(token_count - 1 - start + holders, holders)
+        slot_rows[j] = count
     for copy in copies:
         copy.wait()
 
 
-def load(up, down):
-    vmem = pl.BlockSpec(memory_space=pltpu.VMEM)
+def load(up, down, new_place, devices, token_count):
+    vmem, smem = pl.BlockSpec(memory_space=pltpu.VMEM), pl.BlockSpec(memory_space=pltpu.SMEM)
+    hbm = pl.BlockSpec(memory_space=pltpu.HBM)
     return pl.pallas_call(
-        load_kernel,
+        functools.partial(load_kernel, devices, token_count),
         out_shape=(
             jax.ShapeDtypeStruct(up.shape, up.dtype),
             jax.ShapeDtypeStruct(down.shape, down.dtype),
+            jax.ShapeDtypeStruct((new_place.shape[0] // devices,), jnp.int32),
         ),
-        in_specs=[pl.BlockSpec(memory_space=pltpu.HBM)] * 2,
-        out_specs=(vmem, vmem),
+        in_specs=[smem, hbm, hbm],
+        out_specs=(vmem, vmem, smem),
         scratch_shapes=[pltpu.SemaphoreType.DMA((2,))],
         compiler_params=pltpu.CompilerParams(vmem_limit_bytes=VMEM_BYTES - (14 << 20)),
         cost_estimate=pl.CostEstimate(
             flops=0, bytes_accessed=4 * (up.size + down.size), transcendentals=0
         ),
-    )(up, down)
+    )(new_place, up, down)
 
 
 def expert_kernel(chunks, width, experts, *refs):
     rows, refs = refs[:chunks], refs[chunks:]
     (up_own, up_pair, down_own, down_pair), refs = refs[:4], refs[4:]
-    outs, x_buf = refs[:chunks], refs[chunks]
+    outs, split, x_buf = refs[:chunks], refs[chunks:-1], refs[-1]
     slot, core = lax.axis_index("expert"), lax.axis_index("tensor")
     size = rows[0].shape[0]
     lane = lax.broadcasted_iota(jnp.int32, (size, rows[0].shape[1] - width), 1)
@@ -270,19 +269,28 @@
         y = jnp.dot(hidden, down[...], preferred_element_type=jnp.float32)
         y = y.astype(jnp.bfloat16).astype(jnp.float32) * scale
         for i, out in enumerate(outs):
-            out[:, j * half : (j + 1) * half] = y[i * size : (i + 1) * size].astype(out.dtype)
-
-
-def expert_rows(rows, weights, width, experts, out_types):
+            rows_of = y[i * size : (i + 1) * size]
+            if i < len(split):
+                out = (out, split[i])[j]
+                out[...] = rows_of.astype(out.dtype)
+            else:
+                out[:, j * half : (j + 1) * half] = rows_of.astype(out.dtype)
+
+
+def expert_rows(rows, weights, width, experts, out_types, splits=0):
     chunks, size = len(rows), rows[0].shape[0]
     up = weights[0]
     total = chunks * size
     vmem = pl.BlockSpec(memory_space=pltpu.VMEM)
     return pl.pallas_call(
         functools.partial(expert_kernel, chunks, width, experts),
-        out_shape=[jax.ShapeDtypeStruct((size, width), t) for t in out_types],
+        out_shape=[
+            jax.ShapeDtypeStruct((size, width // 2 if i < splits else width), t)
+            for i, t in enumerate(out_types)
+        ]
+        + [jax.ShapeDtypeStruct((size, width // 2), jnp.bfloat16)] * splits,
         in_specs=[vmem] * (chunks + 4),
-        out_specs=[vmem] * chunks,
+        out_specs=[vmem] * (chunks + splits),
         scratch_shapes=[pltpu.VMEM((total, width), jnp.bfloat16)],
         compiler_params=pltpu.CompilerParams(vmem_limit_bytes=20 << 20),
         cost_estimate=pl.CostEstimate(
@@ -293,44 +301,51 @@
     )(*rows, *weights)
 
 
-def last_add_kernel(part, arrived, kept, leaving):
-    half = kept.shape[1]
-    kept[...] = part[:, :half] + arrived[:, :half].astype(jnp.float32)
-    leaving[...] = (part[:, half:] + arrived[:, half:].astype(jnp.float32)).astype(leaving.dtype)
-
-
-def last_add(part, arrived):
+def split_add_kernel(part, arrived, own, pair):
+    half = own.shape[1]
+    own[...] = (part[:, :half] + arrived[:, :half].astype(jnp.float32)).astype(own.dtype)
+    pair[...] = (part[:, half:] + arrived[:, half:].astype(jnp.float32)).astype(pair.dtype)
+
+
+def split_add(part, arrived):
     size, half = part.shape[0], part.shape[1] // 2
     vmem = pl.BlockSpec(memory_space=pltpu.VMEM)
     return pl.pallas_call(
-        last_add_kernel,
-        out_shape=(
-            jax.ShapeDtypeStruct((size, half), jnp.float32),
-            jax.ShapeDtypeStruct((size, half), jnp.bfloat16),
-        ),
+        split_add_kernel,
+        out_shape=[jax.ShapeDtypeStruct((size, half), jnp.bfloat16)] * 2,
         in_specs=[vmem, vmem],
-        out_specs=(vmem, vmem),
+        out_specs=[vmem, vmem],
         compiler_params=pltpu.CompilerParams(vmem_limit_bytes=4 << 20),
     )(part, arrived)
 
 
-def finish_kernel(kept, from_second, second, from_first, mixed):
+def finish_kernel(pieces, *refs):
+    own, arrived, second_pair, second, crossed, own_pair = (
+        refs[i * pieces : (i + 1) * pieces] for i in range(6)
+    )
+    mixed = refs[-1]
     core = lax.axis_index("tensor")
     half = mixed.shape[2]
-    mixed[core] = (kept[...] + from_second[...].astype(jnp.float32)).astype(mixed.dtype)
-    other = second[:, :half].astype(jnp.float32) + from_first[...].astype(jnp.float32)
-    mixed[1 - core] = other.astype(mixed.dtype)
-
-
-def finish(kept, from_second, second, from_first):
+    size = own[0].shape[0]
+    f32 = jnp.float32
+    for i in range(pieces):
+        rows = slice(i * size, (i + 1) * size)
+        total = own[i][...] + arrived[i][...].astype(f32) + second_pair[i][...].astype(f32)
+        mixed[core, rows] = total.astype(mixed.dtype)
+        total = second[i][:, :half].astype(f32) + crossed[i][...].astype(f32)
+        mixed[1 - core, rows] = (total + own_pair[i][...].astype(f32)).astype(mixed.dtype)
+
+
+def finish(pieces, *groups):
+    size, half = groups[0][0].shape
     vmem = pl.BlockSpec(memory_space=pltpu.VMEM)
     return pl.pallas_call(
-        finish_kernel,
-        out_shape=jax.ShapeDtypeStruct((2, *kept.shape), jnp.bfloat16),
-        in_specs=[vmem] * 4,
+        functools.partial(finish_kernel, pieces),
+        out_shape=jax.ShapeDtypeStruct((2, pieces * size, half), jnp.bfloat16),
+        in_specs=[vmem] * (6 * pieces),
         out_specs=vmem,
         compiler_params=pltpu.CompilerParams(vmem_limit_bytes=4 << 20),
-    )(kept, from_second, second, from_first)
+    )(*sum((list(g) for g in groups), []))
 
 
 def by_ring(ring, tokens, routes, probs, up_weight, down_weight, old_place, new_place):
@@ -345,50 +360,68 @@
         there = ring[(spot + 1) % devices]
         ahead += [(2 * here, 2 * there), (2 * there + 1, 2 * here + 1)]
     back = [(b, a) for a, b in ahead]
+    across = [(b, a ^ 1) for a, b in ahead]
     swap = [(0, 1), (1, 0)]
     f32, bf16 = jnp.float32, jnp.bfloat16
+    half, pieces = width // 2, PIECES if token_count % (PIECES * SUBLANES) == 0 else 1
+    each = range(pieces)
 
     caps = (
         capacity_for(block_rows, experts, token_count),
         capacity_for(block_rows, new_place.shape[0], token_count),
     )
-    own_first, own_second, slot_rows = pack(caps, tokens, routes, probs, old_place, new_place)
-
-    first, second = [own_first], [own_second]
+    packed = pack(caps, pieces, tokens, routes, probs, old_place, new_place)
+    first, second = [packed[:pieces]], [packed[pieces:]]
     for step in range(1, steps + 1):
-        first.append(lax.ppermute(first[-1], both, ahead))
+        first.append([lax.ppermute(first[-1][i], both, ahead) for i in each])
         if step < steps:
-            second.append(lax.ppermute(second[-1], both, ahead))
+            second.append([lax.ppermute(second[-1][i], both, ahead) for i in each])
     up_own, down_own = up_weight[0], down_weight[0]
     up_pair = lax.ppermute(up_own, "tensor", swap)
     down_pair = lax.ppermute(down_own, "tensor", swap)
-    up_here, down_here = load(up_own, down_own)
+    up_here, down_here, slot_rows = load(up_own, down_own, new_place, devices, token_count)
     weights = (up_here, up_pair, down_here, down_pair)
 
-    def run(rows, out_types):
-        return expert_rows(rows, weights, width, experts, out_types)
+    def run(rows, out_types, splits=0):
+        return expert_rows(rows, weights, width, experts, out_types, splits)
 
     part_first, part_second = [None] * (steps + 1), [None] * steps
-    part_first[0], part_first[1], part_second[1] = run([first[0], first[1], second[1]], [f32] * 3)
+    made = run([*first[0], *first[1], *second[1]], [f32] * (3 * pieces), pieces)
+    own, part_first[1], part_second[1], leaving = (
+        made[i * pieces : (i + 1) * pieces] for i in range(4)
+    )
     for step in range(2, steps):
-        part_first[step], part_second[step] = run(
-            [first[step], second[step]], [f32, bf16 if step == steps - 1 else f32]
+        made = run(
+            [*first[step], *second[step]],
+            [f32] * pieces + [bf16 if step == steps - 1 else f32] * pieces,
         )
-    (part_first[steps],) = run([first[steps]], [bf16])
-
-    sum_first, sum_second = part_first[steps], part_second[steps - 1]
-    for step in range(steps - 1, -1, -1):
-        sum_first = lax.ppermute(sum_first, both, back)
+        part_first[step], part_second[step] = made[:pieces], made[pieces:]
+    sum_first = run(first[steps], [bf16] * pieces)
+    sum_second = part_second[steps - 1]
+    own_pair = [lax.ppermute(leaving[i], "tensor", swap) for i in each]
+
+    for step in range(steps - 2, -1, -1):
+        sum_second = [lax.ppermute(sum_second[i], both, back) for i in each]
         if step > 0:
-            sum_first = (part_first[step] + sum_first.astype(f32)).astype(bf16)
-        if step < steps - 1:
-            sum_second = lax.ppermute(sum_second, both, back)
-            if step > 0:
-                sum_second = (part_second[step] + sum_second.astype(f32)).astype(bf16)
-    kept, leaving = last_add(part_first[0], sum_first)
-    from_second = lax.ppermute(sum_second[:, width // 2 :], "tensor", swap)
-    from_first = lax.ppermute(leaving, "tensor", swap)
-    return (finish(kept, from_second, sum_second, from_first), slot_rows)
+            sum_second = [
+                (part + arrived.astype(f32)).astype(bf16)
+                for part, arrived in zip(part_second[step], sum_second)
+            ]
+    second_pair = [lax.ppermute(sum_second[i][:, half:], "tensor", swap) for i in each]
+    for step in range(steps - 1, 1, -1):
+        sum_first = [lax.ppermute(sum_first[i], both, back) for i in each]
+        sum_first = [
+            (part + arrived.astype(f32)).astype(bf16)
+            for part, arrived in zip(part_first[step], sum_first)
+        ]
+    arrived, crossed = [], []
+    for i in each:
+        last = lax.ppermute(sum_first[i], both, back)
+        stays, crosses = split_add(part_first[1][i], last)
+        arrived.append(lax.ppermute(stays, both, back))
+        crossed.append(lax.ppermute(crosses, both, across))
+    mixed = finish(pieces, own, arrived, second_pair, sum_second, crossed, own_pair)
+    return (mixed, slot_rows)
 
 
 def on_device(ring, tokens, routes, probs, up_weight, down_weight, old_place, new_place):

time: 63.5 us -> 64.5 us (1.016)
  waiting for transfers between devices: 24.7 us -> 6.15 us
  starting transfers between devices: 27.4 us -> 44.9 us
  Pallas kernels: 10.2 us -> 11.5 us
  local copies, waits for them, and re-layouts: 0.01 us -> 0.67 us
    ppermute x16 -> x34, waiting for transfers between devices: 24.7 us -> 6.14 us  [the longest x2 2.42 us: by_ring(): crossed.append(lax.ppermute(crosses, both, across))]
    ppermute x16 -> x34, starting transfers between devices: 26.7 us -> 44.3 us  [the longest x8 14 us: by_ring(): first.append([lax.ppermute(first[-1][i], both, ahead) for i in each])]
    pallas_call x4 -> x5, Pallas kernels: 4.68 us -> 5.78 us  [the longest x1 2.95 us: load(): pl.pallas_call(functools.partial(load_kernel, devices, token_count), out_...]
    unnamed x2 -> x6, local copies, waits for them, and re-layouts: 0.01 us -> 0.66 us
  transfers between devices with their start and end apart: 18 -> 36, of which waited for: 12 -> 9; matrix products, arithmetic and copies ran while one was open for 0% -> 0% of each run, Pallas kernels for 15% -> 17%
where the time goes in v1:
time: 64.5 us; the launch traced here: 64.3 us
  starting transfers between devices  44.9 us (70%)
  Pallas kernels  11.5 us (18%)
  waiting for transfers between devices  6.15 us (10%)
  between operations  0.81 us (1%)
  local copies, waits for them, and re-layouts  0.67 us (1%)
    ppermute x8, starting transfers between devices, by_ring(): first.append([lax.ppermute(first[-1][i], both, ahead) for i in each])  14 us
    ppermute x6, starting transfers between devices, by_ring(): second.append([lax.ppermute(second[-1][i], both, ahead) for i in each])  10.8 us
    ppermute x6, starting transfers between devices, by_ring(): sum_second = [lax.ppermute(sum_second[i], both, back) for i in each]  6.94 us
    pallas_call x4, Pallas kernels, expert_rows(): pl.pallas_call(functools.partial(expert_kernel, chunks, width, experts),...  5.69 us
    ppermute x4, starting transfers between devices, by_ring(): sum_first = [lax.ppermute(sum_first[i], both, back) for i in each]  4.21 us
    pallas_call x1, Pallas kernels, load(): pl.pallas_call(functools.partial(load_kernel, devices, token_count), out_...  2.95 us
    ppermute x2, starting transfers between devices, by_ring(): last = lax.ppermute(sum_first[i], both, back)  2.91 us
    ppermute x2, starting transfers between devices, by_ring(): arrived.append(lax.ppermute(stays, both, back))  2.62 us
  transfers between devices with their start and end apart: 36, of which 9 were waited for; matrix products, arithmetic and copies ran while one was open for 0% of the time, Pallas kernels for 17%

profile of v1, /device:TPU:0, one launch (start us, length us, event | category | flops | bytes accessed | tf_op | source)
XLA Modules:
  0.0 64.3 jit_solution(1267650401115230870)
XLA Ops:
  0.6 0.6 collective-permute-start.4
  1.2 0.1 collective-permute-start.5
  1.3 2.0 %shard_map.86 = (bf16[32,2176]{1,0:T(8,128)(2,1)}, bf16[32,2176]{1,0:T(8,128)(2,1)}, bf16[32,2176]{1,0:T(8,128)(2,1)}, bf16[32,2176]{1,0:T(8,128)(2,1)}) custom-call(s32[2,8,64]{2,1,0:T(8,128)} %bitcast.8, f32[2,8,64]{2,1,0:T(8,128)} %bitcast.9, s32[8]{0:T(128)} %old_in.1, s32[16]{0:T(128)} %new_place.1, bf16[2,64,2048]{2,1,0:T(8,128)(2,1)} %tokens.1), custom_call_target="tpu_custom_call" | custom-call | tf_op jit(solution)/shard_map/pallas_call | solution.py:187
  3.3 3.0 %collective-permute-start = (bf16[32,2176]{1,0:T(8,128)(2,1)}, bf16[32,2176]{1,0:T(8,128)(2,1)S(1)}, u32[]{:S(2)}, u32[]{:S(2)}) collective-permute-start(bf16[32,2176]{1,0:T(8,128)(2,1)} %get-tuple-element.31.refs_0_), channel_id=1, source_target_pairs={{0,2},{3,1},{2,6},{7,3},{6,10},{11,7},{10,14},{15,11},{14,12},{13,... | collective-permute-start | bytes 417800 | tf_op jit(solution)/shard_map/ppermute | solution.py:376
  6.2 1.6 %collective-permute-start.1 = (bf16[32,2176]{1,0:T(8,128)(2,1)}, bf16[32,2176]{1,0:T(8,128)(2,1)S(1)}, u32[]{:S(2)}, u32[]{:S(2)}) collective-permute-start(bf16[32,2176]{1,0:T(8,128)(2,1)} %get-tuple-element.32.refs_1_), channel_id=1, source_target_pairs={{0,2},{3,1},{2,6},{7,3},{6,10},{11,7},{10,14},{15,11},{14,12},{13,... | collective-permute-start | bytes 417800 | tf_op jit(solution)/shard_map/ppermute | solution.py:376
  7.8 1.6 %collective-permute-start.2 = (bf16[32,2176]{1,0:T(8,128)(2,1)}, bf16[32,2176]{1,0:T(8,128)(2,1)S(1)}, u32[]{:S(2)}, u32[]{:S(2)}) collective-permute-start(bf16[32,2176]{1,0:T(8,128)(2,1)} %get-tuple-element.33), channel_id=1, source_target_pairs={{0,2},{3,1},{2,6},{7,3},{6,10},{11,7},{10,14},{15,11},{14,12},{13,... | collective-permute-start | bytes 417800 | tf_op jit(solution)/shard_map/ppermute | solution.py:378
  9.4 0.2 collective-permute-done.refs_2_
  9.6 1.9 %collective-permute-start.3 = (bf16[32,2176]{1,0:T(8,128)(2,1)}, bf16[32,2176]{1,0:T(8,128)(2,1)S(1)}, u32[]{:S(2)}, u32[]{:S(2)}) collective-permute-start(bf16[32,2176]{1,0:T(8,128)(2,1)} %get-tuple-element.34), channel_id=1, source_target_pairs={{0,2},{3,1},{2,6},{7,3},{6,10},{11,7},{10,14},{15,11},{14,12},{13,... | collective-permute-start | bytes 417800 | tf_op jit(solution)/shard_map/ppermute | solution.py:378
  11.5 0.0 collective-permute-done.1.refs_3_
  11.5 1.6 %collective-permute-start.6 = (bf16[32,2176]{1,0:T(8,128)(2,1)S(1)}, bf16[32,2176]{1,0:T(8,128)(2,1)S(1)}, u32[]{:S(2)}, u32[]{:S(2)}) collective-permute-start(bf16[32,2176]{1,0:T(8,128)(2,1)S(1)} %collective-permute-done.refs_2_), channel_id=1, source_target_pairs={{0,2},{3,1},{2,6},{7,3},{6,10},{11,7},{10,14},{15,11},{14,12},{13,... | collective-permute-start | bytes 417800 | tf_op jit(solution)/shard_map/ppermute | solution.py:376
  13.1 0.0 collective-permute-done.2.refs_4_
  13.1 1.6 %collective-permute-start.7 = (bf16[32,2176]{1,0:T(8,128)(2,1)S(1)}, bf16[32,2176]{1,0:T(8,128)(2,1)S(1)}, u32[]{:S(2)}, u32[]{:S(2)}) collective-permute-start(bf16[32,2176]{1,0:T(8,128)(2,1)S(1)} %collective-permute-done.1.refs_3_), channel_id=1, source_target_pairs={{0,2},{3,1},{2,6},{7,3},{6,10},{11,7},{10,14},{15,11},{14,12},{13,... | collective-permute-start | bytes 417800 | tf_op jit(solution)/shard_map/ppermute | solution.py:376
  14.6 0.2 collective-permute-done.3.refs_5_
  14.8 1.9 %collective-permute-start.8 = (bf16[32,2176]{1,0:T(8,128)(2,1)S(1)}, bf16[32,2176]{1,0:T(8,128)(2,1)S(1)}, u32[]{:S(2)}, u32[]{:S(2)}) collective-permute-start(bf16[32,2176]{1,0:T(8,128)(2,1)S(1)} %collective-permute-done.2.refs_4_), channel_id=1, source_target_pairs={{0,2},{3,1},{2,6},{7,3},{6,10},{11,7},{10,14},{15,11},{14,12},{13,... | collective-permute-start | bytes 417800 | tf_op jit(solution)/shard_map/ppermute | solution.py:378
  16.8 0.0 collective-permute-done.6.refs_0_
  16.8 1.6 %collective-permute-start.10 = (bf16[32,2176]{1,0:T(8,128)(2,1)S(1)}, bf16[32,2176]{1,0:T(8,128)(2,1)S(1)}, u32[]{:S(2)}, u32[]{:S(2)}) collective-permute-start(bf16[32,2176]{1,0:T(8,128)(2,1)S(1)} %collective-permute-done.6.refs_0_), channel_id=1, source_target_pairs={{0,2},{3,1},{2,6},{7,3},{6,10},{11,7},{10,14},{15,11},{14,12},{13,... | collective-permute-start | bytes 417800 | tf_op jit(solution)/shard_map/ppermute | solution.py:376
  18.3 0.0 collective-permute-done.7.refs_1_
  18.3 1.6 %collective-permute-start.11 = (bf16[32,2176]{1,0:T(8,128)(2,1)S(1)}, bf16[32,2176]{1,0:T(8,128)(2,1)S(1)}, u32[]{:S(2)}, u32[]{:S(2)}) collective-permute-start(bf16[32,2176]{1,0:T(8,128)(2,1)S(1)} %collective-permute-done.7.refs_1_), channel_id=1, source_target_pairs={{0,2},{3,1},{2,6},{7,3},{6,10},{11,7},{10,14},{15,11},{14,12},{13,... | collective-permute-start | bytes 417800 | tf_op jit(solution)/shard_map/ppermute | solution.py:376
  19.9 0.0 collective-permute-done.8.refs_2_
  19.9 1.9 %collective-permute-start.9 = (bf16[32,2176]{1,0:T(8,128)(2,1)S(1)}, bf16[32,2176]{1,0:T(8,128)(2,1)S(1)}, u32[]{:S(2)}, u32[]{:S(2)}) collective-permute-start(bf16[32,2176]{1,0:T(8,128)(2,1)S(1)} %collective-permute-done.3.refs_5_), channel_id=1, source_target_pairs={{0,2},{3,1},{2,6},{7,3},{6,10},{11,7},{10,14},{15,11},{14,12},{13,... | collective-permute-start | bytes 417800 | tf_op jit(solution)/shard_map/ppermute | solution.py:378
  21.8 0.0 collective-permute-done.10.refs_0_
  21.8 1.6 %collective-permute-start.14 = (bf16[32,2176]{1,0:T(8,128)(2,1)S(1)}, bf16[32,2176]{1,0:T(8,128)(2,1)S(1)}, u32[]{:S(2)}, u32[]{:S(2)}) collective-permute-start(bf16[32,2176]{1,0:T(8,128)(2,1)S(1)} %collective-permute-done.10.refs_0_), channel_id=1, source_target_pairs={{0,2},{3,1},{2,6},{7,3},{6,10},{11,7},{10,14},{15,11},{14,12},{13,... | collective-permute-start | bytes 417800 | tf_op jit(solution)/shard_map/ppermute | solution.py:376
  23.4 0.0 collective-permute-done.11.refs_1_
  23.4 1.6 %collective-permute-start.15 = (bf16[32,2176]{1,0:T(8,128)(2,1)S(1)}, bf16[32,2176]{1,0:T(8,128)(2,1)S(1)}, u32[]{:S(2)}, u32[]{:S(2)}) collective-permute-start(bf16[32,2176]{1,0:T(8,128)(2,1)S(1)} %collective-permute-done.11.refs_1_), channel_id=1, source_target_pairs={{0,2},{3,1},{2,6},{7,3},{6,10},{11,7},{10,14},{15,11},{14,12},{13,... | collective-permute-start | bytes 417800 | tf_op jit(solution)/shard_map/ppermute | solution.py:376
  25.0 0.0 collective-permute-done.9.refs_3_
  25.0 1.9 %collective-permute-start.12 = (bf16[32,2176]{1,0:T(8,128)(2,1)S(1)}, bf16[32,2176]{1,0:T(8,128)(2,1)S(1)}, u32[]{:S(2)}, u32[]{:S(2)}) collective-permute-start(bf16[32,2176]{1,0:T(8,128)(2,1)S(1)} %collective-permute-done.8.refs_2_), channel_id=1, source_target_pairs={{0,2},{3,1},{2,6},{7,3},{6,10},{11,7},{10,14},{15,11},{14,12},{13,... | collective-permute-start | bytes 417800 | tf_op jit(solution)/shard_map/ppermute | solution.py:378
  26.9 0.0 collective-permute-done.14.refs_0_
  26.9 1.6 %collective-permute-start.13 = (bf16[32,2176]{1,0:T(8,128)(2,1)S(1)}, bf16[32,2176]{1,0:T(8,128)(2,1)S(1)}, u32[]{:S(2)}, u32[]{:S(2)}) collective-permute-start(bf16[32,2176]{1,0:T(8,128)(2,1)S(1)} %collective-permute-done.9.refs_3_), channel_id=1, source_target_pairs={{0,2},{3,1},{2,6},{7,3},{6,10},{11,7},{10,14},{15,11},{14,12},{13,... | collective-permute-start | bytes 417800 | tf_op jit(solution)/shard_map/ppermute | solution.py:378
  28.4 0.7 %copy-done.2 = s32[16]{0:T(128)S(1)} copy-done((s32[16]{0:T(128)S(1)}, s32[16]{0:T(128)}, u32[]{:S(2)}) %copy-start.2) | copy-done | bytes 88
  29.1 3.0 %shard_map.87 = (bf16[2048,384]{1,0:T(8,128)(2,1)S(1)}, bf16[768,1024]{1,0:T(8,128)(2,1)S(1)}, s32[2]{0:T(128)}) custom-call(s32[16]{0:T(128)S(1)} %copy-done.2, bf16[2048,384]{1,0:T(8,128)(2,1)} %bitcast.5, bf16[768,1024]{1,0:T(8,128)(2,1)} %bitcast.7), custom_call_target="tpu_custom_call" | custom-call | bytes 6291456 | tf_op jit(solution)/shard_map/pallas_call | solution.py:228
  32.1 1.3 %shard_map.91 = (bf16[32,2048]{1,0:T(8,128)(2,1)S(1)}, bf16[32,2048]{1,0:T(8,128)(2,1)S(1)}) custom-call(bf16[32,2176]{1,0:T(8,128)(2,1)S(1)} %collective-permute-done.14.refs_0_, bf16[32,2176]{1,0:T(8,128)(2,1)S(1)} %collective-permute-done.15.refs_1_, bf16[2048,384]{1,0:T(8,128)(2,1)S(1)} %get-tuple-element.35.refs_6_.refs_4_.refs_2_, ...), custom_call_target="tpu_custom_call" | custom-call | flops 402653184 | bytes 1048576 | tf_op jit(solution)/shard_map/pallas_call | solution.py:285
  33.4 0.5 collective-permute-start.16
  33.9 1.6 %collective-permute-start.20 = (bf16[32,2048]{1,0:T(8,128)(2,1)S(1)}, bf16[32,2048]{1,0:T(8,128)(2,1)S(1)}, u32[]{:S(2)}, u32[]{:S(2)}) collective-permute-start(bf16[32,2048]{1,0:T(8,128)(2,1)S(1)} %get-tuple-element.47), channel_id=1, source_target_pairs={{2,0},{1,3},{6,2},{3,7},{10,6},{7,11},{14,10},{11,15},{12,14},{15,... | collective-permute-start | bytes 393224 | tf_op jit(solution)/shard_map/ppermute | solution.py:412
  35.5 1.3 %shard_map.90 = (f32[32,2048]{1,0:T(8,128)S(1)}, f32[32,2048]{1,0:T(8,128)S(1)}, bf16[32,2048]{1,0:T(8,128)(2,1)S(1)}, bf16[32,2048]{1,0:T(8,128)(2,1)S(1)}) custom-call(bf16[32,2176]{1,0:T(8,128)(2,1)S(1)} %collective-permute-done.10.refs_0_, bf16[32,2176]{1,0:T(8,128)(2,1)S(1)} %collective-permute-done.11.refs_1_, ...), custom_call_target="tpu_custom_call" | custom-call | flops 805306368 | bytes 2097152 | tf_op jit(solution)/shard_map/pallas_call | solution.py:285
  36.8 1.6 %collective-permute-start.24 = (bf16[32,2048]{1,0:T(8,128)(2,1)S(1)}, bf16[32,2048]{1,0:T(8,128)(2,1)S(1)}, u32[]{:S(2)}, u32[]{:S(2)}) collective-permute-start(bf16[32,2048]{1,0:T(8,128)(2,1)S(1)} %get-tuple-element.51), channel_id=1, source_target_pairs={{2,0},{1,3},{6,2},{3,7},{10,6},{7,11},{14,10},{11,15},{12,14},{15,... | collective-permute-start | bytes 393224 | tf_op jit(solution)/shard_map/ppermute | solution.py:404
  38.4 1.6 %collective-permute-start.28 = (bf16[32,2048]{1,0:T(8,128)(2,1)S(1)}, bf16[32,2048]{1,0:T(8,128)(2,1)S(1)}, u32[]{:S(2)}, u32[]{:S(2)}) collective-permute-start(bf16[32,2048]{1,0:T(8,128)(2,1)S(1)} %get-tuple-element.54), channel_id=1, source_target_pairs={{2,0},{1,3},{6,2},{3,7},{10,6},{7,11},{14,10},{11,15},{12,14},{15,... | collective-permute-start | bytes 393224 | tf_op jit(solution)/shard_map/ppermute | solution.py:404
  40.0 1.3 %shard_map.89 = (f32[32,2048]{1,0:T(8,128)S(1)}, f32[32,2048]{1,0:T(8,128)S(1)}, f32[32,2048]{1,0:T(8,128)S(1)}, f32[32,2048]{1,0:T(8,128)S(1)}) custom-call(bf16[32,2176]{1,0:T(8,128)(2,1)S(1)} %collective-permute-done.6.refs_0_, bf16[32,2176]{1,0:T(8,128)(2,1)S(1)} %collective-permute-done.7.refs_1_, bf16[32,2176]{1,0:T(8,128)(2,1)S(1)} %collective-permute-done.8.refs_2_, ...), custom_call_target="tpu_custom_call" | custom-call | flops 805306368 | bytes 2097152 | tf_op jit(solution)/shard_map/pallas_call | solution.py:285
  41.3 1.8 %shard_map.88 = (f32[32,1024]{1,0:T(8,128)S(1)}, f32[32,1024]{1,0:T(8,128)S(1)}, f32[32,2048]{1,0:T(8,128)S(1)}, f32[32,2048]{1,0:T(8,128)S(1)}, f32[32,2048]{1,...) custom-call(bf16[32,2176]{1,0:T(8,128)(2,1)S(1)} %copy-done, ...), custom_call_target="tpu_custom_call" | custom-call | flops 1207959552 | bytes 3145728 | tf_op jit(solution)/shard_map/pallas_call | solution.py:285
  43.2 1.5 %collective-permute-start.17 = (bf16[32,2048]{1,0:T(8,128)(2,1)S(1)}, bf16[32,2048]{1,0:T(8,128)(2,1)S(1)}, u32[]{:S(2)}, u32[]{:S(2)}) collective-permute-start(bf16[32,2048]{1,0:T(8,128)(2,1)S(1)} %add_convert_fusion.7), channel_id=1, source_target_pairs={{2,0},{1,3},{6,2},{3,7},{10,6},{7,11},{14,10},{11,15},{12,14},{15,... | collective-permute-start | bytes 393224 | tf_op jit(solution)/shard_map/ppermute | solution.py:412
  44.8 0.6 collective-permute-start.21
  45.4 0.5 collective-permute-start.25
  45.9 0.5 collective-permute-start.29
  46.5 1.7 %collective-permute-done.17 = bf16[32,2048]{1,0:T(8,128)(2,1)S(1)} collective-permute-done((bf16[32,2048]{1,0:T(8,128)(2,1)S(1)}, bf16[32,2048]{1,0:T(8,128)(2,1)S(1)}, u32[]{:S(2)}, u32[]{:S(2)}) %collective-permute-start.17) | collective-permute-done | bytes 131104 | tf_op jit(solution)/shard_map/ppermute | solution.py:412
  48.2 1.5 %collective-permute-start.18 = (bf16[32,2048]{1,0:T(8,128)(2,1)S(1)}, bf16[32,2048]{1,0:T(8,128)(2,1)S(1)}, u32[]{:S(2)}, u32[]{:S(2)}) collective-permute-start(bf16[32,2048]{1,0:T(8,128)(2,1)S(1)} %add_convert_fusion.6), channel_id=1, source_target_pairs={{2,0},{1,3},{6,2},{3,7},{10,6},{7,11},{14,10},{11,15},{12,14},{15,... | collective-permute-start | bytes 393224 | tf_op jit(solution)/shard_map/ppermute | solution.py:419
  49.8 0.0 collective-permute-done.21
  49.8 1.4 %collective-permute-start.22 = (bf16[32,2048]{1,0:T(8,128)(2,1)S(1)}, bf16[32,2048]{1,0:T(8,128)(2,1)S(1)}, u32[]{:S(2)}, u32[]{:S(2)}) collective-permute-start(bf16[32,2048]{1,0:T(8,128)(2,1)S(1)} %add_convert_fusion.4), channel_id=1, source_target_pairs={{2,0},{1,3},{6,2},{3,7},{10,6},{7,11},{14,10},{11,15},{12,14},{15,... | collective-permute-start | bytes 393224 | tf_op jit(solution)/shard_map/ppermute | solution.py:419
  51.2 0.0 collective-permute-done.25
  51.2 1.4 %collective-permute-start.26 = (bf16[32,2048]{1,0:T(8,128)(2,1)S(1)}, bf16[32,2048]{1,0:T(8,128)(2,1)S(1)}, u32[]{:S(2)}, u32[]{:S(2)}) collective-permute-start(bf16[32,2048]{1,0:T(8,128)(2,1)S(1)} %add_convert_fusion.2), channel_id=1, source_target_pairs={{2,0},{1,3},{6,2},{3,7},{10,6},{7,11},{14,10},{11,15},{12,14},{15,... | collective-permute-start | bytes 393224 | tf_op jit(solution)/shard_map/ppermute | solution.py:404
  52.6 0.0 collective-permute-done.29
  52.6 1.4 %collective-permute-start.30 = (bf16[32,2048]{1,0:T(8,128)(2,1)S(1)}, bf16[32,2048]{1,0:T(8,128)(2,1)S(1)}, u32[]{:S(2)}, u32[]{:S(2)}) collective-permute-start(bf16[32,2048]{1,0:T(8,128)(2,1)S(1)} %add_convert_fusion), channel_id=1, source_target_pairs={{2,0},{1,3},{6,2},{3,7},{10,6},{7,11},{14,10},{11,15},{12,14},{15,... | collective-permute-start | bytes 393224 | tf_op jit(solution)/shard_map/ppermute | solution.py:404
  54.0 0.0 collective-permute-done.18.arrived
  54.0 0.5 collective-permute-start.35
  54.5 0.9 %collective-permute-done.22.arrived = bf16[32,2048]{1,0:T(8,128)(2,1)S(1)} collective-permute-done((bf16[32,2048]{1,0:T(8,128)(2,1)S(1)}, bf16[32,2048]{1,0:T(8,128)(2,1)S(1)}, u32[]{:S(2)}, u32[]{:S(2)}) %collective-permute-start.22) | collective-permute-done | bytes 131104 | tf_op jit(solution)/shard_map/ppermute | solution.py:419
  55.4 1.3 %collective-permute-start.19 = (bf16[32,1024]{1,0:T(8,128)(2,1)S(1)}, bf16[32,1024]{1,0:T(8,128)(2,1)S(1)}, u32[]{:S(2)}, u32[]{:S(2)}) collective-permute-start(bf16[32,1024]{1,0:T(8,128)(2,1)S(1)} %get-tuple-element.43), channel_id=1, source_target_pairs={{2,0},{1,3},{6,2},{3,7},{10,6},{7,11},{14,10},{11,15},{12,14},{15,... | collective-permute-start | bytes 196616 | tf_op jit(solution)/shard_map/ppermute | solution.py:421
  56.7 0.1 collective-permute-done.26.refs_6_
  56.8 1.3 %collective-permute-start.23 = (bf16[32,1024]{1,0:T(8,128)(2,1)S(1)}, bf16[32,1024]{1,0:T(8,128)(2,1)S(1)}, u32[]{:S(2)}, u32[]{:S(2)}) collective-permute-start(bf16[32,1024]{1,0:T(8,128)(2,1)S(1)} %get-tuple-element.48), channel_id=1, source_target_pairs={{2,0},{1,3},{6,2},{3,7},{10,6},{7,11},{14,10},{11,15},{12,14},{15,... | collective-permute-start | bytes 196616 | tf_op jit(solution)/shard_map/ppermute | solution.py:421
  58.1 0.1 collective-permute-done.30.refs_7_
  58.2 0.6 collective-permute-start.31
  58.8 1.0 %collective-permute-start.32 = (bf16[32,1024]{1,0:T(8,128)(2,1)S(1)}, bf16[32,1024]{1,0:T(8,128)(2,1)S(1)}, u32[]{:S(2)}, u32[]{:S(2)}) collective-permute-start(bf16[32,1024]{1,0:T(8,128)(2,1)S(1)} %get-tuple-element.55), channel_id=1, source_target_pairs={{2,1},{1,2},{6,3},{3,6},{10,7},{7,10},{14,11},{11,14},{12,15},{15,... | collective-permute-start | bytes 196616 | tf_op jit(solution)/shard_map/ppermute | solution.py:422
  59.8 0.7 %collective-permute-start.33 = (bf16[32,1024]{1,0:T(8,128)(2,1)S(1)}, bf16[32,1024]{1,0:T(8,128)(2,1)S(1)}, u32[]{:S(2)}, u32[]{:S(2)}) collective-permute-start(bf16[32,1024]{1,0:T(8,128)(2,1)S(1)} %get-tuple-element.56), channel_id=1, source_target_pairs={{2,1},{1,2},{6,3},{3,6},{10,7},{7,10},{14,11},{11,14},{12,15},{15,... | collective-permute-start | bytes 196616 | tf_op jit(solution)/shard_map/ppermute | solution.py:422
  60.6 0.5 collective-permute-done.23.refs_3_
  61.1 1.4 %collective-permute-done.32.refs_8_ = bf16[32,1024]{1,0:T(8,128)(2,1)S(1)} collective-permute-done((bf16[32,1024]{1,0:T(8,128)(2,1)S(1)}, bf16[32,1024]{1,0:T(8,128)(2,1)S(1)}, u32[]{:S(2)}, u32[]{:S(2)}) %collective-permute-start.32) | collective-permute-done | bytes 65568 | tf_op jit(solution)/shard_map/ppermute | solution.py:422
  62.5 1.0 %collective-permute-done.33.refs_9_ = bf16[32,1024]{1,0:T(8,128)(2,1)S(1)} collective-permute-done((bf16[32,1024]{1,0:T(8,128)(2,1)S(1)}, bf16[32,1024]{1,0:T(8,128)(2,1)S(1)}, u32[]{:S(2)}, u32[]{:S(2)}) %collective-permute-start.33) | collective-permute-done | bytes 65568 | tf_op jit(solution)/shard_map/ppermute | solution.py:422
  63.5 0.8 %shard_map.94 = bf16[2,64,1024]{2,1,0:T(8,128)(2,1)} custom-call(f32[32,1024]{1,0:T(8,128)S(1)} %get-tuple-element.37.refs_0_, f32[32,1024]{1,0:T(8,128)S(1)} %get-tuple-element.38.refs_1_, bf16[32,1024]{1,0:T(8,128)(2,1)S(1)} %collective-permute-done.19.refs_2_, bf16[32,1024]{1,0:T(8,128)(2,1)S(1)} %collective-permute-done.23.refs_3_, ...), custom_call_target="tpu_custom_call" | custom-call | tf_op jit(solution)/shard_map/pallas_call | solution.py:342
  (33 shorter events, 0.4 us)
Async XLA Ops:
  0.6 31.4 %collective-permute-start.4 = (bf16[2048,384]{1,0:T(8,128)(2,1)}, bf16[2048,384]{1,0:T(8,128)(2,1)S(1)}, u32[]{:S(2)}, u32[]{:S(2)}) collective-permute-start(bf16[2048,384]{1,0:T(8,128)(2,1)} %bitcast.4), channel_id=1, source_target_pairs={{0,1},{1,0},{2,3},{3,2},{4,5},{5,4},{6,7},{7,6},{8,9},{9,8},{10,11... | collective-permute-start | bytes 4718600 | tf_op jit(solution)/shard_map/ppermute | solution.py:380
  1.2 30.9 %collective-permute-start.5 = (bf16[768,1024]{1,0:T(8,128)(2,1)}, bf16[768,1024]{1,0:T(8,128)(2,1)S(1)}, u32[]{:S(2)}, u32[]{:S(2)}) collective-permute-start(bf16[768,1024]{1,0:T(8,128)(2,1)} %bitcast.6), channel_id=1, source_target_pairs={{0,1},{1,0},{2,3},{3,2},{4,5},{5,4},{6,7},{7,6},{8,9},{9,8},{10,11... | collective-permute-start | bytes 4718600 | tf_op jit(solution)/shard_map/ppermute | solution.py:381
  3.3 6.3 %collective-permute-start = (bf16[32,2176]{1,0:T(8,128)(2,1)}, bf16[32,2176]{1,0:T(8,128)(2,1)S(1)}, u32[]{:S(2)}, u32[]{:S(2)}) collective-permute-start(bf16[32,2176]{1,0:T(8,128)(2,1)} %get-tuple-element.31.refs_0_), channel_id=1, source_target_pairs={{0,2},{3,1},{2,6},{7,3},{6,10},{11,7},{10,14},{15,11},{14,12},{13,... | collective-permute-start | bytes 417800 | tf_op jit(solution)/shard_map/ppermute | solution.py:376
  6.2 5.3 %collective-permute-start.1 = (bf16[32,2176]{1,0:T(8,128)(2,1)}, bf16[32,2176]{1,0:T(8,128)(2,1)S(1)}, u32[]{:S(2)}, u32[]{:S(2)}) collective-permute-start(bf16[32,2176]{1,0:T(8,128)(2,1)} %get-tuple-element.32.refs_1_), channel_id=1, source_target_pairs={{0,2},{3,1},{2,6},{7,3},{6,10},{11,7},{10,14},{15,11},{14,12},{13,... | collective-permute-start | bytes 417800 | tf_op jit(solution)/shard_map/ppermute | solution.py:376
  7.8 5.3 %collective-permute-start.2 = (bf16[32,2176]{1,0:T(8,128)(2,1)}, bf16[32,2176]{1,0:T(8,128)(2,1)S(1)}, u32[]{:S(2)}, u32[]{:S(2)}) collective-permute-start(bf16[32,2176]{1,0:T(8,128)(2,1)} %get-tuple-element.33), channel_id=1, source_target_pairs={{0,2},{3,1},{2,6},{7,3},{6,10},{11,7},{10,14},{15,11},{14,12},{13,... | collective-permute-start | bytes 417800 | tf_op jit(solution)/shard_map/ppermute | solution.py:378
  9.6 5.3 %collective-permute-start.3 = (bf16[32,2176]{1,0:T(8,128)(2,1)}, bf16[32,2176]{1,0:T(8,128)(2,1)S(1)}, u32[]{:S(2)}, u32[]{:S(2)}) collective-permute-start(bf16[32,2176]{1,0:T(8,128)(2,1)} %get-tuple-element.34), channel_id=1, source_target_pairs={{0,2},{3,1},{2,6},{7,3},{6,10},{11,7},{10,14},{15,11},{14,12},{13,... | collective-permute-start | bytes 417800 | tf_op jit(solution)/shard_map/ppermute | solution.py:378
  11.5 5.3 %collective-permute-start.6 = (bf16[32,2176]{1,0:T(8,128)(2,1)S(1)}, bf16[32,2176]{1,0:T(8,128)(2,1)S(1)}, u32[]{:S(2)}, u32[]{:S(2)}) collective-permute-start(bf16[32,2176]{1,0:T(8,128)(2,1)S(1)} %collective-permute-done.refs_2_), channel_id=1, source_target_pairs={{0,2},{3,1},{2,6},{7,3},{6,10},{11,7},{10,14},{15,11},{14,12},{13,... | collective-permute-start | bytes 417800 | tf_op jit(solution)/shard_map/ppermute | solution.py:376
  13.1 5.3 %collective-permute-start.7 = (bf16[32,2176]{1,0:T(8,128)(2,1)S(1)}, bf16[32,2176]{1,0:T(8,128)(2,1)S(1)}, u32[]{:S(2)}, u32[]{:S(2)}) collective-permute-start(bf16[32,2176]{1,0:T(8,128)(2,1)S(1)} %collective-permute-done.1.refs_3_), channel_id=1, source_target_pairs={{0,2},{3,1},{2,6},{7,3},{6,10},{11,7},{10,14},{15,11},{14,12},{13,... | collective-permute-start | bytes 417800 | tf_op jit(solution)/shard_map/ppermute | solution.py:376
  14.8 5.1 %collective-permute-start.8 = (bf16[32,2176]{1,0:T(8,128)(2,1)S(1)}, bf16[32,2176]{1,0:T(8,128)(2,1)S(1)}, u32[]{:S(2)}, u32[]{:S(2)}) collective-permute-start(bf16[32,2176]{1,0:T(8,128)(2,1)S(1)} %collective-permute-done.2.refs_4_), channel_id=1, source_target_pairs={{0,2},{3,1},{2,6},{7,3},{6,10},{11,7},{10,14},{15,11},{14,12},{13,... | collective-permute-start | bytes 417800 | tf_op jit(solution)/shard_map/ppermute | solution.py:378
  16.8 5.1 %collective-permute-start.10 = (bf16[32,2176]{1,0:T(8,128)(2,1)S(1)}, bf16[32,2176]{1,0:T(8,128)(2,1)S(1)}, u32[]{:S(2)}, u32[]{:S(2)}) collective-permute-start(bf16[32,2176]{1,0:T(8,128)(2,1)S(1)} %collective-permute-done.6.refs_0_), channel_id=1, source_target_pairs={{0,2},{3,1},{2,6},{7,3},{6,10},{11,7},{10,14},{15,11},{14,12},{13,... | collective-permute-start | bytes 417800 | tf_op jit(solution)/shard_map/ppermute | solution.py:376
  18.3 5.1 %collective-permute-start.11 = (bf16[32,2176]{1,0:T(8,128)(2,1)S(1)}, bf16[32,2176]{1,0:T(8,128)(2,1)S(1)}, u32[]{:S(2)}, u32[]{:S(2)}) collective-permute-start(bf16[32,2176]{1,0:T(8,128)(2,1)S(1)} %collective-permute-done.7.refs_1_), channel_id=1, source_target_pairs={{0,2},{3,1},{2,6},{7,3},{6,10},{11,7},{10,14},{15,11},{14,12},{13,... | collective-permute-start | bytes 417800 | tf_op jit(solution)/shard_map/ppermute | solution.py:376
  19.9 5.1 %collective-permute-start.9 = (bf16[32,2176]{1,0:T(8,128)(2,1)S(1)}, bf16[32,2176]{1,0:T(8,128)(2,1)S(1)}, u32[]{:S(2)}, u32[]{:S(2)}) collective-permute-start(bf16[32,2176]{1,0:T(8,128)(2,1)S(1)} %collective-permute-done.3.refs_5_), channel_id=1, source_target_pairs={{0,2},{3,1},{2,6},{7,3},{6,10},{11,7},{10,14},{15,11},{14,12},{13,... | collective-permute-start | bytes 417800 | tf_op jit(solution)/shard_map/ppermute | solution.py:378
  21.8 5.1 %collective-permute-start.14 = (bf16[32,2176]{1,0:T(8,128)(2,1)S(1)}, bf16[32,2176]{1,0:T(8,128)(2,1)S(1)}, u32[]{:S(2)}, u32[]{:S(2)}) collective-permute-start(bf16[32,2176]{1,0:T(8,128)(2,1)S(1)} %collective-permute-done.10.refs_0_), channel_id=1, source_target_pairs={{0,2},{3,1},{2,6},{7,3},{6,10},{11,7},{10,14},{15,11},{14,12},{13,... | collective-permute-start | bytes 417800 | tf_op jit(solution)/shard_map/ppermute | solution.py:376
  23.4 8.7 %collective-permute-start.15 = (bf16[32,2176]{1,0:T(8,128)(2,1)S(1)}, bf16[32,2176]{1,0:T(8,128)(2,1)S(1)}, u32[]{:S(2)}, u32[]{:S(2)}) collective-permute-start(bf16[32,2176]{1,0:T(8,128)(2,1)S(1)} %collective-permute-done.11.refs_1_), channel_id=1, source_target_pairs={{0,2},{3,1},{2,6},{7,3},{6,10},{11,7},{10,14},{15,11},{14,12},{13,... | collective-permute-start | bytes 417800 | tf_op jit(solution)/shard_map/ppermute | solution.py:376
  25.0 10.5 %collective-permute-start.12 = (bf16[32,2176]{1,0:T(8,128)(2,1)S(1)}, bf16[32,2176]{1,0:T(8,128)(2,1)S(1)}, u32[]{:S(2)}, u32[]{:S(2)}) collective-permute-start(bf16[32,2176]{1,0:T(8,128)(2,1)S(1)} %collective-permute-done.8.refs_2_), channel_id=1, source_target_pairs={{0,2},{3,1},{2,6},{7,3},{6,10},{11,7},{10,14},{15,11},{14,12},{13,... | collective-permute-start | bytes 417800 | tf_op jit(solution)/shard_map/ppermute | solution.py:378
  26.9 8.6 %collective-permute-start.13 = (bf16[32,2176]{1,0:T(8,128)(2,1)S(1)}, bf16[32,2176]{1,0:T(8,128)(2,1)S(1)}, u32[]{:S(2)}, u32[]{:S(2)}) collective-permute-start(bf16[32,2176]{1,0:T(8,128)(2,1)S(1)} %collective-permute-done.9.refs_3_), channel_id=1, source_target_pairs={{0,2},{3,1},{2,6},{7,3},{6,10},{11,7},{10,14},{15,11},{14,12},{13,... | collective-permute-start | bytes 417800 | tf_op jit(solution)/shard_map/ppermute | solution.py:378
  28.4 0.7 %copy-start.2 = (s32[16]{0:T(128)S(1)}, s32[16]{0:T(128)}, u32[]{:S(2)}) copy-start(s32[16]{0:T(128)} %new_place.1) | copy-start | bytes 196
  33.4 9.7 %collective-permute-start.16 = (bf16[32,2048]{1,0:T(8,128)(2,1)S(1)}, bf16[32,2048]{1,0:T(8,128)(2,1)S(1)}, u32[]{:S(2)}, u32[]{:S(2)}) collective-permute-start(bf16[32,2048]{1,0:T(8,128)(2,1)S(1)} %get-tuple-element.42), channel_id=1, source_target_pairs={{2,0},{1,3},{6,2},{3,7},{10,6},{7,11},{14,10},{11,15},{12,14},{15,... | collective-permute-start | bytes 393224 | tf_op jit(solution)/shard_map/ppermute | solution.py:412
  33.9 10.8 %collective-permute-start.20 = (bf16[32,2048]{1,0:T(8,128)(2,1)S(1)}, bf16[32,2048]{1,0:T(8,128)(2,1)S(1)}, u32[]{:S(2)}, u32[]{:S(2)}) collective-permute-start(bf16[32,2048]{1,0:T(8,128)(2,1)S(1)} %get-tuple-element.47), channel_id=1, source_target_pairs={{2,0},{1,3},{6,2},{3,7},{10,6},{7,11},{14,10},{11,15},{12,14},{15,... | collective-permute-start | bytes 393224 | tf_op jit(solution)/shard_map/ppermute | solution.py:412
  36.8 8.6 %collective-permute-start.24 = (bf16[32,2048]{1,0:T(8,128)(2,1)S(1)}, bf16[32,2048]{1,0:T(8,128)(2,1)S(1)}, u32[]{:S(2)}, u32[]{:S(2)}) collective-permute-start(bf16[32,2048]{1,0:T(8,128)(2,1)S(1)} %get-tuple-element.51), channel_id=1, source_target_pairs={{2,0},{1,3},{6,2},{3,7},{10,6},{7,11},{14,10},{11,15},{12,14},{15,... | collective-permute-start | bytes 393224 | tf_op jit(solution)/shard_map/ppermute | solution.py:404
  38.4 2.9 %copy-start = (bf16[32,2176]{1,0:T(8,128)(2,1)S(1)}, bf16[32,2176]{1,0:T(8,128)(2,1)}, u32[]{:S(2)}) copy-start(bf16[32,2176]{1,0:T(8,128)(2,1)} %get-tuple-element.31.refs_0_) | copy-start | bytes 417796
  38.4 2.9 %copy-start.1 = (bf16[32,2176]{1,0:T(8,128)(2,1)S(1)}, bf16[32,2176]{1,0:T(8,128)(2,1)}, u32[]{:S(2)}) copy-start(bf16[32,2176]{1,0:T(8,128)(2,1)} %get-tuple-element.32.refs_1_) | copy-start | bytes 417796
  38.4 7.5 %collective-permute-start.28 = (bf16[32,2048]{1,0:T(8,128)(2,1)S(1)}, bf16[32,2048]{1,0:T(8,128)(2,1)S(1)}, u32[]{:S(2)}, u32[]{:S(2)}) collective-permute-start(bf16[32,2048]{1,0:T(8,128)(2,1)S(1)} %get-tuple-element.54), channel_id=1, source_target_pairs={{2,0},{1,3},{6,2},{3,7},{10,6},{7,11},{14,10},{11,15},{12,14},{15,... | collective-permute-start | bytes 393224 | tf_op jit(solution)/shard_map/ppermute | solution.py:404
  43.2 5.0 %collective-permute-start.17 = (bf16[32,2048]{1,0:T(8,128)(2,1)S(1)}, bf16[32,2048]{1,0:T(8,128)(2,1)S(1)}, u32[]{:S(2)}, u32[]{:S(2)}) collective-permute-start(bf16[32,2048]{1,0:T(8,128)(2,1)S(1)} %add_convert_fusion.7), channel_id=1, source_target_pairs={{2,0},{1,3},{6,2},{3,7},{10,6},{7,11},{14,10},{11,15},{12,14},{15,... | collective-permute-start | bytes 393224 | tf_op jit(solution)/shard_map/ppermute | solution.py:412
  44.8 5.0 %collective-permute-start.21 = (bf16[32,2048]{1,0:T(8,128)(2,1)S(1)}, bf16[32,2048]{1,0:T(8,128)(2,1)S(1)}, u32[]{:S(2)}, u32[]{:S(2)}) collective-permute-start(bf16[32,2048]{1,0:T(8,128)(2,1)S(1)} %add_convert_fusion.5), channel_id=1, source_target_pairs={{2,0},{1,3},{6,2},{3,7},{10,6},{7,11},{14,10},{11,15},{12,14},{15,... | collective-permute-start | bytes 393224 | tf_op jit(solution)/shard_map/ppermute | solution.py:412
  45.4 5.8 %collective-permute-start.25 = (bf16[32,2048]{1,0:T(8,128)(2,1)S(1)}, bf16[32,2048]{1,0:T(8,128)(2,1)S(1)}, u32[]{:S(2)}, u32[]{:S(2)}) collective-permute-start(bf16[32,2048]{1,0:T(8,128)(2,1)S(1)} %add_convert_fusion.3), channel_id=1, source_target_pairs={{2,0},{1,3},{6,2},{3,7},{10,6},{7,11},{14,10},{11,15},{12,14},{15,... | collective-permute-start | bytes 393224 | tf_op jit(solution)/shard_map/ppermute | solution.py:404
  45.9 6.7 %collective-permute-start.29 = (bf16[32,2048]{1,0:T(8,128)(2,1)S(1)}, bf16[32,2048]{1,0:T(8,128)(2,1)S(1)}, u32[]{:S(2)}, u32[]{:S(2)}) collective-permute-start(bf16[32,2048]{1,0:T(8,128)(2,1)S(1)} %add_convert_fusion.1), channel_id=1, source_target_pairs={{2,0},{1,3},{6,2},{3,7},{10,6},{7,11},{14,10},{11,15},{12,14},{15,... | collective-permute-start | bytes 393224 | tf_op jit(solution)/shard_map/ppermute | solution.py:404
  48.2 5.8 %collective-permute-start.18 = (bf16[32,2048]{1,0:T(8,128)(2,1)S(1)}, bf16[32,2048]{1,0:T(8,128)(2,1)S(1)}, u32[]{:S(2)}, u32[]{:S(2)}) collective-permute-start(bf16[32,2048]{1,0:T(8,128)(2,1)S(1)} %add_convert_fusion.6), channel_id=1, source_target_pairs={{2,0},{1,3},{6,2},{3,7},{10,6},{7,11},{14,10},{11,15},{12,14},{15,... | collective-permute-start | bytes 393224 | tf_op jit(solution)/shard_map/ppermute | solution.py:419
  49.8 5.6 %collective-permute-start.22 = (bf16[32,2048]{1,0:T(8,128)(2,1)S(1)}, bf16[32,2048]{1,0:T(8,128)(2,1)S(1)}, u32[]{:S(2)}, u32[]{:S(2)}) collective-permute-start(bf16[32,2048]{1,0:T(8,128)(2,1)S(1)} %add_convert_fusion.4), channel_id=1, source_target_pairs={{2,0},{1,3},{6,2},{3,7},{10,6},{7,11},{14,10},{11,15},{12,14},{15,... | collective-permute-start | bytes 393224 | tf_op jit(solution)/shard_map/ppermute | solution.py:419
  51.2 5.6 %collective-permute-start.26 = (bf16[32,2048]{1,0:T(8,128)(2,1)S(1)}, bf16[32,2048]{1,0:T(8,128)(2,1)S(1)}, u32[]{:S(2)}, u32[]{:S(2)}) collective-permute-start(bf16[32,2048]{1,0:T(8,128)(2,1)S(1)} %add_convert_fusion.2), channel_id=1, source_target_pairs={{2,0},{1,3},{6,2},{3,7},{10,6},{7,11},{14,10},{11,15},{12,14},{15,... | collective-permute-start | bytes 393224 | tf_op jit(solution)/shard_map/ppermute | solution.py:404
  52.6 5.6 %collective-permute-start.30 = (bf16[32,2048]{1,0:T(8,128)(2,1)S(1)}, bf16[32,2048]{1,0:T(8,128)(2,1)S(1)}, u32[]{:S(2)}, u32[]{:S(2)}) collective-permute-start(bf16[32,2048]{1,0:T(8,128)(2,1)S(1)} %add_convert_fusion), channel_id=1, source_target_pairs={{2,0},{1,3},{6,2},{3,7},{10,6},{7,11},{14,10},{11,15},{12,14},{15,... | collective-permute-start | bytes 393224 | tf_op jit(solution)/shard_map/ppermute | solution.py:404
  54.0 4.2 %collective-permute-start.34 = (bf16[32,1024]{1,0:T(8,128)(2,1)S(1)}, bf16[32,1024]{1,0:T(8,128)(2,1)S(1)}, u32[]{:S(2)}, u32[]{:S(2)}) collective-permute-start(bf16[32,1024]{1,0:T(8,128)(2,1)S(1)} %get-tuple-element.57), channel_id=1, source_target_pairs={{0,1},{1,0},{2,3},{3,2},{4,5},{5,4},{6,7},{7,6},{8,9},{9,8},{10,11... | collective-permute-start | bytes 196616 | tf_op jit(solution)/shard_map/ppermute | solution.py:401
  54.0 4.8 %collective-permute-start.35 = (bf16[32,1024]{1,0:T(8,128)(2,1)S(1)}, bf16[32,1024]{1,0:T(8,128)(2,1)S(1)}, u32[]{:S(2)}, u32[]{:S(2)}) collective-permute-start(bf16[32,1024]{1,0:T(8,128)(2,1)S(1)} %get-tuple-element.58), channel_id=1, source_target_pairs={{0,1},{1,0},{2,3},{3,2},{4,5},{5,4},{6,7},{7,6},{8,9},{9,8},{10,11... | collective-permute-start | bytes 196616 | tf_op jit(solution)/shard_map/ppermute | solution.py:401
  55.4 4.4 %collective-permute-start.19 = (bf16[32,1024]{1,0:T(8,128)(2,1)S(1)}, bf16[32,1024]{1,0:T(8,128)(2,1)S(1)}, u32[]{:S(2)}, u32[]{:S(2)}) collective-permute-start(bf16[32,1024]{1,0:T(8,128)(2,1)S(1)} %get-tuple-element.43), channel_id=1, source_target_pairs={{2,0},{1,3},{6,2},{3,7},{10,6},{7,11},{14,10},{11,15},{12,14},{15,... | collective-permute-start | bytes 196616 | tf_op jit(solution)/shard_map/ppermute | solution.py:421
  56.8 4.3 %collective-permute-start.23 = (bf16[32,1024]{1,0:T(8,128)(2,1)S(1)}, bf16[32,1024]{1,0:T(8,128)(2,1)S(1)}, u32[]{:S(2)}, u32[]{:S(2)}) collective-permute-start(bf16[32,1024]{1,0:T(8,128)(2,1)S(1)} %get-tuple-element.48), channel_id=1, source_target_pairs={{2,0},{1,3},{6,2},{3,7},{10,6},{7,11},{14,10},{11,15},{12,14},{15,... | collective-permute-start | bytes 196616 | tf_op jit(solution)/shard_map/ppermute | solution.py:421
  58.2 2.9 %collective-permute-start.27 = (bf16[32,1024]{1,0:T(8,128)(2,1)S(1)}, bf16[32,1024]{1,0:T(8,128)(2,1)S(1)}, u32[]{:S(2)}, u32[]{:S(2)}) collective-permute-start(bf16[32,1024]{1,0:T(8,128)(2,1)S(1)} %slice.8), channel_id=1, source_target_pairs={{0,1},{1,0},{2,3},{3,2},{4,5},{5,4},{6,7},{7,6},{8,9},{9,8},{10,11... | collective-permute-start | bytes 196616 | tf_op jit(solution)/shard_map/ppermute | solution.py:410
  58.2 2.8 %collective-permute-start.31 = (bf16[32,1024]{1,0:T(8,128)(2,1)S(1)}, bf16[32,1024]{1,0:T(8,128)(2,1)S(1)}, u32[]{:S(2)}, u32[]{:S(2)}) collective-permute-start(bf16[32,1024]{1,0:T(8,128)(2,1)S(1)} %slice.9), channel_id=1, source_target_pairs={{0,1},{1,0},{2,3},{3,2},{4,5},{5,4},{6,7},{7,6},{8,9},{9,8},{10,11... | collective-permute-start | bytes 196616 | tf_op jit(solution)/shard_map/ppermute | solution.py:410
  58.8 3.7 %collective-permute-start.32 = (bf16[32,1024]{1,0:T(8,128)(2,1)S(1)}, bf16[32,1024]{1,0:T(8,128)(2,1)S(1)}, u32[]{:S(2)}, u32[]{:S(2)}) collective-permute-start(bf16[32,1024]{1,0:T(8,128)(2,1)S(1)} %get-tuple-element.55), channel_id=1, source_target_pairs={{2,1},{1,2},{6,3},{3,6},{10,7},{7,10},{14,11},{11,14},{12,15},{15,... | collective-permute-start | bytes 196616 | tf_op jit(solution)/shard_map/ppermute | solution.py:422
  59.8 3.7 %collective-permute-start.33 = (bf16[32,1024]{1,0:T(8,128)(2,1)S(1)}, bf16[32,1024]{1,0:T(8,128)(2,1)S(1)}, u32[]{:S(2)}, u32[]{:S(2)}) collective-permute-start(bf16[32,1024]{1,0:T(8,128)(2,1)S(1)} %get-tuple-element.56), channel_id=1, source_target_pairs={{2,1},{1,2},{6,3},{3,6},{10,7},{7,10},{14,11},{11,14},{12,15},{15,... | collective-permute-start | bytes 196616 | tf_op jit(solution)/shard_map/ppermute | solution.py:422

commit v2 on v0

--- a/solution.py
+++ b/solution.py
@@ -10,6 +10,8 @@
 REPLICAS = 4
 LANES = 128
 VMEM_BYTES = 67043328
+PIECES = 2
+SUBLANES = 16
 
 
 def earlier_same(labels):
@@ -131,9 +133,16 @@
     return tuple(extend([0]) or range(count))
 
 
-def pack_kernel(caps, routes_in, probs_in, old_in, new_in, tokens, first, second, slot_rows, *scratch):
-    routes, probs, old_place, new_place, sems = scratch
-    core = lax.axis_index("tensor")
+def count_of(new_place, expert, stop):
+    return sum(
+        ((new_place[s] == expert) & (s < stop)).astype(jnp.int32)
+        for s in range(new_place.shape[0])
+    )
+
+
+def pack_kernel(caps, routes_in, probs_in, old_in, new_in, tokens, *refs):
+    first, second, slot_rows, routes, probs, old_place, new_place, sems = refs
+    core, devices = lax.axis_index("tensor"), lax.axis_size("expert")
     width = tokens.shape[2]
     token_count = routes.shape[2]
     experts, slots = old_place.shape[0], new_place.shape[0]
@@ -152,33 +161,25 @@
     for copy in copies[:4]:
         copy.wait()
     token = lax.broadcasted_iota(jnp.int32, (1, token_count), 1)
-
-    def holders_of(expert):
-        return sum((new_place[s] == expert).astype(jnp.int32) for s in range(slots))
-
-    limits = [[caps[0]] * experts, [caps[1] * holders_of(old_place[e]) for e in range(experts)]]
+    limits = [caps[1] * count_of(new_place, old_place[e], slots) for e in range(experts)]
     for out, batch in ((first, core), (second, 1 - core)):
         highs, lows = [], []
         for e in range(experts):
             named = routes[batch] == old_place[e]
             weight = jnp.sum(jnp.where(named, probs[batch], 0.0), axis=0, keepdims=True)
-            served = jnp.where(batch == 0, limits[0][e], limits[1][e])
+            served = jnp.where(batch == 0, caps[0], limits[e])
             weight = jnp.where(token < served, weight, 0.0)
             high = weight.astype(jnp.bfloat16).astype(jnp.float32)
             highs.append(high)
             lows.append(weight - high)
         pad = jnp.zeros((lanes - 2 * experts, token_count), jnp.float32)
         out[:, width:] = jnp.concatenate(highs + lows + [pad], axis=0).T.astype(jnp.bfloat16)
-
-    devices = lax.axis_size("expert")
-    mine = slots // devices
+    mine = slot_rows.shape[0]
     for j in range(mine):
         slot = lax.axis_index("expert") * mine + j
         expert = new_place[slot]
-        holders = holders_of(expert)
-        place = sum(
-            ((new_place[s] == expert) & (s < slot)).astype(jnp.int32) for s in range(slots)
-        )
+        holders = count_of(new_place, expert, slots)
+        place = count_of(new_place, expert, slot)
         count = jnp.int32(0)
         for source in range(devices):
             start = lax.rem(place - source + devices * holders, holders)
@@ -193,9 +194,9 @@
     experts = old_place.shape[0]
     lanes = -(-2 * experts // LANES) * LANES
     chunk = jax.ShapeDtypeStruct((token_count, width + lanes), tokens.dtype)
+    routes, probs = routes.transpose(0, 2, 1), probs.transpose(0, 2, 1)
+    mine = new_place.shape[0] // lax.axis_size("expert")
     vmem, smem = pl.BlockSpec(memory_space=pltpu.VMEM), pl.BlockSpec(memory_space=pltpu.SMEM)
-    mine = new_place.shape[0] // lax.axis_size("expert")
-    routes, probs = routes.transpose(0, 2, 1), probs.transpose(0, 2, 1)
     return pl.pallas_call(
         functools.partial(pack_kernel, caps),
         out_shape=(chunk, chunk, jax.ShapeDtypeStruct((mine,), jnp.int32)),
@@ -208,9 +209,7 @@
             pltpu.SMEM(new_place.shape, jnp.int32),
             pltpu.SemaphoreType.DMA((6,)),
         ],
-        compiler_params=pltpu.CompilerParams(
-            vmem_limit_bytes=VMEM_BYTES - (4 << 20)
-        ),
+        compiler_params=pltpu.CompilerParams(vmem_limit_bytes=VMEM_BYTES - (4 << 20)),
     )(routes, probs, old_place, new_place, tokens)
 
 
@@ -243,10 +242,11 @@
     )(up, down)
 
 
-def expert_kernel(chunks, width, experts, *refs):
+def expert_kernel(outlets, width, experts, *refs):
+    chunks = len(outlets)
     rows, refs = refs[:chunks], refs[chunks:]
     (up_own, up_pair, down_own, down_pair), refs = refs[:4], refs[4:]
-    outs, x_buf = refs[:chunks], refs[chunks]
+    outs, x_buf = list(refs[:-1]), refs[-1]
     slot, core = lax.axis_index("expert"), lax.axis_index("tensor")
     size = rows[0].shape[0]
     lane = lax.broadcasted_iota(jnp.int32, (size, rows[0].shape[1] - width), 1)
@@ -266,23 +266,39 @@
     high = jnp.where(core == 0, parts[1], parts[0])
     hidden = jnp.concatenate([low, high], axis=1)
     half = down_own.shape[1]
+    groups = []
+    for kind, _ in outlets:
+        groups.append([outs.pop(0) for _ in range(2 if kind == "halves" else kind)])
     for j, down in enumerate((down_own, down_pair)):
         y = jnp.dot(hidden, down[...], preferred_element_type=jnp.float32)
         y = y.astype(jnp.bfloat16).astype(jnp.float32) * scale
-        for i, out in enumerate(outs):
-            out[:, j * half : (j + 1) * half] = y[i * size : (i + 1) * size].astype(out.dtype)
-
-
-def expert_rows(rows, weights, width, experts, out_types):
+        for i, (kind, _) in enumerate(outlets):
+            made = y[i * size : (i + 1) * size]
+            if kind == "halves":
+                groups[i][j][...] = made.astype(groups[i][j].dtype)
+                continue
+            step = size // kind
+            for n, out in enumerate(groups[i]):
+                piece = made[n * step : (n + 1) * step]
+                out[:, j * half : (j + 1) * half] = piece.astype(out.dtype)
+
+
+def expert_rows(rows, weights, width, experts, outlets):
     chunks, size = len(rows), rows[0].shape[0]
     up = weights[0]
     total = chunks * size
     vmem = pl.BlockSpec(memory_space=pltpu.VMEM)
-    return pl.pallas_call(
-        functools.partial(expert_kernel, chunks, width, experts),
-        out_shape=[jax.ShapeDtypeStruct((size, width), t) for t in out_types],
+    shapes = []
+    for kind, held in outlets:
+        if kind == "halves":
+            shapes.append([((size, width // 2), t) for t in (jnp.float32, jnp.bfloat16)])
+        else:
+            shapes.append([((size // kind, width), held)] * kind)
+    made = pl.pallas_call(
+        functools.partial(expert_kernel, outlets, width, experts),
+        out_shape=[jax.ShapeDtypeStruct(*s) for group in shapes for s in group],
         in_specs=[vmem] * (chunks + 4),
-        out_specs=[vmem] * chunks,
+        out_specs=[vmem] * sum(len(group) for group in shapes),
         scratch_shapes=[pltpu.VMEM((total, width), jnp.bfloat16)],
         compiler_params=pltpu.CompilerParams(vmem_limit_bytes=20 << 20),
         cost_estimate=pl.CostEstimate(
@@ -291,46 +307,52 @@
             transcendentals=2 * total * up.shape[1],
         ),
     )(*rows, *weights)
-
-
-def last_add_kernel(part, arrived, kept, leaving):
-    half = kept.shape[1]
-    kept[...] = part[:, :half] + arrived[:, :half].astype(jnp.float32)
-    leaving[...] = (part[:, half:] + arrived[:, half:].astype(jnp.float32)).astype(leaving.dtype)
-
-
-def last_add(part, arrived):
+    made = list(made)
+    return [[made.pop(0) for _ in group] for group in shapes]
+
+
+def split_add_kernel(part, arrived, own, pair):
+    half = own.shape[1]
+    own[...] = (part[:, :half] + arrived[:, :half].astype(jnp.float32)).astype(own.dtype)
+    pair[...] = (part[:, half:] + arrived[:, half:].astype(jnp.float32)).astype(pair.dtype)
+
+
+def split_add(part, arrived):
     size, half = part.shape[0], part.shape[1] // 2
     vmem = pl.BlockSpec(memory_space=pltpu.VMEM)
     return pl.pallas_call(
-        last_add_kernel,
-        out_shape=(
-            jax.ShapeDtypeStruct((size, half), jnp.float32),
-            jax.ShapeDtypeStruct((size, half), jnp.bfloat16),
-        ),
+        split_add_kernel,
+        out_shape=[jax.ShapeDtypeStruct((size, half), jnp.bfloat16)] * 2,
         in_specs=[vmem, vmem],
-        out_specs=(vmem, vmem),
+        out_specs=[vmem, vmem],
         compiler_params=pltpu.CompilerParams(vmem_limit_bytes=4 << 20),
     )(part, arrived)
 
 
-def finish_kernel(kept, from_second, second, from_first, mixed):
+def finish_kernel(pieces, own, own_pair, *refs):
+    arrived, second_pair, second, crossed = (refs[i * pieces : (i + 1) * pieces] for i in range(4))
+    mixed = refs[-1]
     core = lax.axis_index("tensor")
     half = mixed.shape[2]
-    mixed[core] = (kept[...] + from_second[...].astype(jnp.float32)).astype(mixed.dtype)
-    other = second[:, :half].astype(jnp.float32) + from_first[...].astype(jnp.float32)
-    mixed[1 - core] = other.astype(mixed.dtype)
-
-
-def finish(kept, from_second, second, from_first):
+    size = own.shape[0] // pieces
+    f32 = jnp.float32
+    for i in range(pieces):
+        rows = slice(i * size, (i + 1) * size)
+        total = own[rows] + arrived[i][...].astype(f32) + second_pair[i][...].astype(f32)
+        mixed[core, rows] = total.astype(mixed.dtype)
+        total = second[i][:, :half].astype(f32) + crossed[i][...].astype(f32)
+        mixed[1 - core, rows] = (total + own_pair[rows].astype(f32)).astype(mixed.dtype)
+
+
+def finish(pieces, own, own_pair, *groups):
     vmem = pl.BlockSpec(memory_space=pltpu.VMEM)
     return pl.pallas_call(
-        finish_kernel,
-        out_shape=jax.ShapeDtypeStruct((2, *kept.shape), jnp.bfloat16),
-        in_specs=[vmem] * 4,
+        functools.partial(finish_kernel, pieces),
+        out_shape=jax.ShapeDtypeStruct((2, *own.shape), jnp.bfloat16),
+        in_specs=[vmem] * (2 + 4 * pieces),
         out_specs=vmem,
         compiler_params=pltpu.CompilerParams(vmem_limit_bytes=4 << 20),
-    )(kept, from_second, second, from_first)
+    )(own, own_pair, *sum((list(g) for g in groups), []))
 
 
 def by_ring(ring, tokens, routes, probs, up_weight, down_weight, old_place, new_place):
@@ -345,15 +367,17 @@
         there = ring[(spot + 1) % devices]
         ahead += [(2 * here, 2 * there), (2 * there + 1, 2 * here + 1)]
     back = [(b, a) for a, b in ahead]
+    across = [(b, a ^ 1) for a, b in ahead]
     swap = [(0, 1), (1, 0)]
     f32, bf16 = jnp.float32, jnp.bfloat16
+    half, pieces = width // 2, PIECES if token_count % (PIECES * SUBLANES) == 0 else 1
+    each = range(pieces)
 
     caps = (
         capacity_for(block_rows, experts, token_count),
         capacity_for(block_rows, new_place.shape[0], token_count),
     )
     own_first, own_second, slot_rows = pack(caps, tokens, routes, probs, old_place, new_place)
-
     first, second = [own_first], [own_second]
     for step in range(1, steps + 1):
         first.append(lax.ppermute(first[-1], both, ahead))
@@ -365,30 +389,44 @@
     up_here, down_here = load(up_own, down_own)
     weights = (up_here, up_pair, down_here, down_pair)
 
-    def run(rows, out_types):
-        return expert_rows(rows, weights, width, experts, out_types)
-
-    part_first, part_second = [None] * (steps + 1), [None] * steps
-    part_first[0], part_first[1], part_second[1] = run([first[0], first[1], second[1]], [f32] * 3)
+    def run(rows, outlets):
+        return expert_rows(rows, weights, width, experts, outlets)
+
+    part_first, part_second = [None] * steps, [None] * steps
+    (own, leaving), part_first[1], part_second[1] = run(
+        [first[0], first[1], second[1]], [("halves", None), (pieces, f32), (pieces, f32)]
+    )
     for step in range(2, steps):
         part_first[step], part_second[step] = run(
-            [first[step], second[step]], [f32, bf16 if step == steps - 1 else f32]
+            [first[step], second[step]],
+            [(pieces, f32), (pieces, bf16 if step == steps - 1 else f32)],
         )
-    (part_first[steps],) = run([first[steps]], [bf16])
-
-    sum_first, sum_second = part_first[steps], part_second[steps - 1]
-    for step in range(steps - 1, -1, -1):
-        sum_first = lax.ppermute(sum_first, both, back)
+    (sum_first,) = run([first[steps]], [(pieces, bf16)])
+    sum_second = part_second[steps - 1]
+    own_pair = lax.ppermute(leaving, "tensor", swap)
+
+    for step in range(steps - 2, -1, -1):
+        sum_second = [lax.ppermute(sum_second[i], both, back) for i in each]
         if step > 0:
-            sum_first = (part_first[step] + sum_first.astype(f32)).astype(bf16)
-        if step < steps - 1:
-            sum_second = lax.ppermute(sum_second, both, back)
-            if step > 0:
-                sum_second = (part_second[step] + sum_second.astype(f32)).astype(bf16)
-    kept, leaving = last_add(part_first[0], sum_first)
-    from_second = lax.ppermute(sum_second[:, width // 2 :], "tensor", swap)
-    from_first = lax.ppermute(leaving, "tensor", swap)
-    return (finish(kept, from_second, sum_second, from_first), slot_rows)
+            sum_second = [
+                (part + arrived.astype(f32)).astype(bf16)
+                for part, arrived in zip(part_second[step], sum_second)
+            ]
+    second_pair = [lax.ppermute(sum_second[i][:, half:], "tensor", swap) for i in each]
+    for step in range(steps - 1, 1, -1):
+        sum_first = [lax.ppermute(sum_first[i], both, back) for i in each]
+        sum_first = [
+            (part + arrived.astype(f32)).astype(bf16)
+            for part, arrived in zip(part_first[step], sum_first)
+        ]
+    arrived, crossed = [], []
+    for i in each:
+        last = lax.ppermute(sum_first[i], both, back)
+        stays, crosses = split_add(part_first[1][i], last)
+        arrived.append(lax.ppermute(stays, both, back))
+        crossed.append(lax.ppermute(crosses, both, across))
+    mixed = finish(pieces, own, own_pair, arrived, second_pair, sum_second, crossed)
+    return (mixed, slot_rows)
 
 
 def on_device(ring, tokens, routes, probs, up_weight, down_weight, old_place, new_place):

time: 63.5 us -> 64.9 us (1.022)
  starting transfers between devices: 27.4 us -> 36.7 us
  waiting for transfers between devices: 24.7 us -> 16.7 us
    ppermute x9 -> x19, starting transfers between devices: 12.5 us -> 21.8 us  [the longest x6 7.02 us: by_ring(): sum_second = [lax.ppermute(sum_second[i], both, back) for i in each]]
    ppermute x9 -> x19, waiting for transfers between devices: 12.2 us -> 5.14 us  [the longest x2 3.28 us: by_ring(): crossed.append(lax.ppermute(crosses, both, across))]
    ppermute x3, waiting for transfers between devices: 3.01 us -> 2.1 us  [by_ring(): second.append(lax.ppermute(second[-1], both, ahead))]
    pallas_call x6 -> x7, Pallas kernels: 6.38 us -> 6.42 us  [the longest x4 5.57 us: expert_rows(): pl.pallas_call(functools.partial(expert_kernel, outlets, width, experts),...]
  transfers between devices with their start and end apart: 18 -> 28, of which waited for: 12 -> 9; matrix products, arithmetic and copies ran while one was open for 0% -> 0% of each run, Pallas kernels for 15% -> 15%
where the time goes in v2:
time: 64.9 us; the launch traced here: 64.7 us
  starting transfers between devices  36.7 us (57%)
  waiting for transfers between devices  16.7 us (26%)
  Pallas kernels  10.3 us (16%)
  between operations  0.82 us (1%)
    ppermute x4, waiting for transfers between devices, by_ring(): first.append(lax.ppermute(first[-1], both, ahead))  9.49 us
    ppermute x4, starting transfers between devices, by_ring(): first.append(lax.ppermute(first[-1], both, ahead))  8.76 us
    ppermute x6, starting transfers between devices, by_ring(): sum_second = [lax.ppermute(sum_second[i], both, back) for i in each]  7.02 us
    ppermute x4, starting transfers between devices, by_ring(): sum_first = [lax.ppermute(sum_first[i], both, back) for i in each]  6.77 us
    pallas_call x4, Pallas kernels, expert_rows(): pl.pallas_call(functools.partial(expert_kernel, outlets, width, experts),...  5.57 us
    ppermute x3, starting transfers between devices, by_ring(): second.append(lax.ppermute(second[-1], both, ahead))  5.45 us
    ppermute x2, starting transfers between devices, by_ring(): last = lax.ppermute(sum_first[i], both, back)  3.43 us
    ppermute x2, waiting for transfers between devices, by_ring(): crossed.append(lax.ppermute(crosses, both, across))  3.28 us
  transfers between devices with their start and end apart: 28, of which 9 were waited for; matrix products, arithmetic and copies ran while one was open for 0% of the time, Pallas kernels for 15%

profile of v2, /device:TPU:0, one launch (start us, length us, event | category | flops | bytes accessed | tf_op | source)
XLA Modules:
  0.0 64.7 jit_solution(16722614138111252200)
XLA Ops:
  0.6 0.6 collective-permute-start.2
  1.2 0.1 collective-permute-start.3
  1.3 2.0 %shard_map.86 = (bf16[64,2176]{1,0:T(8,128)(2,1)}, bf16[64,2176]{1,0:T(8,128)(2,1)}, s32[2]{0:T(128)}) custom-call(s32[2,8,64]{2,1,0:T(8,128)} %bitcast.8, f32[2,8,64]{2,1,0:T(8,128)} %bitcast.9, s32[8]{0:T(128)} %old_in.1, s32[16]{0:T(128)} %new_in.1, bf16[2,64,2048]{2,1,0:T(8,128)(2,1)} %tokens.1), custom_call_target="tpu_custom_call" | custom-call | tf_op jit(solution)/shard_map/pallas_call | solution.py:200
  3.2 3.0 %collective-permute-start = (bf16[64,2176]{1,0:T(8,128)(2,1)}, bf16[64,2176]{1,0:T(8,128)(2,1)S(1)}, u32[]{:S(2)}, u32[]{:S(2)}) collective-permute-start(bf16[64,2176]{1,0:T(8,128)(2,1)} %get-tuple-element.27.refs_0_), channel_id=1, source_target_pairs={{0,2},{3,1},{2,6},{7,3},{6,10},{11,7},{10,14},{15,11},{14,12},{13,... | collective-permute-start | bytes 835592 | tf_op jit(solution)/shard_map/ppermute | solution.py:383
  6.2 4.8 %collective-permute-done.refs_1_ = bf16[64,2176]{1,0:T(8,128)(2,1)S(1)} collective-permute-done((bf16[64,2176]{1,0:T(8,128)(2,1)}, bf16[64,2176]{1,0:T(8,128)(2,1)S(1)}, u32[]{:S(2)}, u32[]{:S(2)}) %collective-permute-start) | collective-permute-done | bytes 278560 | tf_op jit(solution)/shard_map/ppermute | solution.py:383
  11.0 1.9 %collective-permute-start.5 = (bf16[64,2176]{1,0:T(8,128)(2,1)S(1)}, bf16[64,2176]{1,0:T(8,128)(2,1)S(1)}, u32[]{:S(2)}, u32[]{:S(2)}) collective-permute-start(bf16[64,2176]{1,0:T(8,128)(2,1)S(1)} %collective-permute-done.refs_1_), channel_id=1, source_target_pairs={{0,2},{3,1},{2,6},{7,3},{6,10},{11,7},{10,14},{15,11},{14,12},{13,... | collective-permute-start | bytes 835592 | tf_op jit(solution)/shard_map/ppermute | solution.py:383
  13.0 1.6 %collective-permute-start.1 = (bf16[64,2176]{1,0:T(8,128)(2,1)}, bf16[64,2176]{1,0:T(8,128)(2,1)S(1)}, u32[]{:S(2)}, u32[]{:S(2)}) collective-permute-start(bf16[64,2176]{1,0:T(8,128)(2,1)} %get-tuple-element.28), channel_id=1, source_target_pairs={{0,2},{3,1},{2,6},{7,3},{6,10},{11,7},{10,14},{15,11},{14,12},{13,... | collective-permute-start | bytes 835592 | tf_op jit(solution)/shard_map/ppermute | solution.py:385
  14.5 3.0 %collective-permute-done.5.refs_0_ = bf16[64,2176]{1,0:T(8,128)(2,1)S(1)} collective-permute-done((bf16[64,2176]{1,0:T(8,128)(2,1)S(1)}, bf16[64,2176]{1,0:T(8,128)(2,1)S(1)}, u32[]{:S(2)}, u32[]{:S(2)}) %collective-permute-start.5) | collective-permute-done | bytes 278560 | tf_op jit(solution)/shard_map/ppermute | solution.py:383
  17.6 1.9 %collective-permute-start.7 = (bf16[64,2176]{1,0:T(8,128)(2,1)S(1)}, bf16[64,2176]{1,0:T(8,128)(2,1)S(1)}, u32[]{:S(2)}, u32[]{:S(2)}) collective-permute-start(bf16[64,2176]{1,0:T(8,128)(2,1)S(1)} %collective-permute-done.5.refs_0_), channel_id=1, source_target_pairs={{0,2},{3,1},{2,6},{7,3},{6,10},{11,7},{10,14},{15,11},{14,12},{13,... | collective-permute-start | bytes 835592 | tf_op jit(solution)/shard_map/ppermute | solution.py:383
  19.5 1.0 %collective-permute-done.1.refs_2_ = bf16[64,2176]{1,0:T(8,128)(2,1)S(1)} collective-permute-done((bf16[64,2176]{1,0:T(8,128)(2,1)}, bf16[64,2176]{1,0:T(8,128)(2,1)S(1)}, u32[]{:S(2)}, u32[]{:S(2)}) %collective-permute-start.1) | collective-permute-done | bytes 278560 | tf_op jit(solution)/shard_map/ppermute | solution.py:385
  20.6 1.9 %collective-permute-start.6 = (bf16[64,2176]{1,0:T(8,128)(2,1)S(1)}, bf16[64,2176]{1,0:T(8,128)(2,1)S(1)}, u32[]{:S(2)}, u32[]{:S(2)}) collective-permute-start(bf16[64,2176]{1,0:T(8,128)(2,1)S(1)} %collective-permute-done.1.refs_2_), channel_id=1, source_target_pairs={{0,2},{3,1},{2,6},{7,3},{6,10},{11,7},{10,14},{15,11},{14,12},{13,... | collective-permute-start | bytes 835592 | tf_op jit(solution)/shard_map/ppermute | solution.py:385
  22.5 1.6 %collective-permute-done.7.refs_0_ = bf16[64,2176]{1,0:T(8,128)(2,1)S(1)} collective-permute-done((bf16[64,2176]{1,0:T(8,128)(2,1)S(1)}, bf16[64,2176]{1,0:T(8,128)(2,1)S(1)}, u32[]{:S(2)}, u32[]{:S(2)}) %collective-permute-start.7) | collective-permute-done | bytes 278560 | tf_op jit(solution)/shard_map/ppermute | solution.py:383
  24.1 1.9 %collective-permute-start.9 = (bf16[64,2176]{1,0:T(8,128)(2,1)S(1)}, bf16[64,2176]{1,0:T(8,128)(2,1)S(1)}, u32[]{:S(2)}, u32[]{:S(2)}) collective-permute-start(bf16[64,2176]{1,0:T(8,128)(2,1)S(1)} %collective-permute-done.7.refs_0_), channel_id=1, source_target_pairs={{0,2},{3,1},{2,6},{7,3},{6,10},{11,7},{10,14},{15,11},{14,12},{13,... | collective-permute-start | bytes 835592 | tf_op jit(solution)/shard_map/ppermute | solution.py:383
  26.1 1.0 %collective-permute-done.6.refs_1_ = bf16[64,2176]{1,0:T(8,128)(2,1)S(1)} collective-permute-done((bf16[64,2176]{1,0:T(8,128)(2,1)S(1)}, bf16[64,2176]{1,0:T(8,128)(2,1)S(1)}, u32[]{:S(2)}, u32[]{:S(2)}) %collective-permute-start.6) | collective-permute-done | bytes 278560 | tf_op jit(solution)/shard_map/ppermute | solution.py:385
  27.1 1.9 %collective-permute-start.8 = (bf16[64,2176]{1,0:T(8,128)(2,1)S(1)}, bf16[64,2176]{1,0:T(8,128)(2,1)S(1)}, u32[]{:S(2)}, u32[]{:S(2)}) collective-permute-start(bf16[64,2176]{1,0:T(8,128)(2,1)S(1)} %collective-permute-done.6.refs_1_), channel_id=1, source_target_pairs={{0,2},{3,1},{2,6},{7,3},{6,10},{11,7},{10,14},{15,11},{14,12},{13,... | collective-permute-start | bytes 835592 | tf_op jit(solution)/shard_map/ppermute | solution.py:385
  29.0 1.9 %shard_map.87 = (bf16[2048,384]{1,0:T(8,128)(2,1)S(1)}, bf16[768,1024]{1,0:T(8,128)(2,1)S(1)}) custom-call(bf16[2048,384]{1,0:T(8,128)(2,1)} %bitcast.5, bf16[768,1024]{1,0:T(8,128)(2,1)} %bitcast.7), custom_call_target="tpu_custom_call" | custom-call | bytes 6291456 | tf_op jit(solution)/shard_map/pallas_call | solution.py:229
  30.9 0.0 collective-permute-done.9.refs_0_
  31.0 0.0 collective-permute-done.2.refs_4_.refs_3_.refs_2_
  31.0 0.0 collective-permute-done.3.refs_6_.refs_5_.refs_4_
  31.0 1.3 %shard_map.91 = (bf16[32,2048]{1,0:T(8,128)(2,1)S(1)}, bf16[32,2048]{1,0:T(8,128)(2,1)S(1)}) custom-call(bf16[64,2176]{1,0:T(8,128)(2,1)S(1)} %collective-permute-done.9.refs_0_, bf16[2048,384]{1,0:T(8,128)(2,1)S(1)} %get-tuple-element.29.refs_3_.refs_2_.refs_1_, bf16[2048,384]{1,0:T(8,128)(2,1)S(1)} %collective-permute-done.2.refs_4_.refs_3_.refs_2_, ...), custom_call_target="tpu_custom_call" | custom-call | flops 402653184 | bytes 1048576 | tf_op jit(solution)/shard_map/pallas_call | solution.py:297
  32.3 1.8 %collective-permute-start.10 = (bf16[32,2048]{1,0:T(8,128)(2,1)S(1)}, bf16[32,2048]{1,0:T(8,128)(2,1)S(1)}, u32[]{:S(2)}, u32[]{:S(2)}) collective-permute-start(bf16[32,2048]{1,0:T(8,128)(2,1)S(1)} %get-tuple-element.36), channel_id=1, source_target_pairs={{2,0},{1,3},{6,2},{3,7},{10,6},{7,11},{14,10},{11,15},{12,14},{15,... | collective-permute-start | bytes 393224 | tf_op jit(solution)/shard_map/ppermute | solution.py:417
  34.0 1.6 %collective-permute-start.14 = (bf16[32,2048]{1,0:T(8,128)(2,1)S(1)}, bf16[32,2048]{1,0:T(8,128)(2,1)S(1)}, u32[]{:S(2)}, u32[]{:S(2)}) collective-permute-start(bf16[32,2048]{1,0:T(8,128)(2,1)S(1)} %get-tuple-element.41), channel_id=1, source_target_pairs={{2,0},{1,3},{6,2},{3,7},{10,6},{7,11},{14,10},{11,15},{12,14},{15,... | collective-permute-start | bytes 393224 | tf_op jit(solution)/shard_map/ppermute | solution.py:417
  35.6 0.0 collective-permute-done.8.refs_1_
  35.6 1.3 %shard_map.90 = (f32[32,2048]{1,0:T(8,128)S(1)}, f32[32,2048]{1,0:T(8,128)S(1)}, bf16[32,2048]{1,0:T(8,128)(2,1)S(1)}, bf16[32,2048]{1,0:T(8,128)(2,1)S(1)}) custom-call(bf16[64,2176]{1,0:T(8,128)(2,1)S(1)} %collective-permute-done.7.refs_0_, bf16[64,2176]{1,0:T(8,128)(2,1)S(1)} %collective-permute-done.8.refs_1_, ...), custom_call_target="tpu_custom_call" | custom-call | flops 805306368 | bytes 2097152 | tf_op jit(solution)/shard_map/pallas_call | solution.py:297
  36.9 1.7 %collective-permute-start.18 = (bf16[32,2048]{1,0:T(8,128)(2,1)S(1)}, bf16[32,2048]{1,0:T(8,128)(2,1)S(1)}, u32[]{:S(2)}, u32[]{:S(2)}) collective-permute-start(bf16[32,2048]{1,0:T(8,128)(2,1)S(1)} %get-tuple-element.45), channel_id=1, source_target_pairs={{2,0},{1,3},{6,2},{3,7},{10,6},{7,11},{14,10},{11,15},{12,14},{15,... | collective-permute-start | bytes 393224 | tf_op jit(solution)/shard_map/ppermute | solution.py:409
  38.6 1.6 %collective-permute-start.22 = (bf16[32,2048]{1,0:T(8,128)(2,1)S(1)}, bf16[32,2048]{1,0:T(8,128)(2,1)S(1)}, u32[]{:S(2)}, u32[]{:S(2)}) collective-permute-start(bf16[32,2048]{1,0:T(8,128)(2,1)S(1)} %get-tuple-element.48), channel_id=1, source_target_pairs={{2,0},{1,3},{6,2},{3,7},{10,6},{7,11},{14,10},{11,15},{12,14},{15,... | collective-permute-start | bytes 393224 | tf_op jit(solution)/shard_map/ppermute | solution.py:409
  40.2 1.3 %shard_map.89 = (f32[32,2048]{1,0:T(8,128)S(1)}, f32[32,2048]{1,0:T(8,128)S(1)}, f32[32,2048]{1,0:T(8,128)S(1)}, f32[32,2048]{1,0:T(8,128)S(1)}) custom-call(bf16[64,2176]{1,0:T(8,128)(2,1)S(1)} %collective-permute-done.5.refs_0_, bf16[64,2176]{1,0:T(8,128)(2,1)S(1)} %collective-permute-done.6.refs_1_, ...), custom_call_target="tpu_custom_call" | custom-call | flops 805306368 | bytes 2097152 | tf_op jit(solution)/shard_map/pallas_call | solution.py:297
  41.4 0.0 copy-done
  41.5 1.8 %shard_map.88 = (f32[64,1024]{1,0:T(8,128)S(1)}, bf16[64,1024]{1,0:T(8,128)(2,1)S(1)}, f32[32,2048]{1,0:T(8,128)S(1)}, f32[32,2048]{1,0:T(8,128)S(1)}, f32[32,2048]{1,0:T(8,128)S(1)}, /*index=5*/f32[32,2048]{1,0:T(8,128)S(1)}) custom-call(bf16[64,2176]{1,0:T(8,128)(2,1)S(1)} %copy-done, bf16[64,2176]{1,0:T(8,128)(2,1)S(1)} %collective-permute-done.refs_1_, ...), custom_call_target="tpu_custom_call" | custom-call | flops 1207959552 | bytes 3145728 | tf_op jit(solution)/shard_map/pallas_call | solution.py:297
  43.2 0.0 collective-permute-done.10
  43.3 1.7 %collective-permute-start.11 = (bf16[32,2048]{1,0:T(8,128)(2,1)S(1)}, bf16[32,2048]{1,0:T(8,128)(2,1)S(1)}, u32[]{:S(2)}, u32[]{:S(2)}) collective-permute-start(bf16[32,2048]{1,0:T(8,128)(2,1)S(1)} %add_convert_fusion.7), channel_id=1, source_target_pairs={{2,0},{1,3},{6,2},{3,7},{10,6},{7,11},{14,10},{11,15},{12,14},{15,... | collective-permute-start | bytes 393224 | tf_op jit(solution)/shard_map/ppermute | solution.py:417
  45.0 0.0 collective-permute-done.14
  45.0 1.7 %collective-permute-start.15 = (bf16[32,2048]{1,0:T(8,128)(2,1)S(1)}, bf16[32,2048]{1,0:T(8,128)(2,1)S(1)}, u32[]{:S(2)}, u32[]{:S(2)}) collective-permute-start(bf16[32,2048]{1,0:T(8,128)(2,1)S(1)} %add_convert_fusion.5), channel_id=1, source_target_pairs={{2,0},{1,3},{6,2},{3,7},{10,6},{7,11},{14,10},{11,15},{12,14},{15,... | collective-permute-start | bytes 393224 | tf_op jit(solution)/shard_map/ppermute | solution.py:417
  46.7 0.0 collective-permute-done.18
  46.8 0.5 collective-permute-start.19
  47.3 0.0 collective-permute-done.22
  47.3 0.5 collective-permute-start.23
  47.8 0.5 collective-permute-done.11
  48.3 1.7 %collective-permute-start.12 = (bf16[32,2048]{1,0:T(8,128)(2,1)S(1)}, bf16[32,2048]{1,0:T(8,128)(2,1)S(1)}, u32[]{:S(2)}, u32[]{:S(2)}) collective-permute-start(bf16[32,2048]{1,0:T(8,128)(2,1)S(1)} %add_convert_fusion.6), channel_id=1, source_target_pairs={{2,0},{1,3},{6,2},{3,7},{10,6},{7,11},{14,10},{11,15},{12,14},{15,... | collective-permute-start | bytes 393224 | tf_op jit(solution)/shard_map/ppermute | solution.py:424
  50.0 0.0 collective-permute-done.15
  50.1 1.7 %collective-permute-start.16 = (bf16[32,2048]{1,0:T(8,128)(2,1)S(1)}, bf16[32,2048]{1,0:T(8,128)(2,1)S(1)}, u32[]{:S(2)}, u32[]{:S(2)}) collective-permute-start(bf16[32,2048]{1,0:T(8,128)(2,1)S(1)} %add_convert_fusion.4), channel_id=1, source_target_pairs={{2,0},{1,3},{6,2},{3,7},{10,6},{7,11},{14,10},{11,15},{12,14},{15,... | collective-permute-start | bytes 393224 | tf_op jit(solution)/shard_map/ppermute | solution.py:424
  51.8 0.0 collective-permute-done.19
  51.8 1.4 %collective-permute-start.20 = (bf16[32,2048]{1,0:T(8,128)(2,1)S(1)}, bf16[32,2048]{1,0:T(8,128)(2,1)S(1)}, u32[]{:S(2)}, u32[]{:S(2)}) collective-permute-start(bf16[32,2048]{1,0:T(8,128)(2,1)S(1)} %add_convert_fusion.2), channel_id=1, source_target_pairs={{2,0},{1,3},{6,2},{3,7},{10,6},{7,11},{14,10},{11,15},{12,14},{15,... | collective-permute-start | bytes 393224 | tf_op jit(solution)/shard_map/ppermute | solution.py:409
  53.2 0.0 collective-permute-done.23
  53.2 1.4 %collective-permute-start.24 = (bf16[32,2048]{1,0:T(8,128)(2,1)S(1)}, bf16[32,2048]{1,0:T(8,128)(2,1)S(1)}, u32[]{:S(2)}, u32[]{:S(2)}) collective-permute-start(bf16[32,2048]{1,0:T(8,128)(2,1)S(1)} %add_convert_fusion), channel_id=1, source_target_pairs={{2,0},{1,3},{6,2},{3,7},{10,6},{7,11},{14,10},{11,15},{12,14},{15,... | collective-permute-start | bytes 393224 | tf_op jit(solution)/shard_map/ppermute | solution.py:409
  54.6 0.0 collective-permute-start.4
  54.6 0.0 collective-permute-done.12.arrived
  54.6 1.4 %collective-permute-start.13 = (bf16[32,1024]{1,0:T(8,128)(2,1)S(1)}, bf16[32,1024]{1,0:T(8,128)(2,1)S(1)}, u32[]{:S(2)}, u32[]{:S(2)}) collective-permute-start(bf16[32,1024]{1,0:T(8,128)(2,1)S(1)} %get-tuple-element.37), channel_id=1, source_target_pairs={{2,0},{1,3},{6,2},{3,7},{10,6},{7,11},{14,10},{11,15},{12,14},{15,... | collective-permute-start | bytes 196616 | tf_op jit(solution)/shard_map/ppermute | solution.py:426
  56.0 0.0 collective-permute-done.16.arrived
  56.0 1.4 %collective-permute-start.17 = (bf16[32,1024]{1,0:T(8,128)(2,1)S(1)}, bf16[32,1024]{1,0:T(8,128)(2,1)S(1)}, u32[]{:S(2)}, u32[]{:S(2)}) collective-permute-start(bf16[32,1024]{1,0:T(8,128)(2,1)S(1)} %get-tuple-element.42), channel_id=1, source_target_pairs={{2,0},{1,3},{6,2},{3,7},{10,6},{7,11},{14,10},{11,15},{12,14},{15,... | collective-permute-start | bytes 196616 | tf_op jit(solution)/shard_map/ppermute | solution.py:426
  57.4 0.0 collective-permute-done.20.refs_4_
  57.4 0.1 collective-permute-start.21
  57.5 1.3 %collective-permute-done.24.refs_5_ = bf16[32,2048]{1,0:T(8,128)(2,1)S(1)} collective-permute-done((bf16[32,2048]{1,0:T(8,128)(2,1)S(1)}, bf16[32,2048]{1,0:T(8,128)(2,1)S(1)}, u32[]{:S(2)}, u32[]{:S(2)}) %collective-permute-start.24) | collective-permute-done | bytes 131104 | tf_op jit(solution)/shard_map/ppermute | solution.py:409
  58.8 0.0 collective-permute-start.25
  58.8 0.0 collective-permute-done.4.own_pair
  58.8 1.4 %collective-permute-start.26 = (bf16[32,1024]{1,0:T(8,128)(2,1)S(1)}, bf16[32,1024]{1,0:T(8,128)(2,1)S(1)}, u32[]{:S(2)}, u32[]{:S(2)}) collective-permute-start(bf16[32,1024]{1,0:T(8,128)(2,1)S(1)} %get-tuple-element.49), channel_id=1, source_target_pairs={{2,1},{1,2},{6,3},{3,6},{10,7},{7,10},{14,11},{11,14},{12,15},{15,... | collective-permute-start | bytes 196616 | tf_op jit(solution)/shard_map/ppermute | solution.py:427
  60.3 0.0 collective-permute-done.13.refs_0_
  60.3 0.4 collective-permute-start.27
  60.7 0.0 collective-permute-done.17.refs_1_
  60.7 0.0 collective-permute-done.21.refs_2_
  60.7 0.0 collective-permute-done.25.refs_3_
  60.7 1.9 %collective-permute-done.26.refs_6_ = bf16[32,1024]{1,0:T(8,128)(2,1)S(1)} collective-permute-done((bf16[32,1024]{1,0:T(8,128)(2,1)S(1)}, bf16[32,1024]{1,0:T(8,128)(2,1)S(1)}, u32[]{:S(2)}, u32[]{:S(2)}) %collective-permute-start.26) | collective-permute-done | bytes 65568 | tf_op jit(solution)/shard_map/ppermute | solution.py:427
  62.6 1.4 %collective-permute-done.27.refs_7_ = bf16[32,1024]{1,0:T(8,128)(2,1)S(1)} collective-permute-done((bf16[32,1024]{1,0:T(8,128)(2,1)S(1)}, bf16[32,1024]{1,0:T(8,128)(2,1)S(1)}, u32[]{:S(2)}, u32[]{:S(2)}) %collective-permute-start.27) | collective-permute-done | bytes 65568 | tf_op jit(solution)/shard_map/ppermute | solution.py:427
  64.0 0.8 %shard_map.94 = bf16[2,64,1024]{2,1,0:T(8,128)(2,1)} custom-call(f32[64,1024]{1,0:T(8,128)S(1)} %get-tuple-element.31.own, bf16[64,1024]{1,0:T(8,128)(2,1)S(1)} %collective-permute-done.4.own_pair, bf16[32,1024]{1,0:T(8,128)(2,1)S(1)} %collective-permute-done.13.refs_0_, bf16[32,1024]{1,0:T(8,128)(2,1)S(1)} %collective-permute-done.17.refs_1_, ...), custom_call_target="tpu_custom_call" | custom-call | tf_op jit(solution)/shard_map/pallas_call | solution.py:349
  (13 shorter events, 0.3 us)
Async XLA Ops:
  0.6 30.3 %collective-permute-start.2 = (bf16[2048,384]{1,0:T(8,128)(2,1)}, bf16[2048,384]{1,0:T(8,128)(2,1)S(1)}, u32[]{:S(2)}, u32[]{:S(2)}) collective-permute-start(bf16[2048,384]{1,0:T(8,128)(2,1)} %bitcast.4), channel_id=1, source_target_pairs={{0,1},{1,0},{2,3},{3,2},{4,5},{5,4},{6,7},{7,6},{8,9},{9,8},{10,11... | collective-permute-start | bytes 4718600 | tf_op jit(solution)/shard_map/ppermute | solution.py:387
  1.2 29.8 %collective-permute-start.3 = (bf16[768,1024]{1,0:T(8,128)(2,1)}, bf16[768,1024]{1,0:T(8,128)(2,1)S(1)}, u32[]{:S(2)}, u32[]{:S(2)}) collective-permute-start(bf16[768,1024]{1,0:T(8,128)(2,1)} %bitcast.6), channel_id=1, source_target_pairs={{0,1},{1,0},{2,3},{3,2},{4,5},{5,4},{6,7},{7,6},{8,9},{9,8},{10,11... | collective-permute-start | bytes 4718600 | tf_op jit(solution)/shard_map/ppermute | solution.py:388
  3.2 7.8 %collective-permute-start = (bf16[64,2176]{1,0:T(8,128)(2,1)}, bf16[64,2176]{1,0:T(8,128)(2,1)S(1)}, u32[]{:S(2)}, u32[]{:S(2)}) collective-permute-start(bf16[64,2176]{1,0:T(8,128)(2,1)} %get-tuple-element.27.refs_0_), channel_id=1, source_target_pairs={{0,2},{3,1},{2,6},{7,3},{6,10},{11,7},{10,14},{15,11},{14,12},{13,... | collective-permute-start | bytes 835592 | tf_op jit(solution)/shard_map/ppermute | solution.py:383
  11.0 6.5 %collective-permute-start.5 = (bf16[64,2176]{1,0:T(8,128)(2,1)S(1)}, bf16[64,2176]{1,0:T(8,128)(2,1)S(1)}, u32[]{:S(2)}, u32[]{:S(2)}) collective-permute-start(bf16[64,2176]{1,0:T(8,128)(2,1)S(1)} %collective-permute-done.refs_1_), channel_id=1, source_target_pairs={{0,2},{3,1},{2,6},{7,3},{6,10},{11,7},{10,14},{15,11},{14,12},{13,... | collective-permute-start | bytes 835592 | tf_op jit(solution)/shard_map/ppermute | solution.py:383
  13.0 7.6 %collective-permute-start.1 = (bf16[64,2176]{1,0:T(8,128)(2,1)}, bf16[64,2176]{1,0:T(8,128)(2,1)S(1)}, u32[]{:S(2)}, u32[]{:S(2)}) collective-permute-start(bf16[64,2176]{1,0:T(8,128)(2,1)} %get-tuple-element.28), channel_id=1, source_target_pairs={{0,2},{3,1},{2,6},{7,3},{6,10},{11,7},{10,14},{15,11},{14,12},{13,... | collective-permute-start | bytes 835592 | tf_op jit(solution)/shard_map/ppermute | solution.py:385
  17.6 6.5 %collective-permute-start.7 = (bf16[64,2176]{1,0:T(8,128)(2,1)S(1)}, bf16[64,2176]{1,0:T(8,128)(2,1)S(1)}, u32[]{:S(2)}, u32[]{:S(2)}) collective-permute-start(bf16[64,2176]{1,0:T(8,128)(2,1)S(1)} %collective-permute-done.5.refs_0_), channel_id=1, source_target_pairs={{0,2},{3,1},{2,6},{7,3},{6,10},{11,7},{10,14},{15,11},{14,12},{13,... | collective-permute-start | bytes 835592 | tf_op jit(solution)/shard_map/ppermute | solution.py:383
  20.6 6.5 %collective-permute-start.6 = (bf16[64,2176]{1,0:T(8,128)(2,1)S(1)}, bf16[64,2176]{1,0:T(8,128)(2,1)S(1)}, u32[]{:S(2)}, u32[]{:S(2)}) collective-permute-start(bf16[64,2176]{1,0:T(8,128)(2,1)S(1)} %collective-permute-done.1.refs_2_), channel_id=1, source_target_pairs={{0,2},{3,1},{2,6},{7,3},{6,10},{11,7},{10,14},{15,11},{14,12},{13,... | collective-permute-start | bytes 835592 | tf_op jit(solution)/shard_map/ppermute | solution.py:385
  24.1 6.8 %collective-permute-start.9 = (bf16[64,2176]{1,0:T(8,128)(2,1)S(1)}, bf16[64,2176]{1,0:T(8,128)(2,1)S(1)}, u32[]{:S(2)}, u32[]{:S(2)}) collective-permute-start(bf16[64,2176]{1,0:T(8,128)(2,1)S(1)} %collective-permute-done.7.refs_0_), channel_id=1, source_target_pairs={{0,2},{3,1},{2,6},{7,3},{6,10},{11,7},{10,14},{15,11},{14,12},{13,... | collective-permute-start | bytes 835592 | tf_op jit(solution)/shard_map/ppermute | solution.py:383
  27.1 8.5 %collective-permute-start.8 = (bf16[64,2176]{1,0:T(8,128)(2,1)S(1)}, bf16[64,2176]{1,0:T(8,128)(2,1)S(1)}, u32[]{:S(2)}, u32[]{:S(2)}) collective-permute-start(bf16[64,2176]{1,0:T(8,128)(2,1)S(1)} %collective-permute-done.6.refs_1_), channel_id=1, source_target_pairs={{0,2},{3,1},{2,6},{7,3},{6,10},{11,7},{10,14},{15,11},{14,12},{13,... | collective-permute-start | bytes 835592 | tf_op jit(solution)/shard_map/ppermute | solution.py:385
  32.3 11.0 %collective-permute-start.10 = (bf16[32,2048]{1,0:T(8,128)(2,1)S(1)}, bf16[32,2048]{1,0:T(8,128)(2,1)S(1)}, u32[]{:S(2)}, u32[]{:S(2)}) collective-permute-start(bf16[32,2048]{1,0:T(8,128)(2,1)S(1)} %get-tuple-element.36), channel_id=1, source_target_pairs={{2,0},{1,3},{6,2},{3,7},{10,6},{7,11},{14,10},{11,15},{12,14},{15,... | collective-permute-start | bytes 393224 | tf_op jit(solution)/shard_map/ppermute | solution.py:417
  34.0 11.0 %collective-permute-start.14 = (bf16[32,2048]{1,0:T(8,128)(2,1)S(1)}, bf16[32,2048]{1,0:T(8,128)(2,1)S(1)}, u32[]{:S(2)}, u32[]{:S(2)}) collective-permute-start(bf16[32,2048]{1,0:T(8,128)(2,1)S(1)} %get-tuple-element.41), channel_id=1, source_target_pairs={{2,0},{1,3},{6,2},{3,7},{10,6},{7,11},{14,10},{11,15},{12,14},{15,... | collective-permute-start | bytes 393224 | tf_op jit(solution)/shard_map/ppermute | solution.py:417
  36.9 9.9 %collective-permute-start.18 = (bf16[32,2048]{1,0:T(8,128)(2,1)S(1)}, bf16[32,2048]{1,0:T(8,128)(2,1)S(1)}, u32[]{:S(2)}, u32[]{:S(2)}) collective-permute-start(bf16[32,2048]{1,0:T(8,128)(2,1)S(1)} %get-tuple-element.45), channel_id=1, source_target_pairs={{2,0},{1,3},{6,2},{3,7},{10,6},{7,11},{14,10},{11,15},{12,14},{15,... | collective-permute-start | bytes 393224 | tf_op jit(solution)/shard_map/ppermute | solution.py:409
  38.6 2.9 %copy-start = (bf16[64,2176]{1,0:T(8,128)(2,1)S(1)}, bf16[64,2176]{1,0:T(8,128)(2,1)}, u32[]{:S(2)}) copy-start(bf16[64,2176]{1,0:T(8,128)(2,1)} %get-tuple-element.27.refs_0_) | copy-start | bytes 835588
  38.6 8.7 %collective-permute-start.22 = (bf16[32,2048]{1,0:T(8,128)(2,1)S(1)}, bf16[32,2048]{1,0:T(8,128)(2,1)S(1)}, u32[]{:S(2)}, u32[]{:S(2)}) collective-permute-start(bf16[32,2048]{1,0:T(8,128)(2,1)S(1)} %get-tuple-element.48), channel_id=1, source_target_pairs={{2,0},{1,3},{6,2},{3,7},{10,6},{7,11},{14,10},{11,15},{12,14},{15,... | collective-permute-start | bytes 393224 | tf_op jit(solution)/shard_map/ppermute | solution.py:409
  43.3 5.0 %collective-permute-start.11 = (bf16[32,2048]{1,0:T(8,128)(2,1)S(1)}, bf16[32,2048]{1,0:T(8,128)(2,1)S(1)}, u32[]{:S(2)}, u32[]{:S(2)}) collective-permute-start(bf16[32,2048]{1,0:T(8,128)(2,1)S(1)} %add_convert_fusion.7), channel_id=1, source_target_pairs={{2,0},{1,3},{6,2},{3,7},{10,6},{7,11},{14,10},{11,15},{12,14},{15,... | collective-permute-start | bytes 393224 | tf_op jit(solution)/shard_map/ppermute | solution.py:417
  45.0 5.0 %collective-permute-start.15 = (bf16[32,2048]{1,0:T(8,128)(2,1)S(1)}, bf16[32,2048]{1,0:T(8,128)(2,1)S(1)}, u32[]{:S(2)}, u32[]{:S(2)}) collective-permute-start(bf16[32,2048]{1,0:T(8,128)(2,1)S(1)} %add_convert_fusion.5), channel_id=1, source_target_pairs={{2,0},{1,3},{6,2},{3,7},{10,6},{7,11},{14,10},{11,15},{12,14},{15,... | collective-permute-start | bytes 393224 | tf_op jit(solution)/shard_map/ppermute | solution.py:417
  46.8 5.0 %collective-permute-start.19 = (bf16[32,2048]{1,0:T(8,128)(2,1)S(1)}, bf16[32,2048]{1,0:T(8,128)(2,1)S(1)}, u32[]{:S(2)}, u32[]{:S(2)}) collective-permute-start(bf16[32,2048]{1,0:T(8,128)(2,1)S(1)} %add_convert_fusion.3), channel_id=1, source_target_pairs={{2,0},{1,3},{6,2},{3,7},{10,6},{7,11},{14,10},{11,15},{12,14},{15,... | collective-permute-start | bytes 393224 | tf_op jit(solution)/shard_map/ppermute | solution.py:409
  47.3 5.9 %collective-permute-start.23 = (bf16[32,2048]{1,0:T(8,128)(2,1)S(1)}, bf16[32,2048]{1,0:T(8,128)(2,1)S(1)}, u32[]{:S(2)}, u32[]{:S(2)}) collective-permute-start(bf16[32,2048]{1,0:T(8,128)(2,1)S(1)} %add_convert_fusion.1), channel_id=1, source_target_pairs={{2,0},{1,3},{6,2},{3,7},{10,6},{7,11},{14,10},{11,15},{12,14},{15,... | collective-permute-start | bytes 393224 | tf_op jit(solution)/shard_map/ppermute | solution.py:409
  48.3 6.3 %collective-permute-start.12 = (bf16[32,2048]{1,0:T(8,128)(2,1)S(1)}, bf16[32,2048]{1,0:T(8,128)(2,1)S(1)}, u32[]{:S(2)}, u32[]{:S(2)}) collective-permute-start(bf16[32,2048]{1,0:T(8,128)(2,1)S(1)} %add_convert_fusion.6), channel_id=1, source_target_pairs={{2,0},{1,3},{6,2},{3,7},{10,6},{7,11},{14,10},{11,15},{12,14},{15,... | collective-permute-start | bytes 393224 | tf_op jit(solution)/shard_map/ppermute | solution.py:424
  50.1 5.9 %collective-permute-start.16 = (bf16[32,2048]{1,0:T(8,128)(2,1)S(1)}, bf16[32,2048]{1,0:T(8,128)(2,1)S(1)}, u32[]{:S(2)}, u32[]{:S(2)}) collective-permute-start(bf16[32,2048]{1,0:T(8,128)(2,1)S(1)} %add_convert_fusion.4), channel_id=1, source_target_pairs={{2,0},{1,3},{6,2},{3,7},{10,6},{7,11},{14,10},{11,15},{12,14},{15,... | collective-permute-start | bytes 393224 | tf_op jit(solution)/shard_map/ppermute | solution.py:424
  51.8 5.6 %collective-permute-start.20 = (bf16[32,2048]{1,0:T(8,128)(2,1)S(1)}, bf16[32,2048]{1,0:T(8,128)(2,1)S(1)}, u32[]{:S(2)}, u32[]{:S(2)}) collective-permute-start(bf16[32,2048]{1,0:T(8,128)(2,1)S(1)} %add_convert_fusion.2), channel_id=1, source_target_pairs={{2,0},{1,3},{6,2},{3,7},{10,6},{7,11},{14,10},{11,15},{12,14},{15,... | collective-permute-start | bytes 393224 | tf_op jit(solution)/shard_map/ppermute | solution.py:409
  53.2 5.6 %collective-permute-start.24 = (bf16[32,2048]{1,0:T(8,128)(2,1)S(1)}, bf16[32,2048]{1,0:T(8,128)(2,1)S(1)}, u32[]{:S(2)}, u32[]{:S(2)}) collective-permute-start(bf16[32,2048]{1,0:T(8,128)(2,1)S(1)} %add_convert_fusion), channel_id=1, source_target_pairs={{2,0},{1,3},{6,2},{3,7},{10,6},{7,11},{14,10},{11,15},{12,14},{15,... | collective-permute-start | bytes 393224 | tf_op jit(solution)/shard_map/ppermute | solution.py:409
  54.6 4.2 %collective-permute-start.4 = (bf16[64,1024]{1,0:T(8,128)(2,1)S(1)}, bf16[64,1024]{1,0:T(8,128)(2,1)S(1)}, u32[]{:S(2)}, u32[]{:S(2)}) collective-permute-start(bf16[64,1024]{1,0:T(8,128)(2,1)S(1)} %get-tuple-element.32), channel_id=1, source_target_pairs={{0,1},{1,0},{2,3},{3,2},{4,5},{5,4},{6,7},{7,6},{8,9},{9,8},{10,11... | collective-permute-start | bytes 393224 | tf_op jit(solution)/shard_map/ppermute | solution.py:406
  54.6 5.6 %collective-permute-start.13 = (bf16[32,1024]{1,0:T(8,128)(2,1)S(1)}, bf16[32,1024]{1,0:T(8,128)(2,1)S(1)}, u32[]{:S(2)}, u32[]{:S(2)}) collective-permute-start(bf16[32,1024]{1,0:T(8,128)(2,1)S(1)} %get-tuple-element.37), channel_id=1, source_target_pairs={{2,0},{1,3},{6,2},{3,7},{10,6},{7,11},{14,10},{11,15},{12,14},{15,... | collective-permute-start | bytes 196616 | tf_op jit(solution)/shard_map/ppermute | solution.py:426
  56.0 4.6 %collective-permute-start.17 = (bf16[32,1024]{1,0:T(8,128)(2,1)S(1)}, bf16[32,1024]{1,0:T(8,128)(2,1)S(1)}, u32[]{:S(2)}, u32[]{:S(2)}) collective-permute-start(bf16[32,1024]{1,0:T(8,128)(2,1)S(1)} %get-tuple-element.42), channel_id=1, source_target_pairs={{2,0},{1,3},{6,2},{3,7},{10,6},{7,11},{14,10},{11,15},{12,14},{15,... | collective-permute-start | bytes 196616 | tf_op jit(solution)/shard_map/ppermute | solution.py:426
  57.4 3.2 %collective-permute-start.21 = (bf16[32,1024]{1,0:T(8,128)(2,1)S(1)}, bf16[32,1024]{1,0:T(8,128)(2,1)S(1)}, u32[]{:S(2)}, u32[]{:S(2)}) collective-permute-start(bf16[32,1024]{1,0:T(8,128)(2,1)S(1)} %slice.8), channel_id=1, source_target_pairs={{0,1},{1,0},{2,3},{3,2},{4,5},{5,4},{6,7},{7,6},{8,9},{9,8},{10,11... | collective-permute-start | bytes 196616 | tf_op jit(solution)/shard_map/ppermute | solution.py:415
  58.8 1.8 %collective-permute-start.25 = (bf16[32,1024]{1,0:T(8,128)(2,1)S(1)}, bf16[32,1024]{1,0:T(8,128)(2,1)S(1)}, u32[]{:S(2)}, u32[]{:S(2)}) collective-permute-start(bf16[32,1024]{1,0:T(8,128)(2,1)S(1)} %slice.9), channel_id=1, source_target_pairs={{0,1},{1,0},{2,3},{3,2},{4,5},{5,4},{6,7},{7,6},{8,9},{9,8},{10,11... | collective-permute-start | bytes 196616 | tf_op jit(solution)/shard_map/ppermute | solution.py:415
  58.8 3.8 %collective-permute-start.26 = (bf16[32,1024]{1,0:T(8,128)(2,1)S(1)}, bf16[32,1024]{1,0:T(8,128)(2,1)S(1)}, u32[]{:S(2)}, u32[]{:S(2)}) collective-permute-start(bf16[32,1024]{1,0:T(8,128)(2,1)S(1)} %get-tuple-element.49), channel_id=1, source_target_pairs={{2,1},{1,2},{6,3},{3,6},{10,7},{7,10},{14,11},{11,14},{12,15},{15,... | collective-permute-start | bytes 196616 | tf_op jit(solution)/shard_map/ppermute | solution.py:427
  60.3 3.7 %collective-permute-start.27 = (bf16[32,1024]{1,0:T(8,128)(2,1)S(1)}, bf16[32,1024]{1,0:T(8,128)(2,1)S(1)}, u32[]{:S(2)}, u32[]{:S(2)}) collective-permute-start(bf16[32,1024]{1,0:T(8,128)(2,1)S(1)} %get-tuple-element.50), channel_id=1, source_target_pairs={{2,1},{1,2},{6,3},{3,6},{10,7},{7,10},{14,11},{11,14},{12,15},{15,... | collective-permute-start | bytes 196616 | tf_op jit(solution)/shard_map/ppermute | solution.py:427

commit v3 on v2

--- a/solution.py
+++ b/solution.py
@@ -240,6 +240,10 @@
             flops=0, bytes_accessed=4 * (up.size + down.size), transcendentals=0
         ),
     )(up, down)
+
+
+def half_of(core, half):
+    return pl.ds(pl.multiple_of(core * half, LANES), half)
 
 
 def expert_kernel(outlets, width, experts, *refs):
@@ -280,7 +284,7 @@
             step = size // kind
             for n, out in enumerate(groups[i]):
                 piece = made[n * step : (n + 1) * step]
-                out[:, j * half : (j + 1) * half] = piece.astype(out.dtype)
+                out[:, half_of(core if j == 0 else 1 - core, half)] = piece.astype(out.dtype)
 
 
 def expert_rows(rows, weights, width, experts, outlets):
@@ -311,10 +315,11 @@
     return [[made.pop(0) for _ in group] for group in shapes]
 
 
-def split_add_kernel(part, arrived, own, pair):
-    half = own.shape[1]
-    own[...] = (part[:, :half] + arrived[:, :half].astype(jnp.float32)).astype(own.dtype)
-    pair[...] = (part[:, half:] + arrived[:, half:].astype(jnp.float32)).astype(pair.dtype)
+def split_add_kernel(part, arrived, goes_on, crosses):
+    core, half = lax.axis_index("tensor"), crosses.shape[1]
+    for out, which in ((goes_on, 1 - core), (crosses, core)):
+        columns = half_of(which, half)
+        out[...] = (part[:, columns] + arrived[:, columns].astype(jnp.float32)).astype(out.dtype)
 
 
 def split_add(part, arrived):
@@ -327,6 +332,21 @@
         out_specs=[vmem, vmem],
         compiler_params=pltpu.CompilerParams(vmem_limit_bytes=4 << 20),
     )(part, arrived)
+
+
+def other_half_kernel(x, out):
+    out[...] = x[:, half_of(1 - lax.axis_index("tensor"), out.shape[1])]
+
+
+def other_half(x):
+    vmem = pl.BlockSpec(memory_space=pltpu.VMEM)
+    return pl.pallas_call(
+        other_half_kernel,
+        out_shape=jax.ShapeDtypeStruct((x.shape[0], x.shape[1] // 2), x.dtype),
+        in_specs=[vmem],
+        out_specs=vmem,
+        compiler_params=pltpu.CompilerParams(vmem_limit_bytes=4 << 20),
+    )(x)
 
 
 def finish_kernel(pieces, own, own_pair, *refs):
@@ -340,7 +360,7 @@
         rows = slice(i * size, (i + 1) * size)
         total = own[rows] + arrived[i][...].astype(f32) + second_pair[i][...].astype(f32)
         mixed[core, rows] = total.astype(mixed.dtype)
-        total = second[i][:, :half].astype(f32) + crossed[i][...].astype(f32)
+        total = second[i][:, half_of(core, half)].astype(f32) + crossed[i][...].astype(f32)
         mixed[1 - core, rows] = (total + own_pair[rows].astype(f32)).astype(mixed.dtype)
 
 
@@ -365,12 +385,14 @@
     ahead = []
     for spot, here in enumerate(ring):
         there = ring[(spot + 1) % devices]
-        ahead += [(2 * here, 2 * there), (2 * there + 1, 2 * here + 1)]
+        core, next_core = spot % 2, (spot + 1) % 2
+        ahead.append((2 * here + core, 2 * there + next_core))
+        ahead.append((2 * there + 1 - next_core, 2 * here + 1 - core))
     back = [(b, a) for a, b in ahead]
     across = [(b, a ^ 1) for a, b in ahead]
     swap = [(0, 1), (1, 0)]
     f32, bf16 = jnp.float32, jnp.bfloat16
-    half, pieces = width // 2, PIECES if token_count % (PIECES * SUBLANES) == 0 else 1
+    pieces = PIECES if token_count % (PIECES * SUBLANES) == 0 else 1
     each = range(pieces)
 
     caps = (
@@ -412,7 +434,7 @@
                 (part + arrived.astype(f32)).astype(bf16)
                 for part, arrived in zip(part_second[step], sum_second)
             ]
-    second_pair = [lax.ppermute(sum_second[i][:, half:], "tensor", swap) for i in each]
+    second_pair = [lax.ppermute(other_half(sum_second[i]), "tensor", swap) for i in each]
     for step in range(steps - 1, 1, -1):
         sum_first = [lax.ppermute(sum_first[i], both, back) for i in each]
         sum_first = [

time: 64.9 us -> 61.8 us (0.952)
  starting transfers between devices: 36.7 us -> 34.9 us
  waiting for transfers between devices: 16.7 us -> 15.4 us
    ppermute x4, starting transfers between devices: 6.77 us -> 4.07 us  [by_ring(): sum_first = [lax.ppermute(sum_first[i], both, back) for i in each]]
    ppermute x2, starting transfers between devices: 0.07 us -> 2.54 us  [by_ring(): lax.ppermute(other_half(sum_second[i]), 'tensor', swap)]
    ppermute x6, waiting for transfers between devices: 1.33 us -> 0.13 us  [by_ring(): sum_second = [lax.ppermute(sum_second[i], both, back) for i in each]]
    ppermute x4, waiting for transfers between devices: 0.5 us -> 1.67 us  [by_ring(): sum_first = [lax.ppermute(sum_first[i], both, back) for i in each]]
    ppermute x4, waiting for transfers between devices: 9.49 us -> 8.6 us  [by_ring(): first.append(lax.ppermute(first[-1], both, ahead))]
    ppermute x2, starting transfers between devices: 3.43 us -> 2.77 us  [by_ring(): last = lax.ppermute(sum_first[i], both, back)]
where the time goes in v3:
time: 61.8 us; the launch traced here: 61.6 us
  starting transfers between devices  34.9 us (56%)
  waiting for transfers between devices  15.4 us (25%)
  Pallas kernels  10.3 us (17%)
  between operations  0.8 us (1%)
    ppermute x4, waiting for transfers between devices, by_ring(): first.append(lax.ppermute(first[-1], both, ahead))  8.6 us
    ppermute x4, starting transfers between devices, by_ring(): first.append(lax.ppermute(first[-1], both, ahead))  8.23 us
    ppermute x6, starting transfers between devices, by_ring(): sum_second = [lax.ppermute(sum_second[i], both, back) for i in each]  6.37 us
    pallas_call x4, Pallas kernels, expert_rows(): pl.pallas_call(functools.partial(expert_kernel, outlets, width, experts),...  5.6 us
    ppermute x3, starting transfers between devices, by_ring(): second.append(lax.ppermute(second[-1], both, ahead))  5.48 us
    ppermute x4, starting transfers between devices, by_ring(): sum_first = [lax.ppermute(sum_first[i], both, back) for i in each]  4.07 us
    ppermute x2, waiting for transfers between devices, by_ring(): crossed.append(lax.ppermute(crosses, both, across))  2.92 us
    ppermute x2, starting transfers between devices, by_ring(): last = lax.ppermute(sum_first[i], both, back)  2.77 us
  transfers between devices with their start and end apart: 28, of which 9 were waited for; matrix products, arithmetic and copies ran while one was open for 0% of the time, Pallas kernels for 15%

profile of v3, /device:TPU:0, one launch (start us, length us, event | category | flops | bytes accessed | tf_op | source)
XLA Modules:
  0.0 61.6 jit_solution(10309180401690662909)
XLA Ops:
  0.6 0.6 collective-permute-start.2
  1.2 0.1 collective-permute-start.3
  1.3 2.0 %shard_map.86 = (bf16[64,2176]{1,0:T(8,128)(2,1)}, bf16[64,2176]{1,0:T(8,128)(2,1)}, s32[2]{0:T(128)}) custom-call(s32[2,8,64]{2,1,0:T(8,128)} %bitcast.8, f32[2,8,64]{2,1,0:T(8,128)} %bitcast.9, s32[8]{0:T(128)} %old_in.1, s32[16]{0:T(128)} %new_in.1, bf16[2,64,2048]{2,1,0:T(8,128)(2,1)} %tokens.1), custom_call_target="tpu_custom_call" | custom-call | tf_op jit(solution)/shard_map/pallas_call | solution.py:200
  3.2 2.6 %collective-permute-start = (bf16[64,2176]{1,0:T(8,128)(2,1)}, bf16[64,2176]{1,0:T(8,128)(2,1)S(1)}, u32[]{:S(2)}, u32[]{:S(2)}) collective-permute-start(bf16[64,2176]{1,0:T(8,128)(2,1)} %get-tuple-element.27.refs_0_), channel_id=1, source_target_pairs={{0,3},{2,1},{3,6},{7,2},{6,11},{10,7},{11,14},{15,10},{14,13},{12,... | collective-permute-start | bytes 835592 | tf_op jit(solution)/shard_map/ppermute | solution.py:405
  5.9 4.5 %collective-permute-done.refs_1_ = bf16[64,2176]{1,0:T(8,128)(2,1)S(1)} collective-permute-done((bf16[64,2176]{1,0:T(8,128)(2,1)}, bf16[64,2176]{1,0:T(8,128)(2,1)S(1)}, u32[]{:S(2)}, u32[]{:S(2)}) %collective-permute-start) | collective-permute-done | bytes 278560 | tf_op jit(solution)/shard_map/ppermute | solution.py:405
  10.4 1.7 %collective-permute-start.5 = (bf16[64,2176]{1,0:T(8,128)(2,1)S(1)}, bf16[64,2176]{1,0:T(8,128)(2,1)S(1)}, u32[]{:S(2)}, u32[]{:S(2)}) collective-permute-start(bf16[64,2176]{1,0:T(8,128)(2,1)S(1)} %collective-permute-done.refs_1_), channel_id=1, source_target_pairs={{0,3},{2,1},{3,6},{7,2},{6,11},{10,7},{11,14},{15,10},{14,13},{12,... | collective-permute-start | bytes 835592 | tf_op jit(solution)/shard_map/ppermute | solution.py:405
  12.1 1.6 %collective-permute-start.1 = (bf16[64,2176]{1,0:T(8,128)(2,1)}, bf16[64,2176]{1,0:T(8,128)(2,1)S(1)}, u32[]{:S(2)}, u32[]{:S(2)}) collective-permute-start(bf16[64,2176]{1,0:T(8,128)(2,1)} %get-tuple-element.28), channel_id=1, source_target_pairs={{0,3},{2,1},{3,6},{7,2},{6,11},{10,7},{11,14},{15,10},{14,13},{12,... | collective-permute-start | bytes 835592 | tf_op jit(solution)/shard_map/ppermute | solution.py:407
  13.7 2.7 %collective-permute-done.5.refs_0_ = bf16[64,2176]{1,0:T(8,128)(2,1)S(1)} collective-permute-done((bf16[64,2176]{1,0:T(8,128)(2,1)S(1)}, bf16[64,2176]{1,0:T(8,128)(2,1)S(1)}, u32[]{:S(2)}, u32[]{:S(2)}) %collective-permute-start.5) | collective-permute-done | bytes 278560 | tf_op jit(solution)/shard_map/ppermute | solution.py:405
  16.4 2.0 %collective-permute-start.7 = (bf16[64,2176]{1,0:T(8,128)(2,1)S(1)}, bf16[64,2176]{1,0:T(8,128)(2,1)S(1)}, u32[]{:S(2)}, u32[]{:S(2)}) collective-permute-start(bf16[64,2176]{1,0:T(8,128)(2,1)S(1)} %collective-permute-done.5.refs_0_), channel_id=1, source_target_pairs={{0,3},{2,1},{3,6},{7,2},{6,11},{10,7},{11,14},{15,10},{14,13},{12,... | collective-permute-start | bytes 835592 | tf_op jit(solution)/shard_map/ppermute | solution.py:405
  18.4 1.0 %collective-permute-done.1.refs_2_ = bf16[64,2176]{1,0:T(8,128)(2,1)S(1)} collective-permute-done((bf16[64,2176]{1,0:T(8,128)(2,1)}, bf16[64,2176]{1,0:T(8,128)(2,1)S(1)}, u32[]{:S(2)}, u32[]{:S(2)}) %collective-permute-start.1) | collective-permute-done | bytes 278560 | tf_op jit(solution)/shard_map/ppermute | solution.py:407
  19.4 2.0 %collective-permute-start.6 = (bf16[64,2176]{1,0:T(8,128)(2,1)S(1)}, bf16[64,2176]{1,0:T(8,128)(2,1)S(1)}, u32[]{:S(2)}, u32[]{:S(2)}) collective-permute-start(bf16[64,2176]{1,0:T(8,128)(2,1)S(1)} %collective-permute-done.1.refs_2_), channel_id=1, source_target_pairs={{0,3},{2,1},{3,6},{7,2},{6,11},{10,7},{11,14},{15,10},{14,13},{12,... | collective-permute-start | bytes 835592 | tf_op jit(solution)/shard_map/ppermute | solution.py:407
  21.4 1.3 %collective-permute-done.7.refs_0_ = bf16[64,2176]{1,0:T(8,128)(2,1)S(1)} collective-permute-done((bf16[64,2176]{1,0:T(8,128)(2,1)S(1)}, bf16[64,2176]{1,0:T(8,128)(2,1)S(1)}, u32[]{:S(2)}, u32[]{:S(2)}) %collective-permute-start.7) | collective-permute-done | bytes 278560 | tf_op jit(solution)/shard_map/ppermute | solution.py:405
  22.7 2.0 %collective-permute-start.9 = (bf16[64,2176]{1,0:T(8,128)(2,1)S(1)}, bf16[64,2176]{1,0:T(8,128)(2,1)S(1)}, u32[]{:S(2)}, u32[]{:S(2)}) collective-permute-start(bf16[64,2176]{1,0:T(8,128)(2,1)S(1)} %collective-permute-done.7.refs_0_), channel_id=1, source_target_pairs={{0,3},{2,1},{3,6},{7,2},{6,11},{10,7},{11,14},{15,10},{14,13},{12,... | collective-permute-start | bytes 835592 | tf_op jit(solution)/shard_map/ppermute | solution.py:405
  24.6 1.0 %collective-permute-done.6.refs_1_ = bf16[64,2176]{1,0:T(8,128)(2,1)S(1)} collective-permute-done((bf16[64,2176]{1,0:T(8,128)(2,1)S(1)}, bf16[64,2176]{1,0:T(8,128)(2,1)S(1)}, u32[]{:S(2)}, u32[]{:S(2)}) %collective-permute-start.6) | collective-permute-done | bytes 278560 | tf_op jit(solution)/shard_map/ppermute | solution.py:407
  25.7 2.0 %collective-permute-start.8 = (bf16[64,2176]{1,0:T(8,128)(2,1)S(1)}, bf16[64,2176]{1,0:T(8,128)(2,1)S(1)}, u32[]{:S(2)}, u32[]{:S(2)}) collective-permute-start(bf16[64,2176]{1,0:T(8,128)(2,1)S(1)} %collective-permute-done.6.refs_1_), channel_id=1, source_target_pairs={{0,3},{2,1},{3,6},{7,2},{6,11},{10,7},{11,14},{15,10},{14,13},{12,... | collective-permute-start | bytes 835592 | tf_op jit(solution)/shard_map/ppermute | solution.py:407
  27.6 1.9 %shard_map.87 = (bf16[2048,384]{1,0:T(8,128)(2,1)S(1)}, bf16[768,1024]{1,0:T(8,128)(2,1)S(1)}) custom-call(bf16[2048,384]{1,0:T(8,128)(2,1)} %bitcast.5, bf16[768,1024]{1,0:T(8,128)(2,1)} %bitcast.7), custom_call_target="tpu_custom_call" | custom-call | bytes 6291456 | tf_op jit(solution)/shard_map/pallas_call | solution.py:229
  29.5 0.0 collective-permute-done.9.refs_0_
  29.5 0.0 collective-permute-done.2.refs_4_.refs_3_.refs_2_
  29.6 0.0 collective-permute-done.3.refs_6_.refs_5_.refs_4_
  29.6 1.3 %shard_map.91 = (bf16[32,2048]{1,0:T(8,128)(2,1)S(1)}, bf16[32,2048]{1,0:T(8,128)(2,1)S(1)}) custom-call(bf16[64,2176]{1,0:T(8,128)(2,1)S(1)} %collective-permute-done.9.refs_0_, bf16[2048,384]{1,0:T(8,128)(2,1)S(1)} %get-tuple-element.29.refs_3_.refs_2_.refs_1_, bf16[2048,384]{1,0:T(8,128)(2,1)S(1)} %collective-permute-done.2.refs_4_.refs_3_.refs_2_, ...), custom_call_target="tpu_custom_call" | custom-call | flops 402653184 | bytes 1048576 | tf_op jit(solution)/shard_map/pallas_call | solution.py:301
  30.8 1.5 %collective-permute-start.10 = (bf16[32,2048]{1,0:T(8,128)(2,1)S(1)}, bf16[32,2048]{1,0:T(8,128)(2,1)S(1)}, u32[]{:S(2)}, u32[]{:S(2)}) collective-permute-start(bf16[32,2048]{1,0:T(8,128)(2,1)S(1)} %get-tuple-element.36), channel_id=1, source_target_pairs={{3,0},{1,2},{6,3},{2,7},{11,6},{7,10},{14,11},{10,15},{13,14},{15,... | collective-permute-start | bytes 393224 | tf_op jit(solution)/shard_map/ppermute | solution.py:439
  32.3 0.8 %collective-permute-start.14 = (bf16[32,2048]{1,0:T(8,128)(2,1)S(1)}, bf16[32,2048]{1,0:T(8,128)(2,1)S(1)}, u32[]{:S(2)}, u32[]{:S(2)}) collective-permute-start(bf16[32,2048]{1,0:T(8,128)(2,1)S(1)} %get-tuple-element.41), channel_id=1, source_target_pairs={{3,0},{1,2},{6,3},{2,7},{11,6},{7,10},{14,11},{10,15},{13,14},{15,... | collective-permute-start | bytes 393224 | tf_op jit(solution)/shard_map/ppermute | solution.py:439
  33.2 0.0 collective-permute-done.8.refs_1_
  33.2 1.3 %shard_map.90 = (f32[32,2048]{1,0:T(8,128)S(1)}, f32[32,2048]{1,0:T(8,128)S(1)}, bf16[32,2048]{1,0:T(8,128)(2,1)S(1)}, bf16[32,2048]{1,0:T(8,128)(2,1)S(1)}) custom-call(bf16[64,2176]{1,0:T(8,128)(2,1)S(1)} %collective-permute-done.7.refs_0_, bf16[64,2176]{1,0:T(8,128)(2,1)S(1)} %collective-permute-done.8.refs_1_, ...), custom_call_target="tpu_custom_call" | custom-call | flops 805306368 | bytes 2097152 | tf_op jit(solution)/shard_map/pallas_call | solution.py:301
  34.5 2.1 %collective-permute-start.18 = (bf16[32,2048]{1,0:T(8,128)(2,1)S(1)}, bf16[32,2048]{1,0:T(8,128)(2,1)S(1)}, u32[]{:S(2)}, u32[]{:S(2)}) collective-permute-start(bf16[32,2048]{1,0:T(8,128)(2,1)S(1)} %get-tuple-element.45), channel_id=1, source_target_pairs={{3,0},{1,2},{6,3},{2,7},{11,6},{7,10},{14,11},{10,15},{13,14},{15,... | collective-permute-start | bytes 393224 | tf_op jit(solution)/shard_map/ppermute | solution.py:431
  36.6 0.6 collective-permute-start.22
  37.2 1.3 %shard_map.89 = (f32[32,2048]{1,0:T(8,128)S(1)}, f32[32,2048]{1,0:T(8,128)S(1)}, f32[32,2048]{1,0:T(8,128)S(1)}, f32[32,2048]{1,0:T(8,128)S(1)}) custom-call(bf16[64,2176]{1,0:T(8,128)(2,1)S(1)} %collective-permute-done.5.refs_0_, bf16[64,2176]{1,0:T(8,128)(2,1)S(1)} %collective-permute-done.6.refs_1_, ...), custom_call_target="tpu_custom_call" | custom-call | flops 805306368 | bytes 2097152 | tf_op jit(solution)/shard_map/pallas_call | solution.py:301
  38.4 0.0 copy-done
  38.5 1.8 %shard_map.88 = (f32[64,1024]{1,0:T(8,128)S(1)}, bf16[64,1024]{1,0:T(8,128)(2,1)S(1)}, f32[32,2048]{1,0:T(8,128)S(1)}, f32[32,2048]{1,0:T(8,128)S(1)}, f32[32,2048]{1,0:T(8,128)S(1)}, /*index=5*/f32[32,2048]{1,0:T(8,128)S(1)}) custom-call(bf16[64,2176]{1,0:T(8,128)(2,1)S(1)} %copy-done, bf16[64,2176]{1,0:T(8,128)(2,1)S(1)} %collective-permute-done.refs_1_, ...), custom_call_target="tpu_custom_call" | custom-call | flops 1207959552 | bytes 3145728 | tf_op jit(solution)/shard_map/pallas_call | solution.py:301
  40.2 0.0 collective-permute-done.10
  40.3 1.1 %collective-permute-start.11 = (bf16[32,2048]{1,0:T(8,128)(2,1)S(1)}, bf16[32,2048]{1,0:T(8,128)(2,1)S(1)}, u32[]{:S(2)}, u32[]{:S(2)}) collective-permute-start(bf16[32,2048]{1,0:T(8,128)(2,1)S(1)} %add_convert_fusion.7), channel_id=1, source_target_pairs={{3,0},{1,2},{6,3},{2,7},{11,6},{7,10},{14,11},{10,15},{13,14},{15,... | collective-permute-start | bytes 393224 | tf_op jit(solution)/shard_map/ppermute | solution.py:439
  41.4 0.0 collective-permute-done.14
  41.4 0.6 %collective-permute-start.15 = (bf16[32,2048]{1,0:T(8,128)(2,1)S(1)}, bf16[32,2048]{1,0:T(8,128)(2,1)S(1)}, u32[]{:S(2)}, u32[]{:S(2)}) collective-permute-start(bf16[32,2048]{1,0:T(8,128)(2,1)S(1)} %add_convert_fusion.5), channel_id=1, source_target_pairs={{3,0},{1,2},{6,3},{2,7},{11,6},{7,10},{14,11},{10,15},{13,14},{15,... | collective-permute-start | bytes 393224 | tf_op jit(solution)/shard_map/ppermute | solution.py:439
  42.1 0.0 collective-permute-done.18
  42.1 0.8 %collective-permute-start.19 = (bf16[32,2048]{1,0:T(8,128)(2,1)S(1)}, bf16[32,2048]{1,0:T(8,128)(2,1)S(1)}, u32[]{:S(2)}, u32[]{:S(2)}) collective-permute-start(bf16[32,2048]{1,0:T(8,128)(2,1)S(1)} %add_convert_fusion.3), channel_id=1, source_target_pairs={{3,0},{1,2},{6,3},{2,7},{11,6},{7,10},{14,11},{10,15},{13,14},{15,... | collective-permute-start | bytes 393224 | tf_op jit(solution)/shard_map/ppermute | solution.py:431
  42.9 0.0 collective-permute-done.22
  42.9 0.1 collective-permute-start.23
  43.1 1.7 %collective-permute-done.11 = bf16[32,2048]{1,0:T(8,128)(2,1)S(1)} collective-permute-done((bf16[32,2048]{1,0:T(8,128)(2,1)S(1)}, bf16[32,2048]{1,0:T(8,128)(2,1)S(1)}, u32[]{:S(2)}, u32[]{:S(2)}) %collective-permute-start.11) | collective-permute-done | bytes 131104 | tf_op jit(solution)/shard_map/ppermute | solution.py:439
  44.8 1.4 %collective-permute-start.12 = (bf16[32,2048]{1,0:T(8,128)(2,1)S(1)}, bf16[32,2048]{1,0:T(8,128)(2,1)S(1)}, u32[]{:S(2)}, u32[]{:S(2)}) collective-permute-start(bf16[32,2048]{1,0:T(8,128)(2,1)S(1)} %add_convert_fusion.6), channel_id=1, source_target_pairs={{3,0},{1,2},{6,3},{2,7},{11,6},{7,10},{14,11},{10,15},{13,14},{15,... | collective-permute-start | bytes 393224 | tf_op jit(solution)/shard_map/ppermute | solution.py:446
  46.2 0.0 collective-permute-done.15
  46.2 1.4 %collective-permute-start.16 = (bf16[32,2048]{1,0:T(8,128)(2,1)S(1)}, bf16[32,2048]{1,0:T(8,128)(2,1)S(1)}, u32[]{:S(2)}, u32[]{:S(2)}) collective-permute-start(bf16[32,2048]{1,0:T(8,128)(2,1)S(1)} %add_convert_fusion.4), channel_id=1, source_target_pairs={{3,0},{1,2},{6,3},{2,7},{11,6},{7,10},{14,11},{10,15},{13,14},{15,... | collective-permute-start | bytes 393224 | tf_op jit(solution)/shard_map/ppermute | solution.py:446
  47.6 0.0 collective-permute-done.19
  47.6 1.4 %collective-permute-start.20 = (bf16[32,2048]{1,0:T(8,128)(2,1)S(1)}, bf16[32,2048]{1,0:T(8,128)(2,1)S(1)}, u32[]{:S(2)}, u32[]{:S(2)}) collective-permute-start(bf16[32,2048]{1,0:T(8,128)(2,1)S(1)} %add_convert_fusion.2), channel_id=1, source_target_pairs={{3,0},{1,2},{6,3},{2,7},{11,6},{7,10},{14,11},{10,15},{13,14},{15,... | collective-permute-start | bytes 393224 | tf_op jit(solution)/shard_map/ppermute | solution.py:431
  49.0 0.0 collective-permute-done.23
  49.0 1.4 %collective-permute-start.24 = (bf16[32,2048]{1,0:T(8,128)(2,1)S(1)}, bf16[32,2048]{1,0:T(8,128)(2,1)S(1)}, u32[]{:S(2)}, u32[]{:S(2)}) collective-permute-start(bf16[32,2048]{1,0:T(8,128)(2,1)S(1)} %add_convert_fusion), channel_id=1, source_target_pairs={{3,0},{1,2},{6,3},{2,7},{11,6},{7,10},{14,11},{10,15},{13,14},{15,... | collective-permute-start | bytes 393224 | tf_op jit(solution)/shard_map/ppermute | solution.py:431
  50.4 0.0 collective-permute-start.4
  50.4 0.0 collective-permute-done.12.arrived
  50.4 1.7 %collective-permute-start.13 = (bf16[32,1024]{1,0:T(8,128)(2,1)S(1)}, bf16[32,1024]{1,0:T(8,128)(2,1)S(1)}, u32[]{:S(2)}, u32[]{:S(2)}) collective-permute-start(bf16[32,1024]{1,0:T(8,128)(2,1)S(1)} %get-tuple-element.37), channel_id=1, source_target_pairs={{3,0},{1,2},{6,3},{2,7},{11,6},{7,10},{14,11},{10,15},{13,14},{15,... | collective-permute-start | bytes 196616 | tf_op jit(solution)/shard_map/ppermute | solution.py:448
  52.1 0.0 collective-permute-done.16.arrived
  52.2 1.0 %collective-permute-start.17 = (bf16[32,1024]{1,0:T(8,128)(2,1)S(1)}, bf16[32,1024]{1,0:T(8,128)(2,1)S(1)}, u32[]{:S(2)}, u32[]{:S(2)}) collective-permute-start(bf16[32,1024]{1,0:T(8,128)(2,1)S(1)} %get-tuple-element.42), channel_id=1, source_target_pairs={{3,0},{1,2},{6,3},{2,7},{11,6},{7,10},{14,11},{10,15},{13,14},{15,... | collective-permute-start | bytes 196616 | tf_op jit(solution)/shard_map/ppermute | solution.py:448
  53.2 0.0 collective-permute-done.20.x.refs_4_
  53.2 1.3 %collective-permute-start.21 = (bf16[32,1024]{1,0:T(8,128)(2,1)S(1)}, bf16[32,1024]{1,0:T(8,128)(2,1)S(1)}, u32[]{:S(2)}, u32[]{:S(2)}) collective-permute-start(bf16[32,1024]{1,0:T(8,128)(2,1)S(1)} %shard_map.94), channel_id=1, source_target_pairs={{0,1},{1,0},{2,3},{3,2},{4,5},{5,4},{6,7},{7,6},{8,9},{9,8},{10,11... | collective-permute-start | bytes 196616 | tf_op jit(solution)/shard_map/ppermute | solution.py:437
  54.4 0.1 collective-permute-done.24.x.refs_5_
  54.6 1.3 %collective-permute-start.25 = (bf16[32,1024]{1,0:T(8,128)(2,1)S(1)}, bf16[32,1024]{1,0:T(8,128)(2,1)S(1)}, u32[]{:S(2)}, u32[]{:S(2)}) collective-permute-start(bf16[32,1024]{1,0:T(8,128)(2,1)S(1)} %shard_map.95), channel_id=1, source_target_pairs={{0,1},{1,0},{2,3},{3,2},{4,5},{5,4},{6,7},{7,6},{8,9},{9,8},{10,11... | collective-permute-start | bytes 196616 | tf_op jit(solution)/shard_map/ppermute | solution.py:437
  55.9 0.0 collective-permute-done.4.own_pair
  55.9 0.5 collective-permute-start.26
  56.3 0.0 collective-permute-done.13.refs_0_
  56.3 1.6 %collective-permute-start.27 = (bf16[32,1024]{1,0:T(8,128)(2,1)S(1)}, bf16[32,1024]{1,0:T(8,128)(2,1)S(1)}, u32[]{:S(2)}, u32[]{:S(2)}) collective-permute-start(bf16[32,1024]{1,0:T(8,128)(2,1)S(1)} %get-tuple-element.50), channel_id=1, source_target_pairs={{3,1},{1,3},{6,2},{2,6},{11,7},{7,11},{14,10},{10,14},{13,15},{15,... | collective-permute-start | bytes 196616 | tf_op jit(solution)/shard_map/ppermute | solution.py:449
  57.9 0.0 collective-permute-done.17.refs_1_
  57.9 0.0 collective-permute-done.21.refs_2_
  57.9 0.0 collective-permute-done.25.refs_3_
  57.9 2.2 %collective-permute-done.26.refs_6_ = bf16[32,1024]{1,0:T(8,128)(2,1)S(1)} collective-permute-done((bf16[32,1024]{1,0:T(8,128)(2,1)S(1)}, bf16[32,1024]{1,0:T(8,128)(2,1)S(1)}, u32[]{:S(2)}, u32[]{:S(2)}) %collective-permute-start.26) | collective-permute-done | bytes 65568 | tf_op jit(solution)/shard_map/ppermute | solution.py:449
  60.1 0.7 %collective-permute-done.27.refs_7_ = bf16[32,1024]{1,0:T(8,128)(2,1)S(1)} collective-permute-done((bf16[32,1024]{1,0:T(8,128)(2,1)S(1)}, bf16[32,1024]{1,0:T(8,128)(2,1)S(1)}, u32[]{:S(2)}, u32[]{:S(2)}) %collective-permute-start.27) | collective-permute-done | bytes 65568 | tf_op jit(solution)/shard_map/ppermute | solution.py:449
  60.8 0.8 %shard_map.96 = bf16[2,64,1024]{2,1,0:T(8,128)(2,1)} custom-call(f32[64,1024]{1,0:T(8,128)S(1)} %get-tuple-element.31.own, bf16[64,1024]{1,0:T(8,128)(2,1)S(1)} %collective-permute-done.4.own_pair, bf16[32,1024]{1,0:T(8,128)(2,1)S(1)} %collective-permute-done.13.refs_0_, bf16[32,1024]{1,0:T(8,128)(2,1)S(1)} %collective-permute-done.17.refs_1_, ...), custom_call_target="tpu_custom_call" | custom-call | tf_op jit(solution)/shard_map/pallas_call | solution.py:369
  (13 shorter events, 0.3 us)
Async XLA Ops:
  0.6 28.9 %collective-permute-start.2 = (bf16[2048,384]{1,0:T(8,128)(2,1)}, bf16[2048,384]{1,0:T(8,128)(2,1)S(1)}, u32[]{:S(2)}, u32[]{:S(2)}) collective-permute-start(bf16[2048,384]{1,0:T(8,128)(2,1)} %bitcast.4), channel_id=1, source_target_pairs={{0,1},{1,0},{2,3},{3,2},{4,5},{5,4},{6,7},{7,6},{8,9},{9,8},{10,11... | collective-permute-start | bytes 4718600 | tf_op jit(solution)/shard_map/ppermute | solution.py:409
  1.2 28.4 %collective-permute-start.3 = (bf16[768,1024]{1,0:T(8,128)(2,1)}, bf16[768,1024]{1,0:T(8,128)(2,1)S(1)}, u32[]{:S(2)}, u32[]{:S(2)}) collective-permute-start(bf16[768,1024]{1,0:T(8,128)(2,1)} %bitcast.6), channel_id=1, source_target_pairs={{0,1},{1,0},{2,3},{3,2},{4,5},{5,4},{6,7},{7,6},{8,9},{9,8},{10,11... | collective-permute-start | bytes 4718600 | tf_op jit(solution)/shard_map/ppermute | solution.py:410
  3.2 7.2 %collective-permute-start = (bf16[64,2176]{1,0:T(8,128)(2,1)}, bf16[64,2176]{1,0:T(8,128)(2,1)S(1)}, u32[]{:S(2)}, u32[]{:S(2)}) collective-permute-start(bf16[64,2176]{1,0:T(8,128)(2,1)} %get-tuple-element.27.refs_0_), channel_id=1, source_target_pairs={{0,3},{2,1},{3,6},{7,2},{6,11},{10,7},{11,14},{15,10},{14,13},{12,... | collective-permute-start | bytes 835592 | tf_op jit(solution)/shard_map/ppermute | solution.py:405
  10.4 6.0 %collective-permute-start.5 = (bf16[64,2176]{1,0:T(8,128)(2,1)S(1)}, bf16[64,2176]{1,0:T(8,128)(2,1)S(1)}, u32[]{:S(2)}, u32[]{:S(2)}) collective-permute-start(bf16[64,2176]{1,0:T(8,128)(2,1)S(1)} %collective-permute-done.refs_1_), channel_id=1, source_target_pairs={{0,3},{2,1},{3,6},{7,2},{6,11},{10,7},{11,14},{15,10},{14,13},{12,... | collective-permute-start | bytes 835592 | tf_op jit(solution)/shard_map/ppermute | solution.py:405
  12.1 7.3 %collective-permute-start.1 = (bf16[64,2176]{1,0:T(8,128)(2,1)}, bf16[64,2176]{1,0:T(8,128)(2,1)S(1)}, u32[]{:S(2)}, u32[]{:S(2)}) collective-permute-start(bf16[64,2176]{1,0:T(8,128)(2,1)} %get-tuple-element.28), channel_id=1, source_target_pairs={{0,3},{2,1},{3,6},{7,2},{6,11},{10,7},{11,14},{15,10},{14,13},{12,... | collective-permute-start | bytes 835592 | tf_op jit(solution)/shard_map/ppermute | solution.py:407
  16.4 6.3 %collective-permute-start.7 = (bf16[64,2176]{1,0:T(8,128)(2,1)S(1)}, bf16[64,2176]{1,0:T(8,128)(2,1)S(1)}, u32[]{:S(2)}, u32[]{:S(2)}) collective-permute-start(bf16[64,2176]{1,0:T(8,128)(2,1)S(1)} %collective-permute-done.5.refs_0_), channel_id=1, source_target_pairs={{0,3},{2,1},{3,6},{7,2},{6,11},{10,7},{11,14},{15,10},{14,13},{12,... | collective-permute-start | bytes 835592 | tf_op jit(solution)/shard_map/ppermute | solution.py:405
  19.4 6.3 %collective-permute-start.6 = (bf16[64,2176]{1,0:T(8,128)(2,1)S(1)}, bf16[64,2176]{1,0:T(8,128)(2,1)S(1)}, u32[]{:S(2)}, u32[]{:S(2)}) collective-permute-start(bf16[64,2176]{1,0:T(8,128)(2,1)S(1)} %collective-permute-done.1.refs_2_), channel_id=1, source_target_pairs={{0,3},{2,1},{3,6},{7,2},{6,11},{10,7},{11,14},{15,10},{14,13},{12,... | collective-permute-start | bytes 835592 | tf_op jit(solution)/shard_map/ppermute | solution.py:407
  22.7 6.8 %collective-permute-start.9 = (bf16[64,2176]{1,0:T(8,128)(2,1)S(1)}, bf16[64,2176]{1,0:T(8,128)(2,1)S(1)}, u32[]{:S(2)}, u32[]{:S(2)}) collective-permute-start(bf16[64,2176]{1,0:T(8,128)(2,1)S(1)} %collective-permute-done.7.refs_0_), channel_id=1, source_target_pairs={{0,3},{2,1},{3,6},{7,2},{6,11},{10,7},{11,14},{15,10},{14,13},{12,... | collective-permute-start | bytes 835592 | tf_op jit(solution)/shard_map/ppermute | solution.py:405
  25.7 7.5 %collective-permute-start.8 = (bf16[64,2176]{1,0:T(8,128)(2,1)S(1)}, bf16[64,2176]{1,0:T(8,128)(2,1)S(1)}, u32[]{:S(2)}, u32[]{:S(2)}) collective-permute-start(bf16[64,2176]{1,0:T(8,128)(2,1)S(1)} %collective-permute-done.6.refs_1_), channel_id=1, source_target_pairs={{0,3},{2,1},{3,6},{7,2},{6,11},{10,7},{11,14},{15,10},{14,13},{12,... | collective-permute-start | bytes 835592 | tf_op jit(solution)/shard_map/ppermute | solution.py:407
  30.8 9.4 %collective-permute-start.10 = (bf16[32,2048]{1,0:T(8,128)(2,1)S(1)}, bf16[32,2048]{1,0:T(8,128)(2,1)S(1)}, u32[]{:S(2)}, u32[]{:S(2)}) collective-permute-start(bf16[32,2048]{1,0:T(8,128)(2,1)S(1)} %get-tuple-element.36), channel_id=1, source_target_pairs={{3,0},{1,2},{6,3},{2,7},{11,6},{7,10},{14,11},{10,15},{13,14},{15,... | collective-permute-start | bytes 393224 | tf_op jit(solution)/shard_map/ppermute | solution.py:439
  32.3 9.1 %collective-permute-start.14 = (bf16[32,2048]{1,0:T(8,128)(2,1)S(1)}, bf16[32,2048]{1,0:T(8,128)(2,1)S(1)}, u32[]{:S(2)}, u32[]{:S(2)}) collective-permute-start(bf16[32,2048]{1,0:T(8,128)(2,1)S(1)} %get-tuple-element.41), channel_id=1, source_target_pairs={{3,0},{1,2},{6,3},{2,7},{11,6},{7,10},{14,11},{10,15},{13,14},{15,... | collective-permute-start | bytes 393224 | tf_op jit(solution)/shard_map/ppermute | solution.py:439
  34.5 7.6 %collective-permute-start.18 = (bf16[32,2048]{1,0:T(8,128)(2,1)S(1)}, bf16[32,2048]{1,0:T(8,128)(2,1)S(1)}, u32[]{:S(2)}, u32[]{:S(2)}) collective-permute-start(bf16[32,2048]{1,0:T(8,128)(2,1)S(1)} %get-tuple-element.45), channel_id=1, source_target_pairs={{3,0},{1,2},{6,3},{2,7},{11,6},{7,10},{14,11},{10,15},{13,14},{15,... | collective-permute-start | bytes 393224 | tf_op jit(solution)/shard_map/ppermute | solution.py:431
  36.6 1.9 %copy-start = (bf16[64,2176]{1,0:T(8,128)(2,1)S(1)}, bf16[64,2176]{1,0:T(8,128)(2,1)}, u32[]{:S(2)}) copy-start(bf16[64,2176]{1,0:T(8,128)(2,1)} %get-tuple-element.27.refs_0_) | copy-start | bytes 835588
  36.6 6.3 %collective-permute-start.22 = (bf16[32,2048]{1,0:T(8,128)(2,1)S(1)}, bf16[32,2048]{1,0:T(8,128)(2,1)S(1)}, u32[]{:S(2)}, u32[]{:S(2)}) collective-permute-start(bf16[32,2048]{1,0:T(8,128)(2,1)S(1)} %get-tuple-element.48), channel_id=1, source_target_pairs={{3,0},{1,2},{6,3},{2,7},{11,6},{7,10},{14,11},{10,15},{13,14},{15,... | collective-permute-start | bytes 393224 | tf_op jit(solution)/shard_map/ppermute | solution.py:431
  40.3 4.4 %collective-permute-start.11 = (bf16[32,2048]{1,0:T(8,128)(2,1)S(1)}, bf16[32,2048]{1,0:T(8,128)(2,1)S(1)}, u32[]{:S(2)}, u32[]{:S(2)}) collective-permute-start(bf16[32,2048]{1,0:T(8,128)(2,1)S(1)} %add_convert_fusion.7), channel_id=1, source_target_pairs={{3,0},{1,2},{6,3},{2,7},{11,6},{7,10},{14,11},{10,15},{13,14},{15,... | collective-permute-start | bytes 393224 | tf_op jit(solution)/shard_map/ppermute | solution.py:439
  41.4 4.7 %collective-permute-start.15 = (bf16[32,2048]{1,0:T(8,128)(2,1)S(1)}, bf16[32,2048]{1,0:T(8,128)(2,1)S(1)}, u32[]{:S(2)}, u32[]{:S(2)}) collective-permute-start(bf16[32,2048]{1,0:T(8,128)(2,1)S(1)} %add_convert_fusion.5), channel_id=1, source_target_pairs={{3,0},{1,2},{6,3},{2,7},{11,6},{7,10},{14,11},{10,15},{13,14},{15,... | collective-permute-start | bytes 393224 | tf_op jit(solution)/shard_map/ppermute | solution.py:439
  42.1 5.5 %collective-permute-start.19 = (bf16[32,2048]{1,0:T(8,128)(2,1)S(1)}, bf16[32,2048]{1,0:T(8,128)(2,1)S(1)}, u32[]{:S(2)}, u32[]{:S(2)}) collective-permute-start(bf16[32,2048]{1,0:T(8,128)(2,1)S(1)} %add_convert_fusion.3), channel_id=1, source_target_pairs={{3,0},{1,2},{6,3},{2,7},{11,6},{7,10},{14,11},{10,15},{13,14},{15,... | collective-permute-start | bytes 393224 | tf_op jit(solution)/shard_map/ppermute | solution.py:431
  42.9 6.0 %collective-permute-start.23 = (bf16[32,2048]{1,0:T(8,128)(2,1)S(1)}, bf16[32,2048]{1,0:T(8,128)(2,1)S(1)}, u32[]{:S(2)}, u32[]{:S(2)}) collective-permute-start(bf16[32,2048]{1,0:T(8,128)(2,1)S(1)} %add_convert_fusion.1), channel_id=1, source_target_pairs={{3,0},{1,2},{6,3},{2,7},{11,6},{7,10},{14,11},{10,15},{13,14},{15,... | collective-permute-start | bytes 393224 | tf_op jit(solution)/shard_map/ppermute | solution.py:431
  44.8 5.7 %collective-permute-start.12 = (bf16[32,2048]{1,0:T(8,128)(2,1)S(1)}, bf16[32,2048]{1,0:T(8,128)(2,1)S(1)}, u32[]{:S(2)}, u32[]{:S(2)}) collective-permute-start(bf16[32,2048]{1,0:T(8,128)(2,1)S(1)} %add_convert_fusion.6), channel_id=1, source_target_pairs={{3,0},{1,2},{6,3},{2,7},{11,6},{7,10},{14,11},{10,15},{13,14},{15,... | collective-permute-start | bytes 393224 | tf_op jit(solution)/shard_map/ppermute | solution.py:446
  46.2 6.0 %collective-permute-start.16 = (bf16[32,2048]{1,0:T(8,128)(2,1)S(1)}, bf16[32,2048]{1,0:T(8,128)(2,1)S(1)}, u32[]{:S(2)}, u32[]{:S(2)}) collective-permute-start(bf16[32,2048]{1,0:T(8,128)(2,1)S(1)} %add_convert_fusion.4), channel_id=1, source_target_pairs={{3,0},{1,2},{6,3},{2,7},{11,6},{7,10},{14,11},{10,15},{13,14},{15,... | collective-permute-start | bytes 393224 | tf_op jit(solution)/shard_map/ppermute | solution.py:446
  47.6 5.6 %collective-permute-start.20 = (bf16[32,2048]{1,0:T(8,128)(2,1)S(1)}, bf16[32,2048]{1,0:T(8,128)(2,1)S(1)}, u32[]{:S(2)}, u32[]{:S(2)}) collective-permute-start(bf16[32,2048]{1,0:T(8,128)(2,1)S(1)} %add_convert_fusion.2), channel_id=1, source_target_pairs={{3,0},{1,2},{6,3},{2,7},{11,6},{7,10},{14,11},{10,15},{13,14},{15,... | collective-permute-start | bytes 393224 | tf_op jit(solution)/shard_map/ppermute | solution.py:431
  49.0 5.6 %collective-permute-start.24 = (bf16[32,2048]{1,0:T(8,128)(2,1)S(1)}, bf16[32,2048]{1,0:T(8,128)(2,1)S(1)}, u32[]{:S(2)}, u32[]{:S(2)}) collective-permute-start(bf16[32,2048]{1,0:T(8,128)(2,1)S(1)} %add_convert_fusion), channel_id=1, source_target_pairs={{3,0},{1,2},{6,3},{2,7},{11,6},{7,10},{14,11},{10,15},{13,14},{15,... | collective-permute-start | bytes 393224 | tf_op jit(solution)/shard_map/ppermute | solution.py:431
  50.4 5.5 %collective-permute-start.4 = (bf16[64,1024]{1,0:T(8,128)(2,1)S(1)}, bf16[64,1024]{1,0:T(8,128)(2,1)S(1)}, u32[]{:S(2)}, u32[]{:S(2)}) collective-permute-start(bf16[64,1024]{1,0:T(8,128)(2,1)S(1)} %get-tuple-element.32), channel_id=1, source_target_pairs={{0,1},{1,0},{2,3},{3,2},{4,5},{5,4},{6,7},{7,6},{8,9},{9,8},{10,11... | collective-permute-start | bytes 393224 | tf_op jit(solution)/shard_map/ppermute | solution.py:428
  50.4 5.9 %collective-permute-start.13 = (bf16[32,1024]{1,0:T(8,128)(2,1)S(1)}, bf16[32,1024]{1,0:T(8,128)(2,1)S(1)}, u32[]{:S(2)}, u32[]{:S(2)}) collective-permute-start(bf16[32,1024]{1,0:T(8,128)(2,1)S(1)} %get-tuple-element.37), channel_id=1, source_target_pairs={{3,0},{1,2},{6,3},{2,7},{11,6},{7,10},{14,11},{10,15},{13,14},{15,... | collective-permute-start | bytes 196616 | tf_op jit(solution)/shard_map/ppermute | solution.py:448
  52.2 5.7 %collective-permute-start.17 = (bf16[32,1024]{1,0:T(8,128)(2,1)S(1)}, bf16[32,1024]{1,0:T(8,128)(2,1)S(1)}, u32[]{:S(2)}, u32[]{:S(2)}) collective-permute-start(bf16[32,1024]{1,0:T(8,128)(2,1)S(1)} %get-tuple-element.42), channel_id=1, source_target_pairs={{3,0},{1,2},{6,3},{2,7},{11,6},{7,10},{14,11},{10,15},{13,14},{15,... | collective-permute-start | bytes 196616 | tf_op jit(solution)/shard_map/ppermute | solution.py:448
  53.2 4.7 %collective-permute-start.21 = (bf16[32,1024]{1,0:T(8,128)(2,1)S(1)}, bf16[32,1024]{1,0:T(8,128)(2,1)S(1)}, u32[]{:S(2)}, u32[]{:S(2)}) collective-permute-start(bf16[32,1024]{1,0:T(8,128)(2,1)S(1)} %shard_map.94), channel_id=1, source_target_pairs={{0,1},{1,0},{2,3},{3,2},{4,5},{5,4},{6,7},{7,6},{8,9},{9,8},{10,11... | collective-permute-start | bytes 196616 | tf_op jit(solution)/shard_map/ppermute | solution.py:437
  54.6 3.3 %collective-permute-start.25 = (bf16[32,1024]{1,0:T(8,128)(2,1)S(1)}, bf16[32,1024]{1,0:T(8,128)(2,1)S(1)}, u32[]{:S(2)}, u32[]{:S(2)}) collective-permute-start(bf16[32,1024]{1,0:T(8,128)(2,1)S(1)} %shard_map.95), channel_id=1, source_target_pairs={{0,1},{1,0},{2,3},{3,2},{4,5},{5,4},{6,7},{7,6},{8,9},{9,8},{10,11... | collective-permute-start | bytes 196616 | tf_op jit(solution)/shard_map/ppermute | solution.py:437
  55.9 4.3 %collective-permute-start.26 = (bf16[32,1024]{1,0:T(8,128)(2,1)S(1)}, bf16[32,1024]{1,0:T(8,128)(2,1)S(1)}, u32[]{:S(2)}, u32[]{:S(2)}) collective-permute-start(bf16[32,1024]{1,0:T(8,128)(2,1)S(1)} %get-tuple-element.49), channel_id=1, source_target_pairs={{3,1},{1,3},{6,2},{2,6},{11,7},{7,11},{14,10},{10,14},{13,15},{15,... | collective-permute-start | bytes 196616 | tf_op jit(solution)/shard_map/ppermute | solution.py:449
  56.3 4.5 %collective-permute-start.27 = (bf16[32,1024]{1,0:T(8,128)(2,1)S(1)}, bf16[32,1024]{1,0:T(8,128)(2,1)S(1)}, u32[]{:S(2)}, u32[]{:S(2)}) collective-permute-start(bf16[32,1024]{1,0:T(8,128)(2,1)S(1)} %get-tuple-element.50), channel_id=1, source_target_pairs={{3,1},{1,3},{6,2},{2,6},{11,7},{7,11},{14,10},{10,14},{13,15},{15,... | collective-permute-start | bytes 196616 | tf_op jit(solution)/shard_map/ppermute | solution.py:449

commit v4 on v3

--- a/solution.py
+++ b/solution.py
@@ -11,6 +11,8 @@
 LANES = 128
 VMEM_BYTES = 67043328
 PIECES = 2
+AHEAD_FIRST = 2
+AHEAD_SECOND = 2
 SUBLANES = 16
 
 
@@ -140,21 +142,25 @@
     )
 
 
-def pack_kernel(caps, routes_in, probs_in, old_in, new_in, tokens, *refs):
-    first, second, slot_rows, routes, probs, old_place, new_place, sems = refs
+def pack_kernel(caps, pieces, routes_in, probs_in, old_in, new_in, tokens, *refs):
+    count = sum(pieces)
+    outs, (slot_rows, routes, probs, old_place, new_place, sems) = refs[:count], refs[count:]
     core, devices = lax.axis_index("tensor"), lax.axis_size("expert")
     width = tokens.shape[2]
     token_count = routes.shape[2]
     experts, slots = old_place.shape[0], new_place.shape[0]
-    lanes = first.shape[1] - width
-    pairs = (
+    lanes = outs[0].shape[1] - width
+    chunks = (outs[: pieces[0]], core), (outs[pieces[0] :], 1 - core)
+    pairs = [
         (old_in, old_place),
         (new_in, new_place),
         (routes_in, routes),
         (probs_in, probs),
-        (tokens.at[core], first.at[:, :width]),
-        (tokens.at[1 - core], second.at[:, :width]),
-    )
+    ]
+    for held, batch in chunks:
+        size = token_count // len(held)
+        for i, out in enumerate(held):
+            pairs.append((tokens.at[batch, i * size : (i + 1) * size], out.at[:, :width]))
     copies = [pltpu.make_async_copy(src, dst, sems.at[i]) for i, (src, dst) in enumerate(pairs)]
     for copy in copies:
         copy.start()
@@ -162,7 +168,7 @@
         copy.wait()
     token = lax.broadcasted_iota(jnp.int32, (1, token_count), 1)
     limits = [caps[1] * count_of(new_place, old_place[e], slots) for e in range(experts)]
-    for out, batch in ((first, core), (second, 1 - core)):
+    for held, batch in chunks:
         highs, lows = [], []
         for e in range(experts):
             named = routes[batch] == old_place[e]
@@ -173,41 +179,48 @@
             highs.append(high)
             lows.append(weight - high)
         pad = jnp.zeros((lanes - 2 * experts, token_count), jnp.float32)
-        out[:, width:] = jnp.concatenate(highs + lows + [pad], axis=0).T.astype(jnp.bfloat16)
+        side = jnp.concatenate(highs + lows + [pad], axis=0).T.astype(jnp.bfloat16)
+        size = token_count // len(held)
+        for i, out in enumerate(held):
+            out[:, width:] = side[i * size : (i + 1) * size]
     mine = slot_rows.shape[0]
     for j in range(mine):
         slot = lax.axis_index("expert") * mine + j
         expert = new_place[slot]
         holders = count_of(new_place, expert, slots)
         place = count_of(new_place, expert, slot)
-        count = jnp.int32(0)
+        total = jnp.int32(0)
         for source in range(devices):
             start = lax.rem(place - source + devices * holders, holders)
-            count += lax.div(token_count - 1 - start + holders, holders)
-        slot_rows[j] = count
+            total += lax.div(token_count - 1 - start + holders, holders)
+        slot_rows[j] = total
     for copy in copies[4:]:
         copy.wait()
 
 
-def pack(caps, tokens, routes, probs, old_place, new_place):
+def pack(caps, pieces, tokens, routes, probs, old_place, new_place):
     token_count, width = tokens.shape[1:]
     experts = old_place.shape[0]
     lanes = -(-2 * experts // LANES) * LANES
-    chunk = jax.ShapeDtypeStruct((token_count, width + lanes), tokens.dtype)
+    chunks = [
+        jax.ShapeDtypeStruct((token_count // parts, width + lanes), tokens.dtype)
+        for parts in pieces
+        for _ in range(parts)
+    ]
     routes, probs = routes.transpose(0, 2, 1), probs.transpose(0, 2, 1)
     mine = new_place.shape[0] // lax.axis_size("expert")
     vmem, smem = pl.BlockSpec(memory_space=pltpu.VMEM), pl.BlockSpec(memory_space=pltpu.SMEM)
     return pl.pallas_call(
-        functools.partial(pack_kernel, caps),
-        out_shape=(chunk, chunk, jax.ShapeDtypeStruct((mine,), jnp.int32)),
+        functools.partial(pack_kernel, caps, pieces),
+        out_shape=[*chunks, jax.ShapeDtypeStruct((mine,), jnp.int32)],
         in_specs=[pl.BlockSpec(memory_space=pltpu.HBM)] * 5,
-        out_specs=(vmem, vmem, smem),
+        out_specs=[vmem] * len(chunks) + [smem],
         scratch_shapes=[
             pltpu.VMEM(routes.shape, routes.dtype),
             pltpu.VMEM(probs.shape, probs.dtype),
             pltpu.SMEM(old_place.shape, jnp.int32),
             pltpu.SMEM(new_place.shape, jnp.int32),
-            pltpu.SemaphoreType.DMA((6,)),
+            pltpu.SemaphoreType.DMA((4 + len(chunks),)),
         ],
         compiler_params=pltpu.CompilerParams(vmem_limit_bytes=VMEM_BYTES - (4 << 20)),
     )(routes, probs, old_place, new_place, tokens)
@@ -246,18 +259,18 @@
     return pl.ds(pl.multiple_of(core * half, LANES), half)
 
 
-def expert_kernel(outlets, width, experts, *refs):
-    chunks = len(outlets)
-    rows, refs = refs[:chunks], refs[chunks:]
+def expert_kernel(count, outlets, width, experts, *refs):
+    rows, refs = refs[:count], refs[count:]
     (up_own, up_pair, down_own, down_pair), refs = refs[:4], refs[4:]
     outs, x_buf = list(refs[:-1]), refs[-1]
     slot, core = lax.axis_index("expert"), lax.axis_index("tensor")
-    size = rows[0].shape[0]
-    lane = lax.broadcasted_iota(jnp.int32, (size, rows[0].shape[1] - width), 1)
-    mine = (lane == slot) | (lane == experts + slot)
-    scales = []
-    for i, row in enumerate(rows):
-        x_buf[i * size : (i + 1) * size, :] = row[:, :width]
+    scales, place = [], 0
+    for row in rows:
+        size = row.shape[0]
+        lane = lax.broadcasted_iota(jnp.int32, (size, row.shape[1] - width), 1)
+        mine = (lane == slot) | (lane == experts + slot)
+        x_buf[place : place + size, :] = row[:, :width]
+        place += size
         side = row[:, width:].astype(jnp.float32)
         scales.append(jnp.sum(jnp.where(mine, side, 0.0), axis=1, keepdims=True))
     scale = jnp.concatenate(scales, axis=0)
@@ -270,39 +283,34 @@
     high = jnp.where(core == 0, parts[1], parts[0])
     hidden = jnp.concatenate([low, high], axis=1)
     half = down_own.shape[1]
-    groups = []
-    for kind, _ in outlets:
-        groups.append([outs.pop(0) for _ in range(2 if kind == "halves" else kind)])
+    groups = [[outs.pop(0) for _ in range(1 if held else 2)] for _, _, held in outlets]
     for j, down in enumerate((down_own, down_pair)):
         y = jnp.dot(hidden, down[...], preferred_element_type=jnp.float32)
         y = y.astype(jnp.bfloat16).astype(jnp.float32) * scale
-        for i, (kind, _) in enumerate(outlets):
-            made = y[i * size : (i + 1) * size]
-            if kind == "halves":
-                groups[i][j][...] = made.astype(groups[i][j].dtype)
-                continue
-            step = size // kind
-            for n, out in enumerate(groups[i]):
-                piece = made[n * step : (n + 1) * step]
-                out[:, half_of(core if j == 0 else 1 - core, half)] = piece.astype(out.dtype)
+        for (start, size, held), group in zip(outlets, groups):
+            made = y[start : start + size]
+            if held:
+                columns = half_of(core if j == 0 else 1 - core, half)
+                group[0][:, columns] = made.astype(held)
+            else:
+                group[j][...] = made.astype(group[j].dtype)
 
 
 def expert_rows(rows, weights, width, experts, outlets):
-    chunks, size = len(rows), rows[0].shape[0]
+    total = sum(row.shape[0] for row in rows)
     up = weights[0]
-    total = chunks * size
     vmem = pl.BlockSpec(memory_space=pltpu.VMEM)
     shapes = []
-    for kind, held in outlets:
-        if kind == "halves":
-            shapes.append([((size, width // 2), t) for t in (jnp.float32, jnp.bfloat16)])
+    for _, size, held in outlets:
+        if held:
+            shapes.append(((size, width), held))
         else:
-            shapes.append([((size // kind, width), held)] * kind)
-    made = pl.pallas_call(
-        functools.partial(expert_kernel, outlets, width, experts),
-        out_shape=[jax.ShapeDtypeStruct(*s) for group in shapes for s in group],
-        in_specs=[vmem] * (chunks + 4),
-        out_specs=[vmem] * sum(len(group) for group in shapes),
+            shapes += [((size, width // 2), t) for t in (jnp.float32, jnp.bfloat16)]
+    return pl.pallas_call(
+        functools.partial(expert_kernel, len(rows), outlets, width, experts),
+        out_shape=[jax.ShapeDtypeStruct(*shape) for shape in shapes],
+        in_specs=[vmem] * (len(rows) + 4),
+        out_specs=[vmem] * len(shapes),
         scratch_shapes=[pltpu.VMEM((total, width), jnp.bfloat16)],
         compiler_params=pltpu.CompilerParams(vmem_limit_bytes=20 << 20),
         cost_estimate=pl.CostEstimate(
@@ -311,8 +319,6 @@
             transcendentals=2 * total * up.shape[1],
         ),
     )(*rows, *weights)
-    made = list(made)
-    return [[made.pop(0) for _ in group] for group in shapes]
 
 
 def split_add_kernel(part, arrived, goes_on, crosses):
@@ -392,19 +398,20 @@
     across = [(b, a ^ 1) for a, b in ahead]
     swap = [(0, 1), (1, 0)]
     f32, bf16 = jnp.float32, jnp.bfloat16
-    pieces = PIECES if token_count % (PIECES * SUBLANES) == 0 else 1
-    each = range(pieces)
+    each = range(PIECES)
+    size = token_count // PIECES
+    own_pieces = (AHEAD_FIRST, AHEAD_SECOND)
 
     caps = (
         capacity_for(block_rows, experts, token_count),
         capacity_for(block_rows, new_place.shape[0], token_count),
     )
-    own_first, own_second, slot_rows = pack(caps, tokens, routes, probs, old_place, new_place)
-    first, second = [own_first], [own_second]
+    *packed, slot_rows = pack(caps, own_pieces, tokens, routes, probs, old_place, new_place)
+    first, second = [packed[:AHEAD_FIRST]], [packed[AHEAD_FIRST:]]
     for step in range(1, steps + 1):
-        first.append(lax.ppermute(first[-1], both, ahead))
+        first.append([lax.ppermute(x, both, ahead) for x in first[-1]])
         if step < steps:
-            second.append(lax.ppermute(second[-1], both, ahead))
+            second.append([lax.ppermute(x, both, ahead) for x in second[-1]])
     up_own, down_own = up_weight[0], down_weight[0]
     up_pair = lax.ppermute(up_own, "tensor", swap)
     down_pair = lax.ppermute(down_own, "tensor", swap)
@@ -414,16 +421,18 @@
     def run(rows, outlets):
         return expert_rows(rows, weights, width, experts, outlets)
 
+    def ranges(chunk, held):
+        return [(chunk * token_count + i * size, size, held) for i in each]
+
     part_first, part_second = [None] * steps, [None] * steps
-    (own, leaving), part_first[1], part_second[1] = run(
-        [first[0], first[1], second[1]], [("halves", None), (pieces, f32), (pieces, f32)]
-    )
+    own, leaving, *made = run(
+        [*first[0], *first[1], *second[1]], [(0, token_count, None), *ranges(1, f32), *ranges(2, f32)]
+    )
+    part_first[1], part_second[1] = made[:PIECES], made[PIECES:]
     for step in range(2, steps):
-        part_first[step], part_second[step] = run(
-            [first[step], second[step]],
-            [(pieces, f32), (pieces, bf16 if step == steps - 1 else f32)],
-        )
-    (sum_first,) = run([first[steps]], [(pieces, bf16)])
+        made = run([*first[step], *second[step]], ranges(0, f32) + ranges(1, bf16 if step == steps - 1 else f32))
+        part_first[step], part_second[step] = made[:PIECES], made[PIECES:]
+    sum_first = run(first[steps], ranges(0, bf16))
     sum_second = part_second[steps - 1]
     own_pair = lax.ppermute(leaving, "tensor", swap)
 
@@ -447,7 +456,7 @@
         stays, crosses = split_add(part_first[1][i], last)
         arrived.append(lax.ppermute(stays, both, back))
         crossed.append(lax.ppermute(crosses, both, across))
-    mixed = finish(pieces, own, own_pair, arrived, second_pair, sum_second, crossed)
+    mixed = finish(PIECES, own, own_pair, arrived, second_pair, sum_second, crossed)
     return (mixed, slot_rows)
 
 
@@ -462,6 +471,8 @@
         and devices % 2 == 0
         and lax.axis_size("tensor") == 2
         and tokens.shape[0] == 2
+        and tokens.shape[1] % (SUBLANES * PIECES) == 0
+        and tokens.shape[1] % (SUBLANES * AHEAD_FIRST) == 0
     ):
         return by_ring(ring, *arrays)
     return by_capacity(*arrays)

time: 61.8 us -> 60.2 us (0.974)
  waiting for transfers between devices: 15.4 us -> 8.87 us
  starting transfers between devices: 34.9 us -> 39.8 us
    ppermute x7 -> x14, waiting for transfers between devices: 10.7 us -> 0.2 us  [the longest x8 0.18 us: by_ring(): first.append([lax.ppermute(x, both, ahead) for x in first[-1]])]
    ppermute x7 -> x14, starting transfers between devices: 13.7 us -> 23.5 us  [the longest x8 13.3 us: by_ring(): first.append([lax.ppermute(x, both, ahead) for x in first[-1]])]
    ppermute x6, waiting for transfers between devices: 0.13 us -> 2.87 us  [by_ring(): sum_second = [lax.ppermute(sum_second[i], both, back) for i in each]]
    ppermute x2, starting transfers between devices: 2.77 us -> 1.38 us  [by_ring(): last = lax.ppermute(sum_first[i], both, back)]
    ppermute x2, starting transfers between devices: 2.54 us -> 1.16 us  [by_ring(): lax.ppermute(other_half(sum_second[i]), 'tensor', swap)]
    ppermute x6, starting transfers between devices: 6.37 us -> 5.03 us  [by_ring(): sum_second = [lax.ppermute(sum_second[i], both, back) for i in each]]
    ppermute x2, starting transfers between devices: 2.7 us -> 1.47 us  [by_ring(): arrived.append(lax.ppermute(stays, both, back))]
    ppermute x1, starting transfers between devices: 0.04 us -> 0.96 us  [by_ring(): own_pair = lax.ppermute(leaving, 'tensor', swap)]
  transfers between devices with their start and end apart: 28 -> 35, of which waited for: 9 -> 10; matrix products, arithmetic and copies ran while one was open for 0% -> 0% of each run, Pallas kernels for 15% -> 16%
where the time goes in v4:
time: 60.2 us; the launch traced here: 60 us
  starting transfers between devices  39.8 us (66%)
  Pallas kernels  10.4 us (17%)
  waiting for transfers between devices  8.87 us (15%)
  between operations  0.81 us (1%)
    ppermute x8, starting transfers between devices, by_ring(): first.append([lax.ppermute(x, both, ahead) for x in first[-1]])  13.3 us
    ppermute x6, starting transfers between devices, by_ring(): second.append([lax.ppermute(x, both, ahead) for x in second[-1]])  10.2 us
    pallas_call x4, Pallas kernels, expert_rows(): pl.pallas_call(functools.partial(expert_kernel, len(rows), outlets, width...  5.63 us
    ppermute x6, starting transfers between devices, by_ring(): sum_second = [lax.ppermute(sum_second[i], both, back) for i in each]  5.03 us
    ppermute x4, starting transfers between devices, by_ring(): sum_first = [lax.ppermute(sum_first[i], both, back) for i in each]  3.65 us
    ppermute x2, waiting for transfers between devices, by_ring(): crossed.append(lax.ppermute(crosses, both, across))  2.92 us
    ppermute x6, waiting for transfers between devices, by_ring(): sum_second = [lax.ppermute(sum_second[i], both, back) for i in each]  2.87 us
    ppermute x4, waiting for transfers between devices, by_ring(): sum_first = [lax.ppermute(sum_first[i], both, back) for i in each]  2.55 us
  transfers between devices with their start and end apart: 35, of which 10 were waited for; matrix products, arithmetic and copies ran while one was open for 0% of the time, Pallas kernels for 16%

profile of v4, /device:TPU:0, one launch (start us, length us, event | category | flops | bytes accessed | tf_op | source)
XLA Modules:
  0.0 60.0 jit_solution(10305107511102033818)
XLA Ops:
  0.6 0.6 collective-permute-start.4
  1.2 0.1 collective-permute-start.5
  1.3 2.0 %shard_map.86 = (bf16[32,2176]{1,0:T(8,128)(2,1)}, bf16[32,2176]{1,0:T(8,128)(2,1)}, bf16[32,2176]{1,0:T(8,128)(2,1)}, bf16[32,2176]{1,0:T(8,128)(2,1)}, s32[2]{0:T(128)}) custom-call(s32[2,8,64]{2,1,0:T(8,128)} %bitcast.8, f32[2,8,64]{2,1,0:T(8,128)} %bitcast.9, s32[8]{0:T(128)} %old_in.1, s32[16]{0:T(128)} %new_in.1, bf16[2,64,2048]{2,1,0:T(8,128)(2,1)} %tokens.1), custom_call_target="tpu_custom_call" | custom-call | tf_op jit(solution)/shard_map/pallas_call | solution.py:213
  3.3 2.6 %collective-permute-start = (bf16[32,2176]{1,0:T(8,128)(2,1)}, bf16[32,2176]{1,0:T(8,128)(2,1)S(1)}, u32[]{:S(2)}, u32[]{:S(2)}) collective-permute-start(bf16[32,2176]{1,0:T(8,128)(2,1)} %get-tuple-element.29.refs_0_), channel_id=1, source_target_pairs={{0,3},{2,1},{3,6},{7,2},{6,11},{10,7},{11,14},{15,10},{14,13},{12,... | collective-permute-start | bytes 417800 | tf_op jit(solution)/shard_map/ppermute | solution.py:412
  5.9 1.6 %collective-permute-start.1 = (bf16[32,2176]{1,0:T(8,128)(2,1)}, bf16[32,2176]{1,0:T(8,128)(2,1)S(1)}, u32[]{:S(2)}, u32[]{:S(2)}) collective-permute-start(bf16[32,2176]{1,0:T(8,128)(2,1)} %get-tuple-element.30.refs_1_), channel_id=1, source_target_pairs={{0,3},{2,1},{3,6},{7,2},{6,11},{10,7},{11,14},{15,10},{14,13},{12,... | collective-permute-start | bytes 417800 | tf_op jit(solution)/shard_map/ppermute | solution.py:412
  7.5 1.3 %collective-permute-start.2 = (bf16[32,2176]{1,0:T(8,128)(2,1)}, bf16[32,2176]{1,0:T(8,128)(2,1)S(1)}, u32[]{:S(2)}, u32[]{:S(2)}) collective-permute-start(bf16[32,2176]{1,0:T(8,128)(2,1)} %get-tuple-element.31), channel_id=1, source_target_pairs={{0,3},{2,1},{3,6},{7,2},{6,11},{10,7},{11,14},{15,10},{14,13},{12,... | collective-permute-start | bytes 417800 | tf_op jit(solution)/shard_map/ppermute | solution.py:414
  8.8 0.2 collective-permute-done.refs_2_
  8.9 1.9 %collective-permute-start.3 = (bf16[32,2176]{1,0:T(8,128)(2,1)}, bf16[32,2176]{1,0:T(8,128)(2,1)S(1)}, u32[]{:S(2)}, u32[]{:S(2)}) collective-permute-start(bf16[32,2176]{1,0:T(8,128)(2,1)} %get-tuple-element.32), channel_id=1, source_target_pairs={{0,3},{2,1},{3,6},{7,2},{6,11},{10,7},{11,14},{15,10},{14,13},{12,... | collective-permute-start | bytes 417800 | tf_op jit(solution)/shard_map/ppermute | solution.py:414
  10.9 1.6 %collective-permute-start.7 = (bf16[32,2176]{1,0:T(8,128)(2,1)S(1)}, bf16[32,2176]{1,0:T(8,128)(2,1)S(1)}, u32[]{:S(2)}, u32[]{:S(2)}) collective-permute-start(bf16[32,2176]{1,0:T(8,128)(2,1)S(1)} %collective-permute-done.refs_2_), channel_id=1, source_target_pairs={{0,3},{2,1},{3,6},{7,2},{6,11},{10,7},{11,14},{15,10},{14,13},{12,... | collective-permute-start | bytes 417800 | tf_op jit(solution)/shard_map/ppermute | solution.py:412
  12.5 1.5 %collective-permute-start.8 = (bf16[32,2176]{1,0:T(8,128)(2,1)S(1)}, bf16[32,2176]{1,0:T(8,128)(2,1)S(1)}, u32[]{:S(2)}, u32[]{:S(2)}) collective-permute-start(bf16[32,2176]{1,0:T(8,128)(2,1)S(1)} %collective-permute-done.1.refs_3_), channel_id=1, source_target_pairs={{0,3},{2,1},{3,6},{7,2},{6,11},{10,7},{11,14},{15,10},{14,13},{12,... | collective-permute-start | bytes 417800 | tf_op jit(solution)/shard_map/ppermute | solution.py:412
  14.0 0.0 collective-permute-done.3.refs_5_
  14.0 1.9 %collective-permute-start.9 = (bf16[32,2176]{1,0:T(8,128)(2,1)S(1)}, bf16[32,2176]{1,0:T(8,128)(2,1)S(1)}, u32[]{:S(2)}, u32[]{:S(2)}) collective-permute-start(bf16[32,2176]{1,0:T(8,128)(2,1)S(1)} %collective-permute-done.2.refs_4_), channel_id=1, source_target_pairs={{0,3},{2,1},{3,6},{7,2},{6,11},{10,7},{11,14},{15,10},{14,13},{12,... | collective-permute-start | bytes 417800 | tf_op jit(solution)/shard_map/ppermute | solution.py:414
  15.9 0.0 collective-permute-done.7.refs_0_
  15.9 1.5 %collective-permute-start.11 = (bf16[32,2176]{1,0:T(8,128)(2,1)S(1)}, bf16[32,2176]{1,0:T(8,128)(2,1)S(1)}, u32[]{:S(2)}, u32[]{:S(2)}) collective-permute-start(bf16[32,2176]{1,0:T(8,128)(2,1)S(1)} %collective-permute-done.7.refs_0_), channel_id=1, source_target_pairs={{0,3},{2,1},{3,6},{7,2},{6,11},{10,7},{11,14},{15,10},{14,13},{12,... | collective-permute-start | bytes 417800 | tf_op jit(solution)/shard_map/ppermute | solution.py:412
  17.4 0.0 collective-permute-done.8.refs_1_
  17.4 1.5 %collective-permute-start.12 = (bf16[32,2176]{1,0:T(8,128)(2,1)S(1)}, bf16[32,2176]{1,0:T(8,128)(2,1)S(1)}, u32[]{:S(2)}, u32[]{:S(2)}) collective-permute-start(bf16[32,2176]{1,0:T(8,128)(2,1)S(1)} %collective-permute-done.8.refs_1_), channel_id=1, source_target_pairs={{0,3},{2,1},{3,6},{7,2},{6,11},{10,7},{11,14},{15,10},{14,13},{12,... | collective-permute-start | bytes 417800 | tf_op jit(solution)/shard_map/ppermute | solution.py:412
  18.9 1.8 %collective-permute-start.10 = (bf16[32,2176]{1,0:T(8,128)(2,1)S(1)}, bf16[32,2176]{1,0:T(8,128)(2,1)S(1)}, u32[]{:S(2)}, u32[]{:S(2)}) collective-permute-start(bf16[32,2176]{1,0:T(8,128)(2,1)S(1)} %collective-permute-done.3.refs_5_), channel_id=1, source_target_pairs={{0,3},{2,1},{3,6},{7,2},{6,11},{10,7},{11,14},{15,10},{14,13},{12,... | collective-permute-start | bytes 417800 | tf_op jit(solution)/shard_map/ppermute | solution.py:414
  20.7 1.5 %collective-permute-start.15 = (bf16[32,2176]{1,0:T(8,128)(2,1)S(1)}, bf16[32,2176]{1,0:T(8,128)(2,1)S(1)}, u32[]{:S(2)}, u32[]{:S(2)}) collective-permute-start(bf16[32,2176]{1,0:T(8,128)(2,1)S(1)} %collective-permute-done.11.refs_0_), channel_id=1, source_target_pairs={{0,3},{2,1},{3,6},{7,2},{6,11},{10,7},{11,14},{15,10},{14,13},{12,... | collective-permute-start | bytes 417800 | tf_op jit(solution)/shard_map/ppermute | solution.py:412
  22.2 0.0 collective-permute-done.12.refs_1_
  22.2 1.5 %collective-permute-start.16 = (bf16[32,2176]{1,0:T(8,128)(2,1)S(1)}, bf16[32,2176]{1,0:T(8,128)(2,1)S(1)}, u32[]{:S(2)}, u32[]{:S(2)}) collective-permute-start(bf16[32,2176]{1,0:T(8,128)(2,1)S(1)} %collective-permute-done.12.refs_1_), channel_id=1, source_target_pairs={{0,3},{2,1},{3,6},{7,2},{6,11},{10,7},{11,14},{15,10},{14,13},{12,... | collective-permute-start | bytes 417800 | tf_op jit(solution)/shard_map/ppermute | solution.py:412
  23.6 0.0 collective-permute-done.10.refs_3_
  23.6 1.8 %collective-permute-start.13 = (bf16[32,2176]{1,0:T(8,128)(2,1)S(1)}, bf16[32,2176]{1,0:T(8,128)(2,1)S(1)}, u32[]{:S(2)}, u32[]{:S(2)}) collective-permute-start(bf16[32,2176]{1,0:T(8,128)(2,1)S(1)} %collective-permute-done.9.refs_2_), channel_id=1, source_target_pairs={{0,3},{2,1},{3,6},{7,2},{6,11},{10,7},{11,14},{15,10},{14,13},{12,... | collective-permute-start | bytes 417800 | tf_op jit(solution)/shard_map/ppermute | solution.py:414
  25.4 1.5 %collective-permute-start.14 = (bf16[32,2176]{1,0:T(8,128)(2,1)S(1)}, bf16[32,2176]{1,0:T(8,128)(2,1)S(1)}, u32[]{:S(2)}, u32[]{:S(2)}) collective-permute-start(bf16[32,2176]{1,0:T(8,128)(2,1)S(1)} %collective-permute-done.10.refs_3_), channel_id=1, source_target_pairs={{0,3},{2,1},{3,6},{7,2},{6,11},{10,7},{11,14},{15,10},{14,13},{12,... | collective-permute-start | bytes 417800 | tf_op jit(solution)/shard_map/ppermute | solution.py:414
  26.9 1.9 %shard_map.87 = (bf16[2048,384]{1,0:T(8,128)(2,1)S(1)}, bf16[768,1024]{1,0:T(8,128)(2,1)S(1)}) custom-call(bf16[2048,384]{1,0:T(8,128)(2,1)} %bitcast.5, bf16[768,1024]{1,0:T(8,128)(2,1)} %bitcast.7), custom_call_target="tpu_custom_call" | custom-call | bytes 6291456 | tf_op jit(solution)/shard_map/pallas_call | solution.py:242
  28.8 0.0 collective-permute-done.4.refs_7_.refs_5_.refs_3_
  28.9 0.0 collective-permute-done.5.refs_9_.refs_7_.refs_5_
  28.9 1.3 %shard_map.91 = (bf16[32,2048]{1,0:T(8,128)(2,1)S(1)}, bf16[32,2048]{1,0:T(8,128)(2,1)S(1)}) custom-call(bf16[32,2176]{1,0:T(8,128)(2,1)S(1)} %collective-permute-done.15.refs_0_, bf16[32,2176]{1,0:T(8,128)(2,1)S(1)} %collective-permute-done.16.refs_1_, bf16[2048,384]{1,0:T(8,128)(2,1)S(1)} %get-tuple-element.33.refs_6_.refs_4_.refs_2_, ...), custom_call_target="tpu_custom_call" | custom-call | flops 402653184 | bytes 1048576 | tf_op jit(solution)/shard_map/pallas_call | solution.py:309
  30.2 0.3 collective-permute-start.17
  30.5 1.6 %collective-permute-start.21 = (bf16[32,2048]{1,0:T(8,128)(2,1)S(1)}, bf16[32,2048]{1,0:T(8,128)(2,1)S(1)}, u32[]{:S(2)}, u32[]{:S(2)}) collective-permute-start(bf16[32,2048]{1,0:T(8,128)(2,1)S(1)} %get-tuple-element.45), channel_id=1, source_target_pairs={{3,0},{1,2},{6,3},{2,7},{11,6},{7,10},{14,11},{10,15},{13,14},{15,... | collective-permute-start | bytes 393224 | tf_op jit(solution)/shard_map/ppermute | solution.py:448
  32.0 0.0 collective-permute-done.13.refs_2_
  32.0 0.0 collective-permute-done.14.refs_3_
  32.0 1.3 %shard_map.90 = (f32[32,2048]{1,0:T(8,128)S(1)}, f32[32,2048]{1,0:T(8,128)S(1)}, bf16[32,2048]{1,0:T(8,128)(2,1)S(1)}, bf16[32,2048]{1,0:T(8,128)(2,1)S(1)}) custom-call(bf16[32,2176]{1,0:T(8,128)(2,1)S(1)} %collective-permute-done.11.refs_0_, bf16[32,2176]{1,0:T(8,128)(2,1)S(1)} %collective-permute-done.12.refs_1_, ...), custom_call_target="tpu_custom_call" | custom-call | flops 805306368 | bytes 2097152 | tf_op jit(solution)/shard_map/pallas_call | solution.py:309
  33.3 1.2 %collective-permute-start.25 = (bf16[32,2048]{1,0:T(8,128)(2,1)S(1)}, bf16[32,2048]{1,0:T(8,128)(2,1)S(1)}, u32[]{:S(2)}, u32[]{:S(2)}) collective-permute-start(bf16[32,2048]{1,0:T(8,128)(2,1)S(1)} %get-tuple-element.49), channel_id=1, source_target_pairs={{3,0},{1,2},{6,3},{2,7},{11,6},{7,10},{14,11},{10,15},{13,14},{15,... | collective-permute-start | bytes 393224 | tf_op jit(solution)/shard_map/ppermute | solution.py:440
  34.5 1.7 %collective-permute-start.29 = (bf16[32,2048]{1,0:T(8,128)(2,1)S(1)}, bf16[32,2048]{1,0:T(8,128)(2,1)S(1)}, u32[]{:S(2)}, u32[]{:S(2)}) collective-permute-start(bf16[32,2048]{1,0:T(8,128)(2,1)S(1)} %get-tuple-element.52), channel_id=1, source_target_pairs={{3,0},{1,2},{6,3},{2,7},{11,6},{7,10},{14,11},{10,15},{13,14},{15,... | collective-permute-start | bytes 393224 | tf_op jit(solution)/shard_map/ppermute | solution.py:440
  36.3 1.3 %shard_map.89 = (f32[32,2048]{1,0:T(8,128)S(1)}, f32[32,2048]{1,0:T(8,128)S(1)}, f32[32,2048]{1,0:T(8,128)S(1)}, f32[32,2048]{1,0:T(8,128)S(1)}) custom-call(bf16[32,2176]{1,0:T(8,128)(2,1)S(1)} %collective-permute-done.7.refs_0_, bf16[32,2176]{1,0:T(8,128)(2,1)S(1)} %collective-permute-done.8.refs_1_, bf16[32,2176]{1,0:T(8,128)(2,1)S(1)} %collective-permute-done.9.refs_2_, ...), custom_call_target="tpu_custom_call" | custom-call | flops 805306368 | bytes 2097152 | tf_op jit(solution)/shard_map/pallas_call | solution.py:309
  37.6 1.8 %shard_map.88 = (f32[64,1024]{1,0:T(8,128)S(1)}, bf16[64,1024]{1,0:T(8,128)(2,1)S(1)}, f32[32,2048]{1,0:T(8,128)S(1)}, f32[32,2048]{1,0:T(8,128)S(1)}, f32[32,2048]{1,0:T(8,128)S(1)}, /*index=5*/f32[32,2048]{1,0:T(8,128)S(1)}) custom-call(bf16[32,2176]{1,0:T(8,128)(2,1)S(1)} %copy-done, bf16[32,2176]{1,0:T(8,128)(2,1)S(1)} %copy-done.1, ...), custom_call_target="tpu_custom_call" | custom-call | flops 1207959552 | bytes 3145728 | tf_op jit(solution)/shard_map/pallas_call | solution.py:309
  39.4 0.0 collective-permute-done.17
  39.4 0.4 collective-permute-start.18
  39.8 0.0 collective-permute-done.21
  39.9 1.4 %collective-permute-start.22 = (bf16[32,2048]{1,0:T(8,128)(2,1)S(1)}, bf16[32,2048]{1,0:T(8,128)(2,1)S(1)}, u32[]{:S(2)}, u32[]{:S(2)}) collective-permute-start(bf16[32,2048]{1,0:T(8,128)(2,1)S(1)} %add_convert_fusion.5), channel_id=1, source_target_pairs={{3,0},{1,2},{6,3},{2,7},{11,6},{7,10},{14,11},{10,15},{13,14},{15,... | collective-permute-start | bytes 393224 | tf_op jit(solution)/shard_map/ppermute | solution.py:448
  41.2 0.0 collective-permute-done.25
  41.3 0.3 collective-permute-start.26
  41.6 0.4 collective-permute-start.30
  42.0 1.9 %collective-permute-done.18 = bf16[32,2048]{1,0:T(8,128)(2,1)S(1)} collective-permute-done((bf16[32,2048]{1,0:T(8,128)(2,1)S(1)}, bf16[32,2048]{1,0:T(8,128)(2,1)S(1)}, u32[]{:S(2)}, u32[]{:S(2)}) %collective-permute-start.18) | collective-permute-done | bytes 131104 | tf_op jit(solution)/shard_map/ppermute | solution.py:448
  43.9 0.7 %collective-permute-start.19 = (bf16[32,2048]{1,0:T(8,128)(2,1)S(1)}, bf16[32,2048]{1,0:T(8,128)(2,1)S(1)}, u32[]{:S(2)}, u32[]{:S(2)}) collective-permute-start(bf16[32,2048]{1,0:T(8,128)(2,1)S(1)} %add_convert_fusion.6), channel_id=1, source_target_pairs={{3,0},{1,2},{6,3},{2,7},{11,6},{7,10},{14,11},{10,15},{13,14},{15,... | collective-permute-start | bytes 393224 | tf_op jit(solution)/shard_map/ppermute | solution.py:455
  44.6 0.7 %collective-permute-done.22 = bf16[32,2048]{1,0:T(8,128)(2,1)S(1)} collective-permute-done((bf16[32,2048]{1,0:T(8,128)(2,1)S(1)}, bf16[32,2048]{1,0:T(8,128)(2,1)S(1)}, u32[]{:S(2)}, u32[]{:S(2)}) %collective-permute-start.22) | collective-permute-done | bytes 131104 | tf_op jit(solution)/shard_map/ppermute | solution.py:448
  45.3 0.7 %collective-permute-start.23 = (bf16[32,2048]{1,0:T(8,128)(2,1)S(1)}, bf16[32,2048]{1,0:T(8,128)(2,1)S(1)}, u32[]{:S(2)}, u32[]{:S(2)}) collective-permute-start(bf16[32,2048]{1,0:T(8,128)(2,1)S(1)} %add_convert_fusion.4), channel_id=1, source_target_pairs={{3,0},{1,2},{6,3},{2,7},{11,6},{7,10},{14,11},{10,15},{13,14},{15,... | collective-permute-start | bytes 393224 | tf_op jit(solution)/shard_map/ppermute | solution.py:455
  46.0 0.7 %collective-permute-done.26 = bf16[32,2048]{1,0:T(8,128)(2,1)S(1)} collective-permute-done((bf16[32,2048]{1,0:T(8,128)(2,1)S(1)}, bf16[32,2048]{1,0:T(8,128)(2,1)S(1)}, u32[]{:S(2)}, u32[]{:S(2)}) %collective-permute-start.26) | collective-permute-done | bytes 131104 | tf_op jit(solution)/shard_map/ppermute | solution.py:440
  46.7 0.7 %collective-permute-start.27 = (bf16[32,2048]{1,0:T(8,128)(2,1)S(1)}, bf16[32,2048]{1,0:T(8,128)(2,1)S(1)}, u32[]{:S(2)}, u32[]{:S(2)}) collective-permute-start(bf16[32,2048]{1,0:T(8,128)(2,1)S(1)} %add_convert_fusion.2), channel_id=1, source_target_pairs={{3,0},{1,2},{6,3},{2,7},{11,6},{7,10},{14,11},{10,15},{13,14},{15,... | collective-permute-start | bytes 393224 | tf_op jit(solution)/shard_map/ppermute | solution.py:440
  47.4 0.7 %collective-permute-done.30 = bf16[32,2048]{1,0:T(8,128)(2,1)S(1)} collective-permute-done((bf16[32,2048]{1,0:T(8,128)(2,1)S(1)}, bf16[32,2048]{1,0:T(8,128)(2,1)S(1)}, u32[]{:S(2)}, u32[]{:S(2)}) %collective-permute-start.30) | collective-permute-done | bytes 131104 | tf_op jit(solution)/shard_map/ppermute | solution.py:440
  48.1 0.7 %collective-permute-start.31 = (bf16[32,2048]{1,0:T(8,128)(2,1)S(1)}, bf16[32,2048]{1,0:T(8,128)(2,1)S(1)}, u32[]{:S(2)}, u32[]{:S(2)}) collective-permute-start(bf16[32,2048]{1,0:T(8,128)(2,1)S(1)} %add_convert_fusion), channel_id=1, source_target_pairs={{3,0},{1,2},{6,3},{2,7},{11,6},{7,10},{14,11},{10,15},{13,14},{15,... | collective-permute-start | bytes 393224 | tf_op jit(solution)/shard_map/ppermute | solution.py:440
  48.8 1.0 %collective-permute-start.6 = (bf16[64,1024]{1,0:T(8,128)(2,1)S(1)}, bf16[64,1024]{1,0:T(8,128)(2,1)S(1)}, u32[]{:S(2)}, u32[]{:S(2)}) collective-permute-start(bf16[64,1024]{1,0:T(8,128)(2,1)S(1)} %get-tuple-element.36), channel_id=1, source_target_pairs={{0,1},{1,0},{2,3},{3,2},{4,5},{5,4},{6,7},{7,6},{8,9},{9,8},{10,11... | collective-permute-start | bytes 393224 | tf_op jit(solution)/shard_map/ppermute | solution.py:437
  49.8 0.8 %collective-permute-start.20 = (bf16[32,1024]{1,0:T(8,128)(2,1)S(1)}, bf16[32,1024]{1,0:T(8,128)(2,1)S(1)}, u32[]{:S(2)}, u32[]{:S(2)}) collective-permute-start(bf16[32,1024]{1,0:T(8,128)(2,1)S(1)} %get-tuple-element.41), channel_id=1, source_target_pairs={{3,0},{1,2},{6,3},{2,7},{11,6},{7,10},{14,11},{10,15},{13,14},{15,... | collective-permute-start | bytes 196616 | tf_op jit(solution)/shard_map/ppermute | solution.py:457
  50.6 0.3 collective-permute-done.23.arrived
  50.9 0.7 %collective-permute-start.24 = (bf16[32,1024]{1,0:T(8,128)(2,1)S(1)}, bf16[32,1024]{1,0:T(8,128)(2,1)S(1)}, u32[]{:S(2)}, u32[]{:S(2)}) collective-permute-start(bf16[32,1024]{1,0:T(8,128)(2,1)S(1)} %get-tuple-element.46), channel_id=1, source_target_pairs={{3,0},{1,2},{6,3},{2,7},{11,6},{7,10},{14,11},{10,15},{13,14},{15,... | collective-permute-start | bytes 196616 | tf_op jit(solution)/shard_map/ppermute | solution.py:457
  51.6 0.7 %collective-permute-done.27.x.refs_4_ = bf16[32,2048]{1,0:T(8,128)(2,1)S(1)} collective-permute-done((bf16[32,2048]{1,0:T(8,128)(2,1)S(1)}, bf16[32,2048]{1,0:T(8,128)(2,1)S(1)}, u32[]{:S(2)}, u32[]{:S(2)}) %collective-permute-start.27) | collective-permute-done | bytes 131104 | tf_op jit(solution)/shard_map/ppermute | solution.py:440
  52.3 0.6 collective-permute-start.28
  52.9 0.8 %collective-permute-done.31.x.refs_5_ = bf16[32,2048]{1,0:T(8,128)(2,1)S(1)} collective-permute-done((bf16[32,2048]{1,0:T(8,128)(2,1)S(1)}, bf16[32,2048]{1,0:T(8,128)(2,1)S(1)}, u32[]{:S(2)}, u32[]{:S(2)}) %collective-permute-start.31) | collective-permute-done | bytes 131104 | tf_op jit(solution)/shard_map/ppermute | solution.py:440
  53.7 0.6 collective-permute-start.32
  54.3 0.5 collective-permute-start.33
  54.7 1.6 %collective-permute-start.34 = (bf16[32,1024]{1,0:T(8,128)(2,1)S(1)}, bf16[32,1024]{1,0:T(8,128)(2,1)S(1)}, u32[]{:S(2)}, u32[]{:S(2)}) collective-permute-start(bf16[32,1024]{1,0:T(8,128)(2,1)S(1)} %get-tuple-element.54), channel_id=1, source_target_pairs={{3,1},{1,3},{6,2},{2,6},{11,7},{7,11},{14,10},{10,14},{13,15},{15,... | collective-permute-start | bytes 196616 | tf_op jit(solution)/shard_map/ppermute | solution.py:458
  56.3 2.2 %collective-permute-done.33.refs_6_ = bf16[32,1024]{1,0:T(8,128)(2,1)S(1)} collective-permute-done((bf16[32,1024]{1,0:T(8,128)(2,1)S(1)}, bf16[32,1024]{1,0:T(8,128)(2,1)S(1)}, u32[]{:S(2)}, u32[]{:S(2)}) %collective-permute-start.33) | collective-permute-done | bytes 65568 | tf_op jit(solution)/shard_map/ppermute | solution.py:458
  58.6 0.7 %collective-permute-done.34.refs_7_ = bf16[32,1024]{1,0:T(8,128)(2,1)S(1)} collective-permute-done((bf16[32,1024]{1,0:T(8,128)(2,1)S(1)}, bf16[32,1024]{1,0:T(8,128)(2,1)S(1)}, u32[]{:S(2)}, u32[]{:S(2)}) %collective-permute-start.34) | collective-permute-done | bytes 65568 | tf_op jit(solution)/shard_map/ppermute | solution.py:458
  59.3 0.8 %shard_map.96 = bf16[2,64,1024]{2,1,0:T(8,128)(2,1)} custom-call(f32[64,1024]{1,0:T(8,128)S(1)} %get-tuple-element.35.own, bf16[64,1024]{1,0:T(8,128)(2,1)S(1)} %collective-permute-done.6.own_pair, bf16[32,1024]{1,0:T(8,128)(2,1)S(1)} %collective-permute-done.20.refs_0_, bf16[32,1024]{1,0:T(8,128)(2,1)S(1)} %collective-permute-done.24.refs_1_, ...), custom_call_target="tpu_custom_call" | custom-call | tf_op jit(solution)/shard_map/pallas_call | solution.py:375
  (29 shorter events, 0.3 us)
Async XLA Ops:
  0.6 28.2 %collective-permute-start.4 = (bf16[2048,384]{1,0:T(8,128)(2,1)}, bf16[2048,384]{1,0:T(8,128)(2,1)S(1)}, u32[]{:S(2)}, u32[]{:S(2)}) collective-permute-start(bf16[2048,384]{1,0:T(8,128)(2,1)} %bitcast.4), channel_id=1, source_target_pairs={{0,1},{1,0},{2,3},{3,2},{4,5},{5,4},{6,7},{7,6},{8,9},{9,8},{10,11... | collective-permute-start | bytes 4718600 | tf_op jit(solution)/shard_map/ppermute | solution.py:416
  1.2 27.7 %collective-permute-start.5 = (bf16[768,1024]{1,0:T(8,128)(2,1)}, bf16[768,1024]{1,0:T(8,128)(2,1)S(1)}, u32[]{:S(2)}, u32[]{:S(2)}) collective-permute-start(bf16[768,1024]{1,0:T(8,128)(2,1)} %bitcast.6), channel_id=1, source_target_pairs={{0,1},{1,0},{2,3},{3,2},{4,5},{5,4},{6,7},{7,6},{8,9},{9,8},{10,11... | collective-permute-start | bytes 4718600 | tf_op jit(solution)/shard_map/ppermute | solution.py:417
  3.3 5.7 %collective-permute-start = (bf16[32,2176]{1,0:T(8,128)(2,1)}, bf16[32,2176]{1,0:T(8,128)(2,1)S(1)}, u32[]{:S(2)}, u32[]{:S(2)}) collective-permute-start(bf16[32,2176]{1,0:T(8,128)(2,1)} %get-tuple-element.29.refs_0_), channel_id=1, source_target_pairs={{0,3},{2,1},{3,6},{7,2},{6,11},{10,7},{11,14},{15,10},{14,13},{12,... | collective-permute-start | bytes 417800 | tf_op jit(solution)/shard_map/ppermute | solution.py:412
  5.9 5.0 %collective-permute-start.1 = (bf16[32,2176]{1,0:T(8,128)(2,1)}, bf16[32,2176]{1,0:T(8,128)(2,1)S(1)}, u32[]{:S(2)}, u32[]{:S(2)}) collective-permute-start(bf16[32,2176]{1,0:T(8,128)(2,1)} %get-tuple-element.30.refs_1_), channel_id=1, source_target_pairs={{0,3},{2,1},{3,6},{7,2},{6,11},{10,7},{11,14},{15,10},{14,13},{12,... | collective-permute-start | bytes 417800 | tf_op jit(solution)/shard_map/ppermute | solution.py:412
  7.5 5.0 %collective-permute-start.2 = (bf16[32,2176]{1,0:T(8,128)(2,1)}, bf16[32,2176]{1,0:T(8,128)(2,1)S(1)}, u32[]{:S(2)}, u32[]{:S(2)}) collective-permute-start(bf16[32,2176]{1,0:T(8,128)(2,1)} %get-tuple-element.31), channel_id=1, source_target_pairs={{0,3},{2,1},{3,6},{7,2},{6,11},{10,7},{11,14},{15,10},{14,13},{12,... | collective-permute-start | bytes 417800 | tf_op jit(solution)/shard_map/ppermute | solution.py:414
  8.9 5.1 %collective-permute-start.3 = (bf16[32,2176]{1,0:T(8,128)(2,1)}, bf16[32,2176]{1,0:T(8,128)(2,1)S(1)}, u32[]{:S(2)}, u32[]{:S(2)}) collective-permute-start(bf16[32,2176]{1,0:T(8,128)(2,1)} %get-tuple-element.32), channel_id=1, source_target_pairs={{0,3},{2,1},{3,6},{7,2},{6,11},{10,7},{11,14},{15,10},{14,13},{12,... | collective-permute-start | bytes 417800 | tf_op jit(solution)/shard_map/ppermute | solution.py:414
  10.9 5.0 %collective-permute-start.7 = (bf16[32,2176]{1,0:T(8,128)(2,1)S(1)}, bf16[32,2176]{1,0:T(8,128)(2,1)S(1)}, u32[]{:S(2)}, u32[]{:S(2)}) collective-permute-start(bf16[32,2176]{1,0:T(8,128)(2,1)S(1)} %collective-permute-done.refs_2_), channel_id=1, source_target_pairs={{0,3},{2,1},{3,6},{7,2},{6,11},{10,7},{11,14},{15,10},{14,13},{12,... | collective-permute-start | bytes 417800 | tf_op jit(solution)/shard_map/ppermute | solution.py:412
  12.5 4.9 %collective-permute-start.8 = (bf16[32,2176]{1,0:T(8,128)(2,1)S(1)}, bf16[32,2176]{1,0:T(8,128)(2,1)S(1)}, u32[]{:S(2)}, u32[]{:S(2)}) collective-permute-start(bf16[32,2176]{1,0:T(8,128)(2,1)S(1)} %collective-permute-done.1.refs_3_), channel_id=1, source_target_pairs={{0,3},{2,1},{3,6},{7,2},{6,11},{10,7},{11,14},{15,10},{14,13},{12,... | collective-permute-start | bytes 417800 | tf_op jit(solution)/shard_map/ppermute | solution.py:412
  14.0 4.9 %collective-permute-start.9 = (bf16[32,2176]{1,0:T(8,128)(2,1)S(1)}, bf16[32,2176]{1,0:T(8,128)(2,1)S(1)}, u32[]{:S(2)}, u32[]{:S(2)}) collective-permute-start(bf16[32,2176]{1,0:T(8,128)(2,1)S(1)} %collective-permute-done.2.refs_4_), channel_id=1, source_target_pairs={{0,3},{2,1},{3,6},{7,2},{6,11},{10,7},{11,14},{15,10},{14,13},{12,... | collective-permute-start | bytes 417800 | tf_op jit(solution)/shard_map/ppermute | solution.py:414
  15.9 4.8 %collective-permute-start.11 = (bf16[32,2176]{1,0:T(8,128)(2,1)S(1)}, bf16[32,2176]{1,0:T(8,128)(2,1)S(1)}, u32[]{:S(2)}, u32[]{:S(2)}) collective-permute-start(bf16[32,2176]{1,0:T(8,128)(2,1)S(1)} %collective-permute-done.7.refs_0_), channel_id=1, source_target_pairs={{0,3},{2,1},{3,6},{7,2},{6,11},{10,7},{11,14},{15,10},{14,13},{12,... | collective-permute-start | bytes 417800 | tf_op jit(solution)/shard_map/ppermute | solution.py:412
  17.4 4.8 %collective-permute-start.12 = (bf16[32,2176]{1,0:T(8,128)(2,1)S(1)}, bf16[32,2176]{1,0:T(8,128)(2,1)S(1)}, u32[]{:S(2)}, u32[]{:S(2)}) collective-permute-start(bf16[32,2176]{1,0:T(8,128)(2,1)S(1)} %collective-permute-done.8.refs_1_), channel_id=1, source_target_pairs={{0,3},{2,1},{3,6},{7,2},{6,11},{10,7},{11,14},{15,10},{14,13},{12,... | collective-permute-start | bytes 417800 | tf_op jit(solution)/shard_map/ppermute | solution.py:412
  18.9 4.8 %collective-permute-start.10 = (bf16[32,2176]{1,0:T(8,128)(2,1)S(1)}, bf16[32,2176]{1,0:T(8,128)(2,1)S(1)}, u32[]{:S(2)}, u32[]{:S(2)}) collective-permute-start(bf16[32,2176]{1,0:T(8,128)(2,1)S(1)} %collective-permute-done.3.refs_5_), channel_id=1, source_target_pairs={{0,3},{2,1},{3,6},{7,2},{6,11},{10,7},{11,14},{15,10},{14,13},{12,... | collective-permute-start | bytes 417800 | tf_op jit(solution)/shard_map/ppermute | solution.py:414
  20.7 4.8 %collective-permute-start.15 = (bf16[32,2176]{1,0:T(8,128)(2,1)S(1)}, bf16[32,2176]{1,0:T(8,128)(2,1)S(1)}, u32[]{:S(2)}, u32[]{:S(2)}) collective-permute-start(bf16[32,2176]{1,0:T(8,128)(2,1)S(1)} %collective-permute-done.11.refs_0_), channel_id=1, source_target_pairs={{0,3},{2,1},{3,6},{7,2},{6,11},{10,7},{11,14},{15,10},{14,13},{12,... | collective-permute-start | bytes 417800 | tf_op jit(solution)/shard_map/ppermute | solution.py:412
  22.2 6.7 %collective-permute-start.16 = (bf16[32,2176]{1,0:T(8,128)(2,1)S(1)}, bf16[32,2176]{1,0:T(8,128)(2,1)S(1)}, u32[]{:S(2)}, u32[]{:S(2)}) collective-permute-start(bf16[32,2176]{1,0:T(8,128)(2,1)S(1)} %collective-permute-done.12.refs_1_), channel_id=1, source_target_pairs={{0,3},{2,1},{3,6},{7,2},{6,11},{10,7},{11,14},{15,10},{14,13},{12,... | collective-permute-start | bytes 417800 | tf_op jit(solution)/shard_map/ppermute | solution.py:412
  23.6 8.4 %collective-permute-start.13 = (bf16[32,2176]{1,0:T(8,128)(2,1)S(1)}, bf16[32,2176]{1,0:T(8,128)(2,1)S(1)}, u32[]{:S(2)}, u32[]{:S(2)}) collective-permute-start(bf16[32,2176]{1,0:T(8,128)(2,1)S(1)} %collective-permute-done.9.refs_2_), channel_id=1, source_target_pairs={{0,3},{2,1},{3,6},{7,2},{6,11},{10,7},{11,14},{15,10},{14,13},{12,... | collective-permute-start | bytes 417800 | tf_op jit(solution)/shard_map/ppermute | solution.py:414
  25.4 6.6 %collective-permute-start.14 = (bf16[32,2176]{1,0:T(8,128)(2,1)S(1)}, bf16[32,2176]{1,0:T(8,128)(2,1)S(1)}, u32[]{:S(2)}, u32[]{:S(2)}) collective-permute-start(bf16[32,2176]{1,0:T(8,128)(2,1)S(1)} %collective-permute-done.10.refs_3_), channel_id=1, source_target_pairs={{0,3},{2,1},{3,6},{7,2},{6,11},{10,7},{11,14},{15,10},{14,13},{12,... | collective-permute-start | bytes 417800 | tf_op jit(solution)/shard_map/ppermute | solution.py:414
  30.2 9.2 %collective-permute-start.17 = (bf16[32,2048]{1,0:T(8,128)(2,1)S(1)}, bf16[32,2048]{1,0:T(8,128)(2,1)S(1)}, u32[]{:S(2)}, u32[]{:S(2)}) collective-permute-start(bf16[32,2048]{1,0:T(8,128)(2,1)S(1)} %get-tuple-element.40), channel_id=1, source_target_pairs={{3,0},{1,2},{6,3},{2,7},{11,6},{7,10},{14,11},{10,15},{13,14},{15,... | collective-permute-start | bytes 393224 | tf_op jit(solution)/shard_map/ppermute | solution.py:448
  30.5 9.4 %collective-permute-start.21 = (bf16[32,2048]{1,0:T(8,128)(2,1)S(1)}, bf16[32,2048]{1,0:T(8,128)(2,1)S(1)}, u32[]{:S(2)}, u32[]{:S(2)}) collective-permute-start(bf16[32,2048]{1,0:T(8,128)(2,1)S(1)} %get-tuple-element.45), channel_id=1, source_target_pairs={{3,0},{1,2},{6,3},{2,7},{11,6},{7,10},{14,11},{10,15},{13,14},{15,... | collective-permute-start | bytes 393224 | tf_op jit(solution)/shard_map/ppermute | solution.py:448
  33.3 7.9 %collective-permute-start.25 = (bf16[32,2048]{1,0:T(8,128)(2,1)S(1)}, bf16[32,2048]{1,0:T(8,128)(2,1)S(1)}, u32[]{:S(2)}, u32[]{:S(2)}) collective-permute-start(bf16[32,2048]{1,0:T(8,128)(2,1)S(1)} %get-tuple-element.49), channel_id=1, source_target_pairs={{3,0},{1,2},{6,3},{2,7},{11,6},{7,10},{14,11},{10,15},{13,14},{15,... | collective-permute-start | bytes 393224 | tf_op jit(solution)/shard_map/ppermute | solution.py:440
  34.5 3.0 %copy-start = (bf16[32,2176]{1,0:T(8,128)(2,1)S(1)}, bf16[32,2176]{1,0:T(8,128)(2,1)}, u32[]{:S(2)}) copy-start(bf16[32,2176]{1,0:T(8,128)(2,1)} %get-tuple-element.29.refs_0_) | copy-start | bytes 417796
  34.5 3.0 %copy-start.1 = (bf16[32,2176]{1,0:T(8,128)(2,1)S(1)}, bf16[32,2176]{1,0:T(8,128)(2,1)}, u32[]{:S(2)}) copy-start(bf16[32,2176]{1,0:T(8,128)(2,1)} %get-tuple-element.30.refs_1_) | copy-start | bytes 417796
  34.5 7.0 %collective-permute-start.29 = (bf16[32,2048]{1,0:T(8,128)(2,1)S(1)}, bf16[32,2048]{1,0:T(8,128)(2,1)S(1)}, u32[]{:S(2)}, u32[]{:S(2)}) collective-permute-start(bf16[32,2048]{1,0:T(8,128)(2,1)S(1)} %get-tuple-element.52), channel_id=1, source_target_pairs={{3,0},{1,2},{6,3},{2,7},{11,6},{7,10},{14,11},{10,15},{13,14},{15,... | collective-permute-start | bytes 393224 | tf_op jit(solution)/shard_map/ppermute | solution.py:440
  39.4 4.4 %collective-permute-start.18 = (bf16[32,2048]{1,0:T(8,128)(2,1)S(1)}, bf16[32,2048]{1,0:T(8,128)(2,1)S(1)}, u32[]{:S(2)}, u32[]{:S(2)}) collective-permute-start(bf16[32,2048]{1,0:T(8,128)(2,1)S(1)} %add_convert_fusion.7), channel_id=1, source_target_pairs={{3,0},{1,2},{6,3},{2,7},{11,6},{7,10},{14,11},{10,15},{13,14},{15,... | collective-permute-start | bytes 393224 | tf_op jit(solution)/shard_map/ppermute | solution.py:448
  39.9 5.4 %collective-permute-start.22 = (bf16[32,2048]{1,0:T(8,128)(2,1)S(1)}, bf16[32,2048]{1,0:T(8,128)(2,1)S(1)}, u32[]{:S(2)}, u32[]{:S(2)}) collective-permute-start(bf16[32,2048]{1,0:T(8,128)(2,1)S(1)} %add_convert_fusion.5), channel_id=1, source_target_pairs={{3,0},{1,2},{6,3},{2,7},{11,6},{7,10},{14,11},{10,15},{13,14},{15,... | collective-permute-start | bytes 393224 | tf_op jit(solution)/shard_map/ppermute | solution.py:448
  41.3 5.4 %collective-permute-start.26 = (bf16[32,2048]{1,0:T(8,128)(2,1)S(1)}, bf16[32,2048]{1,0:T(8,128)(2,1)S(1)}, u32[]{:S(2)}, u32[]{:S(2)}) collective-permute-start(bf16[32,2048]{1,0:T(8,128)(2,1)S(1)} %add_convert_fusion.3), channel_id=1, source_target_pairs={{3,0},{1,2},{6,3},{2,7},{11,6},{7,10},{14,11},{10,15},{13,14},{15,... | collective-permute-start | bytes 393224 | tf_op jit(solution)/shard_map/ppermute | solution.py:440
  41.6 6.5 %collective-permute-start.30 = (bf16[32,2048]{1,0:T(8,128)(2,1)S(1)}, bf16[32,2048]{1,0:T(8,128)(2,1)S(1)}, u32[]{:S(2)}, u32[]{:S(2)}) collective-permute-start(bf16[32,2048]{1,0:T(8,128)(2,1)S(1)} %add_convert_fusion.1), channel_id=1, source_target_pairs={{3,0},{1,2},{6,3},{2,7},{11,6},{7,10},{14,11},{10,15},{13,14},{15,... | collective-permute-start | bytes 393224 | tf_op jit(solution)/shard_map/ppermute | solution.py:440
  43.9 5.9 %collective-permute-start.19 = (bf16[32,2048]{1,0:T(8,128)(2,1)S(1)}, bf16[32,2048]{1,0:T(8,128)(2,1)S(1)}, u32[]{:S(2)}, u32[]{:S(2)}) collective-permute-start(bf16[32,2048]{1,0:T(8,128)(2,1)S(1)} %add_convert_fusion.6), channel_id=1, source_target_pairs={{3,0},{1,2},{6,3},{2,7},{11,6},{7,10},{14,11},{10,15},{13,14},{15,... | collective-permute-start | bytes 393224 | tf_op jit(solution)/shard_map/ppermute | solution.py:455
  45.3 5.6 %collective-permute-start.23 = (bf16[32,2048]{1,0:T(8,128)(2,1)S(1)}, bf16[32,2048]{1,0:T(8,128)(2,1)S(1)}, u32[]{:S(2)}, u32[]{:S(2)}) collective-permute-start(bf16[32,2048]{1,0:T(8,128)(2,1)S(1)} %add_convert_fusion.4), channel_id=1, source_target_pairs={{3,0},{1,2},{6,3},{2,7},{11,6},{7,10},{14,11},{10,15},{13,14},{15,... | collective-permute-start | bytes 393224 | tf_op jit(solution)/shard_map/ppermute | solution.py:455
  46.7 5.6 %collective-permute-start.27 = (bf16[32,2048]{1,0:T(8,128)(2,1)S(1)}, bf16[32,2048]{1,0:T(8,128)(2,1)S(1)}, u32[]{:S(2)}, u32[]{:S(2)}) collective-permute-start(bf16[32,2048]{1,0:T(8,128)(2,1)S(1)} %add_convert_fusion.2), channel_id=1, source_target_pairs={{3,0},{1,2},{6,3},{2,7},{11,6},{7,10},{14,11},{10,15},{13,14},{15,... | collective-permute-start | bytes 393224 | tf_op jit(solution)/shard_map/ppermute | solution.py:440
  48.1 5.6 %collective-permute-start.31 = (bf16[32,2048]{1,0:T(8,128)(2,1)S(1)}, bf16[32,2048]{1,0:T(8,128)(2,1)S(1)}, u32[]{:S(2)}, u32[]{:S(2)}) collective-permute-start(bf16[32,2048]{1,0:T(8,128)(2,1)S(1)} %add_convert_fusion), channel_id=1, source_target_pairs={{3,0},{1,2},{6,3},{2,7},{11,6},{7,10},{14,11},{10,15},{13,14},{15,... | collective-permute-start | bytes 393224 | tf_op jit(solution)/shard_map/ppermute | solution.py:440
  48.8 5.5 %collective-permute-start.6 = (bf16[64,1024]{1,0:T(8,128)(2,1)S(1)}, bf16[64,1024]{1,0:T(8,128)(2,1)S(1)}, u32[]{:S(2)}, u32[]{:S(2)}) collective-permute-start(bf16[64,1024]{1,0:T(8,128)(2,1)S(1)} %get-tuple-element.36), channel_id=1, source_target_pairs={{0,1},{1,0},{2,3},{3,2},{4,5},{5,4},{6,7},{7,6},{8,9},{9,8},{10,11... | collective-permute-start | bytes 393224 | tf_op jit(solution)/shard_map/ppermute | solution.py:437
  49.8 4.9 %collective-permute-start.20 = (bf16[32,1024]{1,0:T(8,128)(2,1)S(1)}, bf16[32,1024]{1,0:T(8,128)(2,1)S(1)}, u32[]{:S(2)}, u32[]{:S(2)}) collective-permute-start(bf16[32,1024]{1,0:T(8,128)(2,1)S(1)} %get-tuple-element.41), channel_id=1, source_target_pairs={{3,0},{1,2},{6,3},{2,7},{11,6},{7,10},{14,11},{10,15},{13,14},{15,... | collective-permute-start | bytes 196616 | tf_op jit(solution)/shard_map/ppermute | solution.py:457
  50.9 5.4 %collective-permute-start.24 = (bf16[32,1024]{1,0:T(8,128)(2,1)S(1)}, bf16[32,1024]{1,0:T(8,128)(2,1)S(1)}, u32[]{:S(2)}, u32[]{:S(2)}) collective-permute-start(bf16[32,1024]{1,0:T(8,128)(2,1)S(1)} %get-tuple-element.46), channel_id=1, source_target_pairs={{3,0},{1,2},{6,3},{2,7},{11,6},{7,10},{14,11},{10,15},{13,14},{15,... | collective-permute-start | bytes 196616 | tf_op jit(solution)/shard_map/ppermute | solution.py:457
  52.3 4.0 %collective-permute-start.28 = (bf16[32,1024]{1,0:T(8,128)(2,1)S(1)}, bf16[32,1024]{1,0:T(8,128)(2,1)S(1)}, u32[]{:S(2)}, u32[]{:S(2)}) collective-permute-start(bf16[32,1024]{1,0:T(8,128)(2,1)S(1)} %shard_map.94), channel_id=1, source_target_pairs={{0,1},{1,0},{2,3},{3,2},{4,5},{5,4},{6,7},{7,6},{8,9},{9,8},{10,11... | collective-permute-start | bytes 196616 | tf_op jit(solution)/shard_map/ppermute | solution.py:446
  53.7 2.6 %collective-permute-start.32 = (bf16[32,1024]{1,0:T(8,128)(2,1)S(1)}, bf16[32,1024]{1,0:T(8,128)(2,1)S(1)}, u32[]{:S(2)}, u32[]{:S(2)}) collective-permute-start(bf16[32,1024]{1,0:T(8,128)(2,1)S(1)} %shard_map.95), channel_id=1, source_target_pairs={{0,1},{1,0},{2,3},{3,2},{4,5},{5,4},{6,7},{7,6},{8,9},{9,8},{10,11... | collective-permute-start | bytes 196616 | tf_op jit(solution)/shard_map/ppermute | solution.py:446
  54.3 4.3 %collective-permute-start.33 = (bf16[32,1024]{1,0:T(8,128)(2,1)S(1)}, bf16[32,1024]{1,0:T(8,128)(2,1)S(1)}, u32[]{:S(2)}, u32[]{:S(2)}) collective-permute-start(bf16[32,1024]{1,0:T(8,128)(2,1)S(1)} %get-tuple-element.53), channel_id=1, source_target_pairs={{3,1},{1,3},{6,2},{2,6},{11,7},{7,11},{14,10},{10,14},{13,15},{15,... | collective-permute-start | bytes 196616 | tf_op jit(solution)/shard_map/ppermute | solution.py:458
  54.7 4.5 %collective-permute-start.34 = (bf16[32,1024]{1,0:T(8,128)(2,1)S(1)}, bf16[32,1024]{1,0:T(8,128)(2,1)S(1)}, u32[]{:S(2)}, u32[]{:S(2)}) collective-permute-start(bf16[32,1024]{1,0:T(8,128)(2,1)S(1)} %get-tuple-element.54), channel_id=1, source_target_pairs={{3,1},{1,3},{6,2},{2,6},{11,7},{7,11},{14,10},{10,14},{13,15},{15,... | collective-permute-start | bytes 196616 | tf_op jit(solution)/shard_map/ppermute | solution.py:458

commit v5 on v4

--- a/solution.py
+++ b/solution.py
@@ -11,8 +11,6 @@
 LANES = 128
 VMEM_BYTES = 67043328
 PIECES = 2
-AHEAD_FIRST = 2
-AHEAD_SECOND = 2
 SUBLANES = 16
 
 
@@ -142,53 +140,56 @@
     )
 
 
-def pack_kernel(caps, pieces, routes_in, probs_in, old_in, new_in, tokens, *refs):
-    count = sum(pieces)
-    outs, (slot_rows, routes, probs, old_place, new_place, sems) = refs[:count], refs[count:]
+def side_lanes(experts):
+    return -(-4 * PIECES * experts // LANES) * LANES
+
+
+def pack_kernel(caps, routes_in, probs_in, old_in, new_in, tokens, *refs):
+    outs, refs = refs[: 2 * PIECES], refs[2 * PIECES :]
+    slot_rows, routes, probs, old_place, new_place, sems = refs
     core, devices = lax.axis_index("tensor"), lax.axis_size("expert")
     width = tokens.shape[2]
-    token_count = routes.shape[2]
+    topk_count, token_count = routes.shape[1:]
     experts, slots = old_place.shape[0], new_place.shape[0]
-    lanes = outs[0].shape[1] - width
-    chunks = (outs[: pieces[0]], core), (outs[pieces[0] :], 1 - core)
-    pairs = [
-        (old_in, old_place),
-        (new_in, new_place),
-        (routes_in, routes),
-        (probs_in, probs),
-    ]
-    for held, batch in chunks:
-        size = token_count // len(held)
-        for i, out in enumerate(held):
-            pairs.append((tokens.at[batch, i * size : (i + 1) * size], out.at[:, :width]))
+    size = token_count // PIECES
+    pairs = [(old_in, old_place), (new_in, new_place), (routes_in, routes), (probs_in, probs)]
+    for i, out in enumerate(outs):
+        batch = core if i < PIECES else 1 - core
+        start = i % PIECES * size
+        pairs.append((tokens.at[batch, start : start + size], out.at[:, :width]))
     copies = [pltpu.make_async_copy(src, dst, sems.at[i]) for i, (src, dst) in enumerate(pairs)]
     for copy in copies:
         copy.start()
     for copy in copies[:4]:
         copy.wait()
-    token = lax.broadcasted_iota(jnp.int32, (1, token_count), 1)
-    limits = [caps[1] * count_of(new_place, old_place[e], slots) for e in range(experts)]
-    for held, batch in chunks:
-        highs, lows = [], []
-        for e in range(experts):
-            named = routes[batch] == old_place[e]
-            weight = jnp.sum(jnp.where(named, probs[batch], 0.0), axis=0, keepdims=True)
-            served = jnp.where(batch == 0, caps[0], limits[e])
-            weight = jnp.where(token < served, weight, 0.0)
-            high = weight.astype(jnp.bfloat16).astype(jnp.float32)
-            highs.append(high)
-            lows.append(weight - high)
-        pad = jnp.zeros((lanes - 2 * experts, token_count), jnp.float32)
-        side = jnp.concatenate(highs + lows + [pad], axis=0).T.astype(jnp.bfloat16)
-        size = token_count // len(held)
-        for i, out in enumerate(held):
-            out[:, width:] = side[i * size : (i + 1) * size]
+    slot = lax.broadcasted_iota(jnp.int32, (experts, token_count), 0)
+    token = lax.broadcasted_iota(jnp.int32, (experts, token_count), 1)
+    held, limit = jnp.zeros_like(slot), jnp.zeros_like(slot)
+    for e in range(experts):
+        held = jnp.where(slot == e, old_place[e], held)
+        limit = jnp.where(slot == e, caps[1] * count_of(new_place, old_place[e], slots), limit)
+    kinds = []
+    for batch in (core, 1 - core):
+        named, chance = routes[batch], probs[batch]
+        weight = jnp.zeros((experts, token_count), jnp.float32)
+        for k in range(topk_count):
+            weight += jnp.where(named[k : k + 1] == held, chance[k : k + 1], 0.0)
+        weight = jnp.where(token < jnp.where(batch == 0, caps[0], limit), weight, 0.0)
+        high = weight.astype(jnp.bfloat16).astype(jnp.float32)
+        kinds += [high, weight - high]
+    lanes = side_lanes(experts)
+    kinds.append(jnp.zeros((lanes - 4 * experts, token_count), jnp.float32))
+    turned = jnp.concatenate(kinds, axis=0).T
+    side = turned[:size]
+    for i in range(1, PIECES):
+        side += pltpu.roll(turned[i * size : (i + 1) * size], 4 * experts * i, 1)
+    outs[PIECES - 1][:, width:] = side.astype(jnp.bfloat16)
     mine = slot_rows.shape[0]
     for j in range(mine):
-        slot = lax.axis_index("expert") * mine + j
-        expert = new_place[slot]
+        new_slot = lax.axis_index("expert") * mine + j
+        expert = new_place[new_slot]
         holders = count_of(new_place, expert, slots)
-        place = count_of(new_place, expert, slot)
+        place = count_of(new_place, expert, new_slot)
         total = jnp.int32(0)
         for source in range(devices):
             start = lax.rem(place - source + devices * holders, holders)
@@ -198,80 +199,49 @@
         copy.wait()
 
 
-def pack(caps, pieces, tokens, routes, probs, old_place, new_place):
+def pack(caps, tokens, routes, probs, old_place, new_place):
     token_count, width = tokens.shape[1:]
     experts = old_place.shape[0]
-    lanes = -(-2 * experts // LANES) * LANES
-    chunks = [
-        jax.ShapeDtypeStruct((token_count // parts, width + lanes), tokens.dtype)
-        for parts in pieces
-        for _ in range(parts)
-    ]
+    size = token_count // PIECES
+    widths = [width] * (2 * PIECES)
+    widths[PIECES - 1] += side_lanes(experts)
     routes, probs = routes.transpose(0, 2, 1), probs.transpose(0, 2, 1)
     mine = new_place.shape[0] // lax.axis_size("expert")
     vmem, smem = pl.BlockSpec(memory_space=pltpu.VMEM), pl.BlockSpec(memory_space=pltpu.SMEM)
     return pl.pallas_call(
-        functools.partial(pack_kernel, caps, pieces),
-        out_shape=[*chunks, jax.ShapeDtypeStruct((mine,), jnp.int32)],
+        functools.partial(pack_kernel, caps),
+        out_shape=[jax.ShapeDtypeStruct((size, w), tokens.dtype) for w in widths]
+        + [jax.ShapeDtypeStruct((mine,), jnp.int32)],
         in_specs=[pl.BlockSpec(memory_space=pltpu.HBM)] * 5,
-        out_specs=[vmem] * len(chunks) + [smem],
+        out_specs=[vmem] * len(widths) + [smem],
         scratch_shapes=[
             pltpu.VMEM(routes.shape, routes.dtype),
             pltpu.VMEM(probs.shape, probs.dtype),
             pltpu.SMEM(old_place.shape, jnp.int32),
             pltpu.SMEM(new_place.shape, jnp.int32),
-            pltpu.SemaphoreType.DMA((4 + len(chunks),)),
+            pltpu.SemaphoreType.DMA((4 + len(widths),)),
         ],
         compiler_params=pltpu.CompilerParams(vmem_limit_bytes=VMEM_BYTES - (4 << 20)),
     )(routes, probs, old_place, new_place, tokens)
 
 
-def load_kernel(up, down, up_here, down_here, sems):
-    copies = [
-        pltpu.make_async_copy(up, up_here, sems.at[0]),
-        pltpu.make_async_copy(down, down_here, sems.at[1]),
-    ]
-    for copy in copies:
-        copy.start()
-    for copy in copies:
-        copy.wait()
-
-
-def load(up, down):
-    vmem = pl.BlockSpec(memory_space=pltpu.VMEM)
-    return pl.pallas_call(
-        load_kernel,
-        out_shape=(
-            jax.ShapeDtypeStruct(up.shape, up.dtype),
-            jax.ShapeDtypeStruct(down.shape, down.dtype),
-        ),
-        in_specs=[pl.BlockSpec(memory_space=pltpu.HBM)] * 2,
-        out_specs=(vmem, vmem),
-        scratch_shapes=[pltpu.SemaphoreType.DMA((2,))],
-        compiler_params=pltpu.CompilerParams(vmem_limit_bytes=VMEM_BYTES - (14 << 20)),
-        cost_estimate=pl.CostEstimate(
-            flops=0, bytes_accessed=4 * (up.size + down.size), transcendentals=0
-        ),
-    )(up, down)
-
-
 def half_of(core, half):
     return pl.ds(pl.multiple_of(core * half, LANES), half)
 
 
-def expert_kernel(count, outlets, width, experts, *refs):
+def expert_kernel(sides, outlets, width, experts, *refs):
+    count = len(sides)
     rows, refs = refs[:count], refs[count:]
     (up_own, up_pair, down_own, down_pair), refs = refs[:4], refs[4:]
     outs, x_buf = list(refs[:-1]), refs[-1]
     slot, core = lax.axis_index("expert"), lax.axis_index("tensor")
     scales, place = [], 0
-    for row in rows:
-        size = row.shape[0]
-        lane = lax.broadcasted_iota(jnp.int32, (size, row.shape[1] - width), 1)
-        mine = (lane == slot) | (lane == experts + slot)
-        x_buf[place : place + size, :] = row[:, :width]
-        place += size
-        side = row[:, width:].astype(jnp.float32)
+    for row, (holder, offset) in zip(rows, sides):
+        x_buf[place : place + row.shape[0], :] = row[:, :width]
+        place += row.shape[0]
+        side = rows[holder][:, width:].astype(jnp.float32)
+        lane = lax.broadcasted_iota(jnp.int32, side.shape, 1) - offset - slot
+        mine = (lane == 0) | (lane == experts)
         scales.append(jnp.sum(jnp.where(mine, side, 0.0), axis=1, keepdims=True))
     scale = jnp.concatenate(scales, axis=0)
     x = x_buf[...]
@@ -296,7 +266,14 @@
                 group[j][...] = made.astype(group[j].dtype)
 
 
-def expert_rows(rows, weights, width, experts, outlets):
+def expert_rows(hops, weights, width, experts, outlets):
+    rows, sides = [], []
+    for pieces in hops:
+        holder = len(rows) + PIECES - 1
+        for i in range(len(pieces)):
+            chunk, piece = divmod(i, PIECES)
+            sides.append((holder, (4 * piece + 2 * chunk) * experts))
+        rows += pieces
     total = sum(row.shape[0] for row in rows)
     up = weights[0]
     vmem = pl.BlockSpec(memory_space=pltpu.VMEM)
@@ -307,7 +284,7 @@
         else:
             shapes += [((size, width // 2), t) for t in (jnp.float32, jnp.bfloat16)]
     return pl.pallas_call(
-        functools.partial(expert_kernel, len(rows), outlets, width, experts),
+        functools.partial(expert_kernel, tuple(sides), outlets, width, experts),
         out_shape=[jax.ShapeDtypeStruct(*shape) for shape in shapes],
         in_specs=[vmem] * (len(rows) + 4),
         out_specs=[vmem] * len(shapes),
@@ -400,39 +377,39 @@
     f32, bf16 = jnp.float32, jnp.bfloat16
     each = range(PIECES)
     size = token_count // PIECES
-    own_pieces = (AHEAD_FIRST, AHEAD_SECOND)
 
     caps = (
         capacity_for(block_rows, experts, token_count),
         capacity_for(block_rows, new_place.shape[0], token_count),
     )
-    *packed, slot_rows = pack(caps, own_pieces, tokens, routes, probs, old_place, new_place)
-    first, second = [packed[:AHEAD_FIRST]], [packed[AHEAD_FIRST:]]
+    *packed, slot_rows = pack(caps, tokens, routes, probs, old_place, new_place)
+    first, second = [packed[:PIECES]], [packed[PIECES:]]
     for step in range(1, steps + 1):
-        first.append([lax.ppermute(x, both, ahead) for x in first[-1]])
+        first.append([lax.ppermute(first[-1][i], both, ahead) for i in each])
         if step < steps:
-            second.append([lax.ppermute(x, both, ahead) for x in second[-1]])
+            second.append([lax.ppermute(second[-1][i], both, ahead) for i in each])
     up_own, down_own = up_weight[0], down_weight[0]
     up_pair = lax.ppermute(up_own, "tensor", swap)
     down_pair = lax.ppermute(down_own, "tensor", swap)
-    up_here, down_here = load(up_own, down_own)
+    up_here = lax.ppermute(up_pair, "tensor", swap)
+    down_here = lax.ppermute(down_pair, "tensor", swap)
     weights = (up_here, up_pair, down_here, down_pair)
 
-    def run(rows, outlets):
-        return expert_rows(rows, weights, width, experts, outlets)
+    def run(held, outlets):
+        return expert_rows(held, weights, width, experts, outlets)
 
     def ranges(chunk, held):
         return [(chunk * token_count + i * size, size, held) for i in each]
 
     part_first, part_second = [None] * steps, [None] * steps
     own, leaving, *made = run(
-        [*first[0], *first[1], *second[1]], [(0, token_count, None), *ranges(1, f32), *ranges(2, f32)]
+        [first[0], first[1] + second[1]], [(0, token_count, None), *ranges(1, f32), *ranges(2, f32)]
     )
     part_first[1], part_second[1] = made[:PIECES], made[PIECES:]
     for step in range(2, steps):
-        made = run([*first[step], *second[step]], ranges(0, f32) + ranges(1, bf16 if step == steps - 1 else f32))
+        made = run([first[step] + second[step]], ranges(0, f32) + ranges(1, bf16 if step == steps - 1 else f32))
         part_first[step], part_second[step] = made[:PIECES], made[PIECES:]
-    sum_first = run(first[steps], ranges(0, bf16))
+    sum_first = run([first[steps]], ranges(0, bf16))
     sum_second = part_second[steps - 1]
     own_pair = lax.ppermute(leaving, "tensor", swap)
 
@@ -472,7 +449,6 @@
         and lax.axis_size("tensor") == 2
         and tokens.shape[0] == 2
         and tokens.shape[1] % (SUBLANES * PIECES) == 0
-        and tokens.shape[1] % (SUBLANES * AHEAD_FIRST) == 0
     ):
         return by_ring(ring, *arrays)
     return by_capacity(*arrays)

time: 60.2 us -> 72.4 us (1.20)
  Pallas kernels: 10.4 us -> 16.1 us
  starting transfers between devices: 39.8 us -> 45.2 us
  waiting for transfers between devices: 8.87 us -> 9.95 us
    pallas_call x6 -> x5, Pallas kernels: 9.52 us -> 15.2 us  [the longest x4 13.2 us: expert_rows(): pl.pallas_call(functools.partial(expert_kernel, tuple(sides), outlets, wi...]
    ppermute x1, waiting for transfers between devices: 0.01 us -> 3.17 us  [by_ring(): up_pair = lax.ppermute(up_own, 'tensor', swap)]
    ppermute x6, waiting for transfers between devices: 2.87 us -> 0.02 us  [by_ring(): sum_second = [lax.ppermute(sum_second[i], both, back) for i in each]]
    ppermute x1, waiting for transfers between devices: 0.01 us -> 1.88 us  [by_ring(): down_pair = lax.ppermute(down_own, 'tensor', swap)]
    ppermute x2, starting transfers between devices: 1.38 us -> 3.25 us  [by_ring(): last = lax.ppermute(sum_first[i], both, back)]
    ppermute x2, starting transfers between devices: 1.16 us -> 2.63 us  [by_ring(): lax.ppermute(other_half(sum_second[i]), 'tensor', swap)]
    ppermute x2, starting transfers between devices: 1.47 us -> 2.73 us  [by_ring(): arrived.append(lax.ppermute(stays, both, back))]
    ppermute x1, starting transfers between devices: 0.96 us -> 0.01 us  [by_ring(): own_pair = lax.ppermute(leaving, 'tensor', swap)]
  transfers between devices with their start and end apart: 35 -> 37, of which waited for: 10 -> 6; matrix products, arithmetic and copies ran while one was open for 0% -> 0% of each run, Pallas kernels for 16% -> 21%
where the time goes in v5:
time: 72.4 us; the launch traced here: 72.3 us
  starting transfers between devices  45.2 us (62%)
  Pallas kernels  16.1 us (22%)
  waiting for transfers between devices  9.95 us (14%)
  between operations  0.78 us (1%)
    pallas_call x4, Pallas kernels, expert_rows(): pl.pallas_call(functools.partial(expert_kernel, tuple(sides), outlets, wi...  13.2 us
    ppermute x8, starting transfers between devices, by_ring(): first.append([lax.ppermute(first[-1][i], both, ahead) for i in each])  13 us
    ppermute x6, starting transfers between devices, by_ring(): second.append([lax.ppermute(second[-1][i], both, ahead) for i in each])  10.1 us
    ppermute x6, starting transfers between devices, by_ring(): sum_second = [lax.ppermute(sum_second[i], both, back) for i in each]  5.64 us
    ppermute x4, starting transfers between devices, by_ring(): sum_first = [lax.ppermute(sum_first[i], both, back) for i in each]  4.4 us
    ppermute x2, starting transfers between devices, by_ring(): last = lax.ppermute(sum_first[i], both, back)  3.25 us
    ppermute x1, waiting for transfers between devices, by_ring(): up_pair = lax.ppermute(up_own, 'tensor', swap)  3.17 us
    ppermute x2, waiting for transfers between devices, by_ring(): crossed.append(lax.ppermute(crosses, both, across))  2.92 us
  transfers between devices with their start and end apart: 37, of which 6 were waited for; matrix products, arithmetic and copies ran while one was open for 0% of the time, Pallas kernels for 21%

profile of v5, /device:TPU:0, one launch (start us, length us, event | category | flops | bytes accessed | tf_op | source)
XLA Modules:
  0.0 72.3 jit_solution(18336540016652052825)
XLA Ops:
  0.6 0.6 collective-permute-start.4
  1.2 0.1 collective-permute-start.6
  1.3 3.2 %collective-permute-done.4.refs_7_.refs_5_.refs_3_ = bf16[2048,384]{1,0:T(8,128)(2,1)S(1)} collective-permute-done((bf16[2048,384]{1,0:T(8,128)(2,1)}, bf16[2048,384]{1,0:T(8,128)(2,1)S(1)}, u32[]{:S(2)}, u32[]{:S(2)}) %collective-permute-start.4) | collective-permute-done | bytes 1572896 | tf_op jit(solution)/shard_map/ppermute | solution.py:392
  4.4 0.4 collective-permute-start.5
  4.8 1.9 %collective-permute-done.6.refs_9_.refs_7_.refs_5_ = bf16[768,1024]{1,0:T(8,128)(2,1)S(1)} collective-permute-done((bf16[768,1024]{1,0:T(8,128)(2,1)}, bf16[768,1024]{1,0:T(8,128)(2,1)S(1)}, u32[]{:S(2)}, u32[]{:S(2)}) %collective-permute-start.6) | collective-permute-done | bytes 1572896 | tf_op jit(solution)/shard_map/ppermute | solution.py:393
  6.7 0.4 collective-permute-start.7
  7.1 2.1 %shard_map.86 = (bf16[32,2048]{1,0:T(8,128)(2,1)}, bf16[32,2176]{1,0:T(8,128)(2,1)}, bf16[32,2048]{1,0:T(8,128)(2,1)}, bf16[32,2048]{1,0:T(8,128)(2,1)}, s32[2]{0:T(128)}) custom-call(s32[2,8,64]{2,1,0:T(8,128)} %bitcast.4, f32[2,8,64]{2,1,0:T(8,128)} %bitcast.5, s32[8]{0:T(128)} %old_in.1, s32[16]{0:T(128)} %new_in.1, bf16[2,64,2048]{2,1,0:T(8,128)(2,1)} %tokens.1), custom_call_target="tpu_custom_call" | custom-call | tf_op jit(solution)/shard_map/pallas_call | solution.py:211
  9.1 2.6 %collective-permute-start = (bf16[32,2048]{1,0:T(8,128)(2,1)}, bf16[32,2048]{1,0:T(8,128)(2,1)S(1)}, u32[]{:S(2)}, u32[]{:S(2)}) collective-permute-start(bf16[32,2048]{1,0:T(8,128)(2,1)} %get-tuple-element.27.refs_0_), channel_id=1, source_target_pairs={{0,3},{2,1},{3,6},{7,2},{6,11},{10,7},{11,14},{15,10},{14,13},{12,... | collective-permute-start | bytes 393224 | tf_op jit(solution)/shard_map/ppermute | solution.py:388
  11.8 1.3 %collective-permute-start.2 = (bf16[32,2048]{1,0:T(8,128)(2,1)}, bf16[32,2048]{1,0:T(8,128)(2,1)S(1)}, u32[]{:S(2)}, u32[]{:S(2)}) collective-permute-start(bf16[32,2048]{1,0:T(8,128)(2,1)} %get-tuple-element.29), channel_id=1, source_target_pairs={{0,3},{2,1},{3,6},{7,2},{6,11},{10,7},{11,14},{15,10},{14,13},{12,... | collective-permute-start | bytes 393224 | tf_op jit(solution)/shard_map/ppermute | solution.py:390
  13.1 1.6 %collective-permute-start.1 = (bf16[32,2176]{1,0:T(8,128)(2,1)}, bf16[32,2176]{1,0:T(8,128)(2,1)S(1)}, u32[]{:S(2)}, u32[]{:S(2)}) collective-permute-start(bf16[32,2176]{1,0:T(8,128)(2,1)} %get-tuple-element.28.refs_1_), channel_id=1, source_target_pairs={{0,3},{2,1},{3,6},{7,2},{6,11},{10,7},{11,14},{15,10},{14,13},{12,... | collective-permute-start | bytes 417800 | tf_op jit(solution)/shard_map/ppermute | solution.py:388
  14.7 0.1 collective-permute-done.refs_2_
  14.7 1.9 %collective-permute-start.3 = (bf16[32,2048]{1,0:T(8,128)(2,1)}, bf16[32,2048]{1,0:T(8,128)(2,1)S(1)}, u32[]{:S(2)}, u32[]{:S(2)}) collective-permute-start(bf16[32,2048]{1,0:T(8,128)(2,1)} %get-tuple-element.30), channel_id=1, source_target_pairs={{0,3},{2,1},{3,6},{7,2},{6,11},{10,7},{11,14},{15,10},{14,13},{12,... | collective-permute-start | bytes 393224 | tf_op jit(solution)/shard_map/ppermute | solution.py:390
  16.7 0.0 collective-permute-done.2.refs_4_
  16.7 1.4 %collective-permute-start.9 = (bf16[32,2048]{1,0:T(8,128)(2,1)S(1)}, bf16[32,2048]{1,0:T(8,128)(2,1)S(1)}, u32[]{:S(2)}, u32[]{:S(2)}) collective-permute-start(bf16[32,2048]{1,0:T(8,128)(2,1)S(1)} %collective-permute-done.refs_2_), channel_id=1, source_target_pairs={{0,3},{2,1},{3,6},{7,2},{6,11},{10,7},{11,14},{15,10},{14,13},{12,... | collective-permute-start | bytes 393224 | tf_op jit(solution)/shard_map/ppermute | solution.py:388
  18.1 1.6 %collective-permute-start.10 = (bf16[32,2176]{1,0:T(8,128)(2,1)S(1)}, bf16[32,2176]{1,0:T(8,128)(2,1)S(1)}, u32[]{:S(2)}, u32[]{:S(2)}) collective-permute-start(bf16[32,2176]{1,0:T(8,128)(2,1)S(1)} %collective-permute-done.1.refs_3_), channel_id=1, source_target_pairs={{0,3},{2,1},{3,6},{7,2},{6,11},{10,7},{11,14},{15,10},{14,13},{12,... | collective-permute-start | bytes 417800 | tf_op jit(solution)/shard_map/ppermute | solution.py:388
  19.7 0.0 collective-permute-done.3.refs_5_
  19.7 1.9 %collective-permute-start.11 = (bf16[32,2048]{1,0:T(8,128)(2,1)S(1)}, bf16[32,2048]{1,0:T(8,128)(2,1)S(1)}, u32[]{:S(2)}, u32[]{:S(2)}) collective-permute-start(bf16[32,2048]{1,0:T(8,128)(2,1)S(1)} %collective-permute-done.2.refs_4_), channel_id=1, source_target_pairs={{0,3},{2,1},{3,6},{7,2},{6,11},{10,7},{11,14},{15,10},{14,13},{12,... | collective-permute-start | bytes 393224 | tf_op jit(solution)/shard_map/ppermute | solution.py:390
  21.6 1.4 %collective-permute-start.13 = (bf16[32,2048]{1,0:T(8,128)(2,1)S(1)}, bf16[32,2048]{1,0:T(8,128)(2,1)S(1)}, u32[]{:S(2)}, u32[]{:S(2)}) collective-permute-start(bf16[32,2048]{1,0:T(8,128)(2,1)S(1)} %collective-permute-done.9.refs_0_), channel_id=1, source_target_pairs={{0,3},{2,1},{3,6},{7,2},{6,11},{10,7},{11,14},{15,10},{14,13},{12,... | collective-permute-start | bytes 393224 | tf_op jit(solution)/shard_map/ppermute | solution.py:388
  23.0 0.0 collective-permute-done.10.refs_1_
  23.0 1.5 %collective-permute-start.14 = (bf16[32,2176]{1,0:T(8,128)(2,1)S(1)}, bf16[32,2176]{1,0:T(8,128)(2,1)S(1)}, u32[]{:S(2)}, u32[]{:S(2)}) collective-permute-start(bf16[32,2176]{1,0:T(8,128)(2,1)S(1)} %collective-permute-done.10.refs_1_), channel_id=1, source_target_pairs={{0,3},{2,1},{3,6},{7,2},{6,11},{10,7},{11,14},{15,10},{14,13},{12,... | collective-permute-start | bytes 417800 | tf_op jit(solution)/shard_map/ppermute | solution.py:388
  24.5 0.0 collective-permute-done.11.refs_2_
  24.5 1.8 %collective-permute-start.12 = (bf16[32,2048]{1,0:T(8,128)(2,1)S(1)}, bf16[32,2048]{1,0:T(8,128)(2,1)S(1)}, u32[]{:S(2)}, u32[]{:S(2)}) collective-permute-start(bf16[32,2048]{1,0:T(8,128)(2,1)S(1)} %collective-permute-done.3.refs_5_), channel_id=1, source_target_pairs={{0,3},{2,1},{3,6},{7,2},{6,11},{10,7},{11,14},{15,10},{14,13},{12,... | collective-permute-start | bytes 393224 | tf_op jit(solution)/shard_map/ppermute | solution.py:390
  26.3 1.4 %collective-permute-start.17 = (bf16[32,2048]{1,0:T(8,128)(2,1)S(1)}, bf16[32,2048]{1,0:T(8,128)(2,1)S(1)}, u32[]{:S(2)}, u32[]{:S(2)}) collective-permute-start(bf16[32,2048]{1,0:T(8,128)(2,1)S(1)} %collective-permute-done.13.refs_0_), channel_id=1, source_target_pairs={{0,3},{2,1},{3,6},{7,2},{6,11},{10,7},{11,14},{15,10},{14,13},{12,... | collective-permute-start | bytes 393224 | tf_op jit(solution)/shard_map/ppermute | solution.py:388
  27.7 0.0 collective-permute-done.14.refs_1_
  27.7 1.6 %collective-permute-start.18 = (bf16[32,2176]{1,0:T(8,128)(2,1)S(1)}, bf16[32,2176]{1,0:T(8,128)(2,1)S(1)}, u32[]{:S(2)}, u32[]{:S(2)}) collective-permute-start(bf16[32,2176]{1,0:T(8,128)(2,1)S(1)} %collective-permute-done.14.refs_1_), channel_id=1, source_target_pairs={{0,3},{2,1},{3,6},{7,2},{6,11},{10,7},{11,14},{15,10},{14,13},{12,... | collective-permute-start | bytes 417800 | tf_op jit(solution)/shard_map/ppermute | solution.py:388
  29.3 0.0 collective-permute-done.12.refs_3_
  29.3 1.7 %collective-permute-start.15 = (bf16[32,2048]{1,0:T(8,128)(2,1)S(1)}, bf16[32,2048]{1,0:T(8,128)(2,1)S(1)}, u32[]{:S(2)}, u32[]{:S(2)}) collective-permute-start(bf16[32,2048]{1,0:T(8,128)(2,1)S(1)} %collective-permute-done.11.refs_2_), channel_id=1, source_target_pairs={{0,3},{2,1},{3,6},{7,2},{6,11},{10,7},{11,14},{15,10},{14,13},{12,... | collective-permute-start | bytes 393224 | tf_op jit(solution)/shard_map/ppermute | solution.py:390
  31.0 1.4 %collective-permute-start.16 = (bf16[32,2048]{1,0:T(8,128)(2,1)S(1)}, bf16[32,2048]{1,0:T(8,128)(2,1)S(1)}, u32[]{:S(2)}, u32[]{:S(2)}) collective-permute-start(bf16[32,2048]{1,0:T(8,128)(2,1)S(1)} %collective-permute-done.12.refs_3_), channel_id=1, source_target_pairs={{0,3},{2,1},{3,6},{7,2},{6,11},{10,7},{11,14},{15,10},{14,13},{12,... | collective-permute-start | bytes 393224 | tf_op jit(solution)/shard_map/ppermute | solution.py:390
  32.4 0.0 collective-permute-done.18.refs_1_
  32.4 0.0 collective-permute-done.5.refs_6_.refs_4_.refs_2_
  32.4 0.0 collective-permute-done.7.refs_8_.refs_6_.refs_4_
  32.4 3.2 %shard_map.90 = (bf16[32,2048]{1,0:T(8,128)(2,1)S(1)}, bf16[32,2048]{1,0:T(8,128)(2,1)S(1)}) custom-call(bf16[32,2048]{1,0:T(8,128)(2,1)S(1)} %collective-permute-done.17.refs_0_, bf16[32,2176]{1,0:T(8,128)(2,1)S(1)} %collective-permute-done.18.refs_1_, bf16[2048,384]{1,0:T(8,128)(2,1)} %collective-permute-done.5.refs_6_.refs_4_.refs_2_, ...), custom_call_target="tpu_custom_call" | custom-call | flops 402653184 | bytes 1048576 | tf_op jit(solution)/shard_map/pallas_call | solution.py:286
  35.5 1.8 %collective-permute-start.19 = (bf16[32,2048]{1,0:T(8,128)(2,1)S(1)}, bf16[32,2048]{1,0:T(8,128)(2,1)S(1)}, u32[]{:S(2)}, u32[]{:S(2)}) collective-permute-start(bf16[32,2048]{1,0:T(8,128)(2,1)S(1)} %get-tuple-element.36), channel_id=1, source_target_pairs={{3,0},{1,2},{6,3},{2,7},{11,6},{7,10},{14,11},{10,15},{13,14},{15,... | collective-permute-start | bytes 393224 | tf_op jit(solution)/shard_map/ppermute | solution.py:425
  37.3 0.8 %collective-permute-start.23 = (bf16[32,2048]{1,0:T(8,128)(2,1)S(1)}, bf16[32,2048]{1,0:T(8,128)(2,1)S(1)}, u32[]{:S(2)}, u32[]{:S(2)}) collective-permute-start(bf16[32,2048]{1,0:T(8,128)(2,1)S(1)} %get-tuple-element.41), channel_id=1, source_target_pairs={{3,0},{1,2},{6,3},{2,7},{11,6},{7,10},{14,11},{10,15},{13,14},{15,... | collective-permute-start | bytes 393224 | tf_op jit(solution)/shard_map/ppermute | solution.py:425
  38.2 0.0 collective-permute-done.16.refs_3_
  38.2 3.2 %shard_map.89 = (f32[32,2048]{1,0:T(8,128)S(1)}, f32[32,2048]{1,0:T(8,128)S(1)}, bf16[32,2048]{1,0:T(8,128)(2,1)S(1)}, bf16[32,2048]{1,0:T(8,128)(2,1)S(1)}) custom-call(bf16[32,2048]{1,0:T(8,128)(2,1)S(1)} %collective-permute-done.13.refs_0_, bf16[32,2176]{1,0:T(8,128)(2,1)S(1)} %collective-permute-done.14.refs_1_, ...), custom_call_target="tpu_custom_call" | custom-call | flops 805306368 | bytes 2097152 | tf_op jit(solution)/shard_map/pallas_call | solution.py:286
  41.4 2.1 %collective-permute-start.27 = (bf16[32,2048]{1,0:T(8,128)(2,1)S(1)}, bf16[32,2048]{1,0:T(8,128)(2,1)S(1)}, u32[]{:S(2)}, u32[]{:S(2)}) collective-permute-start(bf16[32,2048]{1,0:T(8,128)(2,1)S(1)} %get-tuple-element.45), channel_id=1, source_target_pairs={{3,0},{1,2},{6,3},{2,7},{11,6},{7,10},{14,11},{10,15},{13,14},{15,... | collective-permute-start | bytes 393224 | tf_op jit(solution)/shard_map/ppermute | solution.py:417
  43.5 0.1 collective-permute-start.31
  43.5 3.2 %shard_map.88 = (f32[32,2048]{1,0:T(8,128)S(1)}, f32[32,2048]{1,0:T(8,128)S(1)}, f32[32,2048]{1,0:T(8,128)S(1)}, f32[32,2048]{1,0:T(8,128)S(1)}) custom-call(bf16[32,2048]{1,0:T(8,128)(2,1)S(1)} %collective-permute-done.9.refs_0_, bf16[32,2176]{1,0:T(8,128)(2,1)S(1)} %collective-permute-done.10.refs_1_, ...), custom_call_target="tpu_custom_call" | custom-call | flops 805306368 | bytes 2097152 | tf_op jit(solution)/shard_map/pallas_call | solution.py:286
  46.7 3.7 %shard_map.87 = (f32[64,1024]{1,0:T(8,128)S(1)}, bf16[64,1024]{1,0:T(8,128)(2,1)S(1)}, f32[32,2048]{1,0:T(8,128)S(1)}, f32[32,2048]{1,0:T(8,128)S(1)}, f32[32,2048]{1,0:T(8,128)S(1)}, /*index=5*/f32[32,2048]{1,0:T(8,128)S(1)}) custom-call(bf16[32,2048]{1,0:T(8,128)(2,1)S(1)} %copy-done.1, bf16[32,2176]{1,0:T(8,128)(2,1)S(1)} %copy-done, ...), custom_call_target="tpu_custom_call" | custom-call | flops 1207959552 | bytes 3145728 | tf_op jit(solution)/shard_map/pallas_call | solution.py:286
  50.4 0.0 collective-permute-done.19
  50.5 1.6 %collective-permute-start.20 = (bf16[32,2048]{1,0:T(8,128)(2,1)S(1)}, bf16[32,2048]{1,0:T(8,128)(2,1)S(1)}, u32[]{:S(2)}, u32[]{:S(2)}) collective-permute-start(bf16[32,2048]{1,0:T(8,128)(2,1)S(1)} %add_convert_fusion.7), channel_id=1, source_target_pairs={{3,0},{1,2},{6,3},{2,7},{11,6},{7,10},{14,11},{10,15},{13,14},{15,... | collective-permute-start | bytes 393224 | tf_op jit(solution)/shard_map/ppermute | solution.py:425
  52.0 0.0 collective-permute-done.23
  52.1 0.2 collective-permute-start.24
  52.3 0.5 collective-permute-start.28
  52.9 0.0 collective-permute-done.31
  52.9 0.2 collective-permute-start.32
  53.1 1.8 %collective-permute-done.20 = bf16[32,2048]{1,0:T(8,128)(2,1)S(1)} collective-permute-done((bf16[32,2048]{1,0:T(8,128)(2,1)S(1)}, bf16[32,2048]{1,0:T(8,128)(2,1)S(1)}, u32[]{:S(2)}, u32[]{:S(2)}) %collective-permute-start.20) | collective-permute-done | bytes 131104 | tf_op jit(solution)/shard_map/ppermute | solution.py:425
  54.9 1.9 %collective-permute-start.21 = (bf16[32,2048]{1,0:T(8,128)(2,1)S(1)}, bf16[32,2048]{1,0:T(8,128)(2,1)S(1)}, u32[]{:S(2)}, u32[]{:S(2)}) collective-permute-start(bf16[32,2048]{1,0:T(8,128)(2,1)S(1)} %add_convert_fusion.6), channel_id=1, source_target_pairs={{3,0},{1,2},{6,3},{2,7},{11,6},{7,10},{14,11},{10,15},{13,14},{15,... | collective-permute-start | bytes 393224 | tf_op jit(solution)/shard_map/ppermute | solution.py:432
  56.8 0.0 collective-permute-done.24
  56.9 1.4 %collective-permute-start.25 = (bf16[32,2048]{1,0:T(8,128)(2,1)S(1)}, bf16[32,2048]{1,0:T(8,128)(2,1)S(1)}, u32[]{:S(2)}, u32[]{:S(2)}) collective-permute-start(bf16[32,2048]{1,0:T(8,128)(2,1)S(1)} %add_convert_fusion.4), channel_id=1, source_target_pairs={{3,0},{1,2},{6,3},{2,7},{11,6},{7,10},{14,11},{10,15},{13,14},{15,... | collective-permute-start | bytes 393224 | tf_op jit(solution)/shard_map/ppermute | solution.py:432
  58.3 1.4 %collective-permute-start.29 = (bf16[32,2048]{1,0:T(8,128)(2,1)S(1)}, bf16[32,2048]{1,0:T(8,128)(2,1)S(1)}, u32[]{:S(2)}, u32[]{:S(2)}) collective-permute-start(bf16[32,2048]{1,0:T(8,128)(2,1)S(1)} %add_convert_fusion.2), channel_id=1, source_target_pairs={{3,0},{1,2},{6,3},{2,7},{11,6},{7,10},{14,11},{10,15},{13,14},{15,... | collective-permute-start | bytes 393224 | tf_op jit(solution)/shard_map/ppermute | solution.py:417
  59.7 1.4 %collective-permute-start.33 = (bf16[32,2048]{1,0:T(8,128)(2,1)S(1)}, bf16[32,2048]{1,0:T(8,128)(2,1)S(1)}, u32[]{:S(2)}, u32[]{:S(2)}) collective-permute-start(bf16[32,2048]{1,0:T(8,128)(2,1)S(1)} %add_convert_fusion), channel_id=1, source_target_pairs={{3,0},{1,2},{6,3},{2,7},{11,6},{7,10},{14,11},{10,15},{13,14},{15,... | collective-permute-start | bytes 393224 | tf_op jit(solution)/shard_map/ppermute | solution.py:417
  61.0 0.0 collective-permute-start.8
  61.0 0.0 collective-permute-done.21.arrived
  61.1 1.7 %collective-permute-start.22 = (bf16[32,1024]{1,0:T(8,128)(2,1)S(1)}, bf16[32,1024]{1,0:T(8,128)(2,1)S(1)}, u32[]{:S(2)}, u32[]{:S(2)}) collective-permute-start(bf16[32,1024]{1,0:T(8,128)(2,1)S(1)} %get-tuple-element.37), channel_id=1, source_target_pairs={{3,0},{1,2},{6,3},{2,7},{11,6},{7,10},{14,11},{10,15},{13,14},{15,... | collective-permute-start | bytes 196616 | tf_op jit(solution)/shard_map/ppermute | solution.py:434
  62.8 1.0 %collective-permute-start.26 = (bf16[32,1024]{1,0:T(8,128)(2,1)S(1)}, bf16[32,1024]{1,0:T(8,128)(2,1)S(1)}, u32[]{:S(2)}, u32[]{:S(2)}) collective-permute-start(bf16[32,1024]{1,0:T(8,128)(2,1)S(1)} %get-tuple-element.42), channel_id=1, source_target_pairs={{3,0},{1,2},{6,3},{2,7},{11,6},{7,10},{14,11},{10,15},{13,14},{15,... | collective-permute-start | bytes 196616 | tf_op jit(solution)/shard_map/ppermute | solution.py:434
  63.9 1.2 %collective-permute-start.30 = (bf16[32,1024]{1,0:T(8,128)(2,1)S(1)}, bf16[32,1024]{1,0:T(8,128)(2,1)S(1)}, u32[]{:S(2)}, u32[]{:S(2)}) collective-permute-start(bf16[32,1024]{1,0:T(8,128)(2,1)S(1)} %shard_map.93), channel_id=1, source_target_pairs={{0,1},{1,0},{2,3},{3,2},{4,5},{5,4},{6,7},{7,6},{8,9},{9,8},{10,11... | collective-permute-start | bytes 196616 | tf_op jit(solution)/shard_map/ppermute | solution.py:423
  65.1 1.4 %collective-permute-start.34 = (bf16[32,1024]{1,0:T(8,128)(2,1)S(1)}, bf16[32,1024]{1,0:T(8,128)(2,1)S(1)}, u32[]{:S(2)}, u32[]{:S(2)}) collective-permute-start(bf16[32,1024]{1,0:T(8,128)(2,1)S(1)} %shard_map.94), channel_id=1, source_target_pairs={{0,1},{1,0},{2,3},{3,2},{4,5},{5,4},{6,7},{7,6},{8,9},{9,8},{10,11... | collective-permute-start | bytes 196616 | tf_op jit(solution)/shard_map/ppermute | solution.py:423
  66.5 0.5 collective-permute-start.35
  67.0 1.5 %collective-permute-start.36 = (bf16[32,1024]{1,0:T(8,128)(2,1)S(1)}, bf16[32,1024]{1,0:T(8,128)(2,1)S(1)}, u32[]{:S(2)}, u32[]{:S(2)}) collective-permute-start(bf16[32,1024]{1,0:T(8,128)(2,1)S(1)} %get-tuple-element.50), channel_id=1, source_target_pairs={{3,1},{1,3},{6,2},{2,6},{11,7},{7,11},{14,10},{10,14},{13,15},{15,... | collective-permute-start | bytes 196616 | tf_op jit(solution)/shard_map/ppermute | solution.py:435
  68.5 2.2 %collective-permute-done.35.refs_6_ = bf16[32,1024]{1,0:T(8,128)(2,1)S(1)} collective-permute-done((bf16[32,1024]{1,0:T(8,128)(2,1)S(1)}, bf16[32,1024]{1,0:T(8,128)(2,1)S(1)}, u32[]{:S(2)}, u32[]{:S(2)}) %collective-permute-start.35) | collective-permute-done | bytes 65568 | tf_op jit(solution)/shard_map/ppermute | solution.py:435
  70.8 0.7 collective-permute-done.36.refs_7_
  71.5 0.8 %shard_map.95 = bf16[2,64,1024]{2,1,0:T(8,128)(2,1)} custom-call(f32[64,1024]{1,0:T(8,128)S(1)} %get-tuple-element.31.own, bf16[64,1024]{1,0:T(8,128)(2,1)S(1)} %collective-permute-done.8.own_pair, bf16[32,1024]{1,0:T(8,128)(2,1)S(1)} %collective-permute-done.22.refs_0_, bf16[32,1024]{1,0:T(8,128)(2,1)S(1)} %collective-permute-done.26.refs_1_, ...), custom_call_target="tpu_custom_call" | custom-call | tf_op jit(solution)/shard_map/pallas_call | solution.py:352
  (32 shorter events, 0.4 us)
Async XLA Ops:
  0.6 3.8 %collective-permute-start.4 = (bf16[2048,384]{1,0:T(8,128)(2,1)}, bf16[2048,384]{1,0:T(8,128)(2,1)S(1)}, u32[]{:S(2)}, u32[]{:S(2)}) collective-permute-start(bf16[2048,384]{1,0:T(8,128)(2,1)} %bitcast.6), channel_id=1, source_target_pairs={{0,1},{1,0},{2,3},{3,2},{4,5},{5,4},{6,7},{7,6},{8,9},{9,8},{10,11... | collective-permute-start | bytes 4718600 | tf_op jit(solution)/shard_map/ppermute | solution.py:392
  1.2 5.5 %collective-permute-start.6 = (bf16[768,1024]{1,0:T(8,128)(2,1)}, bf16[768,1024]{1,0:T(8,128)(2,1)S(1)}, u32[]{:S(2)}, u32[]{:S(2)}) collective-permute-start(bf16[768,1024]{1,0:T(8,128)(2,1)} %bitcast.7), channel_id=1, source_target_pairs={{0,1},{1,0},{2,3},{3,2},{4,5},{5,4},{6,7},{7,6},{8,9},{9,8},{10,11... | collective-permute-start | bytes 4718600 | tf_op jit(solution)/shard_map/ppermute | solution.py:393
  4.4 27.9 %collective-permute-start.5 = (bf16[2048,384]{1,0:T(8,128)(2,1)S(1)}, bf16[2048,384]{1,0:T(8,128)(2,1)}, u32[]{:S(2)}, u32[]{:S(2)}) collective-permute-start(bf16[2048,384]{1,0:T(8,128)(2,1)S(1)} %collective-permute-done.4.refs_7_.refs_5_.refs_3_), channel_id=1, source_target_pairs={{0,1},{1,0},{2,3},{3,2},{4,5},{5,4},{6,7},{7,6},{8,9},{9,8},{10,11... | collective-permute-start | bytes 4718600 | tf_op jit(solution)/shard_map/ppermute | solution.py:394
  6.7 25.7 %collective-permute-start.7 = (bf16[768,1024]{1,0:T(8,128)(2,1)S(1)}, bf16[768,1024]{1,0:T(8,128)(2,1)}, u32[]{:S(2)}, u32[]{:S(2)}) collective-permute-start(bf16[768,1024]{1,0:T(8,128)(2,1)S(1)} %collective-permute-done.6.refs_9_.refs_7_.refs_5_), channel_id=1, source_target_pairs={{0,1},{1,0},{2,3},{3,2},{4,5},{5,4},{6,7},{7,6},{8,9},{9,8},{10,11... | collective-permute-start | bytes 4718600 | tf_op jit(solution)/shard_map/ppermute | solution.py:395
  9.1 5.6 %collective-permute-start = (bf16[32,2048]{1,0:T(8,128)(2,1)}, bf16[32,2048]{1,0:T(8,128)(2,1)S(1)}, u32[]{:S(2)}, u32[]{:S(2)}) collective-permute-start(bf16[32,2048]{1,0:T(8,128)(2,1)} %get-tuple-element.27.refs_0_), channel_id=1, source_target_pairs={{0,3},{2,1},{3,6},{7,2},{6,11},{10,7},{11,14},{15,10},{14,13},{12,... | collective-permute-start | bytes 393224 | tf_op jit(solution)/shard_map/ppermute | solution.py:388
  11.8 4.9 %collective-permute-start.2 = (bf16[32,2048]{1,0:T(8,128)(2,1)}, bf16[32,2048]{1,0:T(8,128)(2,1)S(1)}, u32[]{:S(2)}, u32[]{:S(2)}) collective-permute-start(bf16[32,2048]{1,0:T(8,128)(2,1)} %get-tuple-element.29), channel_id=1, source_target_pairs={{0,3},{2,1},{3,6},{7,2},{6,11},{10,7},{11,14},{15,10},{14,13},{12,... | collective-permute-start | bytes 393224 | tf_op jit(solution)/shard_map/ppermute | solution.py:390
  13.1 5.0 %collective-permute-start.1 = (bf16[32,2176]{1,0:T(8,128)(2,1)}, bf16[32,2176]{1,0:T(8,128)(2,1)S(1)}, u32[]{:S(2)}, u32[]{:S(2)}) collective-permute-start(bf16[32,2176]{1,0:T(8,128)(2,1)} %get-tuple-element.28.refs_1_), channel_id=1, source_target_pairs={{0,3},{2,1},{3,6},{7,2},{6,11},{10,7},{11,14},{15,10},{14,13},{12,... | collective-permute-start | bytes 417800 | tf_op jit(solution)/shard_map/ppermute | solution.py:388
  14.7 4.9 %collective-permute-start.3 = (bf16[32,2048]{1,0:T(8,128)(2,1)}, bf16[32,2048]{1,0:T(8,128)(2,1)S(1)}, u32[]{:S(2)}, u32[]{:S(2)}) collective-permute-start(bf16[32,2048]{1,0:T(8,128)(2,1)} %get-tuple-element.30), channel_id=1, source_target_pairs={{0,3},{2,1},{3,6},{7,2},{6,11},{10,7},{11,14},{15,10},{14,13},{12,... | collective-permute-start | bytes 393224 | tf_op jit(solution)/shard_map/ppermute | solution.py:390
  16.7 4.9 %collective-permute-start.9 = (bf16[32,2048]{1,0:T(8,128)(2,1)S(1)}, bf16[32,2048]{1,0:T(8,128)(2,1)S(1)}, u32[]{:S(2)}, u32[]{:S(2)}) collective-permute-start(bf16[32,2048]{1,0:T(8,128)(2,1)S(1)} %collective-permute-done.refs_2_), channel_id=1, source_target_pairs={{0,3},{2,1},{3,6},{7,2},{6,11},{10,7},{11,14},{15,10},{14,13},{12,... | collective-permute-start | bytes 393224 | tf_op jit(solution)/shard_map/ppermute | solution.py:388
  18.1 4.9 %collective-permute-start.10 = (bf16[32,2176]{1,0:T(8,128)(2,1)S(1)}, bf16[32,2176]{1,0:T(8,128)(2,1)S(1)}, u32[]{:S(2)}, u32[]{:S(2)}) collective-permute-start(bf16[32,2176]{1,0:T(8,128)(2,1)S(1)} %collective-permute-done.1.refs_3_), channel_id=1, source_target_pairs={{0,3},{2,1},{3,6},{7,2},{6,11},{10,7},{11,14},{15,10},{14,13},{12,... | collective-permute-start | bytes 417800 | tf_op jit(solution)/shard_map/ppermute | solution.py:388
  19.7 4.8 %collective-permute-start.11 = (bf16[32,2048]{1,0:T(8,128)(2,1)S(1)}, bf16[32,2048]{1,0:T(8,128)(2,1)S(1)}, u32[]{:S(2)}, u32[]{:S(2)}) collective-permute-start(bf16[32,2048]{1,0:T(8,128)(2,1)S(1)} %collective-permute-done.2.refs_4_), channel_id=1, source_target_pairs={{0,3},{2,1},{3,6},{7,2},{6,11},{10,7},{11,14},{15,10},{14,13},{12,... | collective-permute-start | bytes 393224 | tf_op jit(solution)/shard_map/ppermute | solution.py:390
  21.6 4.7 %collective-permute-start.13 = (bf16[32,2048]{1,0:T(8,128)(2,1)S(1)}, bf16[32,2048]{1,0:T(8,128)(2,1)S(1)}, u32[]{:S(2)}, u32[]{:S(2)}) collective-permute-start(bf16[32,2048]{1,0:T(8,128)(2,1)S(1)} %collective-permute-done.9.refs_0_), channel_id=1, source_target_pairs={{0,3},{2,1},{3,6},{7,2},{6,11},{10,7},{11,14},{15,10},{14,13},{12,... | collective-permute-start | bytes 393224 | tf_op jit(solution)/shard_map/ppermute | solution.py:388
  23.0 4.7 %collective-permute-start.14 = (bf16[32,2176]{1,0:T(8,128)(2,1)S(1)}, bf16[32,2176]{1,0:T(8,128)(2,1)S(1)}, u32[]{:S(2)}, u32[]{:S(2)}) collective-permute-start(bf16[32,2176]{1,0:T(8,128)(2,1)S(1)} %collective-permute-done.10.refs_1_), channel_id=1, source_target_pairs={{0,3},{2,1},{3,6},{7,2},{6,11},{10,7},{11,14},{15,10},{14,13},{12,... | collective-permute-start | bytes 417800 | tf_op jit(solution)/shard_map/ppermute | solution.py:388
  24.5 4.8 %collective-permute-start.12 = (bf16[32,2048]{1,0:T(8,128)(2,1)S(1)}, bf16[32,2048]{1,0:T(8,128)(2,1)S(1)}, u32[]{:S(2)}, u32[]{:S(2)}) collective-permute-start(bf16[32,2048]{1,0:T(8,128)(2,1)S(1)} %collective-permute-done.3.refs_5_), channel_id=1, source_target_pairs={{0,3},{2,1},{3,6},{7,2},{6,11},{10,7},{11,14},{15,10},{14,13},{12,... | collective-permute-start | bytes 393224 | tf_op jit(solution)/shard_map/ppermute | solution.py:390
  26.3 4.7 %collective-permute-start.17 = (bf16[32,2048]{1,0:T(8,128)(2,1)S(1)}, bf16[32,2048]{1,0:T(8,128)(2,1)S(1)}, u32[]{:S(2)}, u32[]{:S(2)}) collective-permute-start(bf16[32,2048]{1,0:T(8,128)(2,1)S(1)} %collective-permute-done.13.refs_0_), channel_id=1, source_target_pairs={{0,3},{2,1},{3,6},{7,2},{6,11},{10,7},{11,14},{15,10},{14,13},{12,... | collective-permute-start | bytes 393224 | tf_op jit(solution)/shard_map/ppermute | solution.py:388
  27.7 4.7 %collective-permute-start.18 = (bf16[32,2176]{1,0:T(8,128)(2,1)S(1)}, bf16[32,2176]{1,0:T(8,128)(2,1)S(1)}, u32[]{:S(2)}, u32[]{:S(2)}) collective-permute-start(bf16[32,2176]{1,0:T(8,128)(2,1)S(1)} %collective-permute-done.14.refs_1_), channel_id=1, source_target_pairs={{0,3},{2,1},{3,6},{7,2},{6,11},{10,7},{11,14},{15,10},{14,13},{12,... | collective-permute-start | bytes 417800 | tf_op jit(solution)/shard_map/ppermute | solution.py:388
  29.3 8.9 %collective-permute-start.15 = (bf16[32,2048]{1,0:T(8,128)(2,1)S(1)}, bf16[32,2048]{1,0:T(8,128)(2,1)S(1)}, u32[]{:S(2)}, u32[]{:S(2)}) collective-permute-start(bf16[32,2048]{1,0:T(8,128)(2,1)S(1)} %collective-permute-done.11.refs_2_), channel_id=1, source_target_pairs={{0,3},{2,1},{3,6},{7,2},{6,11},{10,7},{11,14},{15,10},{14,13},{12,... | collective-permute-start | bytes 393224 | tf_op jit(solution)/shard_map/ppermute | solution.py:390
  31.0 7.2 %collective-permute-start.16 = (bf16[32,2048]{1,0:T(8,128)(2,1)S(1)}, bf16[32,2048]{1,0:T(8,128)(2,1)S(1)}, u32[]{:S(2)}, u32[]{:S(2)}) collective-permute-start(bf16[32,2048]{1,0:T(8,128)(2,1)S(1)} %collective-permute-done.12.refs_3_), channel_id=1, source_target_pairs={{0,3},{2,1},{3,6},{7,2},{6,11},{10,7},{11,14},{15,10},{14,13},{12,... | collective-permute-start | bytes 393224 | tf_op jit(solution)/shard_map/ppermute | solution.py:390
  35.5 14.9 %collective-permute-start.19 = (bf16[32,2048]{1,0:T(8,128)(2,1)S(1)}, bf16[32,2048]{1,0:T(8,128)(2,1)S(1)}, u32[]{:S(2)}, u32[]{:S(2)}) collective-permute-start(bf16[32,2048]{1,0:T(8,128)(2,1)S(1)} %get-tuple-element.36), channel_id=1, source_target_pairs={{3,0},{1,2},{6,3},{2,7},{11,6},{7,10},{14,11},{10,15},{13,14},{15,... | collective-permute-start | bytes 393224 | tf_op jit(solution)/shard_map/ppermute | solution.py:425
  37.3 14.7 %collective-permute-start.23 = (bf16[32,2048]{1,0:T(8,128)(2,1)S(1)}, bf16[32,2048]{1,0:T(8,128)(2,1)S(1)}, u32[]{:S(2)}, u32[]{:S(2)}) collective-permute-start(bf16[32,2048]{1,0:T(8,128)(2,1)S(1)} %get-tuple-element.41), channel_id=1, source_target_pairs={{3,0},{1,2},{6,3},{2,7},{11,6},{7,10},{14,11},{10,15},{13,14},{15,... | collective-permute-start | bytes 393224 | tf_op jit(solution)/shard_map/ppermute | solution.py:425
  41.4 10.9 %collective-permute-start.27 = (bf16[32,2048]{1,0:T(8,128)(2,1)S(1)}, bf16[32,2048]{1,0:T(8,128)(2,1)S(1)}, u32[]{:S(2)}, u32[]{:S(2)}) collective-permute-start(bf16[32,2048]{1,0:T(8,128)(2,1)S(1)} %get-tuple-element.45), channel_id=1, source_target_pairs={{3,0},{1,2},{6,3},{2,7},{11,6},{7,10},{14,11},{10,15},{13,14},{15,... | collective-permute-start | bytes 393224 | tf_op jit(solution)/shard_map/ppermute | solution.py:417
  43.4 3.3 %copy-start = (bf16[32,2176]{1,0:T(8,128)(2,1)S(1)}, bf16[32,2176]{1,0:T(8,128)(2,1)}, u32[]{:S(2)}) copy-start(bf16[32,2176]{1,0:T(8,128)(2,1)} %get-tuple-element.28.refs_1_) | copy-start | bytes 417796
  43.5 3.3 %copy-start.1 = (bf16[32,2048]{1,0:T(8,128)(2,1)S(1)}, bf16[32,2048]{1,0:T(8,128)(2,1)}, u32[]{:S(2)}) copy-start(bf16[32,2048]{1,0:T(8,128)(2,1)} %get-tuple-element.27.refs_0_) | copy-start | bytes 393220
  43.5 9.4 %collective-permute-start.31 = (bf16[32,2048]{1,0:T(8,128)(2,1)S(1)}, bf16[32,2048]{1,0:T(8,128)(2,1)S(1)}, u32[]{:S(2)}, u32[]{:S(2)}) collective-permute-start(bf16[32,2048]{1,0:T(8,128)(2,1)S(1)} %get-tuple-element.48), channel_id=1, source_target_pairs={{3,0},{1,2},{6,3},{2,7},{11,6},{7,10},{14,11},{10,15},{13,14},{15,... | collective-permute-start | bytes 393224 | tf_op jit(solution)/shard_map/ppermute | solution.py:417
  50.5 4.4 %collective-permute-start.20 = (bf16[32,2048]{1,0:T(8,128)(2,1)S(1)}, bf16[32,2048]{1,0:T(8,128)(2,1)S(1)}, u32[]{:S(2)}, u32[]{:S(2)}) collective-permute-start(bf16[32,2048]{1,0:T(8,128)(2,1)S(1)} %add_convert_fusion.7), channel_id=1, source_target_pairs={{3,0},{1,2},{6,3},{2,7},{11,6},{7,10},{14,11},{10,15},{13,14},{15,... | collective-permute-start | bytes 393224 | tf_op jit(solution)/shard_map/ppermute | solution.py:425
  52.1 4.7 %collective-permute-start.24 = (bf16[32,2048]{1,0:T(8,128)(2,1)S(1)}, bf16[32,2048]{1,0:T(8,128)(2,1)S(1)}, u32[]{:S(2)}, u32[]{:S(2)}) collective-permute-start(bf16[32,2048]{1,0:T(8,128)(2,1)S(1)} %add_convert_fusion.5), channel_id=1, source_target_pairs={{3,0},{1,2},{6,3},{2,7},{11,6},{7,10},{14,11},{10,15},{13,14},{15,... | collective-permute-start | bytes 393224 | tf_op jit(solution)/shard_map/ppermute | solution.py:425
  52.3 5.9 %collective-permute-start.28 = (bf16[32,2048]{1,0:T(8,128)(2,1)S(1)}, bf16[32,2048]{1,0:T(8,128)(2,1)S(1)}, u32[]{:S(2)}, u32[]{:S(2)}) collective-permute-start(bf16[32,2048]{1,0:T(8,128)(2,1)S(1)} %add_convert_fusion.3), channel_id=1, source_target_pairs={{3,0},{1,2},{6,3},{2,7},{11,6},{7,10},{14,11},{10,15},{13,14},{15,... | collective-permute-start | bytes 393224 | tf_op jit(solution)/shard_map/ppermute | solution.py:417
  52.9 6.7 %collective-permute-start.32 = (bf16[32,2048]{1,0:T(8,128)(2,1)S(1)}, bf16[32,2048]{1,0:T(8,128)(2,1)S(1)}, u32[]{:S(2)}, u32[]{:S(2)}) collective-permute-start(bf16[32,2048]{1,0:T(8,128)(2,1)S(1)} %add_convert_fusion.1), channel_id=1, source_target_pairs={{3,0},{1,2},{6,3},{2,7},{11,6},{7,10},{14,11},{10,15},{13,14},{15,... | collective-permute-start | bytes 393224 | tf_op jit(solution)/shard_map/ppermute | solution.py:417
  54.9 6.1 %collective-permute-start.21 = (bf16[32,2048]{1,0:T(8,128)(2,1)S(1)}, bf16[32,2048]{1,0:T(8,128)(2,1)S(1)}, u32[]{:S(2)}, u32[]{:S(2)}) collective-permute-start(bf16[32,2048]{1,0:T(8,128)(2,1)S(1)} %add_convert_fusion.6), channel_id=1, source_target_pairs={{3,0},{1,2},{6,3},{2,7},{11,6},{7,10},{14,11},{10,15},{13,14},{15,... | collective-permute-start | bytes 393224 | tf_op jit(solution)/shard_map/ppermute | solution.py:432
  56.9 5.9 %collective-permute-start.25 = (bf16[32,2048]{1,0:T(8,128)(2,1)S(1)}, bf16[32,2048]{1,0:T(8,128)(2,1)S(1)}, u32[]{:S(2)}, u32[]{:S(2)}) collective-permute-start(bf16[32,2048]{1,0:T(8,128)(2,1)S(1)} %add_convert_fusion.4), channel_id=1, source_target_pairs={{3,0},{1,2},{6,3},{2,7},{11,6},{7,10},{14,11},{10,15},{13,14},{15,... | collective-permute-start | bytes 393224 | tf_op jit(solution)/shard_map/ppermute | solution.py:432
  58.3 5.6 %collective-permute-start.29 = (bf16[32,2048]{1,0:T(8,128)(2,1)S(1)}, bf16[32,2048]{1,0:T(8,128)(2,1)S(1)}, u32[]{:S(2)}, u32[]{:S(2)}) collective-permute-start(bf16[32,2048]{1,0:T(8,128)(2,1)S(1)} %add_convert_fusion.2), channel_id=1, source_target_pairs={{3,0},{1,2},{6,3},{2,7},{11,6},{7,10},{14,11},{10,15},{13,14},{15,... | collective-permute-start | bytes 393224 | tf_op jit(solution)/shard_map/ppermute | solution.py:417
  59.7 5.4 %collective-permute-start.33 = (bf16[32,2048]{1,0:T(8,128)(2,1)S(1)}, bf16[32,2048]{1,0:T(8,128)(2,1)S(1)}, u32[]{:S(2)}, u32[]{:S(2)}) collective-permute-start(bf16[32,2048]{1,0:T(8,128)(2,1)S(1)} %add_convert_fusion), channel_id=1, source_target_pairs={{3,0},{1,2},{6,3},{2,7},{11,6},{7,10},{14,11},{10,15},{13,14},{15,... | collective-permute-start | bytes 393224 | tf_op jit(solution)/shard_map/ppermute | solution.py:417
  61.0 5.5 %collective-permute-start.8 = (bf16[64,1024]{1,0:T(8,128)(2,1)S(1)}, bf16[64,1024]{1,0:T(8,128)(2,1)S(1)}, u32[]{:S(2)}, u32[]{:S(2)}) collective-permute-start(bf16[64,1024]{1,0:T(8,128)(2,1)S(1)} %get-tuple-element.32), channel_id=1, source_target_pairs={{0,1},{1,0},{2,3},{3,2},{4,5},{5,4},{6,7},{7,6},{8,9},{9,8},{10,11... | collective-permute-start | bytes 393224 | tf_op jit(solution)/shard_map/ppermute | solution.py:414
  61.1 5.9 %collective-permute-start.22 = (bf16[32,1024]{1,0:T(8,128)(2,1)S(1)}, bf16[32,1024]{1,0:T(8,128)(2,1)S(1)}, u32[]{:S(2)}, u32[]{:S(2)}) collective-permute-start(bf16[32,1024]{1,0:T(8,128)(2,1)S(1)} %get-tuple-element.37), channel_id=1, source_target_pairs={{3,0},{1,2},{6,3},{2,7},{11,6},{7,10},{14,11},{10,15},{13,14},{15,... | collective-permute-start | bytes 196616 | tf_op jit(solution)/shard_map/ppermute | solution.py:434
  62.8 5.7 %collective-permute-start.26 = (bf16[32,1024]{1,0:T(8,128)(2,1)S(1)}, bf16[32,1024]{1,0:T(8,128)(2,1)S(1)}, u32[]{:S(2)}, u32[]{:S(2)}) collective-permute-start(bf16[32,1024]{1,0:T(8,128)(2,1)S(1)} %get-tuple-element.42), channel_id=1, source_target_pairs={{3,0},{1,2},{6,3},{2,7},{11,6},{7,10},{14,11},{10,15},{13,14},{15,... | collective-permute-start | bytes 196616 | tf_op jit(solution)/shard_map/ppermute | solution.py:434
  63.9 4.7 %collective-permute-start.30 = (bf16[32,1024]{1,0:T(8,128)(2,1)S(1)}, bf16[32,1024]{1,0:T(8,128)(2,1)S(1)}, u32[]{:S(2)}, u32[]{:S(2)}) collective-permute-start(bf16[32,1024]{1,0:T(8,128)(2,1)S(1)} %shard_map.93), channel_id=1, source_target_pairs={{0,1},{1,0},{2,3},{3,2},{4,5},{5,4},{6,7},{7,6},{8,9},{9,8},{10,11... | collective-permute-start | bytes 196616 | tf_op jit(solution)/shard_map/ppermute | solution.py:423
  65.1 3.4 %collective-permute-start.34 = (bf16[32,1024]{1,0:T(8,128)(2,1)S(1)}, bf16[32,1024]{1,0:T(8,128)(2,1)S(1)}, u32[]{:S(2)}, u32[]{:S(2)}) collective-permute-start(bf16[32,1024]{1,0:T(8,128)(2,1)S(1)} %shard_map.94), channel_id=1, source_target_pairs={{0,1},{1,0},{2,3},{3,2},{4,5},{5,4},{6,7},{7,6},{8,9},{9,8},{10,11... | collective-permute-start | bytes 196616 | tf_op jit(solution)/shard_map/ppermute | solution.py:423
  66.5 4.3 %collective-permute-start.35 = (bf16[32,1024]{1,0:T(8,128)(2,1)S(1)}, bf16[32,1024]{1,0:T(8,128)(2,1)S(1)}, u32[]{:S(2)}, u32[]{:S(2)}) collective-permute-start(bf16[32,1024]{1,0:T(8,128)(2,1)S(1)} %get-tuple-element.49), channel_id=1, source_target_pairs={{3,1},{1,3},{6,2},{2,6},{11,7},{7,11},{14,10},{10,14},{13,15},{15,... | collective-permute-start | bytes 196616 | tf_op jit(solution)/shard_map/ppermute | solution.py:435
  67.0 4.5 %collective-permute-start.36 = (bf16[32,1024]{1,0:T(8,128)(2,1)S(1)}, bf16[32,1024]{1,0:T(8,128)(2,1)S(1)}, u32[]{:S(2)}, u32[]{:S(2)}) collective-permute-start(bf16[32,1024]{1,0:T(8,128)(2,1)S(1)} %get-tuple-element.50), channel_id=1, source_target_pairs={{3,1},{1,3},{6,2},{2,6},{11,7},{7,11},{14,10},{10,14},{13,15},{15,... | collective-permute-start | bytes 196616 | tf_op jit(solution)/shard_map/ppermute | solution.py:435

commit v6 on v5

--- a/solution.py
+++ b/solution.py
@@ -334,17 +334,23 @@
 
 def finish_kernel(pieces, own, own_pair, *refs):
     arrived, second_pair, second, crossed = (refs[i * pieces : (i + 1) * pieces] for i in range(4))
-    mixed = refs[-1]
+    result, mixed, sems = refs[-3:]
     core = lax.axis_index("tensor")
     half = mixed.shape[2]
     size = own.shape[0] // pieces
     f32 = jnp.float32
+    copies = []
     for i in range(pieces):
         rows = slice(i * size, (i + 1) * size)
         total = own[rows] + arrived[i][...].astype(f32) + second_pair[i][...].astype(f32)
         mixed[core, rows] = total.astype(mixed.dtype)
         total = second[i][:, half_of(core, half)].astype(f32) + crossed[i][...].astype(f32)
         mixed[1 - core, rows] = (total + own_pair[rows].astype(f32)).astype(mixed.dtype)
+        piece = mixed.at[:, rows], result.at[:, rows]
+        copies.append(pltpu.make_async_copy(*piece, sems.at[i]))
+        copies[-1].start()
+    for copy in copies:
+        copy.wait()
 
 
 def finish(pieces, own, own_pair, *groups):
@@ -353,7 +359,11 @@
         functools.partial(finish_kernel, pieces),
         out_shape=jax.ShapeDtypeStruct((2, *own.shape), jnp.bfloat16),
         in_specs=[vmem] * (2 + 4 * pieces),
-        out_specs=vmem,
+        out_specs=pl.BlockSpec(memory_space=pltpu.HBM),
+        scratch_shapes=[
+            pltpu.VMEM((2, *own.shape), jnp.bfloat16),
+            pltpu.SemaphoreType.DMA((pieces,)),
+        ],
         compiler_params=pltpu.CompilerParams(vmem_limit_bytes=4 << 20),
     )(own, own_pair, *sum((list(g) for g in groups), []))
 
@@ -407,7 +417,10 @@
     )
     part_first[1], part_second[1] = made[:PIECES], made[PIECES:]
     for step in range(2, steps):
-        made = run([first[step] + second[step]], ranges(0, f32) + ranges(1, bf16 if step == steps - 1 else f32))
+        made = run(
+            [first[step] + second[step]],
+            ranges(0, f32) + ranges(1, bf16 if step == steps - 1 else f32),
+        )
         part_first[step], part_second[step] = made[:PIECES], made[PIECES:]
     sum_first = run([first[steps]], ranges(0, bf16))
     sum_second = part_second[steps - 1]

time: 72.4 us -> 72.4 us (level)
  no operation moved by 1% of the time
where the time goes in v6:
time: 72.4 us; the launch traced here: 72.2 us
  starting transfers between devices  45.2 us (62%)
  Pallas kernels  16.1 us (22%)
  waiting for transfers between devices  9.95 us (14%)
  between operations  0.78 us (1%)
    pallas_call x4, Pallas kernels, expert_rows(): pl.pallas_call(functools.partial(expert_kernel, tuple(sides), outlets, wi...  13.2 us
    ppermute x8, starting transfers between devices, by_ring(): first.append([lax.ppermute(first[-1][i], both, ahead) for i in each])  13 us
    ppermute x6, starting transfers between devices, by_ring(): second.append([lax.ppermute(second[-1][i], both, ahead) for i in each])  10.1 us
    ppermute x6, starting transfers between devices, by_ring(): sum_second = [lax.ppermute(sum_second[i], both, back) for i in each]  5.64 us
    ppermute x4, starting transfers between devices, by_ring(): sum_first = [lax.ppermute(sum_first[i], both, back) for i in each]  4.4 us
    ppermute x2, starting transfers between devices, by_ring(): last = lax.ppermute(sum_first[i], both, back)  3.25 us
    ppermute x1, waiting for transfers between devices, by_ring(): up_pair = lax.ppermute(up_own, 'tensor', swap)  3.17 us
    ppermute x2, waiting for transfers between devices, by_ring(): crossed.append(lax.ppermute(crosses, both, across))  2.92 us
  transfers between devices with their start and end apart: 37, of which 6 were waited for; matrix products, arithmetic and copies ran while one was open for 0% of the time, Pallas kernels for 21%

profile of v6, /device:TPU:0, one launch (start us, length us, event | category | flops | bytes accessed | tf_op | source)
XLA Modules:
  0.0 72.2 jit_solution(7659900163007342737)
XLA Ops:
  0.6 0.6 collective-permute-start.4
  1.2 0.1 collective-permute-start.6
  1.3 3.2 %collective-permute-done.4.refs_7_.refs_5_.refs_3_ = bf16[2048,384]{1,0:T(8,128)(2,1)S(1)} collective-permute-done((bf16[2048,384]{1,0:T(8,128)(2,1)}, bf16[2048,384]{1,0:T(8,128)(2,1)S(1)}, u32[]{:S(2)}, u32[]{:S(2)}) %collective-permute-start.4) | collective-permute-done | bytes 1572896 | tf_op jit(solution)/shard_map/ppermute | solution.py:402
  4.4 0.4 collective-permute-start.5
  4.8 1.9 %collective-permute-done.6.refs_9_.refs_7_.refs_5_ = bf16[768,1024]{1,0:T(8,128)(2,1)S(1)} collective-permute-done((bf16[768,1024]{1,0:T(8,128)(2,1)}, bf16[768,1024]{1,0:T(8,128)(2,1)S(1)}, u32[]{:S(2)}, u32[]{:S(2)}) %collective-permute-start.6) | collective-permute-done | bytes 1572896 | tf_op jit(solution)/shard_map/ppermute | solution.py:403
  6.7 0.4 collective-permute-start.7
  7.1 2.1 %shard_map.86 = (bf16[32,2048]{1,0:T(8,128)(2,1)}, bf16[32,2176]{1,0:T(8,128)(2,1)}, bf16[32,2048]{1,0:T(8,128)(2,1)}, bf16[32,2048]{1,0:T(8,128)(2,1)}, s32[2]{0:T(128)}) custom-call(s32[2,8,64]{2,1,0:T(8,128)} %bitcast.4, f32[2,8,64]{2,1,0:T(8,128)} %bitcast.5, s32[8]{0:T(128)} %old_in.1, s32[16]{0:T(128)} %new_in.1, bf16[2,64,2048]{2,1,0:T(8,128)(2,1)} %tokens.1), custom_call_target="tpu_custom_call" | custom-call | tf_op jit(solution)/shard_map/pallas_call | solution.py:211
  9.1 2.6 %collective-permute-start = (bf16[32,2048]{1,0:T(8,128)(2,1)}, bf16[32,2048]{1,0:T(8,128)(2,1)S(1)}, u32[]{:S(2)}, u32[]{:S(2)}) collective-permute-start(bf16[32,2048]{1,0:T(8,128)(2,1)} %get-tuple-element.27.refs_0_), channel_id=1, source_target_pairs={{0,3},{2,1},{3,6},{7,2},{6,11},{10,7},{11,14},{15,10},{14,13},{12,... | collective-permute-start | bytes 393224 | tf_op jit(solution)/shard_map/ppermute | solution.py:398
  11.8 1.3 %collective-permute-start.2 = (bf16[32,2048]{1,0:T(8,128)(2,1)}, bf16[32,2048]{1,0:T(8,128)(2,1)S(1)}, u32[]{:S(2)}, u32[]{:S(2)}) collective-permute-start(bf16[32,2048]{1,0:T(8,128)(2,1)} %get-tuple-element.29), channel_id=1, source_target_pairs={{0,3},{2,1},{3,6},{7,2},{6,11},{10,7},{11,14},{15,10},{14,13},{12,... | collective-permute-start | bytes 393224 | tf_op jit(solution)/shard_map/ppermute | solution.py:400
  13.1 1.6 %collective-permute-start.1 = (bf16[32,2176]{1,0:T(8,128)(2,1)}, bf16[32,2176]{1,0:T(8,128)(2,1)S(1)}, u32[]{:S(2)}, u32[]{:S(2)}) collective-permute-start(bf16[32,2176]{1,0:T(8,128)(2,1)} %get-tuple-element.28.refs_1_), channel_id=1, source_target_pairs={{0,3},{2,1},{3,6},{7,2},{6,11},{10,7},{11,14},{15,10},{14,13},{12,... | collective-permute-start | bytes 417800 | tf_op jit(solution)/shard_map/ppermute | solution.py:398
  14.7 0.1 collective-permute-done.refs_2_
  14.7 1.9 %collective-permute-start.3 = (bf16[32,2048]{1,0:T(8,128)(2,1)}, bf16[32,2048]{1,0:T(8,128)(2,1)S(1)}, u32[]{:S(2)}, u32[]{:S(2)}) collective-permute-start(bf16[32,2048]{1,0:T(8,128)(2,1)} %get-tuple-element.30), channel_id=1, source_target_pairs={{0,3},{2,1},{3,6},{7,2},{6,11},{10,7},{11,14},{15,10},{14,13},{12,... | collective-permute-start | bytes 393224 | tf_op jit(solution)/shard_map/ppermute | solution.py:400
  16.7 0.0 collective-permute-done.2.refs_4_
  16.7 1.4 %collective-permute-start.9 = (bf16[32,2048]{1,0:T(8,128)(2,1)S(1)}, bf16[32,2048]{1,0:T(8,128)(2,1)S(1)}, u32[]{:S(2)}, u32[]{:S(2)}) collective-permute-start(bf16[32,2048]{1,0:T(8,128)(2,1)S(1)} %collective-permute-done.refs_2_), channel_id=1, source_target_pairs={{0,3},{2,1},{3,6},{7,2},{6,11},{10,7},{11,14},{15,10},{14,13},{12,... | collective-permute-start | bytes 393224 | tf_op jit(solution)/shard_map/ppermute | solution.py:398
  18.1 1.6 %collective-permute-start.10 = (bf16[32,2176]{1,0:T(8,128)(2,1)S(1)}, bf16[32,2176]{1,0:T(8,128)(2,1)S(1)}, u32[]{:S(2)}, u32[]{:S(2)}) collective-permute-start(bf16[32,2176]{1,0:T(8,128)(2,1)S(1)} %collective-permute-done.1.refs_3_), channel_id=1, source_target_pairs={{0,3},{2,1},{3,6},{7,2},{6,11},{10,7},{11,14},{15,10},{14,13},{12,... | collective-permute-start | bytes 417800 | tf_op jit(solution)/shard_map/ppermute | solution.py:398
  19.7 0.0 collective-permute-done.3.refs_5_
  19.7 1.9 %collective-permute-start.11 = (bf16[32,2048]{1,0:T(8,128)(2,1)S(1)}, bf16[32,2048]{1,0:T(8,128)(2,1)S(1)}, u32[]{:S(2)}, u32[]{:S(2)}) collective-permute-start(bf16[32,2048]{1,0:T(8,128)(2,1)S(1)} %collective-permute-done.2.refs_4_), channel_id=1, source_target_pairs={{0,3},{2,1},{3,6},{7,2},{6,11},{10,7},{11,14},{15,10},{14,13},{12,... | collective-permute-start | bytes 393224 | tf_op jit(solution)/shard_map/ppermute | solution.py:400
  21.6 1.4 %collective-permute-start.13 = (bf16[32,2048]{1,0:T(8,128)(2,1)S(1)}, bf16[32,2048]{1,0:T(8,128)(2,1)S(1)}, u32[]{:S(2)}, u32[]{:S(2)}) collective-permute-start(bf16[32,2048]{1,0:T(8,128)(2,1)S(1)} %collective-permute-done.9.refs_0_), channel_id=1, source_target_pairs={{0,3},{2,1},{3,6},{7,2},{6,11},{10,7},{11,14},{15,10},{14,13},{12,... | collective-permute-start | bytes 393224 | tf_op jit(solution)/shard_map/ppermute | solution.py:398
  23.0 0.0 collective-permute-done.10.refs_1_
  23.0 1.5 %collective-permute-start.14 = (bf16[32,2176]{1,0:T(8,128)(2,1)S(1)}, bf16[32,2176]{1,0:T(8,128)(2,1)S(1)}, u32[]{:S(2)}, u32[]{:S(2)}) collective-permute-start(bf16[32,2176]{1,0:T(8,128)(2,1)S(1)} %collective-permute-done.10.refs_1_), channel_id=1, source_target_pairs={{0,3},{2,1},{3,6},{7,2},{6,11},{10,7},{11,14},{15,10},{14,13},{12,... | collective-permute-start | bytes 417800 | tf_op jit(solution)/shard_map/ppermute | solution.py:398
  24.5 0.0 collective-permute-done.11.refs_2_
  24.5 1.8 %collective-permute-start.12 = (bf16[32,2048]{1,0:T(8,128)(2,1)S(1)}, bf16[32,2048]{1,0:T(8,128)(2,1)S(1)}, u32[]{:S(2)}, u32[]{:S(2)}) collective-permute-start(bf16[32,2048]{1,0:T(8,128)(2,1)S(1)} %collective-permute-done.3.refs_5_), channel_id=1, source_target_pairs={{0,3},{2,1},{3,6},{7,2},{6,11},{10,7},{11,14},{15,10},{14,13},{12,... | collective-permute-start | bytes 393224 | tf_op jit(solution)/shard_map/ppermute | solution.py:400
  26.3 1.4 %collective-permute-start.17 = (bf16[32,2048]{1,0:T(8,128)(2,1)S(1)}, bf16[32,2048]{1,0:T(8,128)(2,1)S(1)}, u32[]{:S(2)}, u32[]{:S(2)}) collective-permute-start(bf16[32,2048]{1,0:T(8,128)(2,1)S(1)} %collective-permute-done.13.refs_0_), channel_id=1, source_target_pairs={{0,3},{2,1},{3,6},{7,2},{6,11},{10,7},{11,14},{15,10},{14,13},{12,... | collective-permute-start | bytes 393224 | tf_op jit(solution)/shard_map/ppermute | solution.py:398
  27.7 0.0 collective-permute-done.14.refs_1_
  27.7 1.6 %collective-permute-start.18 = (bf16[32,2176]{1,0:T(8,128)(2,1)S(1)}, bf16[32,2176]{1,0:T(8,128)(2,1)S(1)}, u32[]{:S(2)}, u32[]{:S(2)}) collective-permute-start(bf16[32,2176]{1,0:T(8,128)(2,1)S(1)} %collective-permute-done.14.refs_1_), channel_id=1, source_target_pairs={{0,3},{2,1},{3,6},{7,2},{6,11},{10,7},{11,14},{15,10},{14,13},{12,... | collective-permute-start | bytes 417800 | tf_op jit(solution)/shard_map/ppermute | solution.py:398
  29.3 0.0 collective-permute-done.12.refs_3_
  29.3 1.7 %collective-permute-start.15 = (bf16[32,2048]{1,0:T(8,128)(2,1)S(1)}, bf16[32,2048]{1,0:T(8,128)(2,1)S(1)}, u32[]{:S(2)}, u32[]{:S(2)}) collective-permute-start(bf16[32,2048]{1,0:T(8,128)(2,1)S(1)} %collective-permute-done.11.refs_2_), channel_id=1, source_target_pairs={{0,3},{2,1},{3,6},{7,2},{6,11},{10,7},{11,14},{15,10},{14,13},{12,... | collective-permute-start | bytes 393224 | tf_op jit(solution)/shard_map/ppermute | solution.py:400
  31.0 1.4 %collective-permute-start.16 = (bf16[32,2048]{1,0:T(8,128)(2,1)S(1)}, bf16[32,2048]{1,0:T(8,128)(2,1)S(1)}, u32[]{:S(2)}, u32[]{:S(2)}) collective-permute-start(bf16[32,2048]{1,0:T(8,128)(2,1)S(1)} %collective-permute-done.12.refs_3_), channel_id=1, source_target_pairs={{0,3},{2,1},{3,6},{7,2},{6,11},{10,7},{11,14},{15,10},{14,13},{12,... | collective-permute-start | bytes 393224 | tf_op jit(solution)/shard_map/ppermute | solution.py:400
  32.4 0.0 collective-permute-done.18.refs_1_
  32.4 0.0 collective-permute-done.5.refs_6_.refs_4_.refs_2_
  32.4 0.0 collective-permute-done.7.refs_8_.refs_6_.refs_4_
  32.4 3.2 %shard_map.90 = (bf16[32,2048]{1,0:T(8,128)(2,1)S(1)}, bf16[32,2048]{1,0:T(8,128)(2,1)S(1)}) custom-call(bf16[32,2048]{1,0:T(8,128)(2,1)S(1)} %collective-permute-done.17.refs_0_, bf16[32,2176]{1,0:T(8,128)(2,1)S(1)} %collective-permute-done.18.refs_1_, bf16[2048,384]{1,0:T(8,128)(2,1)} %collective-permute-done.5.refs_6_.refs_4_.refs_2_, ...), custom_call_target="tpu_custom_call" | custom-call | flops 402653184 | bytes 1048576 | tf_op jit(solution)/shard_map/pallas_call | solution.py:286
  35.5 1.8 %collective-permute-start.19 = (bf16[32,2048]{1,0:T(8,128)(2,1)S(1)}, bf16[32,2048]{1,0:T(8,128)(2,1)S(1)}, u32[]{:S(2)}, u32[]{:S(2)}) collective-permute-start(bf16[32,2048]{1,0:T(8,128)(2,1)S(1)} %get-tuple-element.36), channel_id=1, source_target_pairs={{3,0},{1,2},{6,3},{2,7},{11,6},{7,10},{14,11},{10,15},{13,14},{15,... | collective-permute-start | bytes 393224 | tf_op jit(solution)/shard_map/ppermute | solution.py:438
  37.3 0.8 %collective-permute-start.23 = (bf16[32,2048]{1,0:T(8,128)(2,1)S(1)}, bf16[32,2048]{1,0:T(8,128)(2,1)S(1)}, u32[]{:S(2)}, u32[]{:S(2)}) collective-permute-start(bf16[32,2048]{1,0:T(8,128)(2,1)S(1)} %get-tuple-element.41), channel_id=1, source_target_pairs={{3,0},{1,2},{6,3},{2,7},{11,6},{7,10},{14,11},{10,15},{13,14},{15,... | collective-permute-start | bytes 393224 | tf_op jit(solution)/shard_map/ppermute | solution.py:438
  38.2 0.0 collective-permute-done.16.refs_3_
  38.2 3.2 %shard_map.89 = (f32[32,2048]{1,0:T(8,128)S(1)}, f32[32,2048]{1,0:T(8,128)S(1)}, bf16[32,2048]{1,0:T(8,128)(2,1)S(1)}, bf16[32,2048]{1,0:T(8,128)(2,1)S(1)}) custom-call(bf16[32,2048]{1,0:T(8,128)(2,1)S(1)} %collective-permute-done.13.refs_0_, bf16[32,2176]{1,0:T(8,128)(2,1)S(1)} %collective-permute-done.14.refs_1_, ...), custom_call_target="tpu_custom_call" | custom-call | flops 805306368 | bytes 2097152 | tf_op jit(solution)/shard_map/pallas_call | solution.py:286
  41.4 2.1 %collective-permute-start.27 = (bf16[32,2048]{1,0:T(8,128)(2,1)S(1)}, bf16[32,2048]{1,0:T(8,128)(2,1)S(1)}, u32[]{:S(2)}, u32[]{:S(2)}) collective-permute-start(bf16[32,2048]{1,0:T(8,128)(2,1)S(1)} %get-tuple-element.45), channel_id=1, source_target_pairs={{3,0},{1,2},{6,3},{2,7},{11,6},{7,10},{14,11},{10,15},{13,14},{15,... | collective-permute-start | bytes 393224 | tf_op jit(solution)/shard_map/ppermute | solution.py:430
  43.5 0.1 collective-permute-start.31
  43.5 3.2 %shard_map.88 = (f32[32,2048]{1,0:T(8,128)S(1)}, f32[32,2048]{1,0:T(8,128)S(1)}, f32[32,2048]{1,0:T(8,128)S(1)}, f32[32,2048]{1,0:T(8,128)S(1)}) custom-call(bf16[32,2048]{1,0:T(8,128)(2,1)S(1)} %collective-permute-done.9.refs_0_, bf16[32,2176]{1,0:T(8,128)(2,1)S(1)} %collective-permute-done.10.refs_1_, ...), custom_call_target="tpu_custom_call" | custom-call | flops 805306368 | bytes 2097152 | tf_op jit(solution)/shard_map/pallas_call | solution.py:286
  46.7 3.7 %shard_map.87 = (f32[64,1024]{1,0:T(8,128)S(1)}, bf16[64,1024]{1,0:T(8,128)(2,1)S(1)}, f32[32,2048]{1,0:T(8,128)S(1)}, f32[32,2048]{1,0:T(8,128)S(1)}, f32[32,2048]{1,0:T(8,128)S(1)}, /*index=5*/f32[32,2048]{1,0:T(8,128)S(1)}) custom-call(bf16[32,2048]{1,0:T(8,128)(2,1)S(1)} %copy-done.1, bf16[32,2176]{1,0:T(8,128)(2,1)S(1)} %copy-done, ...), custom_call_target="tpu_custom_call" | custom-call | flops 1207959552 | bytes 3145728 | tf_op jit(solution)/shard_map/pallas_call | solution.py:286
  50.4 0.0 collective-permute-done.19
  50.5 1.6 %collective-permute-start.20 = (bf16[32,2048]{1,0:T(8,128)(2,1)S(1)}, bf16[32,2048]{1,0:T(8,128)(2,1)S(1)}, u32[]{:S(2)}, u32[]{:S(2)}) collective-permute-start(bf16[32,2048]{1,0:T(8,128)(2,1)S(1)} %add_convert_fusion.7), channel_id=1, source_target_pairs={{3,0},{1,2},{6,3},{2,7},{11,6},{7,10},{14,11},{10,15},{13,14},{15,... | collective-permute-start | bytes 393224 | tf_op jit(solution)/shard_map/ppermute | solution.py:438
  52.0 0.0 collective-permute-done.23
  52.1 0.2 collective-permute-start.24
  52.3 0.5 collective-permute-start.28
  52.9 0.0 collective-permute-done.31
  52.9 0.2 collective-permute-start.32
  53.1 1.8 %collective-permute-done.20 = bf16[32,2048]{1,0:T(8,128)(2,1)S(1)} collective-permute-done((bf16[32,2048]{1,0:T(8,128)(2,1)S(1)}, bf16[32,2048]{1,0:T(8,128)(2,1)S(1)}, u32[]{:S(2)}, u32[]{:S(2)}) %collective-permute-start.20) | collective-permute-done | bytes 131104 | tf_op jit(solution)/shard_map/ppermute | solution.py:438
  54.9 1.9 %collective-permute-start.21 = (bf16[32,2048]{1,0:T(8,128)(2,1)S(1)}, bf16[32,2048]{1,0:T(8,128)(2,1)S(1)}, u32[]{:S(2)}, u32[]{:S(2)}) collective-permute-start(bf16[32,2048]{1,0:T(8,128)(2,1)S(1)} %add_convert_fusion.6), channel_id=1, source_target_pairs={{3,0},{1,2},{6,3},{2,7},{11,6},{7,10},{14,11},{10,15},{13,14},{15,... | collective-permute-start | bytes 393224 | tf_op jit(solution)/shard_map/ppermute | solution.py:445
  56.8 0.0 collective-permute-done.24
  56.9 1.4 %collective-permute-start.25 = (bf16[32,2048]{1,0:T(8,128)(2,1)S(1)}, bf16[32,2048]{1,0:T(8,128)(2,1)S(1)}, u32[]{:S(2)}, u32[]{:S(2)}) collective-permute-start(bf16[32,2048]{1,0:T(8,128)(2,1)S(1)} %add_convert_fusion.4), channel_id=1, source_target_pairs={{3,0},{1,2},{6,3},{2,7},{11,6},{7,10},{14,11},{10,15},{13,14},{15,... | collective-permute-start | bytes 393224 | tf_op jit(solution)/shard_map/ppermute | solution.py:445
  58.3 1.4 %collective-permute-start.29 = (bf16[32,2048]{1,0:T(8,128)(2,1)S(1)}, bf16[32,2048]{1,0:T(8,128)(2,1)S(1)}, u32[]{:S(2)}, u32[]{:S(2)}) collective-permute-start(bf16[32,2048]{1,0:T(8,128)(2,1)S(1)} %add_convert_fusion.2), channel_id=1, source_target_pairs={{3,0},{1,2},{6,3},{2,7},{11,6},{7,10},{14,11},{10,15},{13,14},{15,... | collective-permute-start | bytes 393224 | tf_op jit(solution)/shard_map/ppermute | solution.py:430
  59.7 1.4 %collective-permute-start.33 = (bf16[32,2048]{1,0:T(8,128)(2,1)S(1)}, bf16[32,2048]{1,0:T(8,128)(2,1)S(1)}, u32[]{:S(2)}, u32[]{:S(2)}) collective-permute-start(bf16[32,2048]{1,0:T(8,128)(2,1)S(1)} %add_convert_fusion), channel_id=1, source_target_pairs={{3,0},{1,2},{6,3},{2,7},{11,6},{7,10},{14,11},{10,15},{13,14},{15,... | collective-permute-start | bytes 393224 | tf_op jit(solution)/shard_map/ppermute | solution.py:430
  61.0 0.0 collective-permute-start.8
  61.0 0.0 collective-permute-done.21.arrived
  61.1 1.7 %collective-permute-start.22 = (bf16[32,1024]{1,0:T(8,128)(2,1)S(1)}, bf16[32,1024]{1,0:T(8,128)(2,1)S(1)}, u32[]{:S(2)}, u32[]{:S(2)}) collective-permute-start(bf16[32,1024]{1,0:T(8,128)(2,1)S(1)} %get-tuple-element.37), channel_id=1, source_target_pairs={{3,0},{1,2},{6,3},{2,7},{11,6},{7,10},{14,11},{10,15},{13,14},{15,... | collective-permute-start | bytes 196616 | tf_op jit(solution)/shard_map/ppermute | solution.py:447
  62.8 1.0 %collective-permute-start.26 = (bf16[32,1024]{1,0:T(8,128)(2,1)S(1)}, bf16[32,1024]{1,0:T(8,128)(2,1)S(1)}, u32[]{:S(2)}, u32[]{:S(2)}) collective-permute-start(bf16[32,1024]{1,0:T(8,128)(2,1)S(1)} %get-tuple-element.42), channel_id=1, source_target_pairs={{3,0},{1,2},{6,3},{2,7},{11,6},{7,10},{14,11},{10,15},{13,14},{15,... | collective-permute-start | bytes 196616 | tf_op jit(solution)/shard_map/ppermute | solution.py:447
  63.9 1.2 %collective-permute-start.30 = (bf16[32,1024]{1,0:T(8,128)(2,1)S(1)}, bf16[32,1024]{1,0:T(8,128)(2,1)S(1)}, u32[]{:S(2)}, u32[]{:S(2)}) collective-permute-start(bf16[32,1024]{1,0:T(8,128)(2,1)S(1)} %shard_map.93), channel_id=1, source_target_pairs={{0,1},{1,0},{2,3},{3,2},{4,5},{5,4},{6,7},{7,6},{8,9},{9,8},{10,11... | collective-permute-start | bytes 196616 | tf_op jit(solution)/shard_map/ppermute | solution.py:436
  65.1 1.4 %collective-permute-start.34 = (bf16[32,1024]{1,0:T(8,128)(2,1)S(1)}, bf16[32,1024]{1,0:T(8,128)(2,1)S(1)}, u32[]{:S(2)}, u32[]{:S(2)}) collective-permute-start(bf16[32,1024]{1,0:T(8,128)(2,1)S(1)} %shard_map.94), channel_id=1, source_target_pairs={{0,1},{1,0},{2,3},{3,2},{4,5},{5,4},{6,7},{7,6},{8,9},{9,8},{10,11... | collective-permute-start | bytes 196616 | tf_op jit(solution)/shard_map/ppermute | solution.py:436
  66.5 0.5 collective-permute-start.35
  67.0 1.5 %collective-permute-start.36 = (bf16[32,1024]{1,0:T(8,128)(2,1)S(1)}, bf16[32,1024]{1,0:T(8,128)(2,1)S(1)}, u32[]{:S(2)}, u32[]{:S(2)}) collective-permute-start(bf16[32,1024]{1,0:T(8,128)(2,1)S(1)} %get-tuple-element.50), channel_id=1, source_target_pairs={{3,1},{1,3},{6,2},{2,6},{11,7},{7,11},{14,10},{10,14},{13,15},{15,... | collective-permute-start | bytes 196616 | tf_op jit(solution)/shard_map/ppermute | solution.py:448
  68.5 2.2 %collective-permute-done.35.refs_6_ = bf16[32,1024]{1,0:T(8,128)(2,1)S(1)} collective-permute-done((bf16[32,1024]{1,0:T(8,128)(2,1)S(1)}, bf16[32,1024]{1,0:T(8,128)(2,1)S(1)}, u32[]{:S(2)}, u32[]{:S(2)}) %collective-permute-start.35) | collective-permute-done | bytes 65568 | tf_op jit(solution)/shard_map/ppermute | solution.py:448
  70.8 0.7 collective-permute-done.36.refs_7_
  71.5 0.8 %shard_map.95 = bf16[2,64,1024]{2,1,0:T(8,128)(2,1)} custom-call(f32[64,1024]{1,0:T(8,128)S(1)} %get-tuple-element.31.own, bf16[64,1024]{1,0:T(8,128)(2,1)S(1)} %collective-permute-done.8.own_pair, bf16[32,1024]{1,0:T(8,128)(2,1)S(1)} %collective-permute-done.22.refs_0_, bf16[32,1024]{1,0:T(8,128)(2,1)S(1)} %collective-permute-done.26.refs_1_, ...), custom_call_target="tpu_custom_call" | custom-call | tf_op jit(solution)/shard_map/pallas_call | solution.py:358
  (32 shorter events, 0.4 us)
Async XLA Ops:
  0.6 3.8 %collective-permute-start.4 = (bf16[2048,384]{1,0:T(8,128)(2,1)}, bf16[2048,384]{1,0:T(8,128)(2,1)S(1)}, u32[]{:S(2)}, u32[]{:S(2)}) collective-permute-start(bf16[2048,384]{1,0:T(8,128)(2,1)} %bitcast.6), channel_id=1, source_target_pairs={{0,1},{1,0},{2,3},{3,2},{4,5},{5,4},{6,7},{7,6},{8,9},{9,8},{10,11... | collective-permute-start | bytes 4718600 | tf_op jit(solution)/shard_map/ppermute | solution.py:402
  1.2 5.5 %collective-permute-start.6 = (bf16[768,1024]{1,0:T(8,128)(2,1)}, bf16[768,1024]{1,0:T(8,128)(2,1)S(1)}, u32[]{:S(2)}, u32[]{:S(2)}) collective-permute-start(bf16[768,1024]{1,0:T(8,128)(2,1)} %bitcast.7), channel_id=1, source_target_pairs={{0,1},{1,0},{2,3},{3,2},{4,5},{5,4},{6,7},{7,6},{8,9},{9,8},{10,11... | collective-permute-start | bytes 4718600 | tf_op jit(solution)/shard_map/ppermute | solution.py:403
  4.4 27.9 %collective-permute-start.5 = (bf16[2048,384]{1,0:T(8,128)(2,1)S(1)}, bf16[2048,384]{1,0:T(8,128)(2,1)}, u32[]{:S(2)}, u32[]{:S(2)}) collective-permute-start(bf16[2048,384]{1,0:T(8,128)(2,1)S(1)} %collective-permute-done.4.refs_7_.refs_5_.refs_3_), channel_id=1, source_target_pairs={{0,1},{1,0},{2,3},{3,2},{4,5},{5,4},{6,7},{7,6},{8,9},{9,8},{10,11... | collective-permute-start | bytes 4718600 | tf_op jit(solution)/shard_map/ppermute | solution.py:404
  6.7 25.7 %collective-permute-start.7 = (bf16[768,1024]{1,0:T(8,128)(2,1)S(1)}, bf16[768,1024]{1,0:T(8,128)(2,1)}, u32[]{:S(2)}, u32[]{:S(2)}) collective-permute-start(bf16[768,1024]{1,0:T(8,128)(2,1)S(1)} %collective-permute-done.6.refs_9_.refs_7_.refs_5_), channel_id=1, source_target_pairs={{0,1},{1,0},{2,3},{3,2},{4,5},{5,4},{6,7},{7,6},{8,9},{9,8},{10,11... | collective-permute-start | bytes 4718600 | tf_op jit(solution)/shard_map/ppermute | solution.py:405
  9.1 5.6 %collective-permute-start = (bf16[32,2048]{1,0:T(8,128)(2,1)}, bf16[32,2048]{1,0:T(8,128)(2,1)S(1)}, u32[]{:S(2)}, u32[]{:S(2)}) collective-permute-start(bf16[32,2048]{1,0:T(8,128)(2,1)} %get-tuple-element.27.refs_0_), channel_id=1, source_target_pairs={{0,3},{2,1},{3,6},{7,2},{6,11},{10,7},{11,14},{15,10},{14,13},{12,... | collective-permute-start | bytes 393224 | tf_op jit(solution)/shard_map/ppermute | solution.py:398
  11.8 4.9 %collective-permute-start.2 = (bf16[32,2048]{1,0:T(8,128)(2,1)}, bf16[32,2048]{1,0:T(8,128)(2,1)S(1)}, u32[]{:S(2)}, u32[]{:S(2)}) collective-permute-start(bf16[32,2048]{1,0:T(8,128)(2,1)} %get-tuple-element.29), channel_id=1, source_target_pairs={{0,3},{2,1},{3,6},{7,2},{6,11},{10,7},{11,14},{15,10},{14,13},{12,... | collective-permute-start | bytes 393224 | tf_op jit(solution)/shard_map/ppermute | solution.py:400
  13.1 5.0 %collective-permute-start.1 = (bf16[32,2176]{1,0:T(8,128)(2,1)}, bf16[32,2176]{1,0:T(8,128)(2,1)S(1)}, u32[]{:S(2)}, u32[]{:S(2)}) collective-permute-start(bf16[32,2176]{1,0:T(8,128)(2,1)} %get-tuple-element.28.refs_1_), channel_id=1, source_target_pairs={{0,3},{2,1},{3,6},{7,2},{6,11},{10,7},{11,14},{15,10},{14,13},{12,... | collective-permute-start | bytes 417800 | tf_op jit(solution)/shard_map/ppermute | solution.py:398
  14.7 4.9 %collective-permute-start.3 = (bf16[32,2048]{1,0:T(8,128)(2,1)}, bf16[32,2048]{1,0:T(8,128)(2,1)S(1)}, u32[]{:S(2)}, u32[]{:S(2)}) collective-permute-start(bf16[32,2048]{1,0:T(8,128)(2,1)} %get-tuple-element.30), channel_id=1, source_target_pairs={{0,3},{2,1},{3,6},{7,2},{6,11},{10,7},{11,14},{15,10},{14,13},{12,... | collective-permute-start | bytes 393224 | tf_op jit(solution)/shard_map/ppermute | solution.py:400
  16.7 4.9 %collective-permute-start.9 = (bf16[32,2048]{1,0:T(8,128)(2,1)S(1)}, bf16[32,2048]{1,0:T(8,128)(2,1)S(1)}, u32[]{:S(2)}, u32[]{:S(2)}) collective-permute-start(bf16[32,2048]{1,0:T(8,128)(2,1)S(1)} %collective-permute-done.refs_2_), channel_id=1, source_target_pairs={{0,3},{2,1},{3,6},{7,2},{6,11},{10,7},{11,14},{15,10},{14,13},{12,... | collective-permute-start | bytes 393224 | tf_op jit(solution)/shard_map/ppermute | solution.py:398
  18.1 4.9 %collective-permute-start.10 = (bf16[32,2176]{1,0:T(8,128)(2,1)S(1)}, bf16[32,2176]{1,0:T(8,128)(2,1)S(1)}, u32[]{:S(2)}, u32[]{:S(2)}) collective-permute-start(bf16[32,2176]{1,0:T(8,128)(2,1)S(1)} %collective-permute-done.1.refs_3_), channel_id=1, source_target_pairs={{0,3},{2,1},{3,6},{7,2},{6,11},{10,7},{11,14},{15,10},{14,13},{12,... | collective-permute-start | bytes 417800 | tf_op jit(solution)/shard_map/ppermute | solution.py:398
  19.7 4.8 %collective-permute-start.11 = (bf16[32,2048]{1,0:T(8,128)(2,1)S(1)}, bf16[32,2048]{1,0:T(8,128)(2,1)S(1)}, u32[]{:S(2)}, u32[]{:S(2)}) collective-permute-start(bf16[32,2048]{1,0:T(8,128)(2,1)S(1)} %collective-permute-done.2.refs_4_), channel_id=1, source_target_pairs={{0,3},{2,1},{3,6},{7,2},{6,11},{10,7},{11,14},{15,10},{14,13},{12,... | collective-permute-start | bytes 393224 | tf_op jit(solution)/shard_map/ppermute | solution.py:400
  21.6 4.7 %collective-permute-start.13 = (bf16[32,2048]{1,0:T(8,128)(2,1)S(1)}, bf16[32,2048]{1,0:T(8,128)(2,1)S(1)}, u32[]{:S(2)}, u32[]{:S(2)}) collective-permute-start(bf16[32,2048]{1,0:T(8,128)(2,1)S(1)} %collective-permute-done.9.refs_0_), channel_id=1, source_target_pairs={{0,3},{2,1},{3,6},{7,2},{6,11},{10,7},{11,14},{15,10},{14,13},{12,... | collective-permute-start | bytes 393224 | tf_op jit(solution)/shard_map/ppermute | solution.py:398
  23.0 4.7 %collective-permute-start.14 = (bf16[32,2176]{1,0:T(8,128)(2,1)S(1)}, bf16[32,2176]{1,0:T(8,128)(2,1)S(1)}, u32[]{:S(2)}, u32[]{:S(2)}) collective-permute-start(bf16[32,2176]{1,0:T(8,128)(2,1)S(1)} %collective-permute-done.10.refs_1_), channel_id=1, source_target_pairs={{0,3},{2,1},{3,6},{7,2},{6,11},{10,7},{11,14},{15,10},{14,13},{12,... | collective-permute-start | bytes 417800 | tf_op jit(solution)/shard_map/ppermute | solution.py:398
  24.5 4.8 %collective-permute-start.12 = (bf16[32,2048]{1,0:T(8,128)(2,1)S(1)}, bf16[32,2048]{1,0:T(8,128)(2,1)S(1)}, u32[]{:S(2)}, u32[]{:S(2)}) collective-permute-start(bf16[32,2048]{1,0:T(8,128)(2,1)S(1)} %collective-permute-done.3.refs_5_), channel_id=1, source_target_pairs={{0,3},{2,1},{3,6},{7,2},{6,11},{10,7},{11,14},{15,10},{14,13},{12,... | collective-permute-start | bytes 393224 | tf_op jit(solution)/shard_map/ppermute | solution.py:400
  26.3 4.7 %collective-permute-start.17 = (bf16[32,2048]{1,0:T(8,128)(2,1)S(1)}, bf16[32,2048]{1,0:T(8,128)(2,1)S(1)}, u32[]{:S(2)}, u32[]{:S(2)}) collective-permute-start(bf16[32,2048]{1,0:T(8,128)(2,1)S(1)} %collective-permute-done.13.refs_0_), channel_id=1, source_target_pairs={{0,3},{2,1},{3,6},{7,2},{6,11},{10,7},{11,14},{15,10},{14,13},{12,... | collective-permute-start | bytes 393224 | tf_op jit(solution)/shard_map/ppermute | solution.py:398
  27.7 4.7 %collective-permute-start.18 = (bf16[32,2176]{1,0:T(8,128)(2,1)S(1)}, bf16[32,2176]{1,0:T(8,128)(2,1)S(1)}, u32[]{:S(2)}, u32[]{:S(2)}) collective-permute-start(bf16[32,2176]{1,0:T(8,128)(2,1)S(1)} %collective-permute-done.14.refs_1_), channel_id=1, source_target_pairs={{0,3},{2,1},{3,6},{7,2},{6,11},{10,7},{11,14},{15,10},{14,13},{12,... | collective-permute-start | bytes 417800 | tf_op jit(solution)/shard_map/ppermute | solution.py:398
  29.3 8.9 %collective-permute-start.15 = (bf16[32,2048]{1,0:T(8,128)(2,1)S(1)}, bf16[32,2048]{1,0:T(8,128)(2,1)S(1)}, u32[]{:S(2)}, u32[]{:S(2)}) collective-permute-start(bf16[32,2048]{1,0:T(8,128)(2,1)S(1)} %collective-permute-done.11.refs_2_), channel_id=1, source_target_pairs={{0,3},{2,1},{3,6},{7,2},{6,11},{10,7},{11,14},{15,10},{14,13},{12,... | collective-permute-start | bytes 393224 | tf_op jit(solution)/shard_map/ppermute | solution.py:400
  31.0 7.2 %collective-permute-start.16 = (bf16[32,2048]{1,0:T(8,128)(2,1)S(1)}, bf16[32,2048]{1,0:T(8,128)(2,1)S(1)}, u32[]{:S(2)}, u32[]{:S(2)}) collective-permute-start(bf16[32,2048]{1,0:T(8,128)(2,1)S(1)} %collective-permute-done.12.refs_3_), channel_id=1, source_target_pairs={{0,3},{2,1},{3,6},{7,2},{6,11},{10,7},{11,14},{15,10},{14,13},{12,... | collective-permute-start | bytes 393224 | tf_op jit(solution)/shard_map/ppermute | solution.py:400
  35.5 14.9 %collective-permute-start.19 = (bf16[32,2048]{1,0:T(8,128)(2,1)S(1)}, bf16[32,2048]{1,0:T(8,128)(2,1)S(1)}, u32[]{:S(2)}, u32[]{:S(2)}) collective-permute-start(bf16[32,2048]{1,0:T(8,128)(2,1)S(1)} %get-tuple-element.36), channel_id=1, source_target_pairs={{3,0},{1,2},{6,3},{2,7},{11,6},{7,10},{14,11},{10,15},{13,14},{15,... | collective-permute-start | bytes 393224 | tf_op jit(solution)/shard_map/ppermute | solution.py:438
  37.3 14.7 %collective-permute-start.23 = (bf16[32,2048]{1,0:T(8,128)(2,1)S(1)}, bf16[32,2048]{1,0:T(8,128)(2,1)S(1)}, u32[]{:S(2)}, u32[]{:S(2)}) collective-permute-start(bf16[32,2048]{1,0:T(8,128)(2,1)S(1)} %get-tuple-element.41), channel_id=1, source_target_pairs={{3,0},{1,2},{6,3},{2,7},{11,6},{7,10},{14,11},{10,15},{13,14},{15,... | collective-permute-start | bytes 393224 | tf_op jit(solution)/shard_map/ppermute | solution.py:438
  41.4 10.9 %collective-permute-start.27 = (bf16[32,2048]{1,0:T(8,128)(2,1)S(1)}, bf16[32,2048]{1,0:T(8,128)(2,1)S(1)}, u32[]{:S(2)}, u32[]{:S(2)}) collective-permute-start(bf16[32,2048]{1,0:T(8,128)(2,1)S(1)} %get-tuple-element.45), channel_id=1, source_target_pairs={{3,0},{1,2},{6,3},{2,7},{11,6},{7,10},{14,11},{10,15},{13,14},{15,... | collective-permute-start | bytes 393224 | tf_op jit(solution)/shard_map/ppermute | solution.py:430
  43.4 3.3 %copy-start = (bf16[32,2176]{1,0:T(8,128)(2,1)S(1)}, bf16[32,2176]{1,0:T(8,128)(2,1)}, u32[]{:S(2)}) copy-start(bf16[32,2176]{1,0:T(8,128)(2,1)} %get-tuple-element.28.refs_1_) | copy-start | bytes 417796
  43.5 3.3 %copy-start.1 = (bf16[32,2048]{1,0:T(8,128)(2,1)S(1)}, bf16[32,2048]{1,0:T(8,128)(2,1)}, u32[]{:S(2)}) copy-start(bf16[32,2048]{1,0:T(8,128)(2,1)} %get-tuple-element.27.refs_0_) | copy-start | bytes 393220
  43.5 9.4 %collective-permute-start.31 = (bf16[32,2048]{1,0:T(8,128)(2,1)S(1)}, bf16[32,2048]{1,0:T(8,128)(2,1)S(1)}, u32[]{:S(2)}, u32[]{:S(2)}) collective-permute-start(bf16[32,2048]{1,0:T(8,128)(2,1)S(1)} %get-tuple-element.48), channel_id=1, source_target_pairs={{3,0},{1,2},{6,3},{2,7},{11,6},{7,10},{14,11},{10,15},{13,14},{15,... | collective-permute-start | bytes 393224 | tf_op jit(solution)/shard_map/ppermute | solution.py:430
  50.5 4.4 %collective-permute-start.20 = (bf16[32,2048]{1,0:T(8,128)(2,1)S(1)}, bf16[32,2048]{1,0:T(8,128)(2,1)S(1)}, u32[]{:S(2)}, u32[]{:S(2)}) collective-permute-start(bf16[32,2048]{1,0:T(8,128)(2,1)S(1)} %add_convert_fusion.7), channel_id=1, source_target_pairs={{3,0},{1,2},{6,3},{2,7},{11,6},{7,10},{14,11},{10,15},{13,14},{15,... | collective-permute-start | bytes 393224 | tf_op jit(solution)/shard_map/ppermute | solution.py:438
  52.1 4.7 %collective-permute-start.24 = (bf16[32,2048]{1,0:T(8,128)(2,1)S(1)}, bf16[32,2048]{1,0:T(8,128)(2,1)S(1)}, u32[]{:S(2)}, u32[]{:S(2)}) collective-permute-start(bf16[32,2048]{1,0:T(8,128)(2,1)S(1)} %add_convert_fusion.5), channel_id=1, source_target_pairs={{3,0},{1,2},{6,3},{2,7},{11,6},{7,10},{14,11},{10,15},{13,14},{15,... | collective-permute-start | bytes 393224 | tf_op jit(solution)/shard_map/ppermute | solution.py:438
  52.3 5.9 %collective-permute-start.28 = (bf16[32,2048]{1,0:T(8,128)(2,1)S(1)}, bf16[32,2048]{1,0:T(8,128)(2,1)S(1)}, u32[]{:S(2)}, u32[]{:S(2)}) collective-permute-start(bf16[32,2048]{1,0:T(8,128)(2,1)S(1)} %add_convert_fusion.3), channel_id=1, source_target_pairs={{3,0},{1,2},{6,3},{2,7},{11,6},{7,10},{14,11},{10,15},{13,14},{15,... | collective-permute-start | bytes 393224 | tf_op jit(solution)/shard_map/ppermute | solution.py:430
  52.9 6.7 %collective-permute-start.32 = (bf16[32,2048]{1,0:T(8,128)(2,1)S(1)}, bf16[32,2048]{1,0:T(8,128)(2,1)S(1)}, u32[]{:S(2)}, u32[]{:S(2)}) collective-permute-start(bf16[32,2048]{1,0:T(8,128)(2,1)S(1)} %add_convert_fusion.1), channel_id=1, source_target_pairs={{3,0},{1,2},{6,3},{2,7},{11,6},{7,10},{14,11},{10,15},{13,14},{15,... | collective-permute-start | bytes 393224 | tf_op jit(solution)/shard_map/ppermute | solution.py:430
  54.9 6.1 %collective-permute-start.21 = (bf16[32,2048]{1,0:T(8,128)(2,1)S(1)}, bf16[32,2048]{1,0:T(8,128)(2,1)S(1)}, u32[]{:S(2)}, u32[]{:S(2)}) collective-permute-start(bf16[32,2048]{1,0:T(8,128)(2,1)S(1)} %add_convert_fusion.6), channel_id=1, source_target_pairs={{3,0},{1,2},{6,3},{2,7},{11,6},{7,10},{14,11},{10,15},{13,14},{15,... | collective-permute-start | bytes 393224 | tf_op jit(solution)/shard_map/ppermute | solution.py:445
  56.9 5.9 %collective-permute-start.25 = (bf16[32,2048]{1,0:T(8,128)(2,1)S(1)}, bf16[32,2048]{1,0:T(8,128)(2,1)S(1)}, u32[]{:S(2)}, u32[]{:S(2)}) collective-permute-start(bf16[32,2048]{1,0:T(8,128)(2,1)S(1)} %add_convert_fusion.4), channel_id=1, source_target_pairs={{3,0},{1,2},{6,3},{2,7},{11,6},{7,10},{14,11},{10,15},{13,14},{15,... | collective-permute-start | bytes 393224 | tf_op jit(solution)/shard_map/ppermute | solution.py:445
  58.3 5.6 %collective-permute-start.29 = (bf16[32,2048]{1,0:T(8,128)(2,1)S(1)}, bf16[32,2048]{1,0:T(8,128)(2,1)S(1)}, u32[]{:S(2)}, u32[]{:S(2)}) collective-permute-start(bf16[32,2048]{1,0:T(8,128)(2,1)S(1)} %add_convert_fusion.2), channel_id=1, source_target_pairs={{3,0},{1,2},{6,3},{2,7},{11,6},{7,10},{14,11},{10,15},{13,14},{15,... | collective-permute-start | bytes 393224 | tf_op jit(solution)/shard_map/ppermute | solution.py:430
  59.7 5.4 %collective-permute-start.33 = (bf16[32,2048]{1,0:T(8,128)(2,1)S(1)}, bf16[32,2048]{1,0:T(8,128)(2,1)S(1)}, u32[]{:S(2)}, u32[]{:S(2)}) collective-permute-start(bf16[32,2048]{1,0:T(8,128)(2,1)S(1)} %add_convert_fusion), channel_id=1, source_target_pairs={{3,0},{1,2},{6,3},{2,7},{11,6},{7,10},{14,11},{10,15},{13,14},{15,... | collective-permute-start | bytes 393224 | tf_op jit(solution)/shard_map/ppermute | solution.py:430
  61.0 5.5 %collective-permute-start.8 = (bf16[64,1024]{1,0:T(8,128)(2,1)S(1)}, bf16[64,1024]{1,0:T(8,128)(2,1)S(1)}, u32[]{:S(2)}, u32[]{:S(2)}) collective-permute-start(bf16[64,1024]{1,0:T(8,128)(2,1)S(1)} %get-tuple-element.32), channel_id=1, source_target_pairs={{0,1},{1,0},{2,3},{3,2},{4,5},{5,4},{6,7},{7,6},{8,9},{9,8},{10,11... | collective-permute-start | bytes 393224 | tf_op jit(solution)/shard_map/ppermute | solution.py:427
  61.1 5.9 %collective-permute-start.22 = (bf16[32,1024]{1,0:T(8,128)(2,1)S(1)}, bf16[32,1024]{1,0:T(8,128)(2,1)S(1)}, u32[]{:S(2)}, u32[]{:S(2)}) collective-permute-start(bf16[32,1024]{1,0:T(8,128)(2,1)S(1)} %get-tuple-element.37), channel_id=1, source_target_pairs={{3,0},{1,2},{6,3},{2,7},{11,6},{7,10},{14,11},{10,15},{13,14},{15,... | collective-permute-start | bytes 196616 | tf_op jit(solution)/shard_map/ppermute | solution.py:447
  62.8 5.7 %collective-permute-start.26 = (bf16[32,1024]{1,0:T(8,128)(2,1)S(1)}, bf16[32,1024]{1,0:T(8,128)(2,1)S(1)}, u32[]{:S(2)}, u32[]{:S(2)}) collective-permute-start(bf16[32,1024]{1,0:T(8,128)(2,1)S(1)} %get-tuple-element.42), channel_id=1, source_target_pairs={{3,0},{1,2},{6,3},{2,7},{11,6},{7,10},{14,11},{10,15},{13,14},{15,... | collective-permute-start | bytes 196616 | tf_op jit(solution)/shard_map/ppermute | solution.py:447
  63.9 4.7 %collective-permute-start.30 = (bf16[32,1024]{1,0:T(8,128)(2,1)S(1)}, bf16[32,1024]{1,0:T(8,128)(2,1)S(1)}, u32[]{:S(2)}, u32[]{:S(2)}) collective-permute-start(bf16[32,1024]{1,0:T(8,128)(2,1)S(1)} %shard_map.93), channel_id=1, source_target_pairs={{0,1},{1,0},{2,3},{3,2},{4,5},{5,4},{6,7},{7,6},{8,9},{9,8},{10,11... | collective-permute-start | bytes 196616 | tf_op jit(solution)/shard_map/ppermute | solution.py:436
  65.1 3.4 %collective-permute-start.34 = (bf16[32,1024]{1,0:T(8,128)(2,1)S(1)}, bf16[32,1024]{1,0:T(8,128)(2,1)S(1)}, u32[]{:S(2)}, u32[]{:S(2)}) collective-permute-start(bf16[32,1024]{1,0:T(8,128)(2,1)S(1)} %shard_map.94), channel_id=1, source_target_pairs={{0,1},{1,0},{2,3},{3,2},{4,5},{5,4},{6,7},{7,6},{8,9},{9,8},{10,11... | collective-permute-start | bytes 196616 | tf_op jit(solution)/shard_map/ppermute | solution.py:436
  66.5 4.3 %collective-permute-start.35 = (bf16[32,1024]{1,0:T(8,128)(2,1)S(1)}, bf16[32,1024]{1,0:T(8,128)(2,1)S(1)}, u32[]{:S(2)}, u32[]{:S(2)}) collective-permute-start(bf16[32,1024]{1,0:T(8,128)(2,1)S(1)} %get-tuple-element.49), channel_id=1, source_target_pairs={{3,1},{1,3},{6,2},{2,6},{11,7},{7,11},{14,10},{10,14},{13,15},{15,... | collective-permute-start | bytes 196616 | tf_op jit(solution)/shard_map/ppermute | solution.py:448
  67.0 4.5 %collective-permute-start.36 = (bf16[32,1024]{1,0:T(8,128)(2,1)S(1)}, bf16[32,1024]{1,0:T(8,128)(2,1)S(1)}, u32[]{:S(2)}, u32[]{:S(2)}) collective-permute-start(bf16[32,1024]{1,0:T(8,128)(2,1)S(1)} %get-tuple-element.50), channel_id=1, source_target_pairs={{3,1},{1,3},{6,2},{2,6},{11,7},{7,11},{14,10},{10,14},{13,15},{15,... | collective-permute-start | bytes 196616 | tf_op jit(solution)/shard_map/ppermute | solution.py:448
